TPU v7x, 32 devices: a whole 2x2x4 slice. The times are simulated.
32 devices in a mesh: seq: 16 (over z, y, core), head: 2 (over x).
Axes of the slice: x: 2, y: 2, z: 4, core: 2. Of those that a mesh axis runs over, the one named last changes fastest.
Arguments:
- attn_out: bfloat16 [2, 32, 64, 5120], P(None, 'seq', None, 'head'), may hold values from -40 to 40
- w_proj: bfloat16 [5120, 64], P('head'), may hold values from -0.078125 to 0.078125
- norm_gain: float32 [384], replicated, may hold values from 0.1 to 1.9
- entry_weight: bfloat16 [384, 3, 3, 3, 16], replicated, may hold values from -0.3125 to 0.3125
- conv_weight: bfloat16 [384, 3, 3, 3, 384], P('head'), may hold values from -0.0625 to 0.0625
- cotangent: bfloat16 [384, 2, 64, 128], P('head', None, 'seq'), may hold values from -0.09375 to 0.09375
Outputs:
- decoded: bfloat16 [384, 2, 64, 128], P('head', None, 'seq')
- weight_grad: float32 [384, 3, 3, 3, 384], P('head')
All inputs are finite; a program needn't handle non-finite values.
Results may differ from a plain program's by a relative error of at most 0.0058.
Values may be sent and summed in bfloat16 or wider, within the bound.
No kernel may reach another device: no remote copies, remote signals or barrier semaphores. Data moves between devices by JAX's collectives and lax.ppermute only.
A program may use at most 64 MiB of HBM per device.

v0:
```python
import jax
import jax.numpy as jnp
from jax import lax
from jax.sharding import PartitionSpec as P


def extended(cells, sides, width):
    for axis, dim in sides:
        count = lax.axis_size(axis)
        ends = count - 1
        head = lax.slice_in_dim(cells, 0, width, axis=dim)
        tail = lax.slice_in_dim(cells, cells.shape[dim] - width, cells.shape[dim], axis=dim)
        cells = jnp.concatenate(
            [
                lax.ppermute(tail, axis, [(i, (i + 1) % count) for i in range(ends)]),
                cells,
                lax.ppermute(head, axis, [((i + 1) % count, i) for i in range(ends)]),
            ],
            axis=dim,
        )
    return cells


def convolve_causal(inputs, weight):
    kernel = weight.transpose(0, 4, 1, 2, 3)
    result = lax.conv_general_dilated(
        inputs[None],
        kernel,
        (1, 1, 1),
        ((2, 0), (0, 0), (1, 1)),
        dimension_numbers=("NCDHW", "OIDHW", "NCDHW"),
        preferred_element_type=jnp.float32,
    )
    return result[0]


def activate(hidden, norm_gain):
    inverse_rms = lax.rsqrt(jnp.mean(hidden * hidden, axis=0, keepdims=True) + 1e-06)
    return jax.nn.silu(hidden * inverse_rms * norm_gain[:, None, None, None]).astype(jnp.bfloat16)


def unpatchify(latent_tokens, frames, tok_rows, tok_cols, latent_width):
    grid = latent_tokens.reshape(2, 2, latent_width, frames, tok_rows, tok_cols)
    grid = grid.transpose(2, 3, 4, 0, 5, 1)
    return grid.reshape(latent_width, frames, 2 * tok_rows, 2 * tok_cols)


def per_device(attn_out, w_proj, norm_gain, entry_weight, conv_weight, cotangent):
    frames, tok_rows, tok_cols, model_width = attn_out.shape
    latent_width = entry_weight.shape[4]
    channels = entry_weight.shape[0]
    out_channels = conv_weight.shape[0]
    token_count = frames * tok_rows * tok_cols
    flattened = attn_out.reshape(token_count, model_width)
    partial_sum = lax.dot_general(
        w_proj, flattened, (((0,), (1,)), ((), ())), preferred_element_type=jnp.float32
    )
    summed = lax.psum(partial_sum, "head")
    latent_tokens = summed.astype(jnp.bfloat16)
    latent = unpatchify(latent_tokens, frames, tok_rows, tok_cols, latent_width)
    heights = 2 * tok_rows
    widths = 2 * tok_cols
    latent_edge = extended(latent, (("seq", 2),), 1)
    local_act = activate(convolve_causal(latent_edge, entry_weight), norm_gain)
    widened = extended(local_act, (("seq", 2),), 1)
    decoded = convolve_causal(widened, conv_weight).astype(jnp.bfloat16)
    padded = jnp.pad(widened, ((0, 0), (2, 0), (0, 0), (1, 1)))
    upstream = cotangent.reshape(out_channels, frames * heights * widths)
    tap_grads = []
    for kernel_tap in range(27):
        depth_tap = kernel_tap // 9
        row_tap = kernel_tap // 3 % 3
        col_tap = kernel_tap % 3
        window = padded[
            :,
            depth_tap : depth_tap + frames,
            row_tap : row_tap + heights,
            col_tap : col_tap + widths,
        ].reshape(channels, -1)
        tap_grads.append(
            lax.dot_general(
                upstream, window, (((1,), (1,)), ((), ())), preferred_element_type=jnp.float32
            )
        )
    local_grad = jnp.stack(tap_grads, axis=1)
    weight_grad = lax.psum(local_grad, "seq").reshape(conv_weight.shape)
    return (decoded, weight_grad)


def solution(mesh):
    return jax.shard_map(
        per_device,
        mesh=mesh,
        in_specs=(
            P(None, "seq", None, "head"),
            P("head", None),
            P(),
            P(),
            P("head", None, None, None, None),
            P("head", None, "seq", None),
        ),
        out_specs=(P("head", None, "seq", None), P("head", None, None, None, None)),
        check_vma=False,
    )
```

profile of v0, /device:TPU:0, one launch (start us, length us, event | category | flops | bytes accessed | tf_op | source)
XLA Modules:
  0.0 250.4 jit_solution(3661700527586619339)
XLA Ops:
  7.2 1.3 copy-done
  8.5 1.5 fusion.95
  10.0 10.5 %psum.14 = bf16[64,256]{1,0:T(8,128)(2,1)S(1)} all-reduce(f32[64,256]{1,0:T(8,128)S(1)} %fusion.95), channel_id=1, replica_groups=mesh['seq'=16,'head'=2] {'head'}, use_global_device_ids=true, to_apply=%region_0.0 | all-reduce | flops 16384 | bytes 98304 | tf_op jit(solution)/shard_map/psum | solution.py:58
  20.8 1.3 collective-permute-start
  22.1 1.3 collective-permute-start.1
  23.4 1.3 reshape.28
  24.7 1.1 constant_dynamic-update-slice_fusion.8
  25.7 0.7 constant_dynamic-update-slice_fusion.7
  26.5 0.7 constant_dynamic-update-slice_fusion.6
  27.2 0.7 constant_dynamic-update-slice_fusion.5
  27.9 0.7 constant_dynamic-update-slice_fusion.4
  28.7 0.7 constant_dynamic-update-slice_fusion.3
  29.4 0.7 constant_dynamic-update-slice_fusion.2
  30.9 0.7 copy.60
  31.6 1.4 convolution_select_fusion
  33.1 0.4 copy.61
  33.5 1.4 slice.106
  35.0 1.7 copy.104
  36.8 0.5 multiply_convert_fusion
  37.4 4.6 %collective-permute-start.2 = (bf16[384,2,1,128]{3,0,2,1:T(8,128)(2,1)S(1)}, bf16[384,2,1,128]{3,0,2,1:T(8,128)(2,1)S(1)}, u32[]{:S(2)}, u32[]{:S(2)}) collective-permute-start(bf16[384,2,1,128]{3,0,2,1:T(8,128)(2,1)S(1)} %get-tuple-element.8), channel_id=1, source_target_pairs={{0,2},{2,4},{4,6},{6,8},{8,10},{10,12},{12,14},{14,16},{16,18},{18... | collective-permute-start | bytes 589832 | tf_op jit(solution)/shard_map/ppermute | solution.py:15
  42.0 1.3 collective-permute-start.3
  43.3 0.7 constant_dynamic-update-slice_fusion.1
  44.1 0.7 constant_dynamic-update-slice_fusion
  44.8 1.8 collective-permute-done.3
  46.8 1.1 fusion.31
  47.9 1.1 fusion.30
  49.0 1.1 fusion.29
  50.1 1.1 fusion.28
  51.2 1.1 fusion.27
  52.3 1.1 fusion.26
  53.4 1.1 fusion.25
  54.5 1.1 fusion.24
  55.6 1.1 fusion.23
  56.7 1.3 fusion.22
  58.0 1.2 fusion.33
  59.1 1.3 fusion.21
  60.4 1.3 fusion.20
  61.6 1.2 fusion.19
  62.8 1.3 fusion.18
  64.1 1.3 fusion.17
  65.3 1.2 fusion.32
  66.5 1.3 fusion.16
  67.7 3.0 %copy.105 = bf16[384,2,6,1,128]{0,1,4,2,3:T(2,128)(2,1)} copy(bf16[384,2,6,1,128]{4,0,2,1,3:T(8,128)(2,1)S(1)} %get-tuple-element.7) | data formatting | bytes 2359296
  70.7 2.4 pad.7.clone
  73.3 6.1 %fusion.13 = bf16[2,4,8,17,192]{4,2,3,1,0:T(8,128)(2,1)S(1)} fusion(bf16[192,3,3,3,384]{4,0,3,2,1:T(8,128)(2,1)S(1)} %copy-done.3, bf16[384,2,6,1,7,2]{0,4,5,2,1,3:T(8,128)(2,1)S(1)} %slice.109, bf16[384,2,6,1,8,17]{0,4,5,2,1,3:T(8,128)(2,1)S(1)} %copy.65, pred[8,17]{0,1:T(8,128)(4,1)S(1)} %copy-done.5), kind=kOutput, calls=%fused_computation.30 | convolution fusion | flops 2170454016 | bytes 5781640 | tf_op jit(solution)/shard_map/conv_general_dilated | solution.py:26
  79.8 1.1 copy.85
  81.0 155.2 %all-reduce.3.cloned.1.call-done = f32[192,3,3,3,384]{4,0,3,2,1:T(8,128)} async-done(((f32[192,3,3,3,384]{4,0,3,2,1:T(8,128)}), f32[192,3,3,3,384]{4,0,3,2,1:T(8,128)}) %all-reduce.3.cloned.1.call-update) | async-done | bytes 7962640 | tf_op jit(solution)/shard_map/psum | solution.py:86
  236.1 7.4 %copy.169 = f32[192,3,3,3,384]{4,0,3,2,1:T(8,128)} copy(f32[192,3,3,3,384]{4,0,3,2,1:T(8,128)} %all-reduce.3.cloned.1.call-done) | data formatting | bytes 15925248
  (34 shorter events, 2.0 us)
Async XLA Ops:
  7.2 1.3 copy-start
  7.2 229.0 %all-reduce.3.cloned.1.call-start = ((), (), s32[]{:S(2)}) async-start(), calls=%async_computation | async-start | bytes 15925248 | tf_op jit(solution)/shard_map/psum | solution.py:86
  8.5 23.1 %copy-start.4 = (bf16[384,3,3,3,16]{0,4,3,2,1:T(8,128)(2,1)S(1)}, bf16[384,3,3,3,16]{0,4,3,2,1:T(8,128)(2,1)}, u32[]{:S(2)}) copy-start(bf16[384,3,3,3,16]{0,4,3,2,1:T(8,128)(2,1)} %param.9) | copy-start | bytes 995332
  8.5 23.1 %copy-start.5 = (pred[8,17]{0,1:T(8,128)(4,1)S(1)}, pred[8,17]{0,1:T(8,128)(4,1)}, u32[]{:S(2)}) copy-start(pred[8,17]{0,1:T(8,128)(4,1)} %constant.25) | copy-start | bytes 412
  20.8 9.4 %collective-permute-start = (bf16[16,2,1,128]{0,3,2,1:T(8,128)(2,1)S(1)}, bf16[16,2,1,128]{0,3,2,1:T(8,128)(2,1)S(1)}, u32[]{:S(2)}, u32[]{:S(2)}) collective-permute-start(bf16[16,2,1,128]{0,3,2,1:T(8,128)(2,1)S(1)} %get-tuple-element.10), channel_id=1, source_target_pairs={{0,2},{2,4},{4,6},{6,8},{8,10},{10,12},{12,14},{14,16},{16,18},{18... | collective-permute-start | bytes 24584 | tf_op jit(solution)/shard_map/ppermute | solution.py:15
  22.1 8.2 %collective-permute-start.1 = (bf16[16,2,1,128]{0,3,2,1:T(8,128)(2,1)S(1)}, bf16[16,2,1,128]{0,3,2,1:T(8,128)(2,1)S(1)}, u32[]{:S(2)}, u32[]{:S(2)}) collective-permute-start(bf16[16,2,1,128]{0,3,2,1:T(8,128)(2,1)S(1)} %get-tuple-element.11), channel_id=1, source_target_pairs={{2,0},{4,2},{6,4},{8,6},{10,8},{12,10},{14,12},{16,14},{18,16},{20... | collective-permute-start | bytes 24584 | tf_op jit(solution)/shard_map/ppermute | solution.py:17
  33.5 3.3 %copy-start.2 = (f32[384]{0:T(512)S(1)}, f32[384]{0:T(512)}, u32[]{:S(2)}) copy-start(f32[384]{0:T(512)} %param.8) | copy-start | bytes 4612
  36.7 10.1 %copy-start.1 = (bf16[192,2,4,128]{3,2,1,0:T(4,128)(2,1)S(1)}, bf16[192,2,4,128]{3,2,1,0:T(4,128)(2,1)}, u32[]{:S(2)}) copy-start(bf16[192,2,4,128]{3,2,1,0:T(4,128)(2,1)} %param.11) | copy-start | bytes 1179652
  37.4 7.4 %collective-permute-start.2 = (bf16[384,2,1,128]{3,0,2,1:T(8,128)(2,1)S(1)}, bf16[384,2,1,128]{3,0,2,1:T(8,128)(2,1)S(1)}, u32[]{:S(2)}, u32[]{:S(2)}) collective-permute-start(bf16[384,2,1,128]{3,0,2,1:T(8,128)(2,1)S(1)} %get-tuple-element.8), channel_id=1, source_target_pairs={{0,2},{2,4},{4,6},{6,8},{8,10},{10,12},{12,14},{14,16},{16,18},{18... | collective-permute-start | bytes 589832 | tf_op jit(solution)/shard_map/ppermute | solution.py:15
  42.0 4.6 %collective-permute-start.3 = (bf16[384,2,1,128]{3,0,2,1:T(8,128)(2,1)S(1)}, bf16[384,2,1,128]{3,0,2,1:T(8,128)(2,1)S(1)}, u32[]{:S(2)}, u32[]{:S(2)}) collective-permute-start(bf16[384,2,1,128]{3,0,2,1:T(8,128)(2,1)S(1)} %get-tuple-element.9), channel_id=1, source_target_pairs={{2,0},{4,2},{6,4},{8,6},{10,8},{12,10},{14,12},{16,14},{18,16},{20... | collective-permute-start | bytes 589832 | tf_op jit(solution)/shard_map/ppermute | solution.py:17
  70.7 2.6 %copy-start.3 = (bf16[192,3,3,3,384]{4,0,3,2,1:T(8,128)(2,1)S(1)}, bf16[192,3,3,3,384]{4,0,3,2,1:T(8,128)(2,1)}, u32[]{:S(2)}) copy-start(bf16[192,3,3,3,384]{4,0,3,2,1:T(8,128)(2,1)} %param.10) | copy-start | bytes 11943940
Sparse Core Ops, SparseCore 0:
  67.9 168.2 all-reduce.2
where the time goes:
time: 251 us; the launch traced here: 250 us
  waiting for transfers between devices  157 us (63%)
  matrix products  31 us (12%)
  local copies, waits for them, and re-layouts  28.1 us (11%)
  between operations  14.3 us (6%)
  blocking collectives  10.5 us (4%)
  starting transfers between devices  8.56 us (3%)
    psum x1, waiting for transfers between devices, per_device(): weight_grad = lax.psum(local_grad, 'seq').reshape(conv_weight.shape)  155 us
    dot_general x19, matrix products, per_device(): lax.dot_general(upstream, window, (((1,), (1,)), ((), ())), preferred_ele...  22 us
    unnamed x24, local copies, waits for them, and re-layouts  20.3 us
    psum x1, blocking collectives, per_device(): summed = lax.psum(partial_sum, 'head')  10.5 us
    conv_general_dilated x2, matrix products, convolve_causal(): lax.conv_general_dilated(inputs[None], kernel, (1, 1, 1), ((2, 0), (0, 0)...  7.53 us
    ppermute x2, starting transfers between devices, extended(): lax.ppermute(tail, axis, [(i, (i + 1) % count) for i in range(ends)])  5.93 us
  transfers between devices with their start and end apart: 5, of which 2 were waited for; matrix products, arithmetic and copies ran while one was open for 9% of the time, Pallas kernels for 0%

commit v1 on v0

v1 whole, which is shorter than its diff:
```python
import functools

import jax
import jax.numpy as jnp
from jax import lax
from jax.experimental import pallas as pl
from jax.experimental.pallas import tpu as pltpu
from jax.sharding import PartitionSpec as P

LANES = 128
VMEM_LIMIT = 56 * 1024 * 1024
F32 = jnp.float32
BF16 = jnp.bfloat16


def params():
    return pltpu.CompilerParams(vmem_limit_bytes=VMEM_LIMIT)


def vmem():
    return pl.BlockSpec(memory_space=pltpu.VMEM)


def smem():
    return pl.BlockSpec(memory_space=pltpu.SMEM)


def xor_permute(x, axis, mask):
    return lax.ppermute(x, axis, [(i, i ^ mask) for i in range(lax.axis_size(axis))])


def dot(a, b):
    return lax.dot_general(a, b, (((1,), (0,)), ((), ())), preferred_element_type=F32)


def dot_t(a, b):
    return lax.dot_general(a, b, (((1,), (1,)), ((), ())), preferred_element_type=F32)


def unpatchify_kernel(frames, tok_rows, tok_cols, own_ref, other_ref, out_ref):
    latent_width = out_ref.shape[0]
    features = (own_ref[...] + other_ref[...]).astype(BF16)
    width = 2 * tok_cols
    span = tok_rows * tok_cols
    source = lax.broadcasted_iota(jnp.int32, (span, tok_rows * width), 0)
    target = lax.broadcasted_iota(jnp.int32, (span, tok_rows * width), 1)
    same_row = source // tok_cols == target // width
    column = source % tok_cols
    even = (same_row & (target % width == 2 * column)).astype(BF16)
    odd = (same_row & (target % width == 2 * column + 1)).astype(BF16)
    for frame in range(frames):
        tokens = features[:, frame * span : (frame + 1) * span]
        left = dot(tokens, even)
        right = dot(tokens, odd)
        for row in range(tok_rows):
            cols = slice(row * width, (row + 1) * width)
            for half in range(2):
                base = half * 2 * latent_width
                cells = (
                    left[base : base + latent_width, cols]
                    + right[base + latent_width : base + 2 * latent_width, cols]
                )
                at = (frame * 2 * tok_rows + 2 * row + half) * width
                out_ref[:, at : at + width] = cells.astype(BF16)


def shifted(tile, shift):
    if shift == 1:
        return tile
    lane = lax.broadcasted_iota(jnp.int32, tile.shape, 1)
    if shift == 0:
        return jnp.where(lane == 0, 0.0, pltpu.roll(tile, 1, 1))
    return jnp.where(lane == LANES - 1, 0.0, pltpu.roll(tile, LANES - 1, 1))


def place_latent(lat_ref, stack_ref, me, masks, frames, rows):
    latent_width = lat_ref.shape[1]
    total = stack_ref.shape[2]
    zeros = jnp.zeros((stack_ref.shape[1], 2 * LANES), BF16)
    for frame in range(frames):
        stack_ref[frame, :, 0 : 2 * LANES] = zeros
        stack_ref[frame, :, total - 2 * LANES : total] = zeros
    for index, mask in enumerate(masks):
        slab = me ^ mask
        for frame in range(frames):
            for row in range(rows):
                at = (frame * rows + row) * LANES
                tile = lat_ref[index, :, at : at + LANES].astype(F32)
                to = pl.multiple_of((slab * rows + row + 2) * LANES, LANES)
                for shift in range(3):
                    stack_ref[
                        frame,
                        shift * latent_width : (shift + 1) * latent_width,
                        pl.ds(to, LANES),
                    ] = shifted(tile, shift).astype(BF16)


def activation(stack_ref, weight_refs, gain, frame, first, count, height):
    pieces = []
    for source in range(max(0, frame - 2), frame + 1):
        for row_tap in range(3):
            at = pl.multiple_of((first + row_tap) * LANES, LANES)
            pieces.append(stack_ref[source, :, pl.ds(at, count * LANES)])
    patches = jnp.concatenate(pieces, axis=0)
    hidden = dot(weight_refs[frame][...], patches)
    mean = jnp.sum(hidden * hidden, axis=0, keepdims=True) * (1.0 / hidden.shape[0])
    row = first - 1 + lax.broadcasted_iota(jnp.int32, mean.shape, 1) // LANES
    inside = (row >= 0) & (row < height)
    inverse = jnp.where(inside, lax.rsqrt(mean + 1e-6), 0.0)
    half = hidden * inverse * (0.5 * gain)
    return (half + half * jnp.tanh(half)).astype(BF16)


def cotangent_kernel(
    frames, rows, half_rows, chips, pad_channels, me_ref, own_ref, other_ref, out_ref, flat_ref
):
    me = me_ref[0]
    first_slab = (me & 1) * (half_rows // rows)
    channels = own_ref.shape[1]
    group = 3 * pad_channels
    padded = -(-3 * group // 16) * 16
    lanes = (half_rows + 2) * LANES
    for frame in range(frames):
        for edge in (0, half_rows + 2):
            flat_ref[frame, :, edge * LANES : (edge + 2) * LANES] = jnp.zeros((group, 2 * LANES), F32)
    for index in range(half_rows // rows):
        relative = (first_slab + index) ^ me
        chip = relative >> 1
        core = relative & 1
        block = jnp.where(core == 0, own_ref[chip].astype(F32), other_ref[chip].astype(F32))
        for frame in range(frames):
            for row in range(rows):
                at = (frame * rows + row) * LANES
                tile = block[:, at : at + LANES]
                if pad_channels != channels:
                    tile = jnp.concatenate(
                        [tile, jnp.zeros((pad_channels - channels, LANES), F32)], axis=0
                    )
                to = (index * rows + row + 2) * LANES
                for tap in range(3):
                    flat_ref[frame, tap * pad_channels : (tap + 1) * pad_channels, to : to + LANES] = (
                        shifted(tile, 2 - tap)
                    )
    filler = [jnp.zeros((padded - 3 * group, LANES), F32)] if padded != 3 * group else []
    for frame in range(frames):
        for row in range(half_rows + 2):
            taps = [flat_ref[frame, :, (row + 2 - tap) * LANES : (row + 3 - tap) * LANES] for tap in range(3)]
            out_ref[frame * padded : (frame + 1) * padded, row * LANES : (row + 1) * LANES] = (
                jnp.concatenate(taps + filler, axis=0).astype(BF16)
            )


def gradient_kernel(
    frames, rows, half_rows, height, masks, real_rows, step_rows,
    me_ref, lat_ref, cot_ref, gain_ref, *refs,
):
    weight_refs = refs[:frames]
    keep_ref, send_ref, stack_ref, act_ref, sum_ref = refs[frames:]
    me = me_ref[0]
    core = me & 1
    place_latent(lat_ref, stack_ref, me, masks, frames, rows)
    gain = gain_ref[...]
    padded = cot_ref.shape[0] // frames
    start = core * half_rows
    steps = (half_rows + 2) // step_rows
    width = step_rows * LANES
    sum_ref[...] = jnp.zeros_like(sum_ref)
    for frame in range(frames):

        def fill(step, carry):
            at = pl.multiple_of(step * width, LANES)
            act_ref[:, pl.ds(at, width)] = activation(
                stack_ref, weight_refs, gain, frame, start + step * step_rows, step_rows, height
            )
            return carry

        lax.fori_loop(0, steps, fill, 0)
        last = min(frames, frame + 3)
        count = (last - frame) * padded

        def add(step, carry):
            at = pl.multiple_of(step * width, LANES)
            sum_ref[0:count, :] += dot_t(
                cot_ref[frame * padded : last * padded, pl.ds(at, width)],
                act_ref[:, pl.ds(at, width)],
            )
            return carry

        lax.fori_loop(0, steps, add, 0)
    keep_at = pl.multiple_of(core * padded, 16)
    send_at = pl.multiple_of((1 - core) * padded, 16)
    keep_ref[...] = sum_ref[pl.ds(keep_at, padded), :][:real_rows]
    send_ref[...] = sum_ref[pl.ds(send_at, padded), :][:real_rows].astype(BF16)


def decode_kernel(frames, rows, height, masks, me_ref, lat_ref, gain_ref, conv_ref, *refs):
    weight_refs = refs[:frames]
    out_ref, stack_ref, act_ref = refs[frames:]
    me = me_ref[0]
    place_latent(lat_ref, stack_ref, me, masks, frames, rows)
    gain = gain_ref[...]
    live = min(3, frames)
    ext = rows + 2
    for frame in range(frames):
        act = activation(stack_ref, weight_refs, gain, frame, me * rows, ext, height)
        for row in range(ext):
            tile = act[:, row * LANES : (row + 1) * LANES].astype(F32)
            for tap in range(3):
                act_ref[frame, tap, :, row * LANES : (row + 1) * LANES] = shifted(tile, tap).astype(BF16)
    for frame in range(frames):
        total = None
        for depth in range(max(0, 2 - frame), 3):
            source = frame + depth - 2
            for row_tap in range(3):
                for col_tap in range(3):
                    term = dot(
                        conv_ref[(depth - (3 - live)) * 9 + row_tap * 3 + col_tap],
                        act_ref[source, col_tap, :, row_tap * LANES : (row_tap + rows) * LANES],
                    )
                    total = term if total is None else total + term
        out_ref[:, frame * rows * LANES : (frame + 1) * rows * LANES] = total.astype(BF16)


def finish_kernel(live, masks, channels, me_ref, *refs):
    block_refs = refs[:-1]
    out_ref = refs[-1]
    me = me_ref[0]
    chip = me >> 1
    core = me & 1
    depth = pl.program_id(0)
    plane = 2 - depth

    @pl.when(depth < 3 - live)
    def _():
        out_ref[...] = jnp.zeros_like(out_ref)

    @pl.when(depth >= 3 - live)
    def _():
        for index, mask in enumerate(masks):
            at = pl.multiple_of((chip ^ mask) * channels, 8)
            mine = block_refs[0]
            other = block_refs[1]
            for tap in range(out_ref.shape[1]):

                @pl.when(plane == core)
                def _():
                    out_ref[0, tap, pl.ds(at, channels), :] = mine[index, tap].astype(F32)

                @pl.when(plane != core)
                def _():
                    out_ref[0, tap, pl.ds(at, channels), :] = other[index, tap].astype(F32)


def per_device(attn_out, w_proj, norm_gain, entry_weight, conv_weight, cotangent):
    frames, tok_rows, tok_cols, model_width = attn_out.shape
    latent_width = entry_weight.shape[4]
    channels = entry_weight.shape[0]
    out_channels = conv_weight.shape[0]
    slabs = lax.axis_size("seq")
    heads = lax.axis_size("head")
    chips = slabs // 2
    rows = 2 * tok_rows
    width = 2 * tok_cols
    height = rows * slabs
    half_rows = height // 2
    chip_channels = out_channels // chips
    pad_channels = -(-chip_channels // 8) * 8
    real_rows = 9 * pad_channels
    live = min(3, frames)
    me_index = lax.axis_index("seq")
    me = me_index.astype(jnp.int32).reshape(1)
    chip_bits = [b for b in (4, 8, 16, 32, 64, 128) if b < slabs] + [2]

    flat = cotangent.reshape(chips, chip_channels, frames * rows * width)
    chip = me_index // 2
    relative = jnp.stack(
        [lax.dynamic_index_in_dim(flat, chip ^ d, 0, keepdims=False) for d in range(chips)]
    )
    pieces = {(d, 0): relative[d] for d in range(chips)}
    for bit in chip_bits:
        step = bit // 2
        sends = sorted(k for k in pieces if k[0] & step)
        got = xor_permute(jnp.stack([pieces[k] for k in sends]), "seq", bit)
        kept = {k: v for k, v in pieces.items() if not k[0] & step}
        for position, (d, s) in enumerate(sends):
            kept[(d ^ step, s ^ step)] = got[position]
        pieces = kept
    own_cot = jnp.stack([pieces[(0, s)] for s in range(chips)])
    other_cot = xor_permute(own_cot, "seq", 1)
    padded = -(-real_rows // 16) * 16
    lanes = (half_rows + 2) * width
    cot = pl.pallas_call(
        functools.partial(cotangent_kernel, frames, rows, half_rows, chips, pad_channels),
        out_shape=jax.ShapeDtypeStruct((frames * padded, lanes), BF16),
        in_specs=[smem(), vmem(), vmem()],
        out_specs=vmem(),
        scratch_shapes=[pltpu.VMEM((frames, 3 * pad_channels, (half_rows + 4) * width), F32)],
        compiler_params=params(),
        name="cotangent",
    )(me, own_cot, other_cot)

    flattened = attn_out.reshape(frames * tok_rows * tok_cols, model_width)
    partial_sum = lax.dot_general(
        w_proj, flattened, (((0,), (1,)), ((), ())), preferred_element_type=F32
    )
    step = heads // 2
    other = jnp.zeros_like(partial_sum)
    while step >= 1:
        other = xor_permute(partial_sum, "head", step)
        if step > 1:
            partial_sum = partial_sum + other
        step //= 2
    latent = pl.pallas_call(
        functools.partial(unpatchify_kernel, frames, tok_rows, tok_cols),
        out_shape=jax.ShapeDtypeStruct((latent_width, frames * rows * width), BF16),
        in_specs=[vmem(), vmem()],
        out_specs=vmem(),
        compiler_params=params(),
        name="unpatchify",
    )(partial_sum, other)

    masks = [0]
    gathered = latent[None]
    for bit in chip_bits + [1]:
        gathered = jnp.concatenate([gathered, xor_permute(gathered, "seq", bit)], axis=0)
        masks = masks + [m ^ bit for m in masks]

    entry = entry_weight.reshape(channels, 3, 9 * latent_width)
    entries = [
        entry[:, max(0, 2 - f) :].reshape(channels, -1) for f in range(frames)
    ]
    gain = norm_gain.reshape(channels, 1)
    step_rows = 2
    keep, send = pl.pallas_call(
        functools.partial(
            gradient_kernel, frames, rows, half_rows, height, masks, real_rows, step_rows
        ),
        out_shape=(
            jax.ShapeDtypeStruct((real_rows, channels), F32),
            jax.ShapeDtypeStruct((real_rows, channels), BF16),
        ),
        in_specs=[smem(), vmem(), vmem(), vmem()] + [vmem()] * frames,
        out_specs=(vmem(), vmem()),
        scratch_shapes=[
            pltpu.VMEM((frames, 3 * latent_width, (height + 4) * width), BF16),
            pltpu.VMEM((channels, lanes), BF16),
            pltpu.VMEM((live * padded, channels), F32),
        ],
        compiler_params=params(),
        name="gradient",
    )(me, gathered, cot, gain, *entries)

    block = (keep + xor_permute(send, "seq", 1).astype(F32)).astype(BF16)

    far = [b for b in chip_bits if b != 2]
    far_masks = [0]
    for b in far:
        far_masks = far_masks + [m ^ b for m in far_masks]
    parts = [block] + [xor_permute(block, "seq", m) for m in far_masks[1:]]
    mine = jnp.stack(parts + [xor_permute(p, "seq", 2) for p in parts])
    chip_masks = [m // 2 for m in far_masks] + [(m ^ 2) // 2 for m in far_masks]
    theirs = xor_permute(mine, "seq", 1)
    shape = (chips, 9, pad_channels, channels)

    conv = conv_weight.transpose(1, 2, 3, 0, 4).reshape(27, out_channels, channels)
    decoded = pl.pallas_call(
        functools.partial(decode_kernel, frames, rows, height, masks),
        grid=(1,),
        out_shape=jax.ShapeDtypeStruct((out_channels, frames * rows * width), BF16),
        in_specs=[smem(), vmem(), vmem(), vmem()] + [vmem()] * frames,
        out_specs=vmem(),
        scratch_shapes=[
            pltpu.VMEM((frames, 3 * latent_width, (height + 4) * width), BF16),
            pltpu.VMEM((frames, 3, channels, (rows + 2) * width), BF16),
        ],
        compiler_params=params(),
        name="decode",
    )(me, gathered, gain, conv[(3 - live) * 9 :], *entries)

    grad = pl.pallas_call(
        functools.partial(finish_kernel, live, chip_masks, pad_channels),
        grid=(3, 3),
        out_shape=jax.ShapeDtypeStruct((3, 9, chips * pad_channels, channels), F32),
        in_specs=[smem()]
        + [
            pl.BlockSpec((chips, 3, pad_channels, channels), lambda a, b: (0, b, 0, 0)),
            pl.BlockSpec((chips, 3, pad_channels, channels), lambda a, b: (0, b, 0, 0)),
        ],
        out_specs=pl.BlockSpec((1, 3, chips * pad_channels, channels), lambda a, b: (a, b, 0, 0)),
        compiler_params=params(),
        name="finish",
    )(me, mine.reshape(shape), theirs.reshape(shape))
    if pad_channels != chip_channels:
        grad = grad.reshape(27, chips, pad_channels, channels)[:, :, :chip_channels]
    grad = grad.reshape(3, 3, 3, out_channels, channels).transpose(3, 0, 1, 2, 4)
    return decoded.reshape(out_channels, frames, rows, width), grad


def solution(mesh):
    return jax.shard_map(
        per_device,
        mesh=mesh,
        in_specs=(
            P(None, "seq", None, "head"),
            P("head", None),
            P(),
            P(),
            P("head", None, None, None, None),
            P("head", None, "seq", None),
        ),
        out_specs=(P("head", None, "seq", None), P("head", None, None, None, None)),
        check_vma=False,
    )
```

time: 251 us -> 123 us (0.49)
  waiting for transfers between devices: 157 us -> 30.6 us
  Pallas kernels: 0 us -> 47.4 us
  matrix products: 31 us -> 0.51 us
  starting transfers between devices: 8.56 us -> 23.1 us
  between operations: 14.3 us -> 1.07 us
  local copies, waits for them, and re-layouts: 28.1 us -> 16.8 us
  blocking collectives: 10.5 us -> 0 us
    psum x1 -> x0, waiting for transfers between devices: 155 us -> none  [per_device(): weight_grad = lax.psum(local_grad, 'seq').reshape(conv_weight.shape)]
    pallas_call x0 -> x5, Pallas kernels: none -> 47.4 us  [the longest x1 24.7 us: per_device(): pl.pallas_call(functools.partial(gradient_kernel, frames, rows, half_rows...]
    ppermute x4 -> x18, waiting for transfers between devices: 1.8 us -> 30.6 us  [xor_permute(): lax.ppermute(x, axis, [(i, i ^ mask) for i in range(lax.axis_size(axis))])]
    dot_general x19 -> x0, matrix products: 22 us -> none  [per_device(): lax.dot_general(upstream, window, (((1,), (1,)), ((), ())), preferred_ele...]
    ppermute x4 -> x18, starting transfers between devices: 8.52 us -> 23.1 us  [xor_permute(): lax.ppermute(x, axis, [(i, i ^ mask) for i in range(lax.axis_size(axis))])]
    unnamed x24 -> x60, local copies, waits for them, and re-layouts: 20.3 us -> 9.13 us
    psum x1 -> x0, blocking collectives: 10.5 us -> none  [per_device(): summed = lax.psum(partial_sum, 'head')]
    conv_general_dilated x2 -> x0, matrix products: 7.53 us -> none  [convolve_causal(): lax.conv_general_dilated(inputs[None], kernel, (1, 1, 1), ((2, 0), (0, 0)...]
  transfers between devices with their start and end apart: 5 -> 18, of which waited for: 2 -> 10; matrix products, arithmetic and copies ran while one was open for 9% -> 11% of each run, Pallas kernels for 0% -> 7%
where the time goes in v1:
time: 123 us; the launch traced here: 122 us
  Pallas kernels  47.4 us (39%)
  waiting for transfers between devices  30.6 us (25%)
  starting transfers between devices  23.1 us (19%)
  local copies, waits for them, and re-layouts  16.8 us (14%)
  other arithmetic  2.56 us (2%)
    ppermute x18, waiting for transfers between devices, xor_permute(): lax.ppermute(x, axis, [(i, i ^ mask) for i in range(lax.axis_size(axis))])  30.6 us
    pallas_call x1, Pallas kernels, per_device(): pl.pallas_call(functools.partial(gradient_kernel, frames, rows, half_rows...  24.7 us
    ppermute x18, starting transfers between devices, xor_permute(): lax.ppermute(x, axis, [(i, i ^ mask) for i in range(lax.axis_size(axis))])  23.1 us
    pallas_call x1, Pallas kernels, per_device(): pl.pallas_call(functools.partial(finish_kernel, live, chip_masks, pad_cha...  10.1 us
    unnamed x60, local copies, waits for them, and re-layouts  9.13 us
    pallas_call x1, Pallas kernels, per_device(): pl.pallas_call(functools.partial(decode_kernel, frames, rows, height, mas...  7.38 us
    pallas_call x1, Pallas kernels, per_device(): pl.pallas_call(functools.partial(cotangent_kernel, frames, rows, half_row...  3.53 us
  transfers between devices with their start and end apart: 18, of which 10 were waited for; matrix products, arithmetic and copies ran while one was open for 11% of the time, Pallas kernels for 7%

profile of v1, /device:TPU:0, one launch (start us, length us, event | category | flops | bytes accessed | tf_op | source)
XLA Modules:
  0.0 122.0 jit_solution(11080157518033954366)
XLA Ops:
  0.7 1.4 %reshape.60 = bf16[8,24,1024]{2,1,0:T(8,128)(2,1)S(1)} reshape(bf16[192,2,4,128]{3,2,1,0:T(4,128)(2,1)} %param.11) | data formatting | bytes 786432 | tf_op jit(solution)/shard_map/reshape | solution.py:274
  2.2 3.1 %collective-permute-start.5 = (bf16[4,24,1024]{2,1,0:T(8,128)(2,1)S(1)}, bf16[4,24,1024]{2,1,0:T(8,128)(2,1)S(1)}, u32[]{:S(2)}, u32[]{:S(2)}) collective-permute-start(bf16[4,24,1024]{2,1,0:T(8,128)(2,1)S(1)} %pad_maximum_fusion.1), channel_id=1, source_target_pairs={{0,8},{2,10},{4,12},{6,14},{8,0},{10,2},{12,4},{14,6},{16,24},{18,... | collective-permute-start | bytes 589832 | tf_op jit(solution)/shard_map/ppermute | solution.py:29
  5.3 0.5 fusion.1.own_ref
  5.8 1.6 %collective-permute-start = (f32[64,256]{1,0:T(8,128)S(1)}, f32[64,256]{1,0:T(8,128)S(1)}, u32[]{:S(2)}, u32[]{:S(2)}) collective-permute-start(f32[64,256]{1,0:T(8,128)S(1)} %fusion.1.own_ref), channel_id=1, source_target_pairs={{0,1},{1,0},{2,3},{3,2},{4,5},{5,4},{6,7},{7,6},{8,9},{9,8},{10,11... | collective-permute-start | bytes 196616 | tf_op jit(solution)/shard_map/ppermute | solution.py:29
  7.4 2.8 %collective-permute-done.other_ref = f32[64,256]{1,0:T(8,128)S(1)} collective-permute-done((f32[64,256]{1,0:T(8,128)S(1)}, f32[64,256]{1,0:T(8,128)S(1)}, u32[]{:S(2)}, u32[]{:S(2)}) %collective-permute-start) | collective-permute-done | bytes 65568 | tf_op jit(solution)/shard_map/ppermute | solution.py:29
  10.2 0.6 copy-done.16
  10.8 1.7 %unpatchify.1 = bf16[16,1024]{1,0:T(8,128)(2,1)} custom-call(f32[64,256]{1,0:T(8,128)} %copy-done.15, f32[64,256]{1,0:T(8,128)} %copy-done.16), custom_call_target="tpu_custom_call" | custom-call | tf_op jit(solution)/shard_map/unpatchify/pallas_call | solution.py:313
  12.6 3.1 %collective-permute-start.6 = (bf16[4,24,1024]{2,1,0:T(8,128)(2,1)S(1)}, bf16[4,24,1024]{2,1,0:T(8,128)(2,1)S(1)}, u32[]{:S(2)}, u32[]{:S(2)}) collective-permute-start(bf16[4,24,1024]{2,1,0:T(8,128)(2,1)S(1)} %pad_maximum_fusion.2), channel_id=1, source_target_pairs={{0,16},{2,18},{4,20},{6,22},{8,24},{10,26},{12,28},{14,30},{16,0},... | collective-permute-start | bytes 589832 | tf_op jit(solution)/shard_map/ppermute | solution.py:29
  15.6 1.2 collective-permute-done.1
  16.8 0.8 pad_maximum_fusion.5
  17.6 2.6 %collective-permute-start.2 = (bf16[2,16,1024]{2,1,0:T(8,128)(2,1)S(1)}, bf16[2,16,1024]{2,1,0:T(8,128)(2,1)S(1)}, u32[]{:S(2)}, u32[]{:S(2)}) collective-permute-start(bf16[2,16,1024]{2,1,0:T(8,128)(2,1)S(1)} %pad_maximum_fusion.5), channel_id=1, source_target_pairs={{0,16},{2,18},{4,20},{6,22},{8,24},{10,26},{12,28},{14,30},{16,0},... | collective-permute-start | bytes 196616 | tf_op jit(solution)/shard_map/ppermute | solution.py:29
  20.2 0.8 copy.15
  21.1 0.8 reshape.63.gain_ref
  21.8 0.9 copy.12.refs_1_
  22.7 3.4 %collective-permute-done.2 = bf16[2,16,1024]{2,1,0:T(8,128)(2,1)S(1)} collective-permute-done((bf16[2,16,1024]{2,1,0:T(8,128)(2,1)S(1)}, bf16[2,16,1024]{2,1,0:T(8,128)(2,1)S(1)}, u32[]{:S(2)}, u32[]{:S(2)}) %collective-permute-start.2) | collective-permute-done | bytes 65568 | tf_op jit(solution)/shard_map/ppermute | solution.py:29
  26.2 1.6 %collective-permute-start.3 = (bf16[4,16,1024]{2,1,0:T(8,128)(2,1)S(1)}, bf16[4,16,1024]{2,1,0:T(8,128)(2,1)S(1)}, u32[]{:S(2)}, u32[]{:S(2)}) collective-permute-start(bf16[4,16,1024]{2,1,0:T(8,128)(2,1)S(1)} %pad_maximum_fusion.4), channel_id=1, source_target_pairs={{0,4},{2,6},{4,0},{6,2},{8,12},{10,14},{12,8},{14,10},{16,20},{18,... | collective-permute-start | bytes 393224 | tf_op jit(solution)/shard_map/ppermute | solution.py:29
  27.8 0.5 collective-permute-start.7
  28.4 3.9 %collective-permute-done.3 = bf16[4,16,1024]{2,1,0:T(8,128)(2,1)S(1)} collective-permute-done((bf16[4,16,1024]{2,1,0:T(8,128)(2,1)S(1)}, bf16[4,16,1024]{2,1,0:T(8,128)(2,1)S(1)}, u32[]{:S(2)}, u32[]{:S(2)}) %collective-permute-start.3) | collective-permute-done | bytes 131104 | tf_op jit(solution)/shard_map/ppermute | solution.py:29
  32.4 2.0 %collective-permute-done.7 = bf16[4,24,1024]{2,1,0:T(8,128)(2,1)S(1)} collective-permute-done((bf16[4,24,1024]{2,1,0:T(8,128)(2,1)S(1)}, bf16[4,24,1024]{2,1,0:T(8,128)(2,1)S(1)}, u32[]{:S(2)}, u32[]{:S(2)}) %collective-permute-start.7) | collective-permute-done | bytes 196640 | tf_op jit(solution)/shard_map/ppermute | solution.py:29
  34.7 1.6 %collective-permute-done.8.other_ref = bf16[8,24,1024]{2,1,0:T(8,128)(2,1)S(1)} collective-permute-done((bf16[8,24,1024]{2,1,0:T(8,128)(2,1)S(1)}, bf16[8,24,1024]{2,1,0:T(8,128)(2,1)S(1)}, u32[]{:S(2)}, u32[]{:S(2)}) %collective-permute-start.8) | collective-permute-done | bytes 393248 | tf_op jit(solution)/shard_map/ppermute | solution.py:29
  36.3 0.7 copy-done.12
  37.0 3.5 %cotangent.1.cot_ref = bf16[448,4352]{1,0:T(8,128)(2,1)} custom-call(s32[1]{0:T(128)} %bitcast.me_ref, bf16[8,24,1024]{2,1,0:T(8,128)(2,1)} %copy-done.11, bf16[8,24,1024]{2,1,0:T(8,128)(2,1)} %copy-done.12), custom_call_target="tpu_custom_call" | custom-call | tf_op jit(solution)/shard_map/cotangent/pallas_call | solution.py:292
  40.6 24.7 %gradient.1 = (f32[216,384]{1,0:T(8,128)}, bf16[216,384]{1,0:T(8,128)(2,1)}) custom-call(s32[1]{0:T(128)} %bitcast.me_ref, bf16[16,16,1024]{2,1,0:T(8,128)(2,1)} %copy-done.1, bf16[448,4352]{1,0:T(8,128)(2,1)} %cotangent.1.cot_ref, f32[384,1]{1,0:T(8,128)} %reshape.63.gain_ref, bf16[384,144]{1,0:T(8,128)(2,1)} %bitcast.42, bf16[384,288]{1,0:T(8,128)(2,1)} %copy.12.refs_1_), custom_call_target="tpu_custom_call" | custom-call | tf_op jit(solution)/shard_map/gradient/pallas_call | solution.py:334
  65.4 1.5 %collective-permute-done.9 = bf16[216,384]{1,0:T(8,128)(2,1)S(1)} collective-permute-done((bf16[216,384]{1,0:T(8,128)(2,1)}, bf16[216,384]{1,0:T(8,128)(2,1)S(1)}, u32[]{:S(2)}, u32[]{:S(2)}) %collective-permute-start.9) | collective-permute-done | bytes 165920 | tf_op jit(solution)/shard_map/ppermute | solution.py:29
  66.8 1.7 %bitcast_dynamic-update-slice_fusion.7 = (bf16[8,216,384]{2,1,0:T(8,128)(2,1)}, bf16[216,384]{1,0:T(8,128)(2,1)S(1)}) fusion(f32[216,384]{1,0:T(8,128)} %get-tuple-element.4, bf16[216,384]{1,0:T(8,128)(2,1)S(1)} %collective-permute-done.9), kind=kLoop, calls=%fused_computation.12 | loop fusion | flops 248831 | bytes 829440
  68.5 4.7 %collective-permute-start.12 = (bf16[216,384]{1,0:T(8,128)(2,1)S(1)}, bf16[216,384]{1,0:T(8,128)(2,1)S(1)}, u32[]{:S(2)}, u32[]{:S(2)}) collective-permute-start(bf16[216,384]{1,0:T(8,128)(2,1)S(1)} %get-tuple-element.7), channel_id=1, source_target_pairs={{0,24},{2,26},{4,28},{6,30},{8,16},{10,18},{12,20},{14,22},{16,8},... | collective-permute-start | bytes 497672 | tf_op jit(solution)/shard_map/ppermute | solution.py:29
  73.2 0.6 collective-permute-start.10
  73.7 1.5 %collective-permute-start.13 = (bf16[216,384]{1,0:T(8,128)(2,1)S(1)}, bf16[216,384]{1,0:T(8,128)(2,1)S(1)}, u32[]{:S(2)}, u32[]{:S(2)}) collective-permute-start(bf16[216,384]{1,0:T(8,128)(2,1)S(1)} %get-tuple-element.7), channel_id=1, source_target_pairs={{0,4},{2,6},{4,0},{6,2},{8,12},{10,14},{12,8},{14,10},{16,20},{18,... | collective-permute-start | bytes 497672 | tf_op jit(solution)/shard_map/ppermute | solution.py:29
  75.3 3.1 %collective-permute-done.12 = bf16[216,384]{1,0:T(8,128)(2,1)S(1)} collective-permute-done((bf16[216,384]{1,0:T(8,128)(2,1)S(1)}, bf16[216,384]{1,0:T(8,128)(2,1)S(1)}, u32[]{:S(2)}, u32[]{:S(2)}) %collective-permute-start.12) | collective-permute-done | bytes 165920 | tf_op jit(solution)/shard_map/ppermute | solution.py:29
  78.3 1.5 %collective-permute-start.16 = (bf16[216,384]{1,0:T(8,128)(2,1)S(1)}, bf16[216,384]{1,0:T(8,128)(2,1)S(1)}, u32[]{:S(2)}, u32[]{:S(2)}) collective-permute-start(bf16[216,384]{1,0:T(8,128)(2,1)S(1)} %collective-permute-done.12), channel_id=1, source_target_pairs={{0,4},{2,6},{4,0},{6,2},{8,12},{10,14},{12,8},{14,10},{16,20},{18,... | collective-permute-start | bytes 497672 | tf_op jit(solution)/shard_map/ppermute | solution.py:29
  79.8 6.9 %collective-permute-done.11 = bf16[216,384]{1,0:T(8,128)(2,1)S(1)} collective-permute-done((bf16[216,384]{1,0:T(8,128)(2,1)S(1)}, bf16[216,384]{1,0:T(8,128)(2,1)S(1)}, u32[]{:S(2)}, u32[]{:S(2)}) %collective-permute-start.11) | collective-permute-done | bytes 165920 | tf_op jit(solution)/shard_map/ppermute | solution.py:29
  86.8 1.5 %collective-permute-start.15 = (bf16[216,384]{1,0:T(8,128)(2,1)S(1)}, bf16[216,384]{1,0:T(8,128)(2,1)S(1)}, u32[]{:S(2)}, u32[]{:S(2)}) collective-permute-start(bf16[216,384]{1,0:T(8,128)(2,1)S(1)} %collective-permute-done.11), channel_id=1, source_target_pairs={{0,4},{2,6},{4,0},{6,2},{8,12},{10,14},{12,8},{14,10},{16,20},{18,... | collective-permute-start | bytes 497672 | tf_op jit(solution)/shard_map/ppermute | solution.py:29
  88.3 0.5 collective-permute-start.14
  88.8 0.7 bitcast_dynamic-update-slice_fusion.6
  89.5 0.7 bitcast_dynamic-update-slice_fusion.5
  90.1 0.7 bitcast_dynamic-update-slice_fusion.4
  90.8 0.7 bitcast_dynamic-update-slice_fusion.3
  91.5 4.3 %collective-permute-done.14 = bf16[216,384]{1,0:T(8,128)(2,1)S(1)} collective-permute-done((bf16[216,384]{1,0:T(8,128)(2,1)S(1)}, bf16[216,384]{1,0:T(8,128)(2,1)S(1)}, u32[]{:S(2)}, u32[]{:S(2)}) %collective-permute-start.14) | collective-permute-done | bytes 165920 | tf_op jit(solution)/shard_map/ppermute | solution.py:29
  95.8 0.7 bitcast_dynamic-update-slice_fusion.2
  96.5 0.7 bitcast_dynamic-update-slice_fusion.1
  97.3 0.7 bitcast_dynamic-update-slice_fusion
  97.9 1.8 %slice.62 = bf16[2,3,3,192,384]{4,3,2,1,0:T(8,128)(2,1)} slice(bf16[3,3,3,192,384]{4,3,2,1,0:T(8,128)(2,1)S(1)} %bitcast.44), slice={[1:3], [0:3], [0:3], [0:192], [0:384]} | slice | bytes 5308416 | tf_op jit(solution)/shard_map/slice | solution.py:378
  99.7 7.4 %decode.1 = bf16[192,1024]{1,0:T(8,128)(2,1)} custom-call(s32[1]{0:T(128)} %bitcast.me_ref, bf16[16,16,1024]{2,1,0:T(8,128)(2,1)} %copy-done.1, f32[384,1]{1,0:T(8,128)} %reshape.63.gain_ref, bf16[18,192,384]{2,1,0:T(8,128)(2,1)} %bitcast.40, bf16[384,144]{1,0:T(8,128)(2,1)} %bitcast.43, bf16[384,288]{1,0:T(8,128)(2,1)} %copy.12.refs_1_), custom_call_target="tpu_custom_call" | custom-call | tf_op jit(solution)/shard_map/decode/pallas_call | solution.py:366
  107.1 2.0 %reshape.59 = bf16[192,2,4,128]{3,2,1,0:T(4,128)(2,1)} reshape(bf16[192,1024]{1,0:T(8,128)(2,1)} %decode.1) | data formatting | bytes 786432 | tf_op jit(solution)/shard_map/reshape | solution.py:396
  109.1 1.0 constant_dynamic-update-slice_fusion.19
  110.4 1.1 copy-done.3
  111.5 0.4 copy-done.4
  111.9 10.1 %finish.1 = f32[3,9,192,384]{3,2,1,0:T(8,128)} custom-call(s32[1]{0:T(128)} %bitcast.me_ref, bf16[8,9,24,384]{3,2,1,0:T(8,128)(2,1)} %copy-done.3, bf16[8,9,24,384]{3,2,1,0:T(8,128)(2,1)} %bitcast.45), custom_call_target="tpu_custom_call" | custom-call | tf_op jit(solution)/shard_map/finish/pallas_call | solution.py:380
  (75 shorter events, 0.9 us)
Async XLA Ops:
  0.6 4.7 %copy-start = (bf16[2,2,64,2560]{3,2,1,0:T(8,128)(2,1)S(1)}, bf16[2,2,64,2560]{3,2,1,0:T(8,128)(2,1)}, u32[]{:S(2)}) copy-start(bf16[2,2,64,2560]{3,2,1,0:T(8,128)(2,1)} %param.6) | copy-start | bytes 3932164
  0.6 4.7 %copy-start.14 = (bf16[2560,64]{0,1:T(8,128)(2,1)S(1)}, bf16[2560,64]{0,1:T(8,128)(2,1)}, u32[]{:S(2)}) copy-start(bf16[2560,64]{0,1:T(8,128)(2,1)} %param.7) | copy-start | bytes 983044
  2.2 10.3 %collective-permute-start.5 = (bf16[4,24,1024]{2,1,0:T(8,128)(2,1)S(1)}, bf16[4,24,1024]{2,1,0:T(8,128)(2,1)S(1)}, u32[]{:S(2)}, u32[]{:S(2)}) collective-permute-start(bf16[4,24,1024]{2,1,0:T(8,128)(2,1)S(1)} %pad_maximum_fusion.1), channel_id=1, source_target_pairs={{0,8},{2,10},{4,12},{6,14},{8,0},{10,2},{12,4},{14,6},{16,24},{18,... | collective-permute-start | bytes 589832 | tf_op jit(solution)/shard_map/ppermute | solution.py:29
  5.3 14.9 %copy-start.13 = (bf16[384,3,3,3,16]{0,4,3,2,1:T(8,128)(2,1)S(1)}, bf16[384,3,3,3,16]{0,4,3,2,1:T(8,128)(2,1)}, u32[]{:S(2)}) copy-start(bf16[384,3,3,3,16]{0,4,3,2,1:T(8,128)(2,1)} %param.9) | copy-start | bytes 995332
  5.8 4.4 %copy-start.15 = (f32[64,256]{1,0:T(8,128)}, f32[64,256]{1,0:T(8,128)S(1)}, u32[]{:S(2)}) copy-start(f32[64,256]{1,0:T(8,128)S(1)} %fusion.1.own_ref) | copy-start | bytes 196612
  5.8 15.2 %copy-start.17 = (f32[384]{0:T(512)S(1)}, f32[384]{0:T(512)}, u32[]{:S(2)}) copy-start(f32[384]{0:T(512)} %param.8) | copy-start | bytes 4612
  5.8 4.3 %collective-permute-start = (f32[64,256]{1,0:T(8,128)S(1)}, f32[64,256]{1,0:T(8,128)S(1)}, u32[]{:S(2)}, u32[]{:S(2)}) collective-permute-start(f32[64,256]{1,0:T(8,128)S(1)} %fusion.1.own_ref), channel_id=1, source_target_pairs={{0,1},{1,0},{2,3},{3,2},{4,5},{5,4},{6,7},{7,6},{8,9},{9,8},{10,11... | collective-permute-start | bytes 196616 | tf_op jit(solution)/shard_map/ppermute | solution.py:29
  10.2 0.6 copy-start.16
  12.5 13.7 %copy-start.5 = (bf16[16,1024]{1,0:T(8,128)(2,1)S(1)}, bf16[16,1024]{1,0:T(8,128)(2,1)}, u32[]{:S(2)}) copy-start(bf16[16,1024]{1,0:T(8,128)(2,1)} %unpatchify.1) | copy-start | bytes 98308
  12.5 4.3 %collective-permute-start.1 = (bf16[1,16,1024]{2,1,0:T(8,128)(2,1)}, bf16[1,16,1024]{2,1,0:T(8,128)(2,1)S(1)}, u32[]{:S(2)}, u32[]{:S(2)}) collective-permute-start(bf16[1,16,1024]{2,1,0:T(8,128)(2,1)} %bitcast.47), channel_id=1, source_target_pairs={{0,8},{2,10},{4,12},{6,14},{8,0},{10,2},{12,4},{14,6},{16,24},{18,... | collective-permute-start | bytes 98312 | tf_op jit(solution)/shard_map/ppermute | solution.py:29
  12.6 15.2 %collective-permute-start.6 = (bf16[4,24,1024]{2,1,0:T(8,128)(2,1)S(1)}, bf16[4,24,1024]{2,1,0:T(8,128)(2,1)S(1)}, u32[]{:S(2)}, u32[]{:S(2)}) collective-permute-start(bf16[4,24,1024]{2,1,0:T(8,128)(2,1)S(1)} %pad_maximum_fusion.2), channel_id=1, source_target_pairs={{0,16},{2,18},{4,20},{6,22},{8,24},{10,26},{12,28},{14,30},{16,0},... | collective-permute-start | bytes 589832 | tf_op jit(solution)/shard_map/ppermute | solution.py:29
  17.6 8.6 %collective-permute-start.2 = (bf16[2,16,1024]{2,1,0:T(8,128)(2,1)S(1)}, bf16[2,16,1024]{2,1,0:T(8,128)(2,1)S(1)}, u32[]{:S(2)}, u32[]{:S(2)}) collective-permute-start(bf16[2,16,1024]{2,1,0:T(8,128)(2,1)S(1)} %pad_maximum_fusion.5), channel_id=1, source_target_pairs={{0,16},{2,18},{4,20},{6,22},{8,24},{10,26},{12,28},{14,30},{16,0},... | collective-permute-start | bytes 196616 | tf_op jit(solution)/shard_map/ppermute | solution.py:29
  26.2 6.1 %collective-permute-start.3 = (bf16[4,16,1024]{2,1,0:T(8,128)(2,1)S(1)}, bf16[4,16,1024]{2,1,0:T(8,128)(2,1)S(1)}, u32[]{:S(2)}, u32[]{:S(2)}) collective-permute-start(bf16[4,16,1024]{2,1,0:T(8,128)(2,1)S(1)} %pad_maximum_fusion.4), channel_id=1, source_target_pairs={{0,4},{2,6},{4,0},{6,2},{8,12},{10,14},{12,8},{14,10},{16,20},{18,... | collective-permute-start | bytes 393224 | tf_op jit(solution)/shard_map/ppermute | solution.py:29
  27.8 6.5 %collective-permute-start.7 = (bf16[4,24,1024]{2,1,0:T(8,128)(2,1)S(1)}, bf16[4,24,1024]{2,1,0:T(8,128)(2,1)S(1)}, u32[]{:S(2)}, u32[]{:S(2)}) collective-permute-start(bf16[4,24,1024]{2,1,0:T(8,128)(2,1)S(1)} %pad_maximum_fusion.3), channel_id=1, source_target_pairs={{0,4},{2,6},{4,0},{6,2},{8,12},{10,14},{12,8},{14,10},{16,20},{18,... | collective-permute-start | bytes 589832 | tf_op jit(solution)/shard_map/ppermute | solution.py:29
  32.3 2.3 %collective-permute-start.4 = (bf16[8,16,1024]{2,1,0:T(8,128)(2,1)S(1)}, bf16[8,16,1024]{2,1,0:T(8,128)(2,1)S(1)}, u32[]{:S(2)}, u32[]{:S(2)}) collective-permute-start(bf16[8,16,1024]{2,1,0:T(8,128)(2,1)S(1)} %pad_maximum_fusion), channel_id=1, source_target_pairs={{0,2},{2,0},{4,6},{6,4},{8,10},{10,8},{12,14},{14,12},{16,18},{18,... | collective-permute-start | bytes 786440 | tf_op jit(solution)/shard_map/ppermute | solution.py:29
  34.5 1.8 %copy-start.11 = (bf16[8,24,1024]{2,1,0:T(8,128)(2,1)}, bf16[8,24,1024]{2,1,0:T(8,128)(2,1)S(1)}, u32[]{:S(2)}) copy-start(bf16[8,24,1024]{2,1,0:T(8,128)(2,1)S(1)} %constant_dynamic-update-slice_fusion.5.own_ref) | copy-start | bytes 1179652
  34.5 1.8 %collective-permute-start.8 = (bf16[8,24,1024]{2,1,0:T(8,128)(2,1)S(1)}, bf16[8,24,1024]{2,1,0:T(8,128)(2,1)S(1)}, u32[]{:S(2)}, u32[]{:S(2)}) collective-permute-start(bf16[8,24,1024]{2,1,0:T(8,128)(2,1)S(1)} %constant_dynamic-update-slice_fusion.5.own_ref), channel_id=1, source_target_pairs={{0,2},{2,0},{4,6},{6,4},{8,10},{10,8},{12,14},{14,12},{16,18},{18,... | collective-permute-start | bytes 1179656 | tf_op jit(solution)/shard_map/ppermute | solution.py:29
  34.6 5.9 %copy-start.1 = (bf16[16,16,1024]{2,1,0:T(8,128)(2,1)}, bf16[16,16,1024]{2,1,0:T(8,128)(2,1)S(1)}, u32[]{:S(2)}) copy-start(bf16[16,16,1024]{2,1,0:T(8,128)(2,1)S(1)} %constant_dynamic-update-slice_fusion.lat_ref) | copy-start | bytes 1572868
  36.3 0.8 copy-start.12
  40.6 57.4 %copy-start.2 = (bf16[192,3,3,3,384]{4,0,3,2,1:T(8,128)(2,1)S(1)}, bf16[192,3,3,3,384]{4,0,3,2,1:T(8,128)(2,1)}, u32[]{:S(2)}) copy-start(bf16[192,3,3,3,384]{4,0,3,2,1:T(8,128)(2,1)} %param.10) | copy-start | bytes 11943940
  65.2 1.6 %collective-permute-start.9 = (bf16[216,384]{1,0:T(8,128)(2,1)}, bf16[216,384]{1,0:T(8,128)(2,1)S(1)}, u32[]{:S(2)}, u32[]{:S(2)}) collective-permute-start(bf16[216,384]{1,0:T(8,128)(2,1)} %get-tuple-element.5), channel_id=1, source_target_pairs={{0,2},{2,0},{4,6},{6,4},{8,10},{10,8},{12,14},{14,12},{16,18},{18,... | collective-permute-start | bytes 497672 | tf_op jit(solution)/shard_map/ppermute | solution.py:29
  68.5 9.8 %collective-permute-start.12 = (bf16[216,384]{1,0:T(8,128)(2,1)S(1)}, bf16[216,384]{1,0:T(8,128)(2,1)S(1)}, u32[]{:S(2)}, u32[]{:S(2)}) collective-permute-start(bf16[216,384]{1,0:T(8,128)(2,1)S(1)} %get-tuple-element.7), channel_id=1, source_target_pairs={{0,24},{2,26},{4,28},{6,30},{8,16},{10,18},{12,20},{14,22},{16,8},... | collective-permute-start | bytes 497672 | tf_op jit(solution)/shard_map/ppermute | solution.py:29
  73.2 13.6 %collective-permute-start.11 = (bf16[216,384]{1,0:T(8,128)(2,1)S(1)}, bf16[216,384]{1,0:T(8,128)(2,1)S(1)}, u32[]{:S(2)}, u32[]{:S(2)}) collective-permute-start(bf16[216,384]{1,0:T(8,128)(2,1)S(1)} %get-tuple-element.7), channel_id=1, source_target_pairs={{0,16},{2,18},{4,20},{6,22},{8,24},{10,26},{12,28},{14,30},{16,0},... | collective-permute-start | bytes 497672 | tf_op jit(solution)/shard_map/ppermute | solution.py:29
  73.2 15.1 %collective-permute-start.10 = (bf16[216,384]{1,0:T(8,128)(2,1)S(1)}, bf16[216,384]{1,0:T(8,128)(2,1)S(1)}, u32[]{:S(2)}, u32[]{:S(2)}) collective-permute-start(bf16[216,384]{1,0:T(8,128)(2,1)S(1)} %get-tuple-element.7), channel_id=1, source_target_pairs={{0,8},{2,10},{4,12},{6,14},{8,0},{10,2},{12,4},{14,6},{16,24},{18,... | collective-permute-start | bytes 497672 | tf_op jit(solution)/shard_map/ppermute | solution.py:29
  73.7 17.1 %collective-permute-start.13 = (bf16[216,384]{1,0:T(8,128)(2,1)S(1)}, bf16[216,384]{1,0:T(8,128)(2,1)S(1)}, u32[]{:S(2)}, u32[]{:S(2)}) collective-permute-start(bf16[216,384]{1,0:T(8,128)(2,1)S(1)} %get-tuple-element.7), channel_id=1, source_target_pairs={{0,4},{2,6},{4,0},{6,2},{8,12},{10,14},{12,8},{14,10},{16,20},{18,... | collective-permute-start | bytes 497672 | tf_op jit(solution)/shard_map/ppermute | solution.py:29
  78.3 18.9 %collective-permute-start.16 = (bf16[216,384]{1,0:T(8,128)(2,1)S(1)}, bf16[216,384]{1,0:T(8,128)(2,1)S(1)}, u32[]{:S(2)}, u32[]{:S(2)}) collective-permute-start(bf16[216,384]{1,0:T(8,128)(2,1)S(1)} %collective-permute-done.12), channel_id=1, source_target_pairs={{0,4},{2,6},{4,0},{6,2},{8,12},{10,14},{12,8},{14,10},{16,20},{18,... | collective-permute-start | bytes 497672 | tf_op jit(solution)/shard_map/ppermute | solution.py:29
  86.8 9.8 %collective-permute-start.15 = (bf16[216,384]{1,0:T(8,128)(2,1)S(1)}, bf16[216,384]{1,0:T(8,128)(2,1)S(1)}, u32[]{:S(2)}, u32[]{:S(2)}) collective-permute-start(bf16[216,384]{1,0:T(8,128)(2,1)S(1)} %collective-permute-done.11), channel_id=1, source_target_pairs={{0,4},{2,6},{4,0},{6,2},{8,12},{10,14},{12,8},{14,10},{16,20},{18,... | collective-permute-start | bytes 497672 | tf_op jit(solution)/shard_map/ppermute | solution.py:29
  88.3 11.5 %copy-start.6 = (bf16[216,384]{1,0:T(8,128)(2,1)}, bf16[216,384]{1,0:T(8,128)(2,1)S(1)}, u32[]{:S(2)}) copy-start(bf16[216,384]{1,0:T(8,128)(2,1)S(1)} %collective-permute-done.10) | copy-start | bytes 497668
  88.3 7.5 %collective-permute-start.14 = (bf16[216,384]{1,0:T(8,128)(2,1)S(1)}, bf16[216,384]{1,0:T(8,128)(2,1)S(1)}, u32[]{:S(2)}, u32[]{:S(2)}) collective-permute-start(bf16[216,384]{1,0:T(8,128)(2,1)S(1)} %collective-permute-done.10), channel_id=1, source_target_pairs={{0,4},{2,6},{4,0},{6,2},{8,12},{10,14},{12,8},{14,10},{16,20},{18,... | collective-permute-start | bytes 497672 | tf_op jit(solution)/shard_map/ppermute | solution.py:29
  95.8 3.9 %copy-start.9 = (bf16[216,384]{1,0:T(8,128)(2,1)}, bf16[216,384]{1,0:T(8,128)(2,1)S(1)}, u32[]{:S(2)}) copy-start(bf16[216,384]{1,0:T(8,128)(2,1)S(1)} %collective-permute-done.14) | copy-start | bytes 497668
  96.5 3.2 %copy-start.7 = (bf16[216,384]{1,0:T(8,128)(2,1)}, bf16[216,384]{1,0:T(8,128)(2,1)S(1)}, u32[]{:S(2)}) copy-start(bf16[216,384]{1,0:T(8,128)(2,1)S(1)} %collective-permute-done.15) | copy-start | bytes 497668
  97.9 12.5 %collective-permute-start.17 = (bf16[8,216,384]{2,1,0:T(8,128)(2,1)}, bf16[8,216,384]{2,1,0:T(8,128)(2,1)S(1)}, u32[]{:S(2)}, u32[]{:S(2)}) collective-permute-start(bf16[8,216,384]{2,1,0:T(8,128)(2,1)} %bitcast_dynamic-update-slice_fusion), channel_id=1, source_target_pairs={{0,2},{2,0},{4,6},{6,4},{8,10},{10,8},{12,14},{14,12},{16,18},{18,... | collective-permute-start | bytes 3981320 | tf_op jit(solution)/shard_map/ppermute | solution.py:29
  109.1 1.1 copy-start.10
  109.1 1.2 copy-start.8
  110.4 1.1 copy-start.3
  110.4 1.5 %copy-start.4 = (bf16[8,216,384]{2,1,0:T(8,128)(2,1)}, bf16[8,216,384]{2,1,0:T(8,128)(2,1)S(1)}, u32[]{:S(2)}) copy-start(bf16[8,216,384]{2,1,0:T(8,128)(2,1)S(1)} %collective-permute-done.17) | copy-start | bytes 3981316

commit v2 on v1

v2 whole, which is shorter than its diff:
```python
import functools

import jax
import jax.numpy as jnp
from jax import lax
from jax.experimental import pallas as pl
from jax.experimental.pallas import tpu as pltpu
from jax.sharding import PartitionSpec as P

LANES = 128
VMEM_LIMIT = 56 * 1024 * 1024
F32 = jnp.float32
BF16 = jnp.bfloat16


def params():
    return pltpu.CompilerParams(vmem_limit_bytes=VMEM_LIMIT)


def vmem():
    return pl.BlockSpec(memory_space=pltpu.VMEM)


def smem():
    return pl.BlockSpec(memory_space=pltpu.SMEM)


def xor_permute(x, axis, mask):
    return lax.ppermute(x, axis, [(i, i ^ mask) for i in range(lax.axis_size(axis))])


def dot(a, b):
    return lax.dot_general(a, b, (((1,), (0,)), ((), ())), preferred_element_type=F32)


def dot_t(a, b):
    return lax.dot_general(a, b, (((1,), (1,)), ((), ())), preferred_element_type=F32)


def unpatchify_kernel(frames, tok_rows, tok_cols, own_ref, other_ref, out_ref):
    latent_width = out_ref.shape[0]
    features = (own_ref[...] + other_ref[...]).astype(BF16)
    width = 2 * tok_cols
    span = tok_rows * tok_cols
    source = lax.broadcasted_iota(jnp.int32, (span, tok_rows * width), 0)
    target = lax.broadcasted_iota(jnp.int32, (span, tok_rows * width), 1)
    same_row = source // tok_cols == target // width
    column = source % tok_cols
    even = (same_row & (target % width == 2 * column)).astype(BF16)
    odd = (same_row & (target % width == 2 * column + 1)).astype(BF16)
    for frame in range(frames):
        tokens = features[:, frame * span : (frame + 1) * span]
        left = dot(tokens, even)
        right = dot(tokens, odd)
        for row in range(tok_rows):
            cols = slice(row * width, (row + 1) * width)
            for half in range(2):
                base = half * 2 * latent_width
                cells = (
                    left[base : base + latent_width, cols]
                    + right[base + latent_width : base + 2 * latent_width, cols]
                )
                at = (frame * 2 * tok_rows + 2 * row + half) * width
                out_ref[:, at : at + width] = cells.astype(BF16)


def shifted(tile, shift):
    if shift == 1:
        return tile
    lane = lax.broadcasted_iota(jnp.int32, tile.shape, 1)
    if shift == 0:
        return jnp.where(lane == 0, 0.0, pltpu.roll(tile, 1, 1))
    return jnp.where(lane == LANES - 1, 0.0, pltpu.roll(tile, LANES - 1, 1))


def place_latent(lat_refs, mask_lists, stack_ref, me, frames, rows):
    latent_width = lat_refs[0].shape[1]
    total = stack_ref.shape[2]
    zeros = jnp.zeros((stack_ref.shape[1], 2 * LANES), BF16)
    for frame in range(frames):
        stack_ref[frame, :, 0 : 2 * LANES] = zeros
        stack_ref[frame, :, total - 2 * LANES : total] = zeros
    for lat_ref, masks in zip(lat_refs, mask_lists):
        for index, mask in enumerate(masks):
            slab = me ^ mask
            for frame in range(frames):
                for row in range(rows):
                    at = (frame * rows + row) * LANES
                    tile = lat_ref[index, :, at : at + LANES].astype(F32)
                    to = pl.multiple_of((slab * rows + row + 2) * LANES, LANES)
                    for shift in range(3):
                        stack_ref[
                            frame,
                            shift * latent_width : (shift + 1) * latent_width,
                            pl.ds(to, LANES),
                        ] = shifted(tile, shift).astype(BF16)


def hidden_rows(stack_ref, weight_ref, frame, first, count):
    pieces = []
    for source in range(max(0, frame - 2), frame + 1):
        for row_tap in range(3):
            at = pl.multiple_of((first + row_tap) * LANES, LANES)
            pieces.append(stack_ref[source, :, pl.ds(at, count * LANES)])
    return dot(weight_ref[...], jnp.concatenate(pieces, axis=0))


def activate_rows(hidden_ref, gain_ref, act_ref, base, top_row, count, height):
    channels = hidden_ref.shape[0]
    block = 16
    for index in range(count):
        at = pl.multiple_of((base + index) * LANES, LANES)
        hidden = hidden_ref[:, pl.ds(at, LANES)]
        mean = jnp.sum(hidden * hidden, axis=0, keepdims=True) * (1.0 / channels)
        row = top_row + base + index
        inside = ((row >= 0) & (row < height)).astype(F32)
        inverse = jnp.broadcast_to(lax.rsqrt(mean + 1e-6) * inside, (block, LANES))
        for at_channel in range(0, channels, block):
            chunk = slice(at_channel, at_channel + block)
            half = hidden_ref[chunk, pl.ds(at, LANES)] * inverse * gain_ref[chunk, :]
            act_ref[chunk, pl.ds(at, LANES)] = (half + half * jnp.tanh(half)).astype(BF16)


def cotangent_kernel(
    frames, rows, half_rows, pad_channels, mask_lists, me_ref, *refs
):
    block_refs = refs[:-2]
    out_ref, flat_ref = refs[-2:]
    me = me_ref[0]
    slabs_half = half_rows // rows
    first_slab = (me & 1) * slabs_half
    channels = block_refs[0].shape[1]
    group = 3 * pad_channels
    padded = out_ref.shape[0] // frames
    for frame in range(frames):
        for edge in (0, half_rows + 2):
            flat_ref[frame, :, edge * LANES : (edge + 2) * LANES] = jnp.zeros((group, 2 * LANES), F32)
    for block_ref, masks in zip(block_refs, mask_lists):
        for position, mask in enumerate(masks):
            index = (me ^ mask) - first_slab

            @pl.when((index >= 0) & (index < slabs_half))
            def _(block_ref=block_ref, position=position, index=index):
                for frame in range(frames):
                    for row in range(rows):
                        at = (frame * rows + row) * LANES
                        tile = block_ref[position, :, at : at + LANES].astype(F32)
                        if pad_channels != channels:
                            tile = jnp.concatenate(
                                [tile, jnp.zeros((pad_channels - channels, LANES), F32)], axis=0
                            )
                        to = pl.multiple_of((index * rows + row + 2) * LANES, LANES)
                        for tap in range(3):
                            flat_ref[
                                frame, tap * pad_channels : (tap + 1) * pad_channels, pl.ds(to, LANES)
                            ] = shifted(tile, 2 - tap)

    filler = [jnp.zeros((padded - 3 * group, LANES), F32)] if padded != 3 * group else []
    for frame in range(frames):
        for row in range(half_rows + 2):
            taps = [flat_ref[frame, :, (row + 2 - tap) * LANES : (row + 3 - tap) * LANES] for tap in range(3)]
            out_ref[frame * padded : (frame + 1) * padded, row * LANES : (row + 1) * LANES] = (
                jnp.concatenate(taps + filler, axis=0).astype(BF16)
            )


def gradient_kernel(frames, rows, half_rows, height, mask_lists, real_rows, *refs):
    lat_count = len(mask_lists)
    me_ref, cot_hbm, gain_ref = refs[:3]
    weight_refs = refs[3 : 3 + frames]
    lat_refs = refs[3 + frames : 3 + frames + lat_count]
    keep_ref, send_ref = refs[3 + frames + lat_count : 5 + frames + lat_count]
    stack_ref, hid_a, hid_b, act_a, act_b, sum_ref, wide_gain, cot_ref, sem = refs[5 + frames + lat_count :]
    load = pltpu.make_async_copy(cot_hbm, cot_ref, sem)
    load.start()
    me = me_ref[0]
    core = me & 1
    place_latent(lat_refs, mask_lists, stack_ref, me, frames, rows)
    channels = sum_ref.shape[1]
    wide_gain[...] = jnp.broadcast_to(0.5 * gain_ref[...], wide_gain.shape)
    padded = cot_ref.shape[0] // frames
    start = core * half_rows
    ext = half_rows + 2
    count = max(d for d in range(1, 18) if ext % d == 0)
    width = count * LANES
    hidden = (hid_a, hid_b)
    acts = (act_a, act_b)
    hid_a[...] = hidden_rows(stack_ref, weight_refs[0], 0, start, ext)
    sum_ref[...] = jnp.zeros_like(sum_ref)
    for frame in range(frames):
        if frame == 1:
            load.wait()

        def chunk(step, carry):
            at = pl.multiple_of(step * width, LANES)
            if frame + 1 < frames:
                hidden[(frame + 1) % 2][:, pl.ds(at, width)] = hidden_rows(
                    stack_ref, weight_refs[frame + 1], frame + 1, start + step * count, count
                )
            if frame > 0:
                last = min(frames, frame + 2)
                sum_ref[0 : (last - frame + 1) * padded, :] += dot_t(
                    cot_ref[(frame - 1) * padded : last * padded, pl.ds(at, width)],
                    acts[(frame - 1) % 2][:, pl.ds(at, width)],
                )
            activate_rows(
                hidden[frame % 2], wide_gain, acts[frame % 2], step * count, start - 1, count, height
            )
            return carry

        lax.fori_loop(0, ext // count, chunk, 0)
    if frames == 1:
        load.wait()
    final = frames - 1
    sum_ref[0:padded, :] += dot_t(cot_ref[final * padded : frames * padded, :], acts[final % 2][...])
    keep_at = pl.multiple_of(core * padded, 16)
    send_at = pl.multiple_of((1 - core) * padded, 16)
    keep_ref[...] = sum_ref[pl.ds(keep_at, padded), :][:real_rows]
    send_ref[...] = sum_ref[pl.ds(send_at, padded), :][:real_rows].astype(BF16)


def decode_kernel(frames, rows, height, mask_lists, *refs):
    lat_count = len(mask_lists)
    me_ref, gain_ref, conv_hbm = refs[:3]
    weight_refs = refs[3 : 3 + frames]
    lat_refs = refs[3 + frames : 3 + frames + lat_count]
    out_ref, stack_ref, hid_ref, flat_ref, act_ref, wide_gain, conv_ref, sem = refs[3 + frames + lat_count :]
    live = conv_ref.shape[0] // 9
    load = pltpu.make_async_copy(conv_hbm.at[pl.ds((3 - live) * 9, live * 9)], conv_ref, sem)
    load.start()
    me = me_ref[0]
    place_latent(lat_refs, mask_lists, stack_ref, me, frames, rows)
    wide_gain[...] = jnp.broadcast_to(0.5 * gain_ref[...], wide_gain.shape)
    ext = rows + 2
    for frame in range(frames):
        hid_ref[...] = hidden_rows(stack_ref, weight_refs[frame], frame, me * rows, ext)
        activate_rows(hid_ref, wide_gain, flat_ref, 0, me * rows - 1, ext, height)
        for row in range(ext):
            tile = flat_ref[:, row * LANES : (row + 1) * LANES].astype(F32)
            for tap in range(3):
                act_ref[frame, tap, :, row * LANES : (row + 1) * LANES] = shifted(tile, tap).astype(BF16)
    load.wait()
    for frame in range(frames):
        total = None
        for depth in range(max(0, 2 - frame), 3):
            source = frame + depth - 2
            for row_tap in range(3):
                for col_tap in range(3):
                    term = dot(
                        conv_ref[(depth - (3 - live)) * 9 + row_tap * 3 + col_tap],
                        act_ref[source, col_tap, :, row_tap * LANES : (row_tap + rows) * LANES],
                    )
                    total = term if total is None else total + term
        out_ref[:, frame * rows * LANES : (frame + 1) * rows * LANES] = total.astype(BF16)


def finish_kernel(first, pieces, blank, me_ref, *refs):
    count = len(pieces)
    piece_refs = refs[:count]
    out_hbm, wide_ref, zero_ref, sems, zero_sem = refs[count + (0 if first else 1) :]
    me = me_ref[0]
    channels = wide_ref.shape[2]
    copies = []
    if first and blank:
        zero_ref[...] = jnp.zeros_like(zero_ref)
        for plane in range(blank):
            for tap in range(9):
                copies.append(
                    pltpu.make_async_copy(zero_ref, out_hbm.at[plane, tap], zero_sem.at[plane * 9 + tap])
                )
                copies[-1].start()
    for index, mask in enumerate(pieces):
        source = me ^ mask
        wide_ref[index] = piece_refs[index][...].astype(F32)
        at = pl.multiple_of((source >> 1) * channels, 8)
        copy = pltpu.make_async_copy(
            wide_ref.at[index], out_hbm.at[2 - (source & 1), :, pl.ds(at, channels), :], sems.at[index]
        )
        copy.start()
        copies.append(copy)
    for copy in copies:
        copy.wait()


def per_device(attn_out, w_proj, norm_gain, entry_weight, conv_weight, cotangent):
    frames, tok_rows, tok_cols, model_width = attn_out.shape
    latent_width = entry_weight.shape[4]
    channels = entry_weight.shape[0]
    out_channels = conv_weight.shape[0]
    slabs = lax.axis_size("seq")
    heads = lax.axis_size("head")
    chips = slabs // 2
    rows = 2 * tok_rows
    width = 2 * tok_cols
    height = rows * slabs
    half_rows = height // 2
    chip_channels = out_channels // chips
    pad_channels = -(-chip_channels // 8) * 8
    real_rows = 9 * pad_channels
    padded = -(-real_rows // 16) * 16
    lanes = (half_rows + 2) * width
    live = min(3, frames)
    me_index = lax.axis_index("seq")
    me = me_index.astype(jnp.int32).reshape(1)
    top = slabs // 2
    rest = [m for m in range(2, top, 2)]

    flat = cotangent.reshape(chips, chip_channels, frames * rows * width)
    chip = me_index // 2

    def wanted(side):
        return jnp.stack(
            [
                lax.dynamic_index_in_dim(flat, chip ^ ((m ^ side) // 2), 0, keepdims=False)
                for m in [0] + rest
            ]
        )

    near, far = wanted(0), wanted(top)
    got = xor_permute(far, "seq", top)
    cot_blocks = []
    cot_masks = []
    for position, mask in enumerate([0] + rest):
        pair = jnp.stack([near[position], got[position]])
        cot_blocks.append(pair if mask == 0 else xor_permute(pair, "seq", mask))
        cot_masks.append([mask, mask ^ top])
    cot_blocks = cot_blocks + [xor_permute(b, "seq", 1) for b in cot_blocks]
    cot_masks = cot_masks + [[m ^ 1 for m in masks] for masks in cot_masks]
    cot = pl.pallas_call(
        functools.partial(cotangent_kernel, frames, rows, half_rows, pad_channels, cot_masks),
        out_shape=jax.ShapeDtypeStruct((frames * padded, lanes), BF16),
        in_specs=[smem()] + [vmem()] * len(cot_blocks),
        out_specs=vmem(),
        scratch_shapes=[pltpu.VMEM((frames, 3 * pad_channels, (half_rows + 4) * width), F32)],
        compiler_params=params(),
        name="cotangent",
    )(me, *cot_blocks)

    flattened = attn_out.reshape(frames * tok_rows * tok_cols, model_width)
    partial_sum = lax.dot_general(
        w_proj, flattened, (((0,), (1,)), ((), ())), preferred_element_type=F32
    )
    step = heads // 2
    other = jnp.zeros_like(partial_sum)
    while step >= 1:
        other = xor_permute(partial_sum, "head", step)
        if step > 1:
            partial_sum = partial_sum + other
        step //= 2
    latent = pl.pallas_call(
        functools.partial(unpatchify_kernel, frames, tok_rows, tok_cols),
        out_shape=jax.ShapeDtypeStruct((latent_width, frames * rows * width), BF16),
        in_specs=[vmem(), vmem()],
        out_specs=vmem(),
        compiler_params=params(),
        name="unpatchify",
    )(partial_sum, other)

    pair = jnp.stack([latent, xor_permute(latent, "seq", top)])
    lats = [pair] + [xor_permute(pair, "seq", m) for m in rest]
    lat_masks = [[m, m ^ top] for m in [0] + rest]
    lats = lats + [xor_permute(b, "seq", 1) for b in lats]
    lat_masks = lat_masks + [[m ^ 1 for m in masks] for masks in lat_masks]

    entry = entry_weight.reshape(channels, 3, 9 * latent_width)
    entries = [entry[:, max(0, 2 - f) :].reshape(channels, -1) for f in range(frames)]
    gain = norm_gain.reshape(channels, 1)
    keep, send = pl.pallas_call(
        functools.partial(gradient_kernel, frames, rows, half_rows, height, lat_masks, real_rows),
        out_shape=(
            jax.ShapeDtypeStruct((real_rows, channels), F32),
            jax.ShapeDtypeStruct((real_rows, channels), BF16),
        ),
        in_specs=[smem(), pl.BlockSpec(memory_space=pl.ANY), vmem()]
        + [vmem()] * (frames + len(lats)),
        out_specs=(vmem(), vmem()),
        scratch_shapes=[
            pltpu.VMEM((frames, 3 * latent_width, (height + 4) * width), BF16),
            pltpu.VMEM((channels, lanes), F32),
            pltpu.VMEM((channels, lanes), F32),
            pltpu.VMEM((channels, lanes), BF16),
            pltpu.VMEM((channels, lanes), BF16),
            pltpu.VMEM((live * padded, channels), F32),
            pltpu.VMEM((channels, LANES), F32),
            pltpu.VMEM((frames * padded, lanes), BF16),
            pltpu.SemaphoreType.DMA(()),
        ],
        compiler_params=params(),
        name="gradient",
    )(me, cot, gain, *entries, *lats)
    block = (keep + xor_permute(send, "seq", 1).astype(F32)).astype(BF16)

    columns = [m for m in range(0, slabs, 4)]
    direct = [block] + [xor_permute(block, "seq", m) for m in columns[1:]]
    beside = xor_permute(block, "seq", 2)
    held = lax.optimization_barrier((block, *lats))[1:]
    conv = conv_weight.transpose(1, 2, 3, 0, 4).reshape(27, out_channels, channels)
    decoded = pl.pallas_call(
        functools.partial(decode_kernel, frames, rows, height, lat_masks),
        out_shape=jax.ShapeDtypeStruct((out_channels, frames * rows * width), BF16),
        in_specs=[smem(), vmem(), pl.BlockSpec(memory_space=pl.ANY)]
        + [vmem()] * (frames + len(lats)),
        out_specs=vmem(),
        scratch_shapes=[
            pltpu.VMEM((frames, 3 * latent_width, (height + 4) * width), BF16),
            pltpu.VMEM((channels, (rows + 2) * width), F32),
            pltpu.VMEM((channels, (rows + 2) * width), BF16),
            pltpu.VMEM((frames, 3, channels, (rows + 2) * width), BF16),
            pltpu.VMEM((channels, LANES), F32),
            pltpu.VMEM((live * 9, out_channels, channels), BF16),
            pltpu.SemaphoreType.DMA(()),
        ],
        compiler_params=params(),
        name="decode",
    )(me, gain, conv, *entries, *held)
    decoded = decoded.reshape(out_channels, frames, rows, width)

    blank = 3 - live
    shape = (9, pad_channels, channels)
    grad_shape = (3, 9, chips * pad_channels, channels)

    def finish(parts, masks, grad=None):
        first = grad is None
        return pl.pallas_call(
            functools.partial(finish_kernel, first, masks, blank),
            out_shape=jax.ShapeDtypeStruct(grad_shape, F32),
            in_specs=[smem()]
            + [vmem()] * len(parts)
            + ([] if first else [pl.BlockSpec(memory_space=pl.ANY)]),
            out_specs=pl.BlockSpec(memory_space=pl.ANY),
            scratch_shapes=[
                pltpu.VMEM((len(parts),) + shape, F32),
                pltpu.VMEM((chips * pad_channels, channels), F32),
                pltpu.SemaphoreType.DMA((len(parts),)),
                pltpu.SemaphoreType.DMA((max(1, 9 * blank),)),
            ],
            input_output_aliases={} if first else {len(parts) + 1: 0},
            compiler_params=params(),
            name="finish",
        )(me, *[p.reshape(shape) for p in parts], *([] if first else [grad]))

    early = [block, beside]
    early_masks = [0, 2]
    early = early + [xor_permute(p, "seq", 1) for p in early]
    early_masks = early_masks + [m ^ 1 for m in early_masks]
    grad = finish(early, early_masks)
    after = lax.optimization_barrier((decoded, grad, *direct[1:]))
    decoded, grad, late = after[0], after[1], list(after[2:])
    late_masks = columns[1:]
    late = late + [xor_permute(p, "seq", 2) for p in late]
    late_masks = late_masks + [m ^ 2 for m in late_masks]
    late = late + [xor_permute(p, "seq", 1) for p in late]
    late_masks = late_masks + [m ^ 1 for m in late_masks]
    grad = finish(late, late_masks, grad)
    if pad_channels != chip_channels:
        grad = grad.reshape(27, chips, pad_channels, channels)[:, :, :chip_channels]
    grad = grad.reshape(3, 3, 3, out_channels, channels).transpose(3, 0, 1, 2, 4)
    return decoded, grad


def solution(mesh):
    return jax.shard_map(
        per_device,
        mesh=mesh,
        in_specs=(
            P(None, "seq", None, "head"),
            P("head", None),
            P(),
            P(),
            P("head", None, None, None, None),
            P("head", None, "seq", None),
        ),
        out_specs=(P("head", None, "seq", None), P("head", None, None, None, None)),
        check_vma=False,
    )
```

time: 123 us -> 104 us (0.85)
  Pallas kernels: 47.4 us -> 32.4 us
  local copies, waits for them, and re-layouts: 16.8 us -> 10.4 us
  waiting for transfers between devices: 30.6 us -> 32.3 us
    pallas_call x1, Pallas kernels: 24.7 us -> 10.8 us  [per_device(): pl.pallas_call(functools.partial(gradient_kernel, frames, rows, half_rows...]
    unnamed x60 -> x75, local copies, waits for them, and re-layouts: 9.13 us -> 5.34 us
    pallas_call x2 -> x3, Pallas kernels: 17.5 us -> 15.5 us  [the longest x1 8.53 us: per_device(): pl.pallas_call(functools.partial(decode_kernel, frames, rows, height, lat...]
    slice x3 -> x1, local copies, waits for them, and re-layouts: 1.8 us -> 0.01 us  [per_device(): pair = jnp.stack([near[position], got[position]])]
    unnamed x1 -> x0, other arithmetic: 1.67 us -> none
    ppermute x18 -> x33, waiting for transfers between devices: 30.6 us -> 32.3 us  [xor_permute(): lax.ppermute(x, axis, [(i, i ^ mask) for i in range(lax.axis_size(axis))])]
    ppermute x18 -> x33, starting transfers between devices: 23.1 us -> 23.8 us  [xor_permute(): lax.ppermute(x, axis, [(i, i ^ mask) for i in range(lax.axis_size(axis))])]
  transfers between devices with their start and end apart: 18 -> 33, of which waited for: 10 -> 11; matrix products, arithmetic and copies ran while one was open for 11% -> 6% of each run, Pallas kernels for 7% -> 17%
where the time goes in v2:
time: 104 us
  Pallas kernels  32.4 us (31%)
  waiting for transfers between devices  32.3 us (31%)
  starting transfers between devices  23.8 us (23%)
  local copies, waits for them, and re-layouts  10.4 us (10%)
  other arithmetic  1.85 us (2%)
  matrix products  1.48 us (1%)
  between operations  1.39 us (1%)
    ppermute x33, waiting for transfers between devices, xor_permute(): lax.ppermute(x, axis, [(i, i ^ mask) for i in range(lax.axis_size(axis))])  32.3 us
    ppermute x33, starting transfers between devices, xor_permute(): lax.ppermute(x, axis, [(i, i ^ mask) for i in range(lax.axis_size(axis))])  23.8 us
    pallas_call x1, Pallas kernels, per_device(): pl.pallas_call(functools.partial(gradient_kernel, frames, rows, half_rows...  10.8 us
    pallas_call x1, Pallas kernels, per_device(): pl.pallas_call(functools.partial(decode_kernel, frames, rows, height, lat...  8.53 us
    pallas_call x2, Pallas kernels, finish(): pl.pallas_call(functools.partial(finish_kernel, first, masks, blank), out...  6.94 us
    unnamed x75, local copies, waits for them, and re-layouts  5.34 us
    pallas_call x1, Pallas kernels, per_device(): pl.pallas_call(functools.partial(cotangent_kernel, frames, rows, half_row...  4.46 us
  transfers between devices with their start and end apart: 33, of which 11 were waited for; matrix products, arithmetic and copies ran while one was open for 6% of the time, Pallas kernels for 17%

profile of v2, /device:TPU:0, one launch (start us, length us, event | category | flops | bytes accessed | tf_op | source)
XLA Modules:
  0.0 103.6 jit_solution(17614653548600076449)
XLA Ops:
  0.7 1.3 %copy-done = bf16[2,2,64,2560]{3,2,1,0:T(8,128)(2,1)S(1)} copy-done((bf16[2,2,64,2560]{3,2,1,0:T(8,128)(2,1)S(1)}, bf16[2,2,64,2560]{3,2,1,0:T(8,128)(2,1)}, u32[]{:S(2)}) %copy-start) | copy-done | bytes 1310744
  2.0 1.5 %fusion.1.own_ref = f32[64,256]{1,0:T(8,128)S(1)} fusion(bf16[2560,64]{0,1:T(8,128)(2,1)} %param.7, bf16[256,2560]{1,0:T(8,128)(2,1)S(1)} %bitcast.31), kind=kOutput, calls=%fused_computation.16 | convolution fusion | flops 83886080 | bytes 1703936 | tf_op jit(solution)/shard_map/dot_general | solution.py:340
  3.5 3.0 %collective-permute-start.8 = (f32[64,256]{1,0:T(8,128)S(1)}, f32[64,256]{1,0:T(8,128)S(1)}, u32[]{:S(2)}, u32[]{:S(2)}) collective-permute-start(f32[64,256]{1,0:T(8,128)S(1)} %fusion.1.own_ref), channel_id=1, source_target_pairs={{0,1},{1,0},{2,3},{3,2},{4,5},{5,4},{6,7},{7,6},{8,9},{9,8},{10,11... | collective-permute-start | bytes 196616 | tf_op jit(solution)/shard_map/ppermute | solution.py:29
  6.5 1.3 %reshape.88 = bf16[8,24,1024]{2,1,0:T(8,128)(2,1)S(1)} reshape(bf16[192,2,4,128]{3,2,1,0:T(4,128)(2,1)} %param.11) | data formatting | bytes 786432 | tf_op jit(solution)/shard_map/reshape | solution.py:308
  7.8 2.7 %collective-permute-start = (bf16[4,24,1024]{2,1,0:T(8,128)(2,1)S(1)}, bf16[4,24,1024]{2,1,0:T(8,128)(2,1)S(1)}, u32[]{:S(2)}, u32[]{:S(2)}) collective-permute-start(bf16[4,24,1024]{2,1,0:T(8,128)(2,1)S(1)} %pad_maximum_fusion), channel_id=1, source_target_pairs={{0,16},{2,18},{4,20},{6,22},{8,24},{10,26},{12,28},{14,30},{16,0},... | collective-permute-start | bytes 589832 | tf_op jit(solution)/shard_map/ppermute | solution.py:29
  10.5 0.6 copy-done.35
  11.1 1.7 %unpatchify.1 = bf16[16,1024]{1,0:T(8,128)(2,1)} custom-call(f32[64,256]{1,0:T(8,128)} %copy-done.12, f32[64,256]{1,0:T(8,128)} %copy-done.35), custom_call_target="tpu_custom_call" | custom-call | tf_op jit(solution)/shard_map/unpatchify/pallas_call | solution.py:350
  12.8 1.3 %collective-permute-start.9 = (bf16[16,1024]{1,0:T(8,128)(2,1)}, bf16[16,1024]{1,0:T(8,128)(2,1)S(1)}, u32[]{:S(2)}, u32[]{:S(2)}) collective-permute-start(bf16[16,1024]{1,0:T(8,128)(2,1)} %unpatchify.1), channel_id=1, source_target_pairs={{0,16},{2,18},{4,20},{6,22},{8,24},{10,26},{12,28},{14,30},{16,0},... | collective-permute-start | bytes 98312 | tf_op jit(solution)/shard_map/ppermute | solution.py:29
  14.1 6.7 %collective-permute-done.9 = bf16[16,1024]{1,0:T(8,128)(2,1)S(1)} collective-permute-done((bf16[16,1024]{1,0:T(8,128)(2,1)}, bf16[16,1024]{1,0:T(8,128)(2,1)S(1)}, u32[]{:S(2)}, u32[]{:S(2)}) %collective-permute-start.9) | collective-permute-done | bytes 32800 | tf_op jit(solution)/shard_map/ppermute | solution.py:29
  20.8 0.8 pad_maximum_fusion.5.refs_5_
  21.6 1.8 %collective-permute-start.12 = (bf16[2,16,1024]{2,1,0:T(8,128)(2,1)S(1)}, bf16[2,16,1024]{2,1,0:T(8,128)(2,1)S(1)}, u32[]{:S(2)}, u32[]{:S(2)}) collective-permute-start(bf16[2,16,1024]{2,1,0:T(8,128)(2,1)S(1)} %pad_maximum_fusion.5.refs_5_), channel_id=1, source_target_pairs={{0,12},{2,14},{4,8},{6,10},{8,4},{10,6},{12,0},{14,2},{16,28},{18,... | collective-permute-start | bytes 196616 | tf_op jit(solution)/shard_map/ppermute | solution.py:29
  23.4 1.3 %collective-permute-start.11 = (bf16[2,16,1024]{2,1,0:T(8,128)(2,1)S(1)}, bf16[2,16,1024]{2,1,0:T(8,128)(2,1)S(1)}, u32[]{:S(2)}, u32[]{:S(2)}) collective-permute-start(bf16[2,16,1024]{2,1,0:T(8,128)(2,1)S(1)} %pad_maximum_fusion.5.refs_5_), channel_id=1, source_target_pairs={{0,8},{2,10},{4,12},{6,14},{8,0},{10,2},{12,4},{14,6},{16,24},{18,... | collective-permute-start | bytes 196616 | tf_op jit(solution)/shard_map/ppermute | solution.py:29
  24.7 0.6 collective-permute-start.1
  25.2 0.8 collective-permute-start.2
  26.1 2.3 %collective-permute-start.3 = (bf16[2,24,1024]{2,1,0:T(8,128)(2,1)S(1)}, bf16[2,24,1024]{2,1,0:T(8,128)(2,1)S(1)}, u32[]{:S(2)}, u32[]{:S(2)}) collective-permute-start(bf16[2,24,1024]{2,1,0:T(8,128)(2,1)S(1)} %pad_maximum_fusion.4), channel_id=1, source_target_pairs={{0,12},{2,14},{4,8},{6,10},{8,4},{10,6},{12,0},{14,2},{16,28},{18,... | collective-permute-start | bytes 294920 | tf_op jit(solution)/shard_map/ppermute | solution.py:29
  28.5 1.9 %collective-permute-done.1.refs_1_ = bf16[2,24,1024]{2,1,0:T(8,128)(2,1)S(1)} collective-permute-done((bf16[2,24,1024]{2,1,0:T(8,128)(2,1)S(1)}, bf16[2,24,1024]{2,1,0:T(8,128)(2,1)S(1)}, u32[]{:S(2)}, u32[]{:S(2)}) %collective-permute-start.1) | collective-permute-done | bytes 98336 | tf_op jit(solution)/shard_map/ppermute | solution.py:29
  30.4 0.6 collective-permute-done.2.refs_2_
  31.0 0.6 collective-permute-start.10
  32.0 3.5 %collective-permute-done.10.refs_6_ = bf16[2,16,1024]{2,1,0:T(8,128)(2,1)S(1)} collective-permute-done((bf16[2,16,1024]{2,1,0:T(8,128)(2,1)S(1)}, bf16[2,16,1024]{2,1,0:T(8,128)(2,1)S(1)}, u32[]{:S(2)}, u32[]{:S(2)}) %collective-permute-start.10) | collective-permute-done | bytes 65568 | tf_op jit(solution)/shard_map/ppermute | solution.py:29
  35.5 0.5 collective-permute-start.16
  36.1 0.4 collective-permute-start.14
  36.6 0.8 copy.16
  37.4 0.8 reshape.108.refs_2_.refs_1_
  38.2 0.9 copy.15.refs_4_
  39.2 0.6 copy-done.34
  39.7 4.5 %cotangent.1.refs_1_ = bf16[448,4352]{1,0:T(8,128)(2,1)} custom-call(s32[1]{0:T(128)} %bitcast.me_ref.refs_0_, bf16[2,24,1024]{2,1,0:T(8,128)(2,1)} %copy-done.3, bf16[2,24,1024]{2,1,0:T(8,128)(2,1)} %copy-done.28, bf16[2,24,1024]{2,1,0:T(8,128)(2,1)} %copy-done.29, bf16[2,24,1024]{2,1,0:T(8,128)(2,1)} %copy-done.30, bf16[2,24,1024]{2,1,0:T(8,128)(2,1)} %copy-done.31, ...), custom_call_target="tpu_custom_call" | custom-call | tf_op jit(solution)/shard_map/cotangent/pallas_call | solution.py:329
  44.3 0.5 copy-done.8
  44.9 10.8 %gradient.1 = (f32[216,384]{1,0:T(8,128)}, bf16[216,384]{1,0:T(8,128)(2,1)}) custom-call(s32[1]{0:T(128)} %bitcast.me_ref.refs_0_, bf16[448,4352]{1,0:T(8,128)(2,1)} %cotangent.1.refs_1_, f32[384,1]{1,0:T(8,128)} %reshape.108.refs_2_.refs_1_, bf16[384,144]{1,0:T(8,128)(2,1)} %bitcast.34, bf16[384,288]{1,0:T(8,128)(2,1)} %copy.15.refs_4_, ...), custom_call_target="tpu_custom_call" | custom-call | tf_op jit(solution)/shard_map/gradient/pallas_call | solution.py:368
  55.9 1.5 %collective-permute-done.17 = bf16[216,384]{1,0:T(8,128)(2,1)S(1)} collective-permute-done((bf16[216,384]{1,0:T(8,128)(2,1)}, bf16[216,384]{1,0:T(8,128)(2,1)S(1)}, u32[]{:S(2)}, u32[]{:S(2)}) %collective-permute-start.17) | collective-permute-done | bytes 165920 | tf_op jit(solution)/shard_map/ppermute | solution.py:29
  57.4 1.0 add_convert_fusion
  58.4 0.6 collective-permute-start.18
  59.1 5.7 %collective-permute-done.18 = bf16[216,384]{1,0:T(8,128)(2,1)S(1)} collective-permute-done((bf16[216,384]{1,0:T(8,128)(2,1)S(1)}, bf16[216,384]{1,0:T(8,128)(2,1)S(1)}, u32[]{:S(2)}, u32[]{:S(2)}) %collective-permute-start.18) | collective-permute-done | bytes 165920 | tf_op jit(solution)/shard_map/ppermute | solution.py:29
  64.8 3.6 %collective-permute-start.23 = (bf16[216,384]{1,0:T(8,128)(2,1)S(1)}, bf16[216,384]{1,0:T(8,128)(2,1)S(1)}, u32[]{:S(2)}, u32[]{:S(2)}) collective-permute-start(bf16[216,384]{1,0:T(8,128)(2,1)S(1)} %add_convert_fusion), channel_id=1, source_target_pairs={{0,24},{2,26},{4,28},{6,30},{8,16},{10,18},{12,20},{14,22},{16,8},... | collective-permute-start | bytes 497672 | tf_op jit(solution)/shard_map/ppermute | solution.py:29
  68.4 0.8 collective-permute-start.21
  69.2 8.5 %decode.1 = bf16[192,1024]{1,0:T(8,128)(2,1)} custom-call(s32[1]{0:T(128)} %bitcast.me_ref.refs_0_, f32[384,1]{1,0:T(8,128)} %reshape.108.refs_2_.refs_1_, bf16[27,192,384]{2,1,0:T(8,128)(2,1)} %bitcast.33, bf16[384,144]{1,0:T(8,128)(2,1)} %bitcast.35, bf16[384,288]{1,0:T(8,128)(2,1)} %copy.15.refs_4_, bf16[2,16,1024]{2,1,0:T(8,128)(2,1)} %copy-done.2, ...), custom_call_target="tpu_custom_call" | custom-call | tf_op jit(solution)/shard_map/decode/pallas_call | solution.py:398
  77.7 2.0 %reshape.90 = bf16[192,2,4,128]{3,2,1,0:T(4,128)(2,1)} reshape(bf16[192,1024]{1,0:T(8,128)(2,1)} %decode.1) | data formatting | bytes 786432 | tf_op jit(solution)/shard_map/reshape | solution.py:416
  79.8 0.6 copy-done.23
  80.5 3.2 %finish.2.refs_12_ = f32[3,9,192,384]{3,2,1,0:T(8,128)} custom-call(s32[1]{0:T(128)} %bitcast.me_ref.refs_0_, bf16[9,24,384]{2,1,0:T(8,128)(2,1)} %bitcast.37, bf16[9,24,384]{2,1,0:T(8,128)(2,1)} %bitcast.49, bf16[9,24,384]{2,1,0:T(8,128)(2,1)} %bitcast.50, bf16[9,24,384]{2,1,0:T(8,128)(2,1)} %bitcast.52), custom_call_target="tpu_custom_call" | custom-call | tf_op jit(solution)/shard_map/finish/pallas_call | solution.py:424
  83.9 0.6 collective-permute-start.24
  84.5 1.5 %collective-permute-start.25 = (bf16[216,384]{1,0:T(8,128)(2,1)S(1)}, bf16[216,384]{1,0:T(8,128)(2,1)S(1)}, u32[]{:S(2)}, u32[]{:S(2)}) collective-permute-start(bf16[216,384]{1,0:T(8,128)(2,1)S(1)} %collective-permute-done.22), channel_id=1, source_target_pairs={{0,4},{2,6},{4,0},{6,2},{8,12},{10,14},{12,8},{14,10},{16,20},{18,... | collective-permute-start | bytes 497672 | tf_op jit(solution)/shard_map/ppermute | solution.py:29
  86.0 0.5 collective-permute-start.26
  86.5 0.5 collective-permute-start.29
  87.0 4.0 %collective-permute-done.24 = bf16[216,384]{1,0:T(8,128)(2,1)S(1)} collective-permute-done((bf16[216,384]{1,0:T(8,128)(2,1)S(1)}, bf16[216,384]{1,0:T(8,128)(2,1)S(1)}, u32[]{:S(2)}, u32[]{:S(2)}) %collective-permute-start.24) | collective-permute-done | bytes 165920 | tf_op jit(solution)/shard_map/ppermute | solution.py:29
  91.0 3.5 %collective-permute-done.25 = bf16[216,384]{1,0:T(8,128)(2,1)S(1)} collective-permute-done((bf16[216,384]{1,0:T(8,128)(2,1)S(1)}, bf16[216,384]{1,0:T(8,128)(2,1)S(1)}, u32[]{:S(2)}, u32[]{:S(2)}) %collective-permute-start.25) | collective-permute-done | bytes 165920 | tf_op jit(solution)/shard_map/ppermute | solution.py:29
  94.5 3.1 %collective-permute-done.26 = bf16[216,384]{1,0:T(8,128)(2,1)S(1)} collective-permute-done((bf16[216,384]{1,0:T(8,128)(2,1)S(1)}, bf16[216,384]{1,0:T(8,128)(2,1)S(1)}, u32[]{:S(2)}, u32[]{:S(2)}) %collective-permute-start.26) | collective-permute-done | bytes 165920 | tf_op jit(solution)/shard_map/ppermute | solution.py:29
  97.7 1.3 %collective-permute-done.32 = bf16[216,384]{1,0:T(8,128)(2,1)S(1)} collective-permute-done((bf16[216,384]{1,0:T(8,128)(2,1)S(1)}, bf16[216,384]{1,0:T(8,128)(2,1)S(1)}, u32[]{:S(2)}, u32[]{:S(2)}) %collective-permute-start.32) | collective-permute-done | bytes 165920 | tf_op jit(solution)/shard_map/ppermute | solution.py:29
  99.1 0.6 copy-done.27
  99.7 3.7 %finish.3 = f32[3,9,192,384]{3,2,1,0:T(8,128)} custom-call(s32[1]{0:T(128)} %bitcast.me_ref.refs_0_, bf16[9,24,384]{2,1,0:T(8,128)(2,1)} %bitcast.42, bf16[9,24,384]{2,1,0:T(8,128)(2,1)} %bitcast.41, bf16[9,24,384]{2,1,0:T(8,128)(2,1)} %bitcast.40, bf16[9,24,384]{2,1,0:T(8,128)(2,1)} %bitcast.44, ...), custom_call_target="tpu_custom_call", output_to_operand_aliasing={{}: (13, {})} | custom-call | tf_op jit(solution)/shard_map/finish/pallas_call | solution.py:424
  (115 shorter events, 1.3 us)
Async XLA Ops:
  0.6 35.9 %copy-start.4 = (bf16[384,3,3,3,16]{0,4,3,2,1:T(8,128)(2,1)S(1)}, bf16[384,3,3,3,16]{0,4,3,2,1:T(8,128)(2,1)}, u32[]{:S(2)}) copy-start(bf16[384,3,3,3,16]{0,4,3,2,1:T(8,128)(2,1)} %param.9) | copy-start | bytes 995332
  0.7 36.8 %copy-start.36 = (f32[384]{0:T(512)S(1)}, f32[384]{0:T(512)}, u32[]{:S(2)}) copy-start(f32[384]{0:T(512)} %param.8) | copy-start | bytes 4612
  3.5 7.1 %collective-permute-start.8 = (f32[64,256]{1,0:T(8,128)S(1)}, f32[64,256]{1,0:T(8,128)S(1)}, u32[]{:S(2)}, u32[]{:S(2)}) collective-permute-start(f32[64,256]{1,0:T(8,128)S(1)} %fusion.1.own_ref), channel_id=1, source_target_pairs={{0,1},{1,0},{2,3},{3,2},{4,5},{5,4},{6,7},{7,6},{8,9},{9,8},{10,11... | collective-permute-start | bytes 196616 | tf_op jit(solution)/shard_map/ppermute | solution.py:29
  7.8 16.8 %collective-permute-start = (bf16[4,24,1024]{2,1,0:T(8,128)(2,1)S(1)}, bf16[4,24,1024]{2,1,0:T(8,128)(2,1)S(1)}, u32[]{:S(2)}, u32[]{:S(2)}) collective-permute-start(bf16[4,24,1024]{2,1,0:T(8,128)(2,1)S(1)} %pad_maximum_fusion), channel_id=1, source_target_pairs={{0,16},{2,18},{4,20},{6,22},{8,24},{10,26},{12,28},{14,30},{16,0},... | collective-permute-start | bytes 589832 | tf_op jit(solution)/shard_map/ppermute | solution.py:29
  12.8 8.0 %collective-permute-start.9 = (bf16[16,1024]{1,0:T(8,128)(2,1)}, bf16[16,1024]{1,0:T(8,128)(2,1)S(1)}, u32[]{:S(2)}, u32[]{:S(2)}) collective-permute-start(bf16[16,1024]{1,0:T(8,128)(2,1)} %unpatchify.1), channel_id=1, source_target_pairs={{0,16},{2,18},{4,20},{6,22},{8,24},{10,26},{12,28},{14,30},{16,0},... | collective-permute-start | bytes 98312 | tf_op jit(solution)/shard_map/ppermute | solution.py:29
  21.6 22.7 %copy-start.2 = (bf16[2,16,1024]{2,1,0:T(8,128)(2,1)}, bf16[2,16,1024]{2,1,0:T(8,128)(2,1)S(1)}, u32[]{:S(2)}) copy-start(bf16[2,16,1024]{2,1,0:T(8,128)(2,1)S(1)} %pad_maximum_fusion.5.refs_5_) | copy-start | bytes 196612
  21.6 6.8 %collective-permute-start.12 = (bf16[2,16,1024]{2,1,0:T(8,128)(2,1)S(1)}, bf16[2,16,1024]{2,1,0:T(8,128)(2,1)S(1)}, u32[]{:S(2)}, u32[]{:S(2)}) collective-permute-start(bf16[2,16,1024]{2,1,0:T(8,128)(2,1)S(1)} %pad_maximum_fusion.5.refs_5_), channel_id=1, source_target_pairs={{0,12},{2,14},{4,8},{6,10},{8,4},{10,6},{12,0},{14,2},{16,28},{18,... | collective-permute-start | bytes 196616 | tf_op jit(solution)/shard_map/ppermute | solution.py:29
  23.4 7.6 %collective-permute-start.11 = (bf16[2,16,1024]{2,1,0:T(8,128)(2,1)S(1)}, bf16[2,16,1024]{2,1,0:T(8,128)(2,1)S(1)}, u32[]{:S(2)}, u32[]{:S(2)}) collective-permute-start(bf16[2,16,1024]{2,1,0:T(8,128)(2,1)S(1)} %pad_maximum_fusion.5.refs_5_), channel_id=1, source_target_pairs={{0,8},{2,10},{4,12},{6,14},{8,0},{10,2},{12,4},{14,6},{16,24},{18,... | collective-permute-start | bytes 196616 | tf_op jit(solution)/shard_map/ppermute | solution.py:29
  24.7 5.7 %collective-permute-start.1 = (bf16[2,24,1024]{2,1,0:T(8,128)(2,1)S(1)}, bf16[2,24,1024]{2,1,0:T(8,128)(2,1)S(1)}, u32[]{:S(2)}, u32[]{:S(2)}) collective-permute-start(bf16[2,24,1024]{2,1,0:T(8,128)(2,1)S(1)} %pad_maximum_fusion.2), channel_id=1, source_target_pairs={{0,4},{2,6},{4,0},{6,2},{8,12},{10,14},{12,8},{14,10},{16,20},{18,... | collective-permute-start | bytes 294920 | tf_op jit(solution)/shard_map/ppermute | solution.py:29
  25.2 5.7 %collective-permute-start.2 = (bf16[2,24,1024]{2,1,0:T(8,128)(2,1)S(1)}, bf16[2,24,1024]{2,1,0:T(8,128)(2,1)S(1)}, u32[]{:S(2)}, u32[]{:S(2)}) collective-permute-start(bf16[2,24,1024]{2,1,0:T(8,128)(2,1)S(1)} %pad_maximum_fusion.3), channel_id=1, source_target_pairs={{0,8},{2,10},{4,12},{6,14},{8,0},{10,2},{12,4},{14,6},{16,24},{18,... | collective-permute-start | bytes 294920 | tf_op jit(solution)/shard_map/ppermute | solution.py:29
  26.1 5.9 %collective-permute-start.3 = (bf16[2,24,1024]{2,1,0:T(8,128)(2,1)S(1)}, bf16[2,24,1024]{2,1,0:T(8,128)(2,1)S(1)}, u32[]{:S(2)}, u32[]{:S(2)}) collective-permute-start(bf16[2,24,1024]{2,1,0:T(8,128)(2,1)S(1)} %pad_maximum_fusion.4), channel_id=1, source_target_pairs={{0,12},{2,14},{4,8},{6,10},{8,4},{10,6},{12,0},{14,2},{16,28},{18,... | collective-permute-start | bytes 294920 | tf_op jit(solution)/shard_map/ppermute | solution.py:29
  28.4 10.7 %copy-start.3 = (bf16[2,24,1024]{2,1,0:T(8,128)(2,1)}, bf16[2,24,1024]{2,1,0:T(8,128)(2,1)S(1)}, u32[]{:S(2)}) copy-start(bf16[2,24,1024]{2,1,0:T(8,128)(2,1)S(1)} %pad_maximum_fusion.1.refs_0_) | copy-start | bytes 294916
  28.4 15.9 %copy-start.5 = (bf16[2,16,1024]{2,1,0:T(8,128)(2,1)}, bf16[2,16,1024]{2,1,0:T(8,128)(2,1)S(1)}, u32[]{:S(2)}) copy-start(bf16[2,16,1024]{2,1,0:T(8,128)(2,1)S(1)} %collective-permute-done.12.refs_8_) | copy-start | bytes 196612
  28.4 7.1 %collective-permute-start.4 = (bf16[2,24,1024]{2,1,0:T(8,128)(2,1)S(1)}, bf16[2,24,1024]{2,1,0:T(8,128)(2,1)S(1)}, u32[]{:S(2)}, u32[]{:S(2)}) collective-permute-start(bf16[2,24,1024]{2,1,0:T(8,128)(2,1)S(1)} %pad_maximum_fusion.1.refs_0_), channel_id=1, source_target_pairs={{0,2},{2,0},{4,6},{6,4},{8,10},{10,8},{12,14},{14,12},{16,18},{18,... | collective-permute-start | bytes 294920 | tf_op jit(solution)/shard_map/ppermute | solution.py:29
  30.4 8.7 %copy-start.28 = (bf16[2,24,1024]{2,1,0:T(8,128)(2,1)}, bf16[2,24,1024]{2,1,0:T(8,128)(2,1)S(1)}, u32[]{:S(2)}) copy-start(bf16[2,24,1024]{2,1,0:T(8,128)(2,1)S(1)} %collective-permute-done.1.refs_1_) | copy-start | bytes 294916
  30.4 5.6 %collective-permute-start.5 = (bf16[2,24,1024]{2,1,0:T(8,128)(2,1)S(1)}, bf16[2,24,1024]{2,1,0:T(8,128)(2,1)S(1)}, u32[]{:S(2)}, u32[]{:S(2)}) collective-permute-start(bf16[2,24,1024]{2,1,0:T(8,128)(2,1)S(1)} %collective-permute-done.1.refs_1_), channel_id=1, source_target_pairs={{0,2},{2,0},{4,6},{6,4},{8,10},{10,8},{12,14},{14,12},{16,18},{18,... | collective-permute-start | bytes 294920 | tf_op jit(solution)/shard_map/ppermute | solution.py:29
  31.0 8.2 %copy-start.29 = (bf16[2,24,1024]{2,1,0:T(8,128)(2,1)}, bf16[2,24,1024]{2,1,0:T(8,128)(2,1)S(1)}, u32[]{:S(2)}) copy-start(bf16[2,24,1024]{2,1,0:T(8,128)(2,1)S(1)} %collective-permute-done.2.refs_2_) | copy-start | bytes 294916
  31.0 5.1 %collective-permute-start.6 = (bf16[2,24,1024]{2,1,0:T(8,128)(2,1)S(1)}, bf16[2,24,1024]{2,1,0:T(8,128)(2,1)S(1)}, u32[]{:S(2)}, u32[]{:S(2)}) collective-permute-start(bf16[2,24,1024]{2,1,0:T(8,128)(2,1)S(1)} %collective-permute-done.2.refs_2_), channel_id=1, source_target_pairs={{0,2},{2,0},{4,6},{6,4},{8,10},{10,8},{12,14},{14,12},{16,18},{18,... | collective-permute-start | bytes 294920 | tf_op jit(solution)/shard_map/ppermute | solution.py:29
  31.0 13.3 %copy-start.6 = (bf16[2,16,1024]{2,1,0:T(8,128)(2,1)}, bf16[2,16,1024]{2,1,0:T(8,128)(2,1)S(1)}, u32[]{:S(2)}) copy-start(bf16[2,16,1024]{2,1,0:T(8,128)(2,1)S(1)} %collective-permute-done.11.refs_7_) | copy-start | bytes 196612
  31.0 4.5 %collective-permute-start.10 = (bf16[2,16,1024]{2,1,0:T(8,128)(2,1)S(1)}, bf16[2,16,1024]{2,1,0:T(8,128)(2,1)S(1)}, u32[]{:S(2)}, u32[]{:S(2)}) collective-permute-start(bf16[2,16,1024]{2,1,0:T(8,128)(2,1)S(1)} %pad_maximum_fusion.5.refs_5_), channel_id=1, source_target_pairs={{0,4},{2,6},{4,0},{6,2},{8,12},{10,14},{12,8},{14,10},{16,20},{18,... | collective-permute-start | bytes 196616 | tf_op jit(solution)/shard_map/ppermute | solution.py:29
  32.0 7.1 %collective-permute-start.7 = (bf16[2,24,1024]{2,1,0:T(8,128)(2,1)S(1)}, bf16[2,24,1024]{2,1,0:T(8,128)(2,1)S(1)}, u32[]{:S(2)}, u32[]{:S(2)}) collective-permute-start(bf16[2,24,1024]{2,1,0:T(8,128)(2,1)S(1)} %collective-permute-done.3.refs_3_), channel_id=1, source_target_pairs={{0,2},{2,0},{4,6},{6,4},{8,10},{10,8},{12,14},{14,12},{16,18},{18,... | collective-permute-start | bytes 294920 | tf_op jit(solution)/shard_map/ppermute | solution.py:29
  35.5 8.8 %copy-start.7 = (bf16[2,16,1024]{2,1,0:T(8,128)(2,1)}, bf16[2,16,1024]{2,1,0:T(8,128)(2,1)S(1)}, u32[]{:S(2)}) copy-start(bf16[2,16,1024]{2,1,0:T(8,128)(2,1)S(1)} %collective-permute-done.10.refs_6_) | copy-start | bytes 196612
  35.5 8.7 %collective-permute-start.13 = (bf16[2,16,1024]{2,1,0:T(8,128)(2,1)S(1)}, bf16[2,16,1024]{2,1,0:T(8,128)(2,1)S(1)}, u32[]{:S(2)}, u32[]{:S(2)}) collective-permute-start(bf16[2,16,1024]{2,1,0:T(8,128)(2,1)S(1)} %pad_maximum_fusion.5.refs_5_), channel_id=1, source_target_pairs={{0,2},{2,0},{4,6},{6,4},{8,10},{10,8},{12,14},{14,12},{16,18},{18,... | collective-permute-start | bytes 196616 | tf_op jit(solution)/shard_map/ppermute | solution.py:29
  35.5 8.7 %collective-permute-start.16 = (bf16[2,16,1024]{2,1,0:T(8,128)(2,1)S(1)}, bf16[2,16,1024]{2,1,0:T(8,128)(2,1)S(1)}, u32[]{:S(2)}, u32[]{:S(2)}) collective-permute-start(bf16[2,16,1024]{2,1,0:T(8,128)(2,1)S(1)} %collective-permute-done.12.refs_8_), channel_id=1, source_target_pairs={{0,2},{2,0},{4,6},{6,4},{8,10},{10,8},{12,14},{14,12},{16,18},{18,... | collective-permute-start | bytes 196616 | tf_op jit(solution)/shard_map/ppermute | solution.py:29
  36.0 8.2 %collective-permute-start.15 = (bf16[2,16,1024]{2,1,0:T(8,128)(2,1)S(1)}, bf16[2,16,1024]{2,1,0:T(8,128)(2,1)S(1)}, u32[]{:S(2)}, u32[]{:S(2)}) collective-permute-start(bf16[2,16,1024]{2,1,0:T(8,128)(2,1)S(1)} %collective-permute-done.11.refs_7_), channel_id=1, source_target_pairs={{0,2},{2,0},{4,6},{6,4},{8,10},{10,8},{12,14},{14,12},{16,18},{18,... | collective-permute-start | bytes 196616 | tf_op jit(solution)/shard_map/ppermute | solution.py:29
  36.1 8.1 %collective-permute-start.14 = (bf16[2,16,1024]{2,1,0:T(8,128)(2,1)S(1)}, bf16[2,16,1024]{2,1,0:T(8,128)(2,1)S(1)}, u32[]{:S(2)}, u32[]{:S(2)}) collective-permute-start(bf16[2,16,1024]{2,1,0:T(8,128)(2,1)S(1)} %collective-permute-done.10.refs_6_), channel_id=1, source_target_pairs={{0,2},{2,0},{4,6},{6,4},{8,10},{10,8},{12,14},{14,12},{16,18},{18,... | collective-permute-start | bytes 196616 | tf_op jit(solution)/shard_map/ppermute | solution.py:29
  55.7 1.7 %collective-permute-start.17 = (bf16[216,384]{1,0:T(8,128)(2,1)}, bf16[216,384]{1,0:T(8,128)(2,1)S(1)}, u32[]{:S(2)}, u32[]{:S(2)}) collective-permute-start(bf16[216,384]{1,0:T(8,128)(2,1)} %get-tuple-element.18), channel_id=1, source_target_pairs={{0,2},{2,0},{4,6},{6,4},{8,10},{10,8},{12,14},{14,12},{16,18},{18,... | collective-permute-start | bytes 497672 | tf_op jit(solution)/shard_map/ppermute | solution.py:29
  58.4 21.3 %copy-start.1 = (bf16[216,384]{1,0:T(8,128)(2,1)}, bf16[216,384]{1,0:T(8,128)(2,1)S(1)}, u32[]{:S(2)}) copy-start(bf16[216,384]{1,0:T(8,128)(2,1)S(1)} %add_convert_fusion) | copy-start | bytes 497668
  58.4 6.4 %collective-permute-start.18 = (bf16[216,384]{1,0:T(8,128)(2,1)S(1)}, bf16[216,384]{1,0:T(8,128)(2,1)S(1)}, u32[]{:S(2)}, u32[]{:S(2)}) collective-permute-start(bf16[216,384]{1,0:T(8,128)(2,1)S(1)} %add_convert_fusion), channel_id=1, source_target_pairs={{0,4},{2,6},{4,0},{6,2},{8,12},{10,14},{12,8},{14,10},{16,20},{18,... | collective-permute-start | bytes 497672 | tf_op jit(solution)/shard_map/ppermute | solution.py:29
  59.1 20.7 %collective-permute-start.19 = (bf16[216,384]{1,0:T(8,128)(2,1)S(1)}, bf16[216,384]{1,0:T(8,128)(2,1)S(1)}, u32[]{:S(2)}, u32[]{:S(2)}) collective-permute-start(bf16[216,384]{1,0:T(8,128)(2,1)S(1)} %add_convert_fusion), channel_id=1, source_target_pairs={{0,2},{2,0},{4,6},{6,4},{8,10},{10,8},{12,14},{14,12},{16,18},{18,... | collective-permute-start | bytes 497672 | tf_op jit(solution)/shard_map/ppermute | solution.py:29
  64.8 15.0 %copy-start.22 = (bf16[216,384]{1,0:T(8,128)(2,1)}, bf16[216,384]{1,0:T(8,128)(2,1)S(1)}, u32[]{:S(2)}) copy-start(bf16[216,384]{1,0:T(8,128)(2,1)S(1)} %collective-permute-done.18) | copy-start | bytes 497668
  64.8 14.9 %collective-permute-start.20 = (bf16[216,384]{1,0:T(8,128)(2,1)S(1)}, bf16[216,384]{1,0:T(8,128)(2,1)S(1)}, u32[]{:S(2)}, u32[]{:S(2)}) collective-permute-start(bf16[216,384]{1,0:T(8,128)(2,1)S(1)} %collective-permute-done.18), channel_id=1, source_target_pairs={{0,2},{2,0},{4,6},{6,4},{8,10},{10,8},{12,14},{14,12},{16,18},{18,... | collective-permute-start | bytes 497672 | tf_op jit(solution)/shard_map/ppermute | solution.py:29
  64.8 18.9 %collective-permute-start.23 = (bf16[216,384]{1,0:T(8,128)(2,1)S(1)}, bf16[216,384]{1,0:T(8,128)(2,1)S(1)}, u32[]{:S(2)}, u32[]{:S(2)}) collective-permute-start(bf16[216,384]{1,0:T(8,128)(2,1)S(1)} %add_convert_fusion), channel_id=1, source_target_pairs={{0,24},{2,26},{4,28},{6,30},{8,16},{10,18},{12,20},{14,22},{16,8},... | collective-permute-start | bytes 497672 | tf_op jit(solution)/shard_map/ppermute | solution.py:29
  68.4 15.3 %collective-permute-start.22 = (bf16[216,384]{1,0:T(8,128)(2,1)S(1)}, bf16[216,384]{1,0:T(8,128)(2,1)S(1)}, u32[]{:S(2)}, u32[]{:S(2)}) collective-permute-start(bf16[216,384]{1,0:T(8,128)(2,1)S(1)} %add_convert_fusion), channel_id=1, source_target_pairs={{0,16},{2,18},{4,20},{6,22},{8,24},{10,26},{12,28},{14,30},{16,0},... | collective-permute-start | bytes 497672 | tf_op jit(solution)/shard_map/ppermute | solution.py:29
  68.4 15.4 %collective-permute-start.21 = (bf16[216,384]{1,0:T(8,128)(2,1)S(1)}, bf16[216,384]{1,0:T(8,128)(2,1)S(1)}, u32[]{:S(2)}, u32[]{:S(2)}) collective-permute-start(bf16[216,384]{1,0:T(8,128)(2,1)S(1)} %add_convert_fusion), channel_id=1, source_target_pairs={{0,8},{2,10},{4,12},{6,14},{8,0},{10,2},{12,4},{14,6},{16,24},{18,... | collective-permute-start | bytes 497672 | tf_op jit(solution)/shard_map/ppermute | solution.py:29
  83.7 15.3 %copy-start.13 = (bf16[216,384]{1,0:T(8,128)(2,1)}, bf16[216,384]{1,0:T(8,128)(2,1)S(1)}, u32[]{:S(2)}) copy-start(bf16[216,384]{1,0:T(8,128)(2,1)S(1)} %collective-permute-done.23) | copy-start | bytes 497668
  83.7 15.3 %copy-start.14 = (bf16[216,384]{1,0:T(8,128)(2,1)}, bf16[216,384]{1,0:T(8,128)(2,1)S(1)}, u32[]{:S(2)}) copy-start(bf16[216,384]{1,0:T(8,128)(2,1)S(1)} %collective-permute-done.22) | copy-start | bytes 497668
  83.8 15.3 %copy-start.15 = (bf16[216,384]{1,0:T(8,128)(2,1)}, bf16[216,384]{1,0:T(8,128)(2,1)S(1)}, u32[]{:S(2)}) copy-start(bf16[216,384]{1,0:T(8,128)(2,1)S(1)} %collective-permute-done.21) | copy-start | bytes 497668
  83.8 2.7 %collective-permute-start.27 = (bf16[216,384]{1,0:T(8,128)(2,1)S(1)}, bf16[216,384]{1,0:T(8,128)(2,1)S(1)}, u32[]{:S(2)}, u32[]{:S(2)}) collective-permute-start(bf16[216,384]{1,0:T(8,128)(2,1)S(1)} %collective-permute-done.21), channel_id=1, source_target_pairs={{0,2},{2,0},{4,6},{6,4},{8,10},{10,8},{12,14},{14,12},{16,18},{18,... | collective-permute-start | bytes 497672 | tf_op jit(solution)/shard_map/ppermute | solution.py:29
  83.9 7.1 %collective-permute-start.24 = (bf16[216,384]{1,0:T(8,128)(2,1)S(1)}, bf16[216,384]{1,0:T(8,128)(2,1)S(1)}, u32[]{:S(2)}, u32[]{:S(2)}) collective-permute-start(bf16[216,384]{1,0:T(8,128)(2,1)S(1)} %collective-permute-done.21), channel_id=1, source_target_pairs={{0,4},{2,6},{4,0},{6,2},{8,12},{10,14},{12,8},{14,10},{16,20},{18,... | collective-permute-start | bytes 497672 | tf_op jit(solution)/shard_map/ppermute | solution.py:29
  84.5 10.1 %collective-permute-start.25 = (bf16[216,384]{1,0:T(8,128)(2,1)S(1)}, bf16[216,384]{1,0:T(8,128)(2,1)S(1)}, u32[]{:S(2)}, u32[]{:S(2)}) collective-permute-start(bf16[216,384]{1,0:T(8,128)(2,1)S(1)} %collective-permute-done.22), channel_id=1, source_target_pairs={{0,4},{2,6},{4,0},{6,2},{8,12},{10,14},{12,8},{14,10},{16,20},{18,... | collective-permute-start | bytes 497672 | tf_op jit(solution)/shard_map/ppermute | solution.py:29
  86.0 11.7 %collective-permute-start.26 = (bf16[216,384]{1,0:T(8,128)(2,1)S(1)}, bf16[216,384]{1,0:T(8,128)(2,1)S(1)}, u32[]{:S(2)}, u32[]{:S(2)}) collective-permute-start(bf16[216,384]{1,0:T(8,128)(2,1)S(1)} %collective-permute-done.23), channel_id=1, source_target_pairs={{0,4},{2,6},{4,0},{6,2},{8,12},{10,14},{12,8},{14,10},{16,20},{18,... | collective-permute-start | bytes 497672 | tf_op jit(solution)/shard_map/ppermute | solution.py:29
  86.5 11.1 %collective-permute-start.28 = (bf16[216,384]{1,0:T(8,128)(2,1)S(1)}, bf16[216,384]{1,0:T(8,128)(2,1)S(1)}, u32[]{:S(2)}, u32[]{:S(2)}) collective-permute-start(bf16[216,384]{1,0:T(8,128)(2,1)S(1)} %collective-permute-done.22), channel_id=1, source_target_pairs={{0,2},{2,0},{4,6},{6,4},{8,10},{10,8},{12,14},{14,12},{16,18},{18,... | collective-permute-start | bytes 497672 | tf_op jit(solution)/shard_map/ppermute | solution.py:29
  86.5 12.5 %copy-start.16 = (bf16[216,384]{1,0:T(8,128)(2,1)}, bf16[216,384]{1,0:T(8,128)(2,1)S(1)}, u32[]{:S(2)}) copy-start(bf16[216,384]{1,0:T(8,128)(2,1)S(1)} %collective-permute-done.27) | copy-start | bytes 497668
  86.5 11.1 %collective-permute-start.29 = (bf16[216,384]{1,0:T(8,128)(2,1)S(1)}, bf16[216,384]{1,0:T(8,128)(2,1)S(1)}, u32[]{:S(2)}, u32[]{:S(2)}) collective-permute-start(bf16[216,384]{1,0:T(8,128)(2,1)S(1)} %collective-permute-done.23), channel_id=1, source_target_pairs={{0,2},{2,0},{4,6},{6,4},{8,10},{10,8},{12,14},{14,12},{16,18},{18,... | collective-permute-start | bytes 497672 | tf_op jit(solution)/shard_map/ppermute | solution.py:29
  91.0 6.7 %collective-permute-start.30 = (bf16[216,384]{1,0:T(8,128)(2,1)S(1)}, bf16[216,384]{1,0:T(8,128)(2,1)S(1)}, u32[]{:S(2)}, u32[]{:S(2)}) collective-permute-start(bf16[216,384]{1,0:T(8,128)(2,1)S(1)} %collective-permute-done.24), channel_id=1, source_target_pairs={{0,2},{2,0},{4,6},{6,4},{8,10},{10,8},{12,14},{14,12},{16,18},{18,... | collective-permute-start | bytes 497672 | tf_op jit(solution)/shard_map/ppermute | solution.py:29
  94.5 3.2 %collective-permute-start.31 = (bf16[216,384]{1,0:T(8,128)(2,1)S(1)}, bf16[216,384]{1,0:T(8,128)(2,1)S(1)}, u32[]{:S(2)}, u32[]{:S(2)}) collective-permute-start(bf16[216,384]{1,0:T(8,128)(2,1)S(1)} %collective-permute-done.25), channel_id=1, source_target_pairs={{0,2},{2,0},{4,6},{6,4},{8,10},{10,8},{12,14},{14,12},{16,18},{18,... | collective-permute-start | bytes 497672 | tf_op jit(solution)/shard_map/ppermute | solution.py:29
  97.6 1.4 %collective-permute-start.32 = (bf16[216,384]{1,0:T(8,128)(2,1)S(1)}, bf16[216,384]{1,0:T(8,128)(2,1)S(1)}, u32[]{:S(2)}, u32[]{:S(2)}) collective-permute-start(bf16[216,384]{1,0:T(8,128)(2,1)S(1)} %collective-permute-done.26), channel_id=1, source_target_pairs={{0,2},{2,0},{4,6},{6,4},{8,10},{10,8},{12,14},{14,12},{16,18},{18,... | collective-permute-start | bytes 497672 | tf_op jit(solution)/shard_map/ppermute | solution.py:29
  (22 other events, 51.0 us)

commit v3 on v2

--- a/solution.py
+++ b/solution.py
@@ -73,27 +73,42 @@
     return jnp.where(lane == LANES - 1, 0.0, pltpu.roll(tile, LANES - 1, 1))
 
 
-def place_latent(lat_refs, mask_lists, stack_ref, me, frames, rows):
-    latent_width = lat_refs[0].shape[1]
-    total = stack_ref.shape[2]
-    zeros = jnp.zeros((stack_ref.shape[1], 2 * LANES), BF16)
-    for frame in range(frames):
-        stack_ref[frame, :, 0 : 2 * LANES] = zeros
-        stack_ref[frame, :, total - 2 * LANES : total] = zeros
-    for lat_ref, masks in zip(lat_refs, mask_lists):
-        for index, mask in enumerate(masks):
-            slab = me ^ mask
-            for frame in range(frames):
-                for row in range(rows):
-                    at = (frame * rows + row) * LANES
-                    tile = lat_ref[index, :, at : at + LANES].astype(F32)
-                    to = pl.multiple_of((slab * rows + row + 2) * LANES, LANES)
-                    for shift in range(3):
-                        stack_ref[
-                            frame,
-                            shift * latent_width : (shift + 1) * latent_width,
-                            pl.ds(to, LANES),
-                        ] = shifted(tile, shift).astype(BF16)
+def fetch(piece_refs, mask_lists, slot_ref, sems):
+    copies = []
+    for index, (piece_ref, masks) in enumerate(zip(piece_refs, mask_lists)):
+        for position, mask in enumerate(masks):
+            copies.append(
+                pltpu.make_async_copy(
+                    piece_ref.at[position], slot_ref.at[mask], sems.at[index * len(masks) + position]
+                )
+            )
+    for copy in copies:
+        copy.start()
+    return copies
+
+
+def place_latent(slot_ref, stack_ref, me, first_slab, slab_count, frames, rows, slabs):
+    latent_width = slot_ref.shape[1]
+    for offset in range(-1, slab_count + 1):
+        slab = first_slab + offset
+        inside = ((slab >= 0) & (slab < slabs)).astype(F32)
+        source = jnp.clip(slab, 0, slabs - 1) ^ me
+        needed = range(rows)
+        if offset == -1:
+            needed = range(rows - 2, rows)
+        if offset == slab_count:
+            needed = range(2)
+        for frame in range(frames):
+            for row in needed:
+                at = (frame * rows + row) * LANES
+                tile = slot_ref[source, :, at : at + LANES].astype(F32)
+                if offset in (-1, slab_count):
+                    tile = tile * inside
+                to = (offset * rows + row + 2) * LANES
+                for shift in range(3):
+                    stack_ref[
+                        frame, shift * latent_width : (shift + 1) * latent_width, to : to + LANES
+                    ] = shifted(tile, shift).astype(BF16)
 
 
 def hidden_rows(stack_ref, weight_ref, frame, first, count):
@@ -121,40 +136,29 @@
             act_ref[chunk, pl.ds(at, LANES)] = (half + half * jnp.tanh(half)).astype(BF16)
 
 
-def cotangent_kernel(
-    frames, rows, half_rows, pad_channels, mask_lists, me_ref, *refs
-):
-    block_refs = refs[:-2]
-    out_ref, flat_ref = refs[-2:]
-    me = me_ref[0]
-    slabs_half = half_rows // rows
-    first_slab = (me & 1) * slabs_half
-    channels = block_refs[0].shape[1]
+def place_cotangent(slot_ref, flat_ref, out_ref, me, first_slab, slab_count, frames, rows, pad_channels):
+    channels = slot_ref.shape[1]
+    half_rows = slab_count * rows
     group = 3 * pad_channels
     padded = out_ref.shape[0] // frames
     for frame in range(frames):
         for edge in (0, half_rows + 2):
             flat_ref[frame, :, edge * LANES : (edge + 2) * LANES] = jnp.zeros((group, 2 * LANES), F32)
-    for block_ref, masks in zip(block_refs, mask_lists):
-        for position, mask in enumerate(masks):
-            index = (me ^ mask) - first_slab
-
-            @pl.when((index >= 0) & (index < slabs_half))
-            def _(block_ref=block_ref, position=position, index=index):
-                for frame in range(frames):
-                    for row in range(rows):
-                        at = (frame * rows + row) * LANES
-                        tile = block_ref[position, :, at : at + LANES].astype(F32)
-                        if pad_channels != channels:
-                            tile = jnp.concatenate(
-                                [tile, jnp.zeros((pad_channels - channels, LANES), F32)], axis=0
-                            )
-                        to = pl.multiple_of((index * rows + row + 2) * LANES, LANES)
-                        for tap in range(3):
-                            flat_ref[
-                                frame, tap * pad_channels : (tap + 1) * pad_channels, pl.ds(to, LANES)
-                            ] = shifted(tile, 2 - tap)
-
+    for offset in range(slab_count):
+        source = (first_slab + offset) ^ me
+        for frame in range(frames):
+            for row in range(rows):
+                at = (frame * rows + row) * LANES
+                tile = slot_ref[source, :, at : at + LANES].astype(F32)
+                if pad_channels != channels:
+                    tile = jnp.concatenate(
+                        [tile, jnp.zeros((pad_channels - channels, LANES), F32)], axis=0
+                    )
+                to = (offset * rows + row + 2) * LANES
+                for tap in range(3):
+                    flat_ref[frame, tap * pad_channels : (tap + 1) * pad_channels, to : to + LANES] = (
+                        shifted(tile, 2 - tap)
+                    )
     filler = [jnp.zeros((padded - 3 * group, LANES), F32)] if padded != 3 * group else []
     for frame in range(frames):
         for row in range(half_rows + 2):
@@ -164,38 +168,47 @@
             )
 
 
-def gradient_kernel(frames, rows, half_rows, height, mask_lists, real_rows, *refs):
-    lat_count = len(mask_lists)
-    me_ref, cot_hbm, gain_ref = refs[:3]
-    weight_refs = refs[3 : 3 + frames]
-    lat_refs = refs[3 + frames : 3 + frames + lat_count]
-    keep_ref, send_ref = refs[3 + frames + lat_count : 5 + frames + lat_count]
-    stack_ref, hid_a, hid_b, act_a, act_b, sum_ref, wide_gain, cot_ref, sem = refs[5 + frames + lat_count :]
-    load = pltpu.make_async_copy(cot_hbm, cot_ref, sem)
-    load.start()
+def gradient_kernel(frames, rows, slabs, lat_masks, cot_masks, real_rows, pad_channels, *refs):
+    me_ref, gain_ref = refs[:2]
+    refs = refs[2:]
+    weight_refs, refs = refs[:frames], refs[frames:]
+    lat_refs, refs = refs[: len(lat_masks)], refs[len(lat_masks) :]
+    cot_refs, refs = refs[: len(cot_masks)], refs[len(cot_masks) :]
+    keep_ref, send_ref, lat_slots, cot_slots, stack_ref, flat_ref, cot_ref = refs[:7]
+    hid_a, hid_b, act_a, act_b, sum_ref, wide_gain, lat_sems, cot_sems = refs[7:]
+    lat_copies = fetch(lat_refs, lat_masks, lat_slots, lat_sems)
+    cot_copies = fetch(cot_refs, cot_masks, cot_slots, cot_sems)
     me = me_ref[0]
     core = me & 1
-    place_latent(lat_refs, mask_lists, stack_ref, me, frames, rows)
-    channels = sum_ref.shape[1]
-    wide_gain[...] = jnp.broadcast_to(0.5 * gain_ref[...], wide_gain.shape)
+    slab_count = slabs // 2
+    half_rows = slab_count * rows
+    height = slabs * rows
+    first_slab = core * slab_count
     padded = cot_ref.shape[0] // frames
-    start = core * half_rows
+    top_row = core * half_rows - 1
     ext = half_rows + 2
     count = max(d for d in range(1, 18) if ext % d == 0)
     width = count * LANES
     hidden = (hid_a, hid_b)
     acts = (act_a, act_b)
-    hid_a[...] = hidden_rows(stack_ref, weight_refs[0], 0, start, ext)
+    wide_gain[...] = jnp.broadcast_to(0.5 * gain_ref[...], wide_gain.shape)
     sum_ref[...] = jnp.zeros_like(sum_ref)
-    for frame in range(frames):
-        if frame == 1:
-            load.wait()
+    for copy in lat_copies:
+        copy.wait()
+    place_latent(lat_slots, stack_ref, me, first_slab, slab_count, frames, rows, slabs)
+    for copy in cot_copies:
+        copy.wait()
+    hid_a[...] = hidden_rows(stack_ref, weight_refs[0], 0, 0, ext)
+    place_cotangent(
+        cot_slots, flat_ref, cot_ref, me, first_slab, slab_count, frames, rows, pad_channels
+    )
+    for frame in range(frames):
 
         def chunk(step, carry):
             at = pl.multiple_of(step * width, LANES)
             if frame + 1 < frames:
                 hidden[(frame + 1) % 2][:, pl.ds(at, width)] = hidden_rows(
-                    stack_ref, weight_refs[frame + 1], frame + 1, start + step * count, count
+                    stack_ref, weight_refs[frame + 1], frame + 1, step * count, count
                 )
             if frame > 0:
                 last = min(frames, frame + 2)
@@ -204,13 +217,11 @@
                     acts[(frame - 1) % 2][:, pl.ds(at, width)],
                 )
             activate_rows(
-                hidden[frame % 2], wide_gain, acts[frame % 2], step * count, start - 1, count, height
+                hidden[frame % 2], wide_gain, acts[frame % 2], step * count, top_row, count, height
             )
             return carry
 
         lax.fori_loop(0, ext // count, chunk, 0)
-    if frames == 1:
-        load.wait()
     final = frames - 1
     sum_ref[0:padded, :] += dot_t(cot_ref[final * padded : frames * padded, :], acts[final % 2][...])
     keep_at = pl.multiple_of(core * padded, 16)
@@ -219,21 +230,25 @@
     send_ref[...] = sum_ref[pl.ds(send_at, padded), :][:real_rows].astype(BF16)
 
 
-def decode_kernel(frames, rows, height, mask_lists, *refs):
-    lat_count = len(mask_lists)
+def decode_kernel(frames, rows, slabs, lat_masks, *refs):
     me_ref, gain_ref, conv_hbm = refs[:3]
-    weight_refs = refs[3 : 3 + frames]
-    lat_refs = refs[3 + frames : 3 + frames + lat_count]
-    out_ref, stack_ref, hid_ref, flat_ref, act_ref, wide_gain, conv_ref, sem = refs[3 + frames + lat_count :]
+    refs = refs[3:]
+    weight_refs, refs = refs[:frames], refs[frames:]
+    lat_refs, refs = refs[: len(lat_masks)], refs[len(lat_masks) :]
+    out_ref, lat_slots, stack_ref, hid_ref, flat_ref, act_ref, wide_gain, conv_ref, lat_sems, sem = refs
     live = conv_ref.shape[0] // 9
     load = pltpu.make_async_copy(conv_hbm.at[pl.ds((3 - live) * 9, live * 9)], conv_ref, sem)
     load.start()
+    lat_copies = fetch(lat_refs, lat_masks, lat_slots, lat_sems)
     me = me_ref[0]
-    place_latent(lat_refs, mask_lists, stack_ref, me, frames, rows)
+    height = slabs * rows
     wide_gain[...] = jnp.broadcast_to(0.5 * gain_ref[...], wide_gain.shape)
+    for copy in lat_copies:
+        copy.wait()
+    place_latent(lat_slots, stack_ref, me, me, 1, frames, rows, slabs)
     ext = rows + 2
     for frame in range(frames):
-        hid_ref[...] = hidden_rows(stack_ref, weight_refs[frame], frame, me * rows, ext)
+        hid_ref[...] = hidden_rows(stack_ref, weight_refs[frame], frame, 0, ext)
         activate_rows(hid_ref, wide_gain, flat_ref, 0, me * rows - 1, ext, height)
         for row in range(ext):
             tile = flat_ref[:, row * LANES : (row + 1) * LANES].astype(F32)
@@ -241,16 +256,16 @@
                 act_ref[frame, tap, :, row * LANES : (row + 1) * LANES] = shifted(tile, tap).astype(BF16)
     load.wait()
     for frame in range(frames):
-        total = None
+        kernels = []
+        inputs = []
         for depth in range(max(0, 2 - frame), 3):
-            source = frame + depth - 2
             for row_tap in range(3):
                 for col_tap in range(3):
-                    term = dot(
-                        conv_ref[(depth - (3 - live)) * 9 + row_tap * 3 + col_tap],
-                        act_ref[source, col_tap, :, row_tap * LANES : (row_tap + rows) * LANES],
+                    kernels.append(conv_ref[(depth - (3 - live)) * 9 + row_tap * 3 + col_tap])
+                    inputs.append(
+                        act_ref[frame + depth - 2, col_tap, :, row_tap * LANES : (row_tap + rows) * LANES]
                     )
-                    total = term if total is None else total + term
+        total = dot(jnp.concatenate(kernels, axis=1), jnp.concatenate(inputs, axis=0))
         out_ref[:, frame * rows * LANES : (frame + 1) * rows * LANES] = total.astype(BF16)
 
 
@@ -326,16 +341,7 @@
         cot_masks.append([mask, mask ^ top])
     cot_blocks = cot_blocks + [xor_permute(b, "seq", 1) for b in cot_blocks]
     cot_masks = cot_masks + [[m ^ 1 for m in masks] for masks in cot_masks]
-    cot = pl.pallas_call(
-        functools.partial(cotangent_kernel, frames, rows, half_rows, pad_channels, cot_masks),
-        out_shape=jax.ShapeDtypeStruct((frames * padded, lanes), BF16),
-        in_specs=[smem()] + [vmem()] * len(cot_blocks),
-        out_specs=vmem(),
-        scratch_shapes=[pltpu.VMEM((frames, 3 * pad_channels, (half_rows + 4) * width), F32)],
-        compiler_params=params(),
-        name="cotangent",
-    )(me, *cot_blocks)
-
+    attn_out = lax.optimization_barrier((attn_out, far))[0]
     flattened = attn_out.reshape(frames * tok_rows * tok_cols, model_width)
     partial_sum = lax.dot_general(
         w_proj, flattened, (((0,), (1,)), ((), ())), preferred_element_type=F32
@@ -365,29 +371,35 @@
     entry = entry_weight.reshape(channels, 3, 9 * latent_width)
     entries = [entry[:, max(0, 2 - f) :].reshape(channels, -1) for f in range(frames)]
     gain = norm_gain.reshape(channels, 1)
+    hbm = pl.BlockSpec(memory_space=pl.ANY)
     keep, send = pl.pallas_call(
-        functools.partial(gradient_kernel, frames, rows, half_rows, height, lat_masks, real_rows),
+        functools.partial(
+            gradient_kernel, frames, rows, slabs, lat_masks, cot_masks, real_rows, pad_channels
+        ),
         out_shape=(
             jax.ShapeDtypeStruct((real_rows, channels), F32),
             jax.ShapeDtypeStruct((real_rows, channels), BF16),
         ),
-        in_specs=[smem(), pl.BlockSpec(memory_space=pl.ANY), vmem()]
-        + [vmem()] * (frames + len(lats)),
+        in_specs=[smem(), vmem()] + [vmem()] * frames + [hbm] * (len(lats) + len(cot_blocks)),
         out_specs=(vmem(), vmem()),
         scratch_shapes=[
-            pltpu.VMEM((frames, 3 * latent_width, (height + 4) * width), BF16),
+            pltpu.VMEM((slabs, latent_width, frames * rows * width), BF16),
+            pltpu.VMEM((slabs, chip_channels, frames * rows * width), BF16),
+            pltpu.VMEM((frames, 3 * latent_width, (half_rows + 4) * width), BF16),
+            pltpu.VMEM((frames, 3 * pad_channels, (half_rows + 4) * width), F32),
+            pltpu.VMEM((frames * padded, lanes), BF16),
             pltpu.VMEM((channels, lanes), F32),
             pltpu.VMEM((channels, lanes), F32),
             pltpu.VMEM((channels, lanes), BF16),
             pltpu.VMEM((channels, lanes), BF16),
             pltpu.VMEM((live * padded, channels), F32),
             pltpu.VMEM((channels, LANES), F32),
-            pltpu.VMEM((frames * padded, lanes), BF16),
-            pltpu.SemaphoreType.DMA(()),
+            pltpu.SemaphoreType.DMA((slabs,)),
+            pltpu.SemaphoreType.DMA((slabs,)),
         ],
         compiler_params=params(),
         name="gradient",
-    )(me, cot, gain, *entries, *lats)
+    )(me, gain, *entries, *lats, *cot_blocks)
     block = (keep + xor_permute(send, "seq", 1).astype(F32)).astype(BF16)
 
     columns = [m for m in range(0, slabs, 4)]
@@ -396,18 +408,19 @@
     held = lax.optimization_barrier((block, *lats))[1:]
     conv = conv_weight.transpose(1, 2, 3, 0, 4).reshape(27, out_channels, channels)
     decoded = pl.pallas_call(
-        functools.partial(decode_kernel, frames, rows, height, lat_masks),
+        functools.partial(decode_kernel, frames, rows, slabs, lat_masks),
         out_shape=jax.ShapeDtypeStruct((out_channels, frames * rows * width), BF16),
-        in_specs=[smem(), vmem(), pl.BlockSpec(memory_space=pl.ANY)]
-        + [vmem()] * (frames + len(lats)),
+        in_specs=[smem(), vmem(), hbm] + [vmem()] * frames + [hbm] * len(lats),
         out_specs=vmem(),
         scratch_shapes=[
-            pltpu.VMEM((frames, 3 * latent_width, (height + 4) * width), BF16),
+            pltpu.VMEM((slabs, latent_width, frames * rows * width), BF16),
+            pltpu.VMEM((frames, 3 * latent_width, (rows + 4) * width), BF16),
             pltpu.VMEM((channels, (rows + 2) * width), F32),
             pltpu.VMEM((channels, (rows + 2) * width), BF16),
             pltpu.VMEM((frames, 3, channels, (rows + 2) * width), BF16),
             pltpu.VMEM((channels, LANES), F32),
             pltpu.VMEM((live * 9, out_channels, channels), BF16),
+            pltpu.SemaphoreType.DMA((slabs,)),
             pltpu.SemaphoreType.DMA(()),
         ],
         compiler_params=params(),
@@ -444,14 +457,18 @@
     early = early + [xor_permute(p, "seq", 1) for p in early]
     early_masks = early_masks + [m ^ 1 for m in early_masks]
     grad = finish(early, early_masks)
-    after = lax.optimization_barrier((decoded, grad, *direct[1:]))
-    decoded, grad, late = after[0], after[1], list(after[2:])
-    late_masks = columns[1:]
-    late = late + [xor_permute(p, "seq", 2) for p in late]
-    late_masks = late_masks + [m ^ 2 for m in late_masks]
-    late = late + [xor_permute(p, "seq", 1) for p in late]
-    late_masks = late_masks + [m ^ 1 for m in late_masks]
-    grad = finish(late, late_masks, grad)
+    after = lax.optimization_barrier((decoded, *direct[1:]))
+    decoded = after[0]
+    groups = [([], []), ([], [])]
+    for mask, piece in zip(columns[1:], after[1:]):
+        across = xor_permute(piece, "seq", 2)
+        parts, masks = groups[0 if mask == 4 else 1]
+        for part, m in ((piece, mask), (across, mask ^ 2)):
+            parts += [part, xor_permute(part, "seq", 1)]
+            masks += [m, m ^ 1]
+    for parts, masks in groups:
+        if parts:
+            grad = finish(parts, masks, grad)
     if pad_channels != chip_channels:
         grad = grad.reshape(27, chips, pad_channels, channels)[:, :, :chip_channels]
     grad = grad.reshape(3, 3, 3, out_channels, channels).transpose(3, 0, 1, 2, 4)

time: 104 us -> 95.2 us (0.915)
  waiting for transfers between devices: 32.3 us -> 24.9 us
  Pallas kernels: 32.4 us -> 30.7 us
  local copies, waits for them, and re-layouts: 10.4 us -> 8.8 us
  starting transfers between devices: 23.8 us -> 25.4 us
    ppermute x33, waiting for transfers between devices: 32.3 us -> 24.9 us  [xor_permute(): lax.ppermute(x, axis, [(i, i ^ mask) for i in range(lax.axis_size(axis))])]
    pallas_call x3 -> x2, Pallas kernels: 23.8 us -> 20.4 us  [the longest x1 12.4 us: per_device(): pl.pallas_call(functools.partial(gradient_kernel, frames, rows, slabs, la...]
    unnamed x75, local copies, waits for them, and re-layouts: 5.34 us -> 3.63 us
    pallas_call x2 -> x3, Pallas kernels: 6.94 us -> 8.65 us  [finish(): pl.pallas_call(functools.partial(finish_kernel, first, masks, blank), out...]
    ppermute x33, starting transfers between devices: 23.8 us -> 25.4 us  [xor_permute(): lax.ppermute(x, axis, [(i, i ^ mask) for i in range(lax.axis_size(axis))])]
  transfers between devices with their start and end apart: 33 -> 33, of which waited for: 11 -> 11; matrix products, arithmetic and copies ran while one was open for 6% -> 6% of each run, Pallas kernels for 17% -> 14%
where the time goes in v3:
time: 95.2 us; the launch traced here: 94.6 us
  Pallas kernels  30.7 us (32%)
  starting transfers between devices  25.4 us (27%)
  waiting for transfers between devices  24.9 us (26%)
  local copies, waits for them, and re-layouts  8.8 us (9%)
  other arithmetic  1.85 us (2%)
  matrix products  1.48 us (2%)
  between operations  1.46 us (2%)
    ppermute x33, starting transfers between devices, xor_permute(): lax.ppermute(x, axis, [(i, i ^ mask) for i in range(lax.axis_size(axis))])  25.4 us
    ppermute x33, waiting for transfers between devices, xor_permute(): lax.ppermute(x, axis, [(i, i ^ mask) for i in range(lax.axis_size(axis))])  24.9 us
    pallas_call x1, Pallas kernels, per_device(): pl.pallas_call(functools.partial(gradient_kernel, frames, rows, slabs, la...  12.4 us
    pallas_call x3, Pallas kernels, finish(): pl.pallas_call(functools.partial(finish_kernel, first, masks, blank), out...  8.65 us
    pallas_call x1, Pallas kernels, per_device(): pl.pallas_call(functools.partial(decode_kernel, frames, rows, slabs, lat_...  7.98 us
    unnamed x75, local copies, waits for them, and re-layouts  3.63 us
    reshape x1, local copies, waits for them, and re-layouts, per_device(): decoded = decoded.reshape(out_channels, frames, rows, width)  2.01 us
  transfers between devices with their start and end apart: 33, of which 11 were waited for; matrix products, arithmetic and copies ran while one was open for 6% of the time, Pallas kernels for 14%

profile of v3, /device:TPU:0, one launch (start us, length us, event | category | flops | bytes accessed | tf_op | source)
XLA Modules:
  0.0 94.6 jit_solution(9144373507129635768)
XLA Ops:
  0.7 1.4 %reshape.88 = bf16[8,24,1024]{2,1,0:T(8,128)(2,1)S(1)} reshape(bf16[192,2,4,128]{3,2,1,0:T(4,128)(2,1)} %param.11) | data formatting | bytes 786432 | tf_op jit(solution)/shard_map/reshape | solution.py:323
  2.2 1.5 %convolution_bitcast_fusion.own_ref = f32[64,256]{1,0:T(8,128)S(1)} fusion(bf16[256,2560]{1,0:T(8,128)(2,1)S(1)} %bitcast.33, bf16[2560,64]{0,1:T(8,128)(2,1)} %param.7), kind=kOutput, calls=%fused_computation | convolution fusion | flops 83886080 | bytes 1703936 | tf_op jit(solution)/shard_map/dot_general | solution.py:346
  3.7 3.0 %collective-permute-start = (f32[64,256]{1,0:T(8,128)S(1)}, f32[64,256]{1,0:T(8,128)S(1)}, u32[]{:S(2)}, u32[]{:S(2)}) collective-permute-start(f32[64,256]{1,0:T(8,128)S(1)} %convolution_bitcast_fusion.own_ref), channel_id=1, source_target_pairs={{0,1},{1,0},{2,3},{3,2},{4,5},{5,4},{6,7},{7,6},{8,9},{9,8},{10,11... | collective-permute-start | bytes 196616 | tf_op jit(solution)/shard_map/ppermute | solution.py:29
  6.7 2.2 %collective-permute-done.other_ref = f32[64,256]{1,0:T(8,128)S(1)} collective-permute-done((f32[64,256]{1,0:T(8,128)S(1)}, f32[64,256]{1,0:T(8,128)S(1)}, u32[]{:S(2)}, u32[]{:S(2)}) %collective-permute-start) | collective-permute-done | bytes 65568 | tf_op jit(solution)/shard_map/ppermute | solution.py:29
  9.0 0.6 copy-done.35
  9.6 1.7 %unpatchify.1 = bf16[16,1024]{1,0:T(8,128)(2,1)} custom-call(f32[64,256]{1,0:T(8,128)} %copy-done.12, f32[64,256]{1,0:T(8,128)} %copy-done.35), custom_call_target="tpu_custom_call" | custom-call | tf_op jit(solution)/shard_map/unpatchify/pallas_call | solution.py:356
  11.3 3.1 %collective-permute-start.1 = (bf16[16,1024]{1,0:T(8,128)(2,1)}, bf16[16,1024]{1,0:T(8,128)(2,1)S(1)}, u32[]{:S(2)}, u32[]{:S(2)}) collective-permute-start(bf16[16,1024]{1,0:T(8,128)(2,1)} %unpatchify.1), channel_id=1, source_target_pairs={{0,16},{2,18},{4,20},{6,22},{8,24},{10,26},{12,28},{14,30},{16,0},... | collective-permute-start | bytes 98312 | tf_op jit(solution)/shard_map/ppermute | solution.py:29
  14.4 2.3 %collective-permute-done.1 = bf16[16,1024]{1,0:T(8,128)(2,1)S(1)} collective-permute-done((bf16[16,1024]{1,0:T(8,128)(2,1)}, bf16[16,1024]{1,0:T(8,128)(2,1)S(1)}, u32[]{:S(2)}, u32[]{:S(2)}) %collective-permute-start.1) | collective-permute-done | bytes 32800 | tf_op jit(solution)/shard_map/ppermute | solution.py:29
  16.7 0.8 pad_maximum_fusion.5.refs_4_.refs_5_
  17.5 2.1 %collective-permute-start.2 = (bf16[2,16,1024]{2,1,0:T(8,128)(2,1)S(1)}, bf16[2,16,1024]{2,1,0:T(8,128)(2,1)S(1)}, u32[]{:S(2)}, u32[]{:S(2)}) collective-permute-start(bf16[2,16,1024]{2,1,0:T(8,128)(2,1)S(1)} %pad_maximum_fusion.5.refs_4_.refs_5_), channel_id=1, source_target_pairs={{0,4},{2,6},{4,0},{6,2},{8,12},{10,14},{12,8},{14,10},{16,20},{18,... | collective-permute-start | bytes 196616 | tf_op jit(solution)/shard_map/ppermute | solution.py:29
  19.5 3.4 %collective-permute-start.3 = (bf16[2,16,1024]{2,1,0:T(8,128)(2,1)S(1)}, bf16[2,16,1024]{2,1,0:T(8,128)(2,1)S(1)}, u32[]{:S(2)}, u32[]{:S(2)}) collective-permute-start(bf16[2,16,1024]{2,1,0:T(8,128)(2,1)S(1)} %pad_maximum_fusion.5.refs_4_.refs_5_), channel_id=1, source_target_pairs={{0,8},{2,10},{4,12},{6,14},{8,0},{10,2},{12,4},{14,6},{16,24},{18,... | collective-permute-start | bytes 196616 | tf_op jit(solution)/shard_map/ppermute | solution.py:29
  23.0 0.5 collective-permute-start.6
  23.5 3.3 %collective-permute-done.3.refs_6_.refs_7_ = bf16[2,16,1024]{2,1,0:T(8,128)(2,1)S(1)} collective-permute-done((bf16[2,16,1024]{2,1,0:T(8,128)(2,1)S(1)}, bf16[2,16,1024]{2,1,0:T(8,128)(2,1)S(1)}, u32[]{:S(2)}, u32[]{:S(2)}) %collective-permute-start.3) | collective-permute-done | bytes 65568 | tf_op jit(solution)/shard_map/ppermute | solution.py:29
  26.8 0.7 collective-permute-start.12
  27.6 1.6 %collective-permute-done.4.refs_7_.refs_8_ = bf16[2,16,1024]{2,1,0:T(8,128)(2,1)S(1)} collective-permute-done((bf16[2,16,1024]{2,1,0:T(8,128)(2,1)S(1)}, bf16[2,16,1024]{2,1,0:T(8,128)(2,1)S(1)}, u32[]{:S(2)}, u32[]{:S(2)}) %collective-permute-start.4) | collective-permute-done | bytes 65568 | tf_op jit(solution)/shard_map/ppermute | solution.py:29
  29.2 1.0 %collective-permute-start.11 = (bf16[2,24,1024]{2,1,0:T(8,128)(2,1)S(1)}, bf16[2,24,1024]{2,1,0:T(8,128)(2,1)S(1)}, u32[]{:S(2)}, u32[]{:S(2)}) collective-permute-start(bf16[2,24,1024]{2,1,0:T(8,128)(2,1)S(1)} %pad_maximum_fusion.3), channel_id=1, source_target_pairs={{0,8},{2,10},{4,12},{6,14},{8,0},{10,2},{12,4},{14,6},{16,24},{18,... | collective-permute-start | bytes 294920 | tf_op jit(solution)/shard_map/ppermute | solution.py:29
  30.1 0.4 collective-permute-start.10
  30.6 2.8 %collective-permute-done.12.refs_15_ = bf16[2,24,1024]{2,1,0:T(8,128)(2,1)S(1)} collective-permute-done((bf16[2,24,1024]{2,1,0:T(8,128)(2,1)S(1)}, bf16[2,24,1024]{2,1,0:T(8,128)(2,1)S(1)}, u32[]{:S(2)}, u32[]{:S(2)}) %collective-permute-start.12) | collective-permute-done | bytes 98336 | tf_op jit(solution)/shard_map/ppermute | solution.py:29
  33.4 1.9 %collective-permute-done.11.refs_14_ = bf16[2,24,1024]{2,1,0:T(8,128)(2,1)S(1)} collective-permute-done((bf16[2,24,1024]{2,1,0:T(8,128)(2,1)S(1)}, bf16[2,24,1024]{2,1,0:T(8,128)(2,1)S(1)}, u32[]{:S(2)}, u32[]{:S(2)}) %collective-permute-start.11) | collective-permute-done | bytes 98336 | tf_op jit(solution)/shard_map/ppermute | solution.py:29
  35.3 0.5 collective-permute-start.14
  35.8 0.1 collective-permute-start.8
  36.0 0.9 copy.16.refs_3_.refs_4_
  36.9 0.8 copy.17
  37.7 0.8 reshape.108.refs_1_
  38.7 0.4 copy-done.11
  39.3 12.4 %gradient.1 = (f32[216,384]{1,0:T(8,128)}, bf16[216,384]{1,0:T(8,128)(2,1)}) custom-call(s32[1]{0:T(128)} %bitcast.refs_0_.me_ref, f32[384,1]{1,0:T(8,128)} %reshape.108.refs_1_, bf16[384,144]{1,0:T(8,128)(2,1)} %bitcast.36, bf16[384,288]{1,0:T(8,128)(2,1)} %copy.16.refs_3_.refs_4_, bf16[2,16,1024]{2,1,0:T(8,128)(2,1)} %copy-done.2, ...), custom_call_target="tpu_custom_call" | custom-call | tf_op jit(solution)/shard_map/gradient/pallas_call | solution.py:375
  51.7 0.5 collective-permute-start.17
  52.2 1.2 %collective-permute-done.17 = bf16[216,384]{1,0:T(8,128)(2,1)S(1)} collective-permute-done((bf16[216,384]{1,0:T(8,128)(2,1)}, bf16[216,384]{1,0:T(8,128)(2,1)S(1)}, u32[]{:S(2)}, u32[]{:S(2)}) %collective-permute-start.17) | collective-permute-done | bytes 165920 | tf_op jit(solution)/shard_map/ppermute | solution.py:29
  53.5 1.0 %add_convert_fusion = bf16[216,384]{1,0:T(8,128)(2,1)S(1)} fusion(f32[216,384]{1,0:T(8,128)} %get-tuple-element.18, bf16[216,384]{1,0:T(8,128)(2,1)S(1)} %collective-permute-done.17), kind=kLoop, calls=%fused_computation.1 | loop fusion | flops 248832 | bytes 663552 | tf_op jit(solution)/shard_map/convert_element_type | solution.py:403
  54.5 0.5 collective-permute-start.18
  54.9 3.1 %collective-permute-start.19 = (bf16[216,384]{1,0:T(8,128)(2,1)S(1)}, bf16[216,384]{1,0:T(8,128)(2,1)S(1)}, u32[]{:S(2)}, u32[]{:S(2)}) collective-permute-start(bf16[216,384]{1,0:T(8,128)(2,1)S(1)} %add_convert_fusion), channel_id=1, source_target_pairs={{0,16},{2,18},{4,20},{6,22},{8,24},{10,26},{12,28},{14,30},{16,0},... | collective-permute-start | bytes 497672 | tf_op jit(solution)/shard_map/ppermute | solution.py:29
  58.1 0.9 collective-permute-start.20
  58.9 1.3 %collective-permute-start.30 = (bf16[216,384]{1,0:T(8,128)(2,1)S(1)}, bf16[216,384]{1,0:T(8,128)(2,1)S(1)}, u32[]{:S(2)}, u32[]{:S(2)}) collective-permute-start(bf16[216,384]{1,0:T(8,128)(2,1)S(1)} %add_convert_fusion), channel_id=1, source_target_pairs={{0,4},{2,6},{4,0},{6,2},{8,12},{10,14},{12,8},{14,10},{16,20},{18,... | collective-permute-start | bytes 497672 | tf_op jit(solution)/shard_map/ppermute | solution.py:29
  60.2 8.0 %decode.1 = bf16[192,1024]{1,0:T(8,128)(2,1)} custom-call(s32[1]{0:T(128)} %bitcast.refs_0_.me_ref, f32[384,1]{1,0:T(8,128)} %reshape.108.refs_1_, bf16[27,192,384]{2,1,0:T(8,128)(2,1)} %bitcast.35, bf16[384,144]{1,0:T(8,128)(2,1)} %bitcast.37, bf16[384,288]{1,0:T(8,128)(2,1)} %copy.16.refs_3_.refs_4_, bf16[2,16,1024]{2,1,0:T(8,128)(2,1)} %copy-done.2, ...), custom_call_target="tpu_custom_call" | custom-call | tf_op jit(solution)/shard_map/decode/pallas_call | solution.py:410
  68.2 2.0 %reshape.90 = bf16[192,2,4,128]{3,2,1,0:T(4,128)(2,1)} reshape(bf16[192,1024]{1,0:T(8,128)(2,1)} %decode.1) | data formatting | bytes 786432 | tf_op jit(solution)/shard_map/reshape | solution.py:429
  70.3 1.1 %collective-permute-start.28 = (bf16[216,384]{1,0:T(8,128)(2,1)S(1)}, bf16[216,384]{1,0:T(8,128)(2,1)S(1)}, u32[]{:S(2)}, u32[]{:S(2)}) collective-permute-start(bf16[216,384]{1,0:T(8,128)(2,1)S(1)} %collective-permute-done.18), channel_id=1, source_target_pairs={{0,4},{2,6},{4,0},{6,2},{8,12},{10,14},{12,8},{14,10},{16,20},{18,... | collective-permute-start | bytes 497672 | tf_op jit(solution)/shard_map/ppermute | solution.py:29
  71.4 0.5 collective-permute-start.27
  71.9 1.0 %collective-permute-start.22 = (bf16[216,384]{1,0:T(8,128)(2,1)S(1)}, bf16[216,384]{1,0:T(8,128)(2,1)S(1)}, u32[]{:S(2)}, u32[]{:S(2)}) collective-permute-start(bf16[216,384]{1,0:T(8,128)(2,1)S(1)} %collective-permute-done.19), channel_id=1, source_target_pairs={{0,4},{2,6},{4,0},{6,2},{8,12},{10,14},{12,8},{14,10},{16,20},{18,... | collective-permute-start | bytes 497672 | tf_op jit(solution)/shard_map/ppermute | solution.py:29
  72.9 1.0 %collective-permute-start.25 = (bf16[216,384]{1,0:T(8,128)(2,1)S(1)}, bf16[216,384]{1,0:T(8,128)(2,1)S(1)}, u32[]{:S(2)}, u32[]{:S(2)}) collective-permute-start(bf16[216,384]{1,0:T(8,128)(2,1)S(1)} %collective-permute-done.20), channel_id=1, source_target_pairs={{0,4},{2,6},{4,0},{6,2},{8,12},{10,14},{12,8},{14,10},{16,20},{18,... | collective-permute-start | bytes 497672 | tf_op jit(solution)/shard_map/ppermute | solution.py:29
  74.0 3.4 %collective-permute-done.28 = bf16[216,384]{1,0:T(8,128)(2,1)S(1)} collective-permute-done((bf16[216,384]{1,0:T(8,128)(2,1)S(1)}, bf16[216,384]{1,0:T(8,128)(2,1)S(1)}, u32[]{:S(2)}, u32[]{:S(2)}) %collective-permute-start.28) | collective-permute-done | bytes 165920 | tf_op jit(solution)/shard_map/ppermute | solution.py:29
  77.4 0.5 collective-permute-start.21
  78.0 2.9 %collective-permute-done.22 = bf16[216,384]{1,0:T(8,128)(2,1)S(1)} collective-permute-done((bf16[216,384]{1,0:T(8,128)(2,1)S(1)}, bf16[216,384]{1,0:T(8,128)(2,1)S(1)}, u32[]{:S(2)}, u32[]{:S(2)}) %collective-permute-start.22) | collective-permute-done | bytes 165920 | tf_op jit(solution)/shard_map/ppermute | solution.py:29
  81.0 3.1 %collective-permute-done.25 = bf16[216,384]{1,0:T(8,128)(2,1)S(1)} collective-permute-done((bf16[216,384]{1,0:T(8,128)(2,1)S(1)}, bf16[216,384]{1,0:T(8,128)(2,1)S(1)}, u32[]{:S(2)}, u32[]{:S(2)}) %collective-permute-start.25) | collective-permute-done | bytes 165920 | tf_op jit(solution)/shard_map/ppermute | solution.py:29
  84.2 3.2 %finish.3.refs_4_ = f32[3,9,192,384]{3,2,1,0:T(8,128)} custom-call(s32[1]{0:T(128)} %bitcast.refs_0_.me_ref, bf16[9,24,384]{2,1,0:T(8,128)(2,1)} %bitcast.39, bf16[9,24,384]{2,1,0:T(8,128)(2,1)} %bitcast.45, bf16[9,24,384]{2,1,0:T(8,128)(2,1)} %bitcast.46, bf16[9,24,384]{2,1,0:T(8,128)(2,1)} %bitcast.51), custom_call_target="tpu_custom_call" | custom-call | tf_op jit(solution)/shard_map/finish/pallas_call | solution.py:437
  87.5 0.6 copy-done.26
  88.1 2.3 %finish.4.refs_8_ = f32[3,9,192,384]{3,2,1,0:T(8,128)} custom-call(s32[1]{0:T(128)} %bitcast.refs_0_.me_ref, bf16[9,24,384]{2,1,0:T(8,128)(2,1)} %bitcast.44, bf16[9,24,384]{2,1,0:T(8,128)(2,1)} %bitcast.50, bf16[9,24,384]{2,1,0:T(8,128)(2,1)} %bitcast.48, bf16[9,24,384]{2,1,0:T(8,128)(2,1)} %bitcast.55, ...), custom_call_target="tpu_custom_call", output_to_operand_aliasing={{}: (5, {})} | custom-call | tf_op jit(solution)/shard_map/finish/pallas_call | solution.py:437
  90.6 0.6 copy-done.23
  91.4 3.1 %finish.5 = f32[3,9,192,384]{3,2,1,0:T(8,128)} custom-call(s32[1]{0:T(128)} %bitcast.refs_0_.me_ref, bf16[9,24,384]{2,1,0:T(8,128)(2,1)} %bitcast.42, bf16[9,24,384]{2,1,0:T(8,128)(2,1)} %bitcast.52, bf16[9,24,384]{2,1,0:T(8,128)(2,1)} %bitcast.47, bf16[9,24,384]{2,1,0:T(8,128)(2,1)} %bitcast.54, ...), custom_call_target="tpu_custom_call", output_to_operand_aliasing={{}: (9, {})} | custom-call | tf_op jit(solution)/shard_map/finish/pallas_call | solution.py:437
  (115 shorter events, 1.0 us)
Async XLA Ops:
  0.6 35.3 %copy-start.4 = (bf16[384,3,3,3,16]{0,4,3,2,1:T(8,128)(2,1)S(1)}, bf16[384,3,3,3,16]{0,4,3,2,1:T(8,128)(2,1)}, u32[]{:S(2)}) copy-start(bf16[384,3,3,3,16]{0,4,3,2,1:T(8,128)(2,1)} %param.9) | copy-start | bytes 995332
  0.7 37.0 %copy-start.36 = (f32[384]{0:T(512)S(1)}, f32[384]{0:T(512)}, u32[]{:S(2)}) copy-start(f32[384]{0:T(512)} %param.8) | copy-start | bytes 4612
  3.7 5.3 %collective-permute-start = (f32[64,256]{1,0:T(8,128)S(1)}, f32[64,256]{1,0:T(8,128)S(1)}, u32[]{:S(2)}, u32[]{:S(2)}) collective-permute-start(f32[64,256]{1,0:T(8,128)S(1)} %convolution_bitcast_fusion.own_ref), channel_id=1, source_target_pairs={{0,1},{1,0},{2,3},{3,2},{4,5},{5,4},{6,7},{7,6},{8,9},{9,8},{10,11... | collective-permute-start | bytes 196616 | tf_op jit(solution)/shard_map/ppermute | solution.py:29
  11.3 5.4 %collective-permute-start.1 = (bf16[16,1024]{1,0:T(8,128)(2,1)}, bf16[16,1024]{1,0:T(8,128)(2,1)S(1)}, u32[]{:S(2)}, u32[]{:S(2)}) collective-permute-start(bf16[16,1024]{1,0:T(8,128)(2,1)} %unpatchify.1), channel_id=1, source_target_pairs={{0,16},{2,18},{4,20},{6,22},{8,24},{10,26},{12,28},{14,30},{16,0},... | collective-permute-start | bytes 98312 | tf_op jit(solution)/shard_map/ppermute | solution.py:29
  14.4 12.4 %collective-permute-start.9 = (bf16[4,24,1024]{2,1,0:T(8,128)(2,1)S(1)}, bf16[4,24,1024]{2,1,0:T(8,128)(2,1)S(1)}, u32[]{:S(2)}, u32[]{:S(2)}) collective-permute-start(bf16[4,24,1024]{2,1,0:T(8,128)(2,1)S(1)} %pad_maximum_fusion), channel_id=1, source_target_pairs={{0,16},{2,18},{4,20},{6,22},{8,24},{10,26},{12,28},{14,30},{16,0},... | collective-permute-start | bytes 589832 | tf_op jit(solution)/shard_map/ppermute | solution.py:29
  17.5 21.1 %copy-start.2 = (bf16[2,16,1024]{2,1,0:T(8,128)(2,1)}, bf16[2,16,1024]{2,1,0:T(8,128)(2,1)S(1)}, u32[]{:S(2)}) copy-start(bf16[2,16,1024]{2,1,0:T(8,128)(2,1)S(1)} %pad_maximum_fusion.5.refs_4_.refs_5_) | copy-start | bytes 196612
  17.5 5.5 %collective-permute-start.2 = (bf16[2,16,1024]{2,1,0:T(8,128)(2,1)S(1)}, bf16[2,16,1024]{2,1,0:T(8,128)(2,1)S(1)}, u32[]{:S(2)}, u32[]{:S(2)}) collective-permute-start(bf16[2,16,1024]{2,1,0:T(8,128)(2,1)S(1)} %pad_maximum_fusion.5.refs_4_.refs_5_), channel_id=1, source_target_pairs={{0,4},{2,6},{4,0},{6,2},{8,12},{10,14},{12,8},{14,10},{16,20},{18,... | collective-permute-start | bytes 196616 | tf_op jit(solution)/shard_map/ppermute | solution.py:29
  19.5 7.2 %collective-permute-start.3 = (bf16[2,16,1024]{2,1,0:T(8,128)(2,1)S(1)}, bf16[2,16,1024]{2,1,0:T(8,128)(2,1)S(1)}, u32[]{:S(2)}, u32[]{:S(2)}) collective-permute-start(bf16[2,16,1024]{2,1,0:T(8,128)(2,1)S(1)} %pad_maximum_fusion.5.refs_4_.refs_5_), channel_id=1, source_target_pairs={{0,8},{2,10},{4,12},{6,14},{8,0},{10,2},{12,4},{14,6},{16,24},{18,... | collective-permute-start | bytes 196616 | tf_op jit(solution)/shard_map/ppermute | solution.py:29
  23.0 6.2 %collective-permute-start.4 = (bf16[2,16,1024]{2,1,0:T(8,128)(2,1)S(1)}, bf16[2,16,1024]{2,1,0:T(8,128)(2,1)S(1)}, u32[]{:S(2)}, u32[]{:S(2)}) collective-permute-start(bf16[2,16,1024]{2,1,0:T(8,128)(2,1)S(1)} %pad_maximum_fusion.5.refs_4_.refs_5_), channel_id=1, source_target_pairs={{0,12},{2,14},{4,8},{6,10},{8,4},{10,6},{12,0},{14,2},{16,28},{18,... | collective-permute-start | bytes 196616 | tf_op jit(solution)/shard_map/ppermute | solution.py:29
  23.0 7.2 %collective-permute-start.5 = (bf16[2,16,1024]{2,1,0:T(8,128)(2,1)S(1)}, bf16[2,16,1024]{2,1,0:T(8,128)(2,1)S(1)}, u32[]{:S(2)}, u32[]{:S(2)}) collective-permute-start(bf16[2,16,1024]{2,1,0:T(8,128)(2,1)S(1)} %pad_maximum_fusion.5.refs_4_.refs_5_), channel_id=1, source_target_pairs={{0,2},{2,0},{4,6},{6,4},{8,10},{10,8},{12,14},{14,12},{16,18},{18,... | collective-permute-start | bytes 196616 | tf_op jit(solution)/shard_map/ppermute | solution.py:29
  23.0 15.6 %copy-start.5 = (bf16[2,16,1024]{2,1,0:T(8,128)(2,1)}, bf16[2,16,1024]{2,1,0:T(8,128)(2,1)S(1)}, u32[]{:S(2)}) copy-start(bf16[2,16,1024]{2,1,0:T(8,128)(2,1)S(1)} %collective-permute-done.2.refs_5_.refs_6_) | copy-start | bytes 196612
  23.0 7.5 %collective-permute-start.6 = (bf16[2,16,1024]{2,1,0:T(8,128)(2,1)S(1)}, bf16[2,16,1024]{2,1,0:T(8,128)(2,1)S(1)}, u32[]{:S(2)}, u32[]{:S(2)}) collective-permute-start(bf16[2,16,1024]{2,1,0:T(8,128)(2,1)S(1)} %collective-permute-done.2.refs_5_.refs_6_), channel_id=1, source_target_pairs={{0,2},{2,0},{4,6},{6,4},{8,10},{10,8},{12,14},{14,12},{16,18},{18,... | collective-permute-start | bytes 196616 | tf_op jit(solution)/shard_map/ppermute | solution.py:29
  26.8 11.8 %copy-start.6 = (bf16[2,16,1024]{2,1,0:T(8,128)(2,1)}, bf16[2,16,1024]{2,1,0:T(8,128)(2,1)S(1)}, u32[]{:S(2)}) copy-start(bf16[2,16,1024]{2,1,0:T(8,128)(2,1)S(1)} %collective-permute-done.3.refs_6_.refs_7_) | copy-start | bytes 196612
  26.8 9.0 %collective-permute-start.7 = (bf16[2,16,1024]{2,1,0:T(8,128)(2,1)S(1)}, bf16[2,16,1024]{2,1,0:T(8,128)(2,1)S(1)}, u32[]{:S(2)}, u32[]{:S(2)}) collective-permute-start(bf16[2,16,1024]{2,1,0:T(8,128)(2,1)S(1)} %collective-permute-done.3.refs_6_.refs_7_), channel_id=1, source_target_pairs={{0,2},{2,0},{4,6},{6,4},{8,10},{10,8},{12,14},{14,12},{16,18},{18,... | collective-permute-start | bytes 196616 | tf_op jit(solution)/shard_map/ppermute | solution.py:29
  26.8 6.6 %collective-permute-start.12 = (bf16[2,24,1024]{2,1,0:T(8,128)(2,1)S(1)}, bf16[2,24,1024]{2,1,0:T(8,128)(2,1)S(1)}, u32[]{:S(2)}, u32[]{:S(2)}) collective-permute-start(bf16[2,24,1024]{2,1,0:T(8,128)(2,1)S(1)} %pad_maximum_fusion.4), channel_id=1, source_target_pairs={{0,12},{2,14},{4,8},{6,10},{8,4},{10,6},{12,0},{14,2},{16,28},{18,... | collective-permute-start | bytes 294920 | tf_op jit(solution)/shard_map/ppermute | solution.py:29
  29.2 9.4 %copy-start.7 = (bf16[2,16,1024]{2,1,0:T(8,128)(2,1)}, bf16[2,16,1024]{2,1,0:T(8,128)(2,1)S(1)}, u32[]{:S(2)}) copy-start(bf16[2,16,1024]{2,1,0:T(8,128)(2,1)S(1)} %collective-permute-done.4.refs_7_.refs_8_) | copy-start | bytes 196612
  29.2 6.1 %collective-permute-start.11 = (bf16[2,24,1024]{2,1,0:T(8,128)(2,1)S(1)}, bf16[2,24,1024]{2,1,0:T(8,128)(2,1)S(1)}, u32[]{:S(2)}, u32[]{:S(2)}) collective-permute-start(bf16[2,24,1024]{2,1,0:T(8,128)(2,1)S(1)} %pad_maximum_fusion.3), channel_id=1, source_target_pairs={{0,8},{2,10},{4,12},{6,14},{8,0},{10,2},{12,4},{14,6},{16,24},{18,... | collective-permute-start | bytes 294920 | tf_op jit(solution)/shard_map/ppermute | solution.py:29
  30.1 8.5 %copy-start.8 = (bf16[2,16,1024]{2,1,0:T(8,128)(2,1)}, bf16[2,16,1024]{2,1,0:T(8,128)(2,1)S(1)}, u32[]{:S(2)}) copy-start(bf16[2,16,1024]{2,1,0:T(8,128)(2,1)S(1)} %collective-permute-done.5.refs_8_.refs_9_) | copy-start | bytes 196612
  30.1 5.2 %collective-permute-start.10 = (bf16[2,24,1024]{2,1,0:T(8,128)(2,1)S(1)}, bf16[2,24,1024]{2,1,0:T(8,128)(2,1)S(1)}, u32[]{:S(2)}, u32[]{:S(2)}) collective-permute-start(bf16[2,24,1024]{2,1,0:T(8,128)(2,1)S(1)} %pad_maximum_fusion.2), channel_id=1, source_target_pairs={{0,4},{2,6},{4,0},{6,2},{8,12},{10,14},{12,8},{14,10},{16,20},{18,... | collective-permute-start | bytes 294920 | tf_op jit(solution)/shard_map/ppermute | solution.py:29
  30.5 8.0 %collective-permute-start.13 = (bf16[2,24,1024]{2,1,0:T(8,128)(2,1)S(1)}, bf16[2,24,1024]{2,1,0:T(8,128)(2,1)S(1)}, u32[]{:S(2)}, u32[]{:S(2)}) collective-permute-start(bf16[2,24,1024]{2,1,0:T(8,128)(2,1)S(1)} %pad_maximum_fusion.1.refs_12_), channel_id=1, source_target_pairs={{0,2},{2,0},{4,6},{6,4},{8,10},{10,8},{12,14},{14,12},{16,18},{18,... | collective-permute-start | bytes 294920 | tf_op jit(solution)/shard_map/ppermute | solution.py:29
  33.4 5.1 %collective-permute-start.16 = (bf16[2,24,1024]{2,1,0:T(8,128)(2,1)S(1)}, bf16[2,24,1024]{2,1,0:T(8,128)(2,1)S(1)}, u32[]{:S(2)}, u32[]{:S(2)}) collective-permute-start(bf16[2,24,1024]{2,1,0:T(8,128)(2,1)S(1)} %collective-permute-done.12.refs_15_), channel_id=1, source_target_pairs={{0,2},{2,0},{4,6},{6,4},{8,10},{10,8},{12,14},{14,12},{16,18},{18,... | collective-permute-start | bytes 294920 | tf_op jit(solution)/shard_map/ppermute | solution.py:29
  35.3 3.2 %collective-permute-start.15 = (bf16[2,24,1024]{2,1,0:T(8,128)(2,1)S(1)}, bf16[2,24,1024]{2,1,0:T(8,128)(2,1)S(1)}, u32[]{:S(2)}, u32[]{:S(2)}) collective-permute-start(bf16[2,24,1024]{2,1,0:T(8,128)(2,1)S(1)} %collective-permute-done.11.refs_14_), channel_id=1, source_target_pairs={{0,2},{2,0},{4,6},{6,4},{8,10},{10,8},{12,14},{14,12},{16,18},{18,... | collective-permute-start | bytes 294920 | tf_op jit(solution)/shard_map/ppermute | solution.py:29
  35.3 3.2 %collective-permute-start.14 = (bf16[2,24,1024]{2,1,0:T(8,128)(2,1)S(1)}, bf16[2,24,1024]{2,1,0:T(8,128)(2,1)S(1)}, u32[]{:S(2)}, u32[]{:S(2)}) collective-permute-start(bf16[2,24,1024]{2,1,0:T(8,128)(2,1)S(1)} %collective-permute-done.10.refs_13_), channel_id=1, source_target_pairs={{0,2},{2,0},{4,6},{6,4},{8,10},{10,8},{12,14},{14,12},{16,18},{18,... | collective-permute-start | bytes 294920 | tf_op jit(solution)/shard_map/ppermute | solution.py:29
  35.8 2.7 %collective-permute-start.8 = (bf16[2,16,1024]{2,1,0:T(8,128)(2,1)S(1)}, bf16[2,16,1024]{2,1,0:T(8,128)(2,1)S(1)}, u32[]{:S(2)}, u32[]{:S(2)}) collective-permute-start(bf16[2,16,1024]{2,1,0:T(8,128)(2,1)S(1)} %collective-permute-done.4.refs_7_.refs_8_), channel_id=1, source_target_pairs={{0,2},{2,0},{4,6},{6,4},{8,10},{10,8},{12,14},{14,12},{16,18},{18,... | collective-permute-start | bytes 196616 | tf_op jit(solution)/shard_map/ppermute | solution.py:29
  51.7 1.7 %collective-permute-start.17 = (bf16[216,384]{1,0:T(8,128)(2,1)}, bf16[216,384]{1,0:T(8,128)(2,1)S(1)}, u32[]{:S(2)}, u32[]{:S(2)}) collective-permute-start(bf16[216,384]{1,0:T(8,128)(2,1)} %get-tuple-element.19), channel_id=1, source_target_pairs={{0,2},{2,0},{4,6},{6,4},{8,10},{10,8},{12,14},{14,12},{16,18},{18,... | collective-permute-start | bytes 497672 | tf_op jit(solution)/shard_map/ppermute | solution.py:29
  54.5 29.7 %copy-start.1 = (bf16[216,384]{1,0:T(8,128)(2,1)}, bf16[216,384]{1,0:T(8,128)(2,1)S(1)}, u32[]{:S(2)}) copy-start(bf16[216,384]{1,0:T(8,128)(2,1)S(1)} %add_convert_fusion) | copy-start | bytes 497668
  54.5 15.8 %collective-permute-start.18 = (bf16[216,384]{1,0:T(8,128)(2,1)S(1)}, bf16[216,384]{1,0:T(8,128)(2,1)S(1)}, u32[]{:S(2)}, u32[]{:S(2)}) collective-permute-start(bf16[216,384]{1,0:T(8,128)(2,1)S(1)} %add_convert_fusion), channel_id=1, source_target_pairs={{0,8},{2,10},{4,12},{6,14},{8,0},{10,2},{12,4},{14,6},{16,24},{18,... | collective-permute-start | bytes 497672 | tf_op jit(solution)/shard_map/ppermute | solution.py:29
  54.9 15.4 %collective-permute-start.19 = (bf16[216,384]{1,0:T(8,128)(2,1)S(1)}, bf16[216,384]{1,0:T(8,128)(2,1)S(1)}, u32[]{:S(2)}, u32[]{:S(2)}) collective-permute-start(bf16[216,384]{1,0:T(8,128)(2,1)S(1)} %add_convert_fusion), channel_id=1, source_target_pairs={{0,16},{2,18},{4,20},{6,22},{8,24},{10,26},{12,28},{14,30},{16,0},... | collective-permute-start | bytes 497672 | tf_op jit(solution)/shard_map/ppermute | solution.py:29
  58.1 12.2 %collective-permute-start.20 = (bf16[216,384]{1,0:T(8,128)(2,1)S(1)}, bf16[216,384]{1,0:T(8,128)(2,1)S(1)}, u32[]{:S(2)}, u32[]{:S(2)}) collective-permute-start(bf16[216,384]{1,0:T(8,128)(2,1)S(1)} %add_convert_fusion), channel_id=1, source_target_pairs={{0,24},{2,26},{4,28},{6,30},{8,16},{10,18},{12,20},{14,22},{16,8},... | collective-permute-start | bytes 497672 | tf_op jit(solution)/shard_map/ppermute | solution.py:29
  58.9 12.5 %collective-permute-start.30 = (bf16[216,384]{1,0:T(8,128)(2,1)S(1)}, bf16[216,384]{1,0:T(8,128)(2,1)S(1)}, u32[]{:S(2)}, u32[]{:S(2)}) collective-permute-start(bf16[216,384]{1,0:T(8,128)(2,1)S(1)} %add_convert_fusion), channel_id=1, source_target_pairs={{0,4},{2,6},{4,0},{6,2},{8,12},{10,14},{12,8},{14,10},{16,20},{18,... | collective-permute-start | bytes 497672 | tf_op jit(solution)/shard_map/ppermute | solution.py:29
  60.2 12.7 %collective-permute-start.31 = (bf16[216,384]{1,0:T(8,128)(2,1)S(1)}, bf16[216,384]{1,0:T(8,128)(2,1)S(1)}, u32[]{:S(2)}, u32[]{:S(2)}) collective-permute-start(bf16[216,384]{1,0:T(8,128)(2,1)S(1)} %add_convert_fusion), channel_id=1, source_target_pairs={{0,2},{2,0},{4,6},{6,4},{8,10},{10,8},{12,14},{14,12},{16,18},{18,... | collective-permute-start | bytes 497672 | tf_op jit(solution)/shard_map/ppermute | solution.py:29
  70.2 17.2 %copy-start.15 = (bf16[216,384]{1,0:T(8,128)(2,1)}, bf16[216,384]{1,0:T(8,128)(2,1)S(1)}, u32[]{:S(2)}) copy-start(bf16[216,384]{1,0:T(8,128)(2,1)S(1)} %collective-permute-done.18) | copy-start | bytes 497668
  70.3 17.1 %copy-start.13 = (bf16[216,384]{1,0:T(8,128)(2,1)}, bf16[216,384]{1,0:T(8,128)(2,1)S(1)}, u32[]{:S(2)}) copy-start(bf16[216,384]{1,0:T(8,128)(2,1)S(1)} %collective-permute-done.19) | copy-start | bytes 497668
  70.3 17.1 %copy-start.14 = (bf16[216,384]{1,0:T(8,128)(2,1)}, bf16[216,384]{1,0:T(8,128)(2,1)S(1)}, u32[]{:S(2)}) copy-start(bf16[216,384]{1,0:T(8,128)(2,1)S(1)} %collective-permute-done.20) | copy-start | bytes 497668
  70.3 7.1 %collective-permute-start.28 = (bf16[216,384]{1,0:T(8,128)(2,1)S(1)}, bf16[216,384]{1,0:T(8,128)(2,1)S(1)}, u32[]{:S(2)}, u32[]{:S(2)}) collective-permute-start(bf16[216,384]{1,0:T(8,128)(2,1)S(1)} %collective-permute-done.18), channel_id=1, source_target_pairs={{0,4},{2,6},{4,0},{6,2},{8,12},{10,14},{12,8},{14,10},{16,20},{18,... | collective-permute-start | bytes 497672 | tf_op jit(solution)/shard_map/ppermute | solution.py:29
  71.4 12.7 %copy-start.16 = (bf16[216,384]{1,0:T(8,128)(2,1)}, bf16[216,384]{1,0:T(8,128)(2,1)S(1)}, u32[]{:S(2)}) copy-start(bf16[216,384]{1,0:T(8,128)(2,1)S(1)} %collective-permute-done.30) | copy-start | bytes 497668
  71.4 6.0 %collective-permute-start.32 = (bf16[216,384]{1,0:T(8,128)(2,1)S(1)}, bf16[216,384]{1,0:T(8,128)(2,1)S(1)}, u32[]{:S(2)}, u32[]{:S(2)}) collective-permute-start(bf16[216,384]{1,0:T(8,128)(2,1)S(1)} %collective-permute-done.30), channel_id=1, source_target_pairs={{0,2},{2,0},{4,6},{6,4},{8,10},{10,8},{12,14},{14,12},{16,18},{18,... | collective-permute-start | bytes 497672 | tf_op jit(solution)/shard_map/ppermute | solution.py:29
  71.4 6.5 %collective-permute-start.27 = (bf16[216,384]{1,0:T(8,128)(2,1)S(1)}, bf16[216,384]{1,0:T(8,128)(2,1)S(1)}, u32[]{:S(2)}, u32[]{:S(2)}) collective-permute-start(bf16[216,384]{1,0:T(8,128)(2,1)S(1)} %collective-permute-done.18), channel_id=1, source_target_pairs={{0,2},{2,0},{4,6},{6,4},{8,10},{10,8},{12,14},{14,12},{16,18},{18,... | collective-permute-start | bytes 497672 | tf_op jit(solution)/shard_map/ppermute | solution.py:29
  71.9 9.0 %collective-permute-start.22 = (bf16[216,384]{1,0:T(8,128)(2,1)S(1)}, bf16[216,384]{1,0:T(8,128)(2,1)S(1)}, u32[]{:S(2)}, u32[]{:S(2)}) collective-permute-start(bf16[216,384]{1,0:T(8,128)(2,1)S(1)} %collective-permute-done.19), channel_id=1, source_target_pairs={{0,4},{2,6},{4,0},{6,2},{8,12},{10,14},{12,8},{14,10},{16,20},{18,... | collective-permute-start | bytes 497672 | tf_op jit(solution)/shard_map/ppermute | solution.py:29
  72.9 11.2 %copy-start.17 = (bf16[216,384]{1,0:T(8,128)(2,1)}, bf16[216,384]{1,0:T(8,128)(2,1)S(1)}, u32[]{:S(2)}) copy-start(bf16[216,384]{1,0:T(8,128)(2,1)S(1)} %collective-permute-done.31) | copy-start | bytes 497668
  72.9 11.2 %collective-permute-start.25 = (bf16[216,384]{1,0:T(8,128)(2,1)S(1)}, bf16[216,384]{1,0:T(8,128)(2,1)S(1)}, u32[]{:S(2)}, u32[]{:S(2)}) collective-permute-start(bf16[216,384]{1,0:T(8,128)(2,1)S(1)} %collective-permute-done.20), channel_id=1, source_target_pairs={{0,4},{2,6},{4,0},{6,2},{8,12},{10,14},{12,8},{14,10},{16,20},{18,... | collective-permute-start | bytes 497672 | tf_op jit(solution)/shard_map/ppermute | solution.py:29
  77.4 10.0 %copy-start.19 = (bf16[216,384]{1,0:T(8,128)(2,1)}, bf16[216,384]{1,0:T(8,128)(2,1)S(1)}, u32[]{:S(2)}) copy-start(bf16[216,384]{1,0:T(8,128)(2,1)S(1)} %collective-permute-done.28) | copy-start | bytes 497668
  77.4 10.1 %collective-permute-start.29 = (bf16[216,384]{1,0:T(8,128)(2,1)S(1)}, bf16[216,384]{1,0:T(8,128)(2,1)S(1)}, u32[]{:S(2)}, u32[]{:S(2)}) collective-permute-start(bf16[216,384]{1,0:T(8,128)(2,1)S(1)} %collective-permute-done.28), channel_id=1, source_target_pairs={{0,2},{2,0},{4,6},{6,4},{8,10},{10,8},{12,14},{14,12},{16,18},{18,... | collective-permute-start | bytes 497672 | tf_op jit(solution)/shard_map/ppermute | solution.py:29
  77.4 13.1 %collective-permute-start.21 = (bf16[216,384]{1,0:T(8,128)(2,1)S(1)}, bf16[216,384]{1,0:T(8,128)(2,1)S(1)}, u32[]{:S(2)}, u32[]{:S(2)}) collective-permute-start(bf16[216,384]{1,0:T(8,128)(2,1)S(1)} %collective-permute-done.19), channel_id=1, source_target_pairs={{0,2},{2,0},{4,6},{6,4},{8,10},{10,8},{12,14},{14,12},{16,18},{18,... | collective-permute-start | bytes 497672 | tf_op jit(solution)/shard_map/ppermute | solution.py:29
  77.9 9.5 %copy-start.21 = (bf16[216,384]{1,0:T(8,128)(2,1)}, bf16[216,384]{1,0:T(8,128)(2,1)S(1)}, u32[]{:S(2)}) copy-start(bf16[216,384]{1,0:T(8,128)(2,1)S(1)} %collective-permute-done.27) | copy-start | bytes 497668
  77.9 12.6 %collective-permute-start.24 = (bf16[216,384]{1,0:T(8,128)(2,1)S(1)}, bf16[216,384]{1,0:T(8,128)(2,1)S(1)}, u32[]{:S(2)}, u32[]{:S(2)}) collective-permute-start(bf16[216,384]{1,0:T(8,128)(2,1)S(1)} %collective-permute-done.20), channel_id=1, source_target_pairs={{0,2},{2,0},{4,6},{6,4},{8,10},{10,8},{12,14},{14,12},{16,18},{18,... | collective-permute-start | bytes 497672 | tf_op jit(solution)/shard_map/ppermute | solution.py:29
  81.0 9.6 %collective-permute-start.23 = (bf16[216,384]{1,0:T(8,128)(2,1)S(1)}, bf16[216,384]{1,0:T(8,128)(2,1)S(1)}, u32[]{:S(2)}, u32[]{:S(2)}) collective-permute-start(bf16[216,384]{1,0:T(8,128)(2,1)S(1)} %collective-permute-done.22), channel_id=1, source_target_pairs={{0,2},{2,0},{4,6},{6,4},{8,10},{10,8},{12,14},{14,12},{16,18},{18,... | collective-permute-start | bytes 497672 | tf_op jit(solution)/shard_map/ppermute | solution.py:29
  84.1 6.4 %collective-permute-start.26 = (bf16[216,384]{1,0:T(8,128)(2,1)S(1)}, bf16[216,384]{1,0:T(8,128)(2,1)S(1)}, u32[]{:S(2)}, u32[]{:S(2)}) collective-permute-start(bf16[216,384]{1,0:T(8,128)(2,1)S(1)} %collective-permute-done.25), channel_id=1, source_target_pairs={{0,2},{2,0},{4,6},{6,4},{8,10},{10,8},{12,14},{14,12},{16,18},{18,... | collective-permute-start | bytes 497672 | tf_op jit(solution)/shard_map/ppermute | solution.py:29
  (22 other events, 62.1 us)

commit v4 on v3

--- a/solution.py
+++ b/solution.py
@@ -15,6 +15,10 @@
 
 def params():
     return pltpu.CompilerParams(vmem_limit_bytes=VMEM_LIMIT)
+
+
+def cost(flops, size):
+    return pl.CostEstimate(flops=flops, transcendentals=0, bytes_accessed=size)
 
 
 def vmem():
@@ -88,7 +92,7 @@
 
 
 def place_latent(slot_ref, stack_ref, me, first_slab, slab_count, frames, rows, slabs):
-    latent_width = slot_ref.shape[1]
+    latent_width = stack_ref.shape[1] // 3
     for offset in range(-1, slab_count + 1):
         slab = first_slab + offset
         inside = ((slab >= 0) & (slab < slabs)).astype(F32)
@@ -101,7 +105,7 @@
         for frame in range(frames):
             for row in needed:
                 at = (frame * rows + row) * LANES
-                tile = slot_ref[source, :, at : at + LANES].astype(F32)
+                tile = slot_ref[source, :latent_width, at : at + LANES].astype(F32)
                 if offset in (-1, slab_count):
                     tile = tile * inside
                 to = (offset * rows + row + 2) * LANES
@@ -136,8 +140,10 @@
             act_ref[chunk, pl.ds(at, LANES)] = (half + half * jnp.tanh(half)).astype(BF16)
 
 
-def place_cotangent(slot_ref, flat_ref, out_ref, me, first_slab, slab_count, frames, rows, pad_channels):
-    channels = slot_ref.shape[1]
+def place_cotangent(
+    slot_ref, flat_ref, out_ref, me, first_slab, slab_count, frames, rows, pad_channels, skip
+):
+    channels = slot_ref.shape[1] - skip
     half_rows = slab_count * rows
     group = 3 * pad_channels
     padded = out_ref.shape[0] // frames
@@ -149,7 +155,7 @@
         for frame in range(frames):
             for row in range(rows):
                 at = (frame * rows + row) * LANES
-                tile = slot_ref[source, :, at : at + LANES].astype(F32)
+                tile = slot_ref[source, skip:, at : at + LANES].astype(F32)
                 if pad_channels != channels:
                     tile = jnp.concatenate(
                         [tile, jnp.zeros((pad_channels - channels, LANES), F32)], axis=0
@@ -168,16 +174,14 @@
             )
 
 
-def gradient_kernel(frames, rows, slabs, lat_masks, cot_masks, real_rows, pad_channels, *refs):
+def gradient_kernel(frames, rows, slabs, masks, real_rows, pad_channels, *refs):
     me_ref, gain_ref = refs[:2]
     refs = refs[2:]
     weight_refs, refs = refs[:frames], refs[frames:]
-    lat_refs, refs = refs[: len(lat_masks)], refs[len(lat_masks) :]
-    cot_refs, refs = refs[: len(cot_masks)], refs[len(cot_masks) :]
-    keep_ref, send_ref, lat_slots, cot_slots, stack_ref, flat_ref, cot_ref = refs[:7]
-    hid_a, hid_b, act_a, act_b, sum_ref, wide_gain, lat_sems, cot_sems = refs[7:]
-    lat_copies = fetch(lat_refs, lat_masks, lat_slots, lat_sems)
-    cot_copies = fetch(cot_refs, cot_masks, cot_slots, cot_sems)
+    piece_refs, refs = refs[: len(masks)], refs[len(masks) :]
+    keep_ref, send_ref, slots, stack_ref, flat_ref, cot_ref = refs[:6]
+    hid_a, hid_b, act_a, act_b, sum_ref, wide_gain, sems = refs[6:]
+    copies = fetch(piece_refs, masks, slots, sems)
     me = me_ref[0]
     core = me & 1
     slab_count = slabs // 2
@@ -193,14 +197,13 @@
     acts = (act_a, act_b)
     wide_gain[...] = jnp.broadcast_to(0.5 * gain_ref[...], wide_gain.shape)
     sum_ref[...] = jnp.zeros_like(sum_ref)
-    for copy in lat_copies:
+    for copy in copies:
         copy.wait()
-    place_latent(lat_slots, stack_ref, me, first_slab, slab_count, frames, rows, slabs)
-    for copy in cot_copies:
-        copy.wait()
+    place_latent(slots, stack_ref, me, first_slab, slab_count, frames, rows, slabs)
     hid_a[...] = hidden_rows(stack_ref, weight_refs[0], 0, 0, ext)
     place_cotangent(
-        cot_slots, flat_ref, cot_ref, me, first_slab, slab_count, frames, rows, pad_channels
+        slots, flat_ref, cot_ref, me, first_slab, slab_count, frames, rows, pad_channels,
+        stack_ref.shape[1] // 3,
     )
     for frame in range(frames):
 
@@ -230,60 +233,63 @@
     send_ref[...] = sum_ref[pl.ds(send_at, padded), :][:real_rows].astype(BF16)
 
 
-def decode_kernel(frames, rows, slabs, lat_masks, *refs):
-    me_ref, gain_ref, conv_hbm = refs[:3]
-    refs = refs[3:]
-    weight_refs, refs = refs[:frames], refs[frames:]
-    lat_refs, refs = refs[: len(lat_masks)], refs[len(lat_masks) :]
-    out_ref, lat_slots, stack_ref, hid_ref, flat_ref, act_ref, wide_gain, conv_ref, lat_sems, sem = refs
-    live = conv_ref.shape[0] // 9
-    load = pltpu.make_async_copy(conv_hbm.at[pl.ds((3 - live) * 9, live * 9)], conv_ref, sem)
+def decode_kernel(frame, frames, rows, slabs, masks, me_ref, gain_ref, conv_hbm, *refs):
+    first_source = max(0, frame - 2)
+    sources = range(first_source, frame + 1)
+    weight_refs, refs = refs[: len(sources)], refs[len(sources) :]
+    piece_refs, refs = refs[: len(masks)], refs[len(masks) :]
+    out_ref, slots, stack_ref, hid_ref, flat_ref, act_ref, wide_gain, conv_ref, sems, sem = refs
+    taps = conv_ref.shape[0]
+    load = pltpu.make_async_copy(conv_hbm.at[pl.ds(27 - taps, taps)], conv_ref, sem)
     load.start()
-    lat_copies = fetch(lat_refs, lat_masks, lat_slots, lat_sems)
+    copies = fetch(piece_refs, masks, slots, sems)
     me = me_ref[0]
     height = slabs * rows
     wide_gain[...] = jnp.broadcast_to(0.5 * gain_ref[...], wide_gain.shape)
-    for copy in lat_copies:
+    for copy in copies:
         copy.wait()
-    place_latent(lat_slots, stack_ref, me, me, 1, frames, rows, slabs)
+    place_latent(slots, stack_ref, me, me, 1, frames, rows, slabs)
     ext = rows + 2
-    for frame in range(frames):
-        hid_ref[...] = hidden_rows(stack_ref, weight_refs[frame], frame, 0, ext)
+    kernels = []
+    inputs = []
+    for position, source in enumerate(sources):
+        hid_ref[...] = hidden_rows(stack_ref, weight_refs[position], source, 0, ext)
         activate_rows(hid_ref, wide_gain, flat_ref, 0, me * rows - 1, ext, height)
         for row in range(ext):
             tile = flat_ref[:, row * LANES : (row + 1) * LANES].astype(F32)
             for tap in range(3):
-                act_ref[frame, tap, :, row * LANES : (row + 1) * LANES] = shifted(tile, tap).astype(BF16)
+                act_ref[position, tap, :, row * LANES : (row + 1) * LANES] = shifted(tile, tap).astype(BF16)
     load.wait()
-    for frame in range(frames):
-        kernels = []
-        inputs = []
-        for depth in range(max(0, 2 - frame), 3):
-            for row_tap in range(3):
-                for col_tap in range(3):
-                    kernels.append(conv_ref[(depth - (3 - live)) * 9 + row_tap * 3 + col_tap])
-                    inputs.append(
-                        act_ref[frame + depth - 2, col_tap, :, row_tap * LANES : (row_tap + rows) * LANES]
-                    )
-        total = dot(jnp.concatenate(kernels, axis=1), jnp.concatenate(inputs, axis=0))
-        out_ref[:, frame * rows * LANES : (frame + 1) * rows * LANES] = total.astype(BF16)
-
-
-def finish_kernel(first, pieces, blank, me_ref, *refs):
+    for position, source in enumerate(sources):
+        plane = position * 9
+        for row_tap in range(3):
+            for col_tap in range(3):
+                kernels.append(conv_ref[plane + row_tap * 3 + col_tap])
+                inputs.append(act_ref[position, col_tap, :, row_tap * LANES : (row_tap + rows) * LANES])
+    total = dot(jnp.concatenate(kernels, axis=1), jnp.concatenate(inputs, axis=0))
+    out_ref[...] = total.astype(BF16)
+
+
+def blank_kernel(blank, out_hbm, zero_ref, sems):
+    zero_ref[...] = jnp.zeros_like(zero_ref)
+    copies = [
+        pltpu.make_async_copy(zero_ref, out_hbm.at[plane, tap], sems.at[plane * 9 + tap])
+        for plane in range(blank)
+        for tap in range(9)
+    ]
+    for copy in copies:
+        copy.start()
+    for copy in copies:
+        copy.wait()
+
+
+def finish_kernel(pieces, me_ref, *refs):
     count = len(pieces)
     piece_refs = refs[:count]
-    out_hbm, wide_ref, zero_ref, sems, zero_sem = refs[count + (0 if first else 1) :]
+    out_hbm, wide_ref, sems = refs[count + 1 :]
     me = me_ref[0]
     channels = wide_ref.shape[2]
     copies = []
-    if first and blank:
-        zero_ref[...] = jnp.zeros_like(zero_ref)
-        for plane in range(blank):
-            for tap in range(9):
-                copies.append(
-                    pltpu.make_async_copy(zero_ref, out_hbm.at[plane, tap], zero_sem.at[plane * 9 + tap])
-                )
-                copies[-1].start()
     for index, mask in enumerate(pieces):
         source = me ^ mask
         wide_ref[index] = piece_refs[index][...].astype(F32)
@@ -333,14 +339,7 @@
 
     near, far = wanted(0), wanted(top)
     got = xor_permute(far, "seq", top)
-    cot_blocks = []
-    cot_masks = []
-    for position, mask in enumerate([0] + rest):
-        pair = jnp.stack([near[position], got[position]])
-        cot_blocks.append(pair if mask == 0 else xor_permute(pair, "seq", mask))
-        cot_masks.append([mask, mask ^ top])
-    cot_blocks = cot_blocks + [xor_permute(b, "seq", 1) for b in cot_blocks]
-    cot_masks = cot_masks + [[m ^ 1 for m in masks] for masks in cot_masks]
+
     attn_out = lax.optimization_barrier((attn_out, far))[0]
     flattened = attn_out.reshape(frames * tok_rows * tok_cols, model_width)
     partial_sum = lax.dot_general(
@@ -353,6 +352,10 @@
         if step > 1:
             partial_sum = partial_sum + other
         step //= 2
+    entry = entry_weight.reshape(channels, 3, 9 * latent_width)
+    entries = [entry[:, max(0, 2 - f) :].reshape(channels, -1) for f in range(frames)]
+    gain = norm_gain.reshape(channels, 1)
+    other, gain, *entries = lax.optimization_barrier((other, gain, *entries))
     latent = pl.pallas_call(
         functools.partial(unpatchify_kernel, frames, tok_rows, tok_cols),
         out_shape=jax.ShapeDtypeStruct((latent_width, frames * rows * width), BF16),
@@ -362,29 +365,45 @@
         name="unpatchify",
     )(partial_sum, other)
 
-    pair = jnp.stack([latent, xor_permute(latent, "seq", top)])
-    lats = [pair] + [xor_permute(pair, "seq", m) for m in rest]
-    lat_masks = [[m, m ^ top] for m in [0] + rest]
-    lats = lats + [xor_permute(b, "seq", 1) for b in lats]
-    lat_masks = lat_masks + [[m ^ 1 for m in masks] for masks in lat_masks]
-
-    entry = entry_weight.reshape(channels, 3, 9 * latent_width)
-    entries = [entry[:, max(0, 2 - f) :].reshape(channels, -1) for f in range(frames)]
-    gain = norm_gain.reshape(channels, 1)
+    blank = 3 - live
     hbm = pl.BlockSpec(memory_space=pl.ANY)
+    grad_shape = (3, 9, chips * pad_channels, channels)
+    grad = pl.pallas_call(
+        functools.partial(blank_kernel, blank),
+        out_shape=jax.ShapeDtypeStruct(grad_shape, F32),
+        out_specs=hbm,
+        scratch_shapes=[
+            pltpu.VMEM((chips * pad_channels, channels), F32),
+            pltpu.SemaphoreType.DMA((max(1, 9 * blank),)),
+        ],
+        compiler_params=params(),
+        cost_estimate=cost(0, blank * 9 * out_channels * channels * 4),
+        name="blank",
+    )()
+
+    across = xor_permute(latent, "seq", top)
+    across, grad = lax.optimization_barrier((across, grad))
+    latents = jnp.stack([latent, across])
+    pieces = []
+    masks = []
+    for position, mask in enumerate([0] + rest):
+        both = jnp.concatenate([latents, jnp.stack([near[position], got[position]])], axis=1)
+        pieces.append(both if mask == 0 else xor_permute(both, "seq", mask))
+        masks.append([mask, mask ^ top])
+    pieces = pieces + [xor_permute(p, "seq", 1) for p in pieces]
+    masks = masks + [[m ^ 1 for m in pair] for pair in masks]
+    slot_shape = (slabs, latent_width + chip_channels, frames * rows * width)
+
     keep, send = pl.pallas_call(
-        functools.partial(
-            gradient_kernel, frames, rows, slabs, lat_masks, cot_masks, real_rows, pad_channels
-        ),
+        functools.partial(gradient_kernel, frames, rows, slabs, masks, real_rows, pad_channels),
         out_shape=(
             jax.ShapeDtypeStruct((real_rows, channels), F32),
             jax.ShapeDtypeStruct((real_rows, channels), BF16),
         ),
-        in_specs=[smem(), vmem()] + [vmem()] * frames + [hbm] * (len(lats) + len(cot_blocks)),
+        in_specs=[smem(), vmem()] + [vmem()] * frames + [hbm] * len(pieces),
         out_specs=(vmem(), vmem()),
         scratch_shapes=[
-            pltpu.VMEM((slabs, latent_width, frames * rows * width), BF16),
-            pltpu.VMEM((slabs, chip_channels, frames * rows * width), BF16),
+            pltpu.VMEM(slot_shape, BF16),
             pltpu.VMEM((frames, 3 * latent_width, (half_rows + 4) * width), BF16),
             pltpu.VMEM((frames, 3 * pad_channels, (half_rows + 4) * width), F32),
             pltpu.VMEM((frames * padded, lanes), BF16),
@@ -395,80 +414,85 @@
             pltpu.VMEM((live * padded, channels), F32),
             pltpu.VMEM((channels, LANES), F32),
             pltpu.SemaphoreType.DMA((slabs,)),
-            pltpu.SemaphoreType.DMA((slabs,)),
         ],
         compiler_params=params(),
         name="gradient",
-    )(me, gain, *entries, *lats, *cot_blocks)
+    )(me, gain, *entries, *pieces)
     block = (keep + xor_permute(send, "seq", 1).astype(F32)).astype(BF16)
 
-    columns = [m for m in range(0, slabs, 4)]
-    direct = [block] + [xor_permute(block, "seq", m) for m in columns[1:]]
+    columns = [m for m in range(4, slabs, 4)]
+    direct = [xor_permute(block, "seq", m) for m in columns]
     beside = xor_permute(block, "seq", 2)
-    held = lax.optimization_barrier((block, *lats))[1:]
     conv = conv_weight.transpose(1, 2, 3, 0, 4).reshape(27, out_channels, channels)
-    decoded = pl.pallas_call(
-        functools.partial(decode_kernel, frames, rows, slabs, lat_masks),
-        out_shape=jax.ShapeDtypeStruct((out_channels, frames * rows * width), BF16),
-        in_specs=[smem(), vmem(), hbm] + [vmem()] * frames + [hbm] * len(lats),
-        out_specs=vmem(),
-        scratch_shapes=[
-            pltpu.VMEM((slabs, latent_width, frames * rows * width), BF16),
-            pltpu.VMEM((frames, 3 * latent_width, (rows + 4) * width), BF16),
-            pltpu.VMEM((channels, (rows + 2) * width), F32),
-            pltpu.VMEM((channels, (rows + 2) * width), BF16),
-            pltpu.VMEM((frames, 3, channels, (rows + 2) * width), BF16),
-            pltpu.VMEM((channels, LANES), F32),
-            pltpu.VMEM((live * 9, out_channels, channels), BF16),
-            pltpu.SemaphoreType.DMA((slabs,)),
-            pltpu.SemaphoreType.DMA(()),
-        ],
-        compiler_params=params(),
-        name="decode",
-    )(me, gain, conv, *entries, *held)
-    decoded = decoded.reshape(out_channels, frames, rows, width)
-
-    blank = 3 - live
+
+    def decode(frame, pieces):
+        first = max(0, frame - 2)
+        count = frame + 1 - first
+        return pl.pallas_call(
+            functools.partial(decode_kernel, frame, frames, rows, slabs, masks),
+            out_shape=jax.ShapeDtypeStruct((out_channels, rows * width), BF16),
+            in_specs=[smem(), vmem(), hbm] + [vmem()] * count + [hbm] * len(pieces),
+            out_specs=vmem(),
+            scratch_shapes=[
+                pltpu.VMEM(slot_shape, BF16),
+                pltpu.VMEM((frames, 3 * latent_width, (rows + 4) * width), BF16),
+                pltpu.VMEM((channels, (rows + 2) * width), F32),
+                pltpu.VMEM((channels, (rows + 2) * width), BF16),
+                pltpu.VMEM((count, 3, channels, (rows + 2) * width), BF16),
+                pltpu.VMEM((channels, LANES), F32),
+                pltpu.VMEM((count * 9, out_channels, channels), BF16),
+                pltpu.SemaphoreType.DMA((slabs,)),
+                pltpu.SemaphoreType.DMA(()),
+            ],
+            compiler_params=params(),
+            cost_estimate=cost(
+                count * 18 * out_channels * channels * rows * width,
+                count * 18 * out_channels * channels,
+            ),
+            name="decode",
+        )(me, gain, conv, *entries[first : frame + 1], *pieces)
+
+    gate = block
+    decoded = []
+    across = []
+    for frame in range(frames):
+        held = lax.optimization_barrier((gate, *pieces))
+        result = decode(frame, held[1:])
+        decoded.append(result)
+        gate = result
+        ready = columns[frame:] if frame == frames - 1 else columns[frame : frame + 1]
+        for mask in ready:
+            position = columns.index(mask)
+            gated = lax.optimization_barrier((direct[position], result))[0]
+            across.append(xor_permute(gated, "seq", 2))
+    decoded = jnp.stack([d.reshape(out_channels, rows, width) for d in decoded], axis=1)
+
     shape = (9, pad_channels, channels)
-    grad_shape = (3, 9, chips * pad_channels, channels)
-
-    def finish(parts, masks, grad=None):
-        first = grad is None
+
+    def finish(parts, sources, grad):
         return pl.pallas_call(
-            functools.partial(finish_kernel, first, masks, blank),
+            functools.partial(finish_kernel, sources),
             out_shape=jax.ShapeDtypeStruct(grad_shape, F32),
-            in_specs=[smem()]
-            + [vmem()] * len(parts)
-            + ([] if first else [pl.BlockSpec(memory_space=pl.ANY)]),
-            out_specs=pl.BlockSpec(memory_space=pl.ANY),
+            in_specs=[smem()] + [vmem()] * len(parts) + [hbm],
+            out_specs=hbm,
             scratch_shapes=[
                 pltpu.VMEM((len(parts),) + shape, F32),
-                pltpu.VMEM((chips * pad_channels, channels), F32),
                 pltpu.SemaphoreType.DMA((len(parts),)),
-                pltpu.SemaphoreType.DMA((max(1, 9 * blank),)),
             ],
-            input_output_aliases={} if first else {len(parts) + 1: 0},
+            input_output_aliases={len(parts) + 1: 0},
             compiler_params=params(),
+            cost_estimate=cost(0, len(parts) * real_rows * channels * 6),
             name="finish",
-        )(me, *[p.reshape(shape) for p in parts], *([] if first else [grad]))
-
-    early = [block, beside]
-    early_masks = [0, 2]
-    early = early + [xor_permute(p, "seq", 1) for p in early]
-    early_masks = early_masks + [m ^ 1 for m in early_masks]
-    grad = finish(early, early_masks)
-    after = lax.optimization_barrier((decoded, *direct[1:]))
-    decoded = after[0]
-    groups = [([], []), ([], [])]
-    for mask, piece in zip(columns[1:], after[1:]):
-        across = xor_permute(piece, "seq", 2)
-        parts, masks = groups[0 if mask == 4 else 1]
-        for part, m in ((piece, mask), (across, mask ^ 2)):
-            parts += [part, xor_permute(part, "seq", 1)]
-            masks += [m, m ^ 1]
-    for parts, masks in groups:
+        )(me, *[p.reshape(shape) for p in parts], grad)
+
+    groups = [[(block, 0), (beside, 2)], []]
+    for position, mask in enumerate(columns):
+        groups[0 if position == 0 else 1] += [(direct[position], mask), (across[position], mask ^ 2)]
+    for group in groups:
+        parts = [p for p, _ in group] + [xor_permute(p, "seq", 1) for p, _ in group]
+        sources = [m for _, m in group] + [m ^ 1 for _, m in group]
         if parts:
-            grad = finish(parts, masks, grad)
+            grad = finish(parts, sources, grad)
     if pad_channels != chip_channels:
         grad = grad.reshape(27, chips, pad_channels, channels)[:, :, :chip_channels]
     grad = grad.reshape(3, 3, 3, out_channels, channels).transpose(3, 0, 1, 2, 4)

time: 95.2 us -> 85.8 us (0.901)
  starting transfers between devices: 25.4 us -> 18.9 us
  waiting for transfers between devices: 24.9 us -> 19.3 us
  Pallas kernels: 30.7 us -> 34.7 us
  local copies, waits for them, and re-layouts: 8.8 us -> 7.45 us
    ppermute x33 -> x26, starting transfers between devices: 25.4 us -> 18.9 us  [xor_permute(): lax.ppermute(x, axis, [(i, i ^ mask) for i in range(lax.axis_size(axis))])]
    ppermute x33 -> x26, waiting for transfers between devices: 24.9 us -> 19.3 us  [xor_permute(): lax.ppermute(x, axis, [(i, i ^ mask) for i in range(lax.axis_size(axis))])]
    pallas_call x5 -> x6, Pallas kernels: 29 us -> 33 us  [the longest x2 13.2 us: decode(): pl.pallas_call(functools.partial(decode_kernel, frame, frames, rows, slab...]
    reshape x2 -> x0, local copies, waits for them, and re-layouts: 2.9 us -> none  [the longest x1 2.01 us: per_device(): decoded = decoded.reshape(out_channels, frames, rows, width)]
    optimization_barrier x0 -> x2, local copies, waits for them, and re-layouts: none -> 1.71 us  [per_device(): other, gain, *entries = lax.optimization_barrier((other, gain, *entries))]
    unnamed x75 -> x53, local copies, waits for them, and re-layouts: 3.63 us -> 2.29 us
    another operation x0 -> x2, local copies, waits for them, and re-layouts: none -> 1.09 us  [per_device(): jnp.stack([d.reshape(out_channels, rows, width) for d in decoded], axis=1)]
  transfers between devices with their start and end apart: 33 -> 26, of which waited for: 11 -> 8; matrix products, arithmetic and copies ran while one was open for 6% -> 8% of each run, Pallas kernels for 14% -> 23%
where the time goes in v4:
time: 85.8 us; the launch traced here: 85.3 us
  Pallas kernels  34.7 us (40%)
  waiting for transfers between devices  19.3 us (22%)
  starting transfers between devices  18.9 us (22%)
  local copies, waits for them, and re-layouts  7.45 us (9%)
  other arithmetic  2.13 us (2%)
  matrix products  1.48 us (2%)
  between operations  1.36 us (2%)
    ppermute x26, waiting for transfers between devices, xor_permute(): lax.ppermute(x, axis, [(i, i ^ mask) for i in range(lax.axis_size(axis))])  19.3 us
    ppermute x26, starting transfers between devices, xor_permute(): lax.ppermute(x, axis, [(i, i ^ mask) for i in range(lax.axis_size(axis))])  18.9 us
    pallas_call x2, Pallas kernels, decode(): pl.pallas_call(functools.partial(decode_kernel, frame, frames, rows, slab...  13.2 us
    pallas_call x1, Pallas kernels, per_device(): pl.pallas_call(functools.partial(gradient_kernel, frames, rows, slabs, ma...  12.2 us
    pallas_call x2, Pallas kernels, finish(): pl.pallas_call(functools.partial(finish_kernel, sources), out_shape=jax.S...  5.96 us
    unnamed x53, local copies, waits for them, and re-layouts  2.29 us
  transfers between devices with their start and end apart: 26, of which 8 were waited for; matrix products, arithmetic and copies ran while one was open for 8% of the time, Pallas kernels for 23%

profile of v4, /device:TPU:0, one launch (start us, length us, event | category | flops | bytes accessed | tf_op | source)
XLA Modules:
  0.0 85.3 jit_solution(15529029873672066270)
XLA Ops:
  0.7 1.4 %reshape.80 = bf16[8,24,1024]{2,1,0:T(8,128)(2,1)S(1)} reshape(bf16[192,2,4,128]{3,2,1,0:T(4,128)(2,1)} %param.11) | data formatting | bytes 786432 | tf_op jit(solution)/shard_map/reshape | solution.py:329
  2.2 4.1 %collective-permute-start.2 = (bf16[4,24,1024]{2,1,0:T(8,128)(2,1)S(1)}, bf16[4,24,1024]{2,1,0:T(8,128)(2,1)S(1)}, u32[]{:S(2)}, u32[]{:S(2)}) collective-permute-start(bf16[4,24,1024]{2,1,0:T(8,128)(2,1)S(1)} %pad_maximum_fusion.1), channel_id=1, source_target_pairs={{0,16},{2,18},{4,20},{6,22},{8,24},{10,26},{12,28},{14,30},{16,0},... | collective-permute-start | bytes 589832 | tf_op jit(solution)/shard_map/ppermute | solution.py:33
  6.3 1.5 %convolution_bitcast_fusion.own_ref = f32[64,256]{1,0:T(8,128)S(1)} fusion(bf16[256,2560]{1,0:T(8,128)(2,1)S(1)} %bitcast.35, bf16[2560,64]{0,1:T(8,128)(2,1)} %param.7), kind=kOutput, calls=%fused_computation | convolution fusion | flops 83886080 | bytes 1703936 | tf_op jit(solution)/shard_map/dot_general | solution.py:345
  7.8 1.6 %collective-permute-start = (f32[64,256]{1,0:T(8,128)S(1)}, f32[64,256]{1,0:T(8,128)S(1)}, u32[]{:S(2)}, u32[]{:S(2)}) collective-permute-start(f32[64,256]{1,0:T(8,128)S(1)} %convolution_bitcast_fusion.own_ref), channel_id=1, source_target_pairs={{0,1},{1,0},{2,3},{3,2},{4,5},{5,4},{6,7},{7,6},{8,9},{9,8},{10,11... | collective-permute-start | bytes 196616 | tf_op jit(solution)/shard_map/ppermute | solution.py:33
  9.4 0.9 %slice.24 = bf16[384,1,144]{0,2,1:T(8,128)(2,1)S(1)} slice(bf16[384,3,144]{0,2,1:T(8,128)(2,1)} %bitcast.46), slice={[0:384], [2:3], [0:144]} | slice | bytes 221184 | tf_op jit(solution)/shard_map/slice | solution.py:356
  10.4 0.8 copy.22
  11.2 1.0 %collective-permute-done.other_ref = f32[64,256]{1,0:T(8,128)S(1)} collective-permute-done((f32[64,256]{1,0:T(8,128)S(1)}, f32[64,256]{1,0:T(8,128)S(1)}, u32[]{:S(2)}, u32[]{:S(2)}) %collective-permute-start) | collective-permute-done | bytes 65568 | tf_op jit(solution)/shard_map/ppermute | solution.py:33
  12.2 0.6 copy-done.24
  12.8 1.7 %unpatchify.1 = bf16[16,1024]{1,0:T(8,128)(2,1)} custom-call(f32[64,256]{1,0:T(8,128)} %copy-done.12, f32[64,256]{1,0:T(8,128)} %copy-done.24), custom_call_target="tpu_custom_call" | custom-call | tf_op jit(solution)/shard_map/unpatchify/pallas_call | solution.py:359
  14.5 1.6 %blank.1.refs_8_ = f32[3,9,192,384]{3,2,1,0:T(8,128)} custom-call(), custom_call_target="tpu_custom_call" | custom-call | bytes 2654208 | tf_op jit(solution)/shard_map/blank/pallas_call | solution.py:371
  16.1 3.4 %collective-permute-done.1 = bf16[16,1024]{1,0:T(8,128)(2,1)S(1)} collective-permute-done((bf16[16,1024]{1,0:T(8,128)(2,1)}, bf16[16,1024]{1,0:T(8,128)(2,1)S(1)}, u32[]{:S(2)}, u32[]{:S(2)}) %collective-permute-start.1) | collective-permute-done | bytes 32800 | tf_op jit(solution)/shard_map/ppermute | solution.py:33
  19.5 0.1 maximum_maximum_fusion.3
  19.6 2.6 %collective-permute-start.5 = (bf16[2,40,1024]{2,1,0:T(8,128)(2,1)S(1)}, bf16[2,40,1024]{2,1,0:T(8,128)(2,1)S(1)}, u32[]{:S(2)}, u32[]{:S(2)}) collective-permute-start(bf16[2,40,1024]{2,1,0:T(8,128)(2,1)S(1)} %get-tuple-element.70), channel_id=1, source_target_pairs={{0,12},{2,14},{4,8},{6,10},{8,4},{10,6},{12,0},{14,2},{16,28},{18,... | collective-permute-start | bytes 491528 | tf_op jit(solution)/shard_map/ppermute | solution.py:33
  22.2 0.5 collective-permute-start.3
  22.7 0.4 collective-permute-start.4
  23.1 3.7 %collective-permute-done.5.refs_7_.refs_4_.refs_5_ = bf16[2,40,1024]{2,1,0:T(8,128)(2,1)S(1)} collective-permute-done((bf16[2,40,1024]{2,1,0:T(8,128)(2,1)S(1)}, bf16[2,40,1024]{2,1,0:T(8,128)(2,1)S(1)}, u32[]{:S(2)}, u32[]{:S(2)}) %collective-permute-start.5) | collective-permute-done | bytes 163872 | tf_op jit(solution)/shard_map/ppermute | solution.py:33
  26.8 1.6 %collective-permute-done.3.refs_5_.refs_2_.refs_3_ = bf16[2,40,1024]{2,1,0:T(8,128)(2,1)S(1)} collective-permute-done((bf16[2,40,1024]{2,1,0:T(8,128)(2,1)S(1)}, bf16[2,40,1024]{2,1,0:T(8,128)(2,1)S(1)}, u32[]{:S(2)}, u32[]{:S(2)}) %collective-permute-start.3) | collective-permute-done | bytes 163872 | tf_op jit(solution)/shard_map/ppermute | solution.py:33
  28.4 0.5 collective-permute-start.8
  28.9 0.8 copy.17.refs_1_.gain_ref
  29.8 0.9 %copy.16.refs_3_.refs_1_ = bf16[384,288]{1,0:T(8,128)(2,1)} copy(bf16[384,288]{0,1:T(8,128)(2,1)S(1)} %bitcast.42) | data formatting | bytes 442368 | tf_op jit(solution)/shard_map/optimization_barrier | solution.py:358
  30.8 0.6 copy-done.5
  31.3 0.1 copy-done.6
  31.4 0.1 copy-done.8
  31.5 12.2 %gradient.1 = (f32[216,384]{1,0:T(8,128)}, bf16[216,384]{1,0:T(8,128)(2,1)}) custom-call(s32[1]{0:T(128)} %bitcast.refs_0_.me_ref, f32[384,1]{1,0:T(8,128)} %copy.17.refs_1_.gain_ref, bf16[384,144]{1,0:T(8,128)(2,1)} %bitcast.39, bf16[384,288]{1,0:T(8,128)(2,1)} %copy.16.refs_3_.refs_1_, bf16[2,40,1024]{2,1,0:T(8,128)(2,1)} %copy-done.1, ...), custom_call_target="tpu_custom_call" | custom-call | tf_op jit(solution)/shard_map/gradient/pallas_call | solution.py:397
  43.7 0.1 collective-permute-start.10
  43.9 1.5 %collective-permute-done.10 = bf16[216,384]{1,0:T(8,128)(2,1)S(1)} collective-permute-done((bf16[216,384]{1,0:T(8,128)(2,1)}, bf16[216,384]{1,0:T(8,128)(2,1)S(1)}, u32[]{:S(2)}, u32[]{:S(2)}) %collective-permute-start.10) | collective-permute-done | bytes 165920 | tf_op jit(solution)/shard_map/ppermute | solution.py:33
  45.4 1.0 %add_convert_fusion = bf16[216,384]{1,0:T(8,128)(2,1)S(1)} fusion(f32[216,384]{1,0:T(8,128)} %get-tuple-element.36, bf16[216,384]{1,0:T(8,128)(2,1)S(1)} %collective-permute-done.10), kind=kLoop, calls=%fused_computation.2 | loop fusion | flops 248832 | bytes 663552 | tf_op jit(solution)/shard_map/convert_element_type | solution.py:421
  46.4 0.2 collective-permute-start.22
  46.6 0.9 %collective-permute-start.20 = (bf16[216,384]{1,0:T(8,128)(2,1)S(1)}, bf16[216,384]{1,0:T(8,128)(2,1)S(1)}, u32[]{:S(2)}, u32[]{:S(2)}) collective-permute-start(bf16[216,384]{1,0:T(8,128)(2,1)S(1)} %add_convert_fusion), channel_id=1, source_target_pairs={{0,8},{2,10},{4,12},{6,14},{8,0},{10,2},{12,4},{14,6},{16,24},{18,... | collective-permute-start | bytes 497672 | tf_op jit(solution)/shard_map/ppermute | solution.py:33
  47.6 0.9 %collective-permute-start.19 = (bf16[216,384]{1,0:T(8,128)(2,1)S(1)}, bf16[216,384]{1,0:T(8,128)(2,1)S(1)}, u32[]{:S(2)}, u32[]{:S(2)}) collective-permute-start(bf16[216,384]{1,0:T(8,128)(2,1)S(1)} %add_convert_fusion), channel_id=1, source_target_pairs={{0,4},{2,6},{4,0},{6,2},{8,12},{10,14},{12,8},{14,10},{16,20},{18,... | collective-permute-start | bytes 497672 | tf_op jit(solution)/shard_map/ppermute | solution.py:33
  48.4 1.2 %collective-permute-start.13 = (bf16[216,384]{1,0:T(8,128)(2,1)S(1)}, bf16[216,384]{1,0:T(8,128)(2,1)S(1)}, u32[]{:S(2)}, u32[]{:S(2)}) collective-permute-start(bf16[216,384]{1,0:T(8,128)(2,1)S(1)} %add_convert_fusion), channel_id=1, source_target_pairs={{0,24},{2,26},{4,28},{6,30},{8,16},{10,18},{12,20},{14,22},{16,8},... | collective-permute-start | bytes 497672 | tf_op jit(solution)/shard_map/ppermute | solution.py:33
  49.7 1.4 %collective-permute-start.11 = (bf16[216,384]{1,0:T(8,128)(2,1)S(1)}, bf16[216,384]{1,0:T(8,128)(2,1)S(1)}, u32[]{:S(2)}, u32[]{:S(2)}) collective-permute-start(bf16[216,384]{1,0:T(8,128)(2,1)S(1)} %add_convert_fusion), channel_id=1, source_target_pairs={{0,16},{2,18},{4,20},{6,22},{8,24},{10,26},{12,28},{14,30},{16,0},... | collective-permute-start | bytes 497672 | tf_op jit(solution)/shard_map/ppermute | solution.py:33
  51.1 5.6 %decode.2 = bf16[192,512]{1,0:T(8,128)(2,1)} custom-call(s32[1]{0:T(128)} %bitcast.refs_0_.me_ref, f32[384,1]{1,0:T(8,128)} %copy.17.refs_1_.gain_ref, bf16[27,192,384]{2,1,0:T(8,128)(2,1)} %bitcast.37, bf16[384,144]{1,0:T(8,128)(2,1)} %bitcast.40, bf16[2,40,1024]{2,1,0:T(8,128)(2,1)} %copy-done.1, bf16[2,40,1024]{2,1,0:T(8,128)(2,1)} %copy-done.3, ...), custom_call_target="tpu_custom_call" | custom-call | flops 679477248 | bytes 1327104 | tf_op jit(solution)/shard_map/decode/pallas_call | solution.py:431
  56.7 7.6 %decode.3 = bf16[192,512]{1,0:T(8,128)(2,1)} custom-call(s32[1]{0:T(128)} %bitcast.refs_0_.me_ref, f32[384,1]{1,0:T(8,128)} %copy.17.refs_1_.gain_ref, bf16[27,192,384]{2,1,0:T(8,128)(2,1)} %bitcast.38, bf16[384,144]{1,0:T(8,128)(2,1)} %bitcast.41, bf16[384,288]{1,0:T(8,128)(2,1)} %copy.16.refs_3_.refs_1_, bf16[2,40,1024]{2,1,0:T(8,128)(2,1)} %copy-done.1, ...), custom_call_target="tpu_custom_call" | custom-call | flops 1358954496 | bytes 2654208 | tf_op jit(solution)/shard_map/decode/pallas_call | solution.py:431
  64.4 1.2 %collective-permute-start.21 = (bf16[216,384]{1,0:T(8,128)(2,1)S(1)}, bf16[216,384]{1,0:T(8,128)(2,1)S(1)}, u32[]{:S(2)}, u32[]{:S(2)}) collective-permute-start(bf16[216,384]{1,0:T(8,128)(2,1)S(1)} %collective-permute-done.20), channel_id=1, source_target_pairs={{0,4},{2,6},{4,0},{6,2},{8,12},{10,14},{12,8},{14,10},{16,20},{18,... | collective-permute-start | bytes 497672 | tf_op jit(solution)/shard_map/ppermute | solution.py:33
  65.5 0.1 collective-permute-start.24
  65.6 0.5 collective-permute-start.23
  66.1 1.2 %collective-permute-start.12 = (bf16[216,384]{1,0:T(8,128)(2,1)S(1)}, bf16[216,384]{1,0:T(8,128)(2,1)S(1)}, u32[]{:S(2)}, u32[]{:S(2)}) collective-permute-start(bf16[216,384]{1,0:T(8,128)(2,1)S(1)} %collective-permute-done.11), channel_id=1, source_target_pairs={{0,4},{2,6},{4,0},{6,2},{8,12},{10,14},{12,8},{14,10},{16,20},{18,... | collective-permute-start | bytes 497672 | tf_op jit(solution)/shard_map/ppermute | solution.py:33
  67.3 0.9 %collective-permute-start.14 = (bf16[216,384]{1,0:T(8,128)(2,1)S(1)}, bf16[216,384]{1,0:T(8,128)(2,1)S(1)}, u32[]{:S(2)}, u32[]{:S(2)}) collective-permute-start(bf16[216,384]{1,0:T(8,128)(2,1)S(1)} %collective-permute-done.13), channel_id=1, source_target_pairs={{0,4},{2,6},{4,0},{6,2},{8,12},{10,14},{12,8},{14,10},{16,20},{18,... | collective-permute-start | bytes 497672 | tf_op jit(solution)/shard_map/ppermute | solution.py:33
  68.1 2.6 %collective-permute-done.21 = bf16[216,384]{1,0:T(8,128)(2,1)S(1)} collective-permute-done((bf16[216,384]{1,0:T(8,128)(2,1)S(1)}, bf16[216,384]{1,0:T(8,128)(2,1)S(1)}, u32[]{:S(2)}, u32[]{:S(2)}) %collective-permute-start.21) | collective-permute-done | bytes 165920 | tf_op jit(solution)/shard_map/ppermute | solution.py:33
  70.8 0.5 collective-permute-start.17
  71.3 0.1 collective-permute-start.15
  71.4 2.9 %collective-permute-done.12 = bf16[216,384]{1,0:T(8,128)(2,1)S(1)} collective-permute-done((bf16[216,384]{1,0:T(8,128)(2,1)S(1)}, bf16[216,384]{1,0:T(8,128)(2,1)S(1)}, u32[]{:S(2)}, u32[]{:S(2)}) %collective-permute-start.12) | collective-permute-done | bytes 165920 | tf_op jit(solution)/shard_map/ppermute | solution.py:33
  74.3 2.6 %collective-permute-done.14 = bf16[216,384]{1,0:T(8,128)(2,1)S(1)} collective-permute-done((bf16[216,384]{1,0:T(8,128)(2,1)S(1)}, bf16[216,384]{1,0:T(8,128)(2,1)S(1)}, u32[]{:S(2)}, u32[]{:S(2)}) %collective-permute-start.14) | collective-permute-done | bytes 165920 | tf_op jit(solution)/shard_map/ppermute | solution.py:33
  76.9 1.0 %stack_reshape.7 = bf16[192,1,4,128]{3,2,0,1:T(4,128)(2,1)S(1)} reshape(bf16[192,512]{1,0:T(8,128)(2,1)} %decode.3) | data formatting | bytes 393216 | tf_op jit(solution)/shard_map/stack;reshape | solution.py:468
  78.0 1.0 %pad_maximum_fusion = bf16[192,2,4,128]{3,2,1,0:T(4,128)(2,1)} fusion(bf16[192,1,4,128]{3,2,1,0:T(4,128)(2,1)S(1)} %bitcast.43, bf16[192,1,4,128]{3,2,1,0:T(4,128)(2,1)S(1)} %bitcast.44), kind=kLoop, calls=%fused_computation.1 | loop fusion | flops 196608 | bytes 786432 | tf_op jit(solution)/shard_map/stack | solution.py:468
  79.1 3.0 %finish.2.refs_8_ = f32[3,9,192,384]{3,2,1,0:T(8,128)} custom-call(s32[1]{0:T(128)} %bitcast.refs_0_.me_ref, bf16[9,24,384]{2,1,0:T(8,128)(2,1)} %bitcast.45, bf16[9,24,384]{2,1,0:T(8,128)(2,1)} %bitcast.52, bf16[9,24,384]{2,1,0:T(8,128)(2,1)} %bitcast.51, bf16[9,24,384]{2,1,0:T(8,128)(2,1)} %bitcast.53, ...), custom_call_target="tpu_custom_call", output_to_operand_aliasing={{}: (9, {})} | custom-call | bytes 3981312 | tf_op jit(solution)/shard_map/finish/pallas_call | solution.py:473
  82.1 3.0 %finish.3 = f32[3,9,192,384]{3,2,1,0:T(8,128)} custom-call(s32[1]{0:T(128)} %bitcast.refs_0_.me_ref, bf16[9,24,384]{2,1,0:T(8,128)(2,1)} %bitcast.49, bf16[9,24,384]{2,1,0:T(8,128)(2,1)} %bitcast.54, bf16[9,24,384]{2,1,0:T(8,128)(2,1)} %bitcast.48, bf16[9,24,384]{2,1,0:T(8,128)(2,1)} %bitcast.55, ...), custom_call_target="tpu_custom_call", output_to_operand_aliasing={{}: (9, {})} | custom-call | bytes 3981312 | tf_op jit(solution)/shard_map/finish/pallas_call | solution.py:473
  (79 shorter events, 0.4 us)
Async XLA Ops:
  0.6 5.7 %copy-start = (bf16[2,2,64,2560]{3,2,1,0:T(8,128)(2,1)S(1)}, bf16[2,2,64,2560]{3,2,1,0:T(8,128)(2,1)}, u32[]{:S(2)}) copy-start(bf16[2,2,64,2560]{3,2,1,0:T(8,128)(2,1)} %param.6) | copy-start | bytes 3932164
  0.6 9.6 %copy-start.11 = (bf16[384,3,3,3,16]{0,4,3,2,1:T(8,128)(2,1)S(1)}, bf16[384,3,3,3,16]{0,4,3,2,1:T(8,128)(2,1)}, u32[]{:S(2)}) copy-start(bf16[384,3,3,3,16]{0,4,3,2,1:T(8,128)(2,1)} %param.9) | copy-start | bytes 995332
  0.7 9.7 %copy-start.25 = (f32[384]{0:T(512)S(1)}, f32[384]{0:T(512)}, u32[]{:S(2)}) copy-start(f32[384]{0:T(512)} %param.8) | copy-start | bytes 4612
  2.2 17.3 %collective-permute-start.2 = (bf16[4,24,1024]{2,1,0:T(8,128)(2,1)S(1)}, bf16[4,24,1024]{2,1,0:T(8,128)(2,1)S(1)}, u32[]{:S(2)}, u32[]{:S(2)}) collective-permute-start(bf16[4,24,1024]{2,1,0:T(8,128)(2,1)S(1)} %pad_maximum_fusion.1), channel_id=1, source_target_pairs={{0,16},{2,18},{4,20},{6,22},{8,24},{10,26},{12,28},{14,30},{16,0},... | collective-permute-start | bytes 589832 | tf_op jit(solution)/shard_map/ppermute | solution.py:33
  7.8 4.3 %copy-start.12 = (f32[64,256]{1,0:T(8,128)}, f32[64,256]{1,0:T(8,128)S(1)}, u32[]{:S(2)}) copy-start(f32[64,256]{1,0:T(8,128)S(1)} %convolution_bitcast_fusion.own_ref) | copy-start | bytes 196612
  7.8 4.3 %collective-permute-start = (f32[64,256]{1,0:T(8,128)S(1)}, f32[64,256]{1,0:T(8,128)S(1)}, u32[]{:S(2)}, u32[]{:S(2)}) collective-permute-start(f32[64,256]{1,0:T(8,128)S(1)} %convolution_bitcast_fusion.own_ref), channel_id=1, source_target_pairs={{0,1},{1,0},{2,3},{3,2},{4,5},{5,4},{6,7},{7,6},{8,9},{9,8},{10,11... | collective-permute-start | bytes 196616 | tf_op jit(solution)/shard_map/ppermute | solution.py:33
  14.4 5.1 %copy-start.23 = (bf16[16,1024]{1,0:T(8,128)(2,1)S(1)}, bf16[16,1024]{1,0:T(8,128)(2,1)}, u32[]{:S(2)}) copy-start(bf16[16,1024]{1,0:T(8,128)(2,1)} %unpatchify.1) | copy-start | bytes 98308
  14.4 5.0 %collective-permute-start.1 = (bf16[16,1024]{1,0:T(8,128)(2,1)}, bf16[16,1024]{1,0:T(8,128)(2,1)S(1)}, u32[]{:S(2)}, u32[]{:S(2)}) collective-permute-start(bf16[16,1024]{1,0:T(8,128)(2,1)} %unpatchify.1), channel_id=1, source_target_pairs={{0,16},{2,18},{4,20},{6,22},{8,24},{10,26},{12,28},{14,30},{16,0},... | collective-permute-start | bytes 98312 | tf_op jit(solution)/shard_map/ppermute | solution.py:33
  19.6 11.1 %copy-start.1 = (bf16[2,40,1024]{2,1,0:T(8,128)(2,1)}, bf16[2,40,1024]{2,1,0:T(8,128)(2,1)S(1)}, u32[]{:S(2)}) copy-start(bf16[2,40,1024]{2,1,0:T(8,128)(2,1)S(1)} %get-tuple-element.46.refs_4_.refs_1_.refs_2_) | copy-start | bytes 491524
  19.6 7.2 %collective-permute-start.5 = (bf16[2,40,1024]{2,1,0:T(8,128)(2,1)S(1)}, bf16[2,40,1024]{2,1,0:T(8,128)(2,1)S(1)}, u32[]{:S(2)}, u32[]{:S(2)}) collective-permute-start(bf16[2,40,1024]{2,1,0:T(8,128)(2,1)S(1)} %get-tuple-element.70), channel_id=1, source_target_pairs={{0,12},{2,14},{4,8},{6,10},{8,4},{10,6},{12,0},{14,2},{16,28},{18,... | collective-permute-start | bytes 491528 | tf_op jit(solution)/shard_map/ppermute | solution.py:33
  22.2 6.2 %collective-permute-start.3 = (bf16[2,40,1024]{2,1,0:T(8,128)(2,1)S(1)}, bf16[2,40,1024]{2,1,0:T(8,128)(2,1)S(1)}, u32[]{:S(2)}, u32[]{:S(2)}) collective-permute-start(bf16[2,40,1024]{2,1,0:T(8,128)(2,1)S(1)} %get-tuple-element.71), channel_id=1, source_target_pairs={{0,4},{2,6},{4,0},{6,2},{8,12},{10,14},{12,8},{14,10},{16,20},{18,... | collective-permute-start | bytes 491528 | tf_op jit(solution)/shard_map/ppermute | solution.py:33
  22.7 5.7 %collective-permute-start.4 = (bf16[2,40,1024]{2,1,0:T(8,128)(2,1)S(1)}, bf16[2,40,1024]{2,1,0:T(8,128)(2,1)S(1)}, u32[]{:S(2)}, u32[]{:S(2)}) collective-permute-start(bf16[2,40,1024]{2,1,0:T(8,128)(2,1)S(1)} %get-tuple-element.72), channel_id=1, source_target_pairs={{0,8},{2,10},{4,12},{6,14},{8,0},{10,2},{12,4},{14,6},{16,24},{18,... | collective-permute-start | bytes 491528 | tf_op jit(solution)/shard_map/ppermute | solution.py:33
  23.1 7.5 %collective-permute-start.6 = (bf16[2,40,1024]{2,1,0:T(8,128)(2,1)S(1)}, bf16[2,40,1024]{2,1,0:T(8,128)(2,1)S(1)}, u32[]{:S(2)}, u32[]{:S(2)}) collective-permute-start(bf16[2,40,1024]{2,1,0:T(8,128)(2,1)S(1)} %get-tuple-element.46.refs_4_.refs_1_.refs_2_), channel_id=1, source_target_pairs={{0,2},{2,0},{4,6},{6,4},{8,10},{10,8},{12,14},{14,12},{16,18},{18,... | collective-permute-start | bytes 491528 | tf_op jit(solution)/shard_map/ppermute | solution.py:33
  26.8 3.9 %copy-start.2 = (bf16[2,40,1024]{2,1,0:T(8,128)(2,1)}, bf16[2,40,1024]{2,1,0:T(8,128)(2,1)S(1)}, u32[]{:S(2)}) copy-start(bf16[2,40,1024]{2,1,0:T(8,128)(2,1)S(1)} %collective-permute-done.5.refs_7_.refs_4_.refs_5_) | copy-start | bytes 491524
  26.8 3.9 %collective-permute-start.9 = (bf16[2,40,1024]{2,1,0:T(8,128)(2,1)S(1)}, bf16[2,40,1024]{2,1,0:T(8,128)(2,1)S(1)}, u32[]{:S(2)}, u32[]{:S(2)}) collective-permute-start(bf16[2,40,1024]{2,1,0:T(8,128)(2,1)S(1)} %collective-permute-done.5.refs_7_.refs_4_.refs_5_), channel_id=1, source_target_pairs={{0,2},{2,0},{4,6},{6,4},{8,10},{10,8},{12,14},{14,12},{16,18},{18,... | collective-permute-start | bytes 491528 | tf_op jit(solution)/shard_map/ppermute | solution.py:33
  28.4 2.3 %copy-start.3 = (bf16[2,40,1024]{2,1,0:T(8,128)(2,1)}, bf16[2,40,1024]{2,1,0:T(8,128)(2,1)S(1)}, u32[]{:S(2)}) copy-start(bf16[2,40,1024]{2,1,0:T(8,128)(2,1)S(1)} %collective-permute-done.3.refs_5_.refs_2_.refs_3_) | copy-start | bytes 491524
  28.4 2.2 %collective-permute-start.7 = (bf16[2,40,1024]{2,1,0:T(8,128)(2,1)S(1)}, bf16[2,40,1024]{2,1,0:T(8,128)(2,1)S(1)}, u32[]{:S(2)}, u32[]{:S(2)}) collective-permute-start(bf16[2,40,1024]{2,1,0:T(8,128)(2,1)S(1)} %collective-permute-done.3.refs_5_.refs_2_.refs_3_), channel_id=1, source_target_pairs={{0,2},{2,0},{4,6},{6,4},{8,10},{10,8},{12,14},{14,12},{16,18},{18,... | collective-permute-start | bytes 491528 | tf_op jit(solution)/shard_map/ppermute | solution.py:33
  28.4 2.3 %copy-start.4 = (bf16[2,40,1024]{2,1,0:T(8,128)(2,1)}, bf16[2,40,1024]{2,1,0:T(8,128)(2,1)S(1)}, u32[]{:S(2)}) copy-start(bf16[2,40,1024]{2,1,0:T(8,128)(2,1)S(1)} %collective-permute-done.4.refs_6_.refs_3_.refs_4_) | copy-start | bytes 491524
  28.4 2.2 %collective-permute-start.8 = (bf16[2,40,1024]{2,1,0:T(8,128)(2,1)S(1)}, bf16[2,40,1024]{2,1,0:T(8,128)(2,1)S(1)}, u32[]{:S(2)}, u32[]{:S(2)}) collective-permute-start(bf16[2,40,1024]{2,1,0:T(8,128)(2,1)S(1)} %collective-permute-done.4.refs_6_.refs_3_.refs_4_), channel_id=1, source_target_pairs={{0,2},{2,0},{4,6},{6,4},{8,10},{10,8},{12,14},{14,12},{16,18},{18,... | collective-permute-start | bytes 491528 | tf_op jit(solution)/shard_map/ppermute | solution.py:33
  30.7 0.8 copy-start.8
  43.7 1.7 %collective-permute-start.10 = (bf16[216,384]{1,0:T(8,128)(2,1)}, bf16[216,384]{1,0:T(8,128)(2,1)S(1)}, u32[]{:S(2)}, u32[]{:S(2)}) collective-permute-start(bf16[216,384]{1,0:T(8,128)(2,1)} %get-tuple-element.37), channel_id=1, source_target_pairs={{0,2},{2,0},{4,6},{6,4},{8,10},{10,8},{12,14},{14,12},{16,18},{18,... | collective-permute-start | bytes 497672 | tf_op jit(solution)/shard_map/ppermute | solution.py:33
  46.4 17.9 %copy-start.10 = (bf16[216,384]{1,0:T(8,128)(2,1)}, bf16[216,384]{1,0:T(8,128)(2,1)S(1)}, u32[]{:S(2)}) copy-start(bf16[216,384]{1,0:T(8,128)(2,1)S(1)} %add_convert_fusion) | copy-start | bytes 497668
  46.4 20.8 %collective-permute-start.22 = (bf16[216,384]{1,0:T(8,128)(2,1)S(1)}, bf16[216,384]{1,0:T(8,128)(2,1)S(1)}, u32[]{:S(2)}, u32[]{:S(2)}) collective-permute-start(bf16[216,384]{1,0:T(8,128)(2,1)S(1)} %add_convert_fusion), channel_id=1, source_target_pairs={{0,2},{2,0},{4,6},{6,4},{8,10},{10,8},{12,14},{14,12},{16,18},{18,... | collective-permute-start | bytes 497672 | tf_op jit(solution)/shard_map/ppermute | solution.py:33
  46.6 17.7 %collective-permute-start.20 = (bf16[216,384]{1,0:T(8,128)(2,1)S(1)}, bf16[216,384]{1,0:T(8,128)(2,1)S(1)}, u32[]{:S(2)}, u32[]{:S(2)}) collective-permute-start(bf16[216,384]{1,0:T(8,128)(2,1)S(1)} %add_convert_fusion), channel_id=1, source_target_pairs={{0,8},{2,10},{4,12},{6,14},{8,0},{10,2},{12,4},{14,6},{16,24},{18,... | collective-permute-start | bytes 497672 | tf_op jit(solution)/shard_map/ppermute | solution.py:33
  47.6 18.0 %collective-permute-start.19 = (bf16[216,384]{1,0:T(8,128)(2,1)S(1)}, bf16[216,384]{1,0:T(8,128)(2,1)S(1)}, u32[]{:S(2)}, u32[]{:S(2)}) collective-permute-start(bf16[216,384]{1,0:T(8,128)(2,1)S(1)} %add_convert_fusion), channel_id=1, source_target_pairs={{0,4},{2,6},{4,0},{6,2},{8,12},{10,14},{12,8},{14,10},{16,20},{18,... | collective-permute-start | bytes 497672 | tf_op jit(solution)/shard_map/ppermute | solution.py:33
  48.4 17.1 %collective-permute-start.13 = (bf16[216,384]{1,0:T(8,128)(2,1)S(1)}, bf16[216,384]{1,0:T(8,128)(2,1)S(1)}, u32[]{:S(2)}, u32[]{:S(2)}) collective-permute-start(bf16[216,384]{1,0:T(8,128)(2,1)S(1)} %add_convert_fusion), channel_id=1, source_target_pairs={{0,24},{2,26},{4,28},{6,30},{8,16},{10,18},{12,20},{14,22},{16,8},... | collective-permute-start | bytes 497672 | tf_op jit(solution)/shard_map/ppermute | solution.py:33
  49.7 15.9 %collective-permute-start.11 = (bf16[216,384]{1,0:T(8,128)(2,1)S(1)}, bf16[216,384]{1,0:T(8,128)(2,1)S(1)}, u32[]{:S(2)}, u32[]{:S(2)}) collective-permute-start(bf16[216,384]{1,0:T(8,128)(2,1)S(1)} %add_convert_fusion), channel_id=1, source_target_pairs={{0,16},{2,18},{4,20},{6,22},{8,24},{10,26},{12,28},{14,30},{16,0},... | collective-permute-start | bytes 497672 | tf_op jit(solution)/shard_map/ppermute | solution.py:33
  56.7 21.2 %copy-start.9 = (bf16[192,512]{1,0:T(8,128)(2,1)S(1)}, bf16[192,512]{1,0:T(8,128)(2,1)}, u32[]{:S(2)}) copy-start(bf16[192,512]{1,0:T(8,128)(2,1)} %decode.2) | copy-start | bytes 589828
  64.3 14.7 %copy-start.16 = (bf16[216,384]{1,0:T(8,128)(2,1)}, bf16[216,384]{1,0:T(8,128)(2,1)S(1)}, u32[]{:S(2)}) copy-start(bf16[216,384]{1,0:T(8,128)(2,1)S(1)} %collective-permute-done.20) | copy-start | bytes 497668
  64.4 6.4 %collective-permute-start.21 = (bf16[216,384]{1,0:T(8,128)(2,1)S(1)}, bf16[216,384]{1,0:T(8,128)(2,1)S(1)}, u32[]{:S(2)}, u32[]{:S(2)}) collective-permute-start(bf16[216,384]{1,0:T(8,128)(2,1)S(1)} %collective-permute-done.20), channel_id=1, source_target_pairs={{0,4},{2,6},{4,0},{6,2},{8,12},{10,14},{12,8},{14,10},{16,20},{18,... | collective-permute-start | bytes 497672 | tf_op jit(solution)/shard_map/ppermute | solution.py:33
  65.5 16.5 %copy-start.13 = (bf16[216,384]{1,0:T(8,128)(2,1)}, bf16[216,384]{1,0:T(8,128)(2,1)S(1)}, u32[]{:S(2)}) copy-start(bf16[216,384]{1,0:T(8,128)(2,1)S(1)} %collective-permute-done.13) | copy-start | bytes 497668
  65.5 16.5 %copy-start.14 = (bf16[216,384]{1,0:T(8,128)(2,1)}, bf16[216,384]{1,0:T(8,128)(2,1)S(1)}, u32[]{:S(2)}) copy-start(bf16[216,384]{1,0:T(8,128)(2,1)S(1)} %collective-permute-done.11) | copy-start | bytes 497668
  65.5 5.2 %collective-permute-start.24 = (bf16[216,384]{1,0:T(8,128)(2,1)S(1)}, bf16[216,384]{1,0:T(8,128)(2,1)S(1)}, u32[]{:S(2)}, u32[]{:S(2)}) collective-permute-start(bf16[216,384]{1,0:T(8,128)(2,1)S(1)} %collective-permute-done.20), channel_id=1, source_target_pairs={{0,2},{2,0},{4,6},{6,4},{8,10},{10,8},{12,14},{14,12},{16,18},{18,... | collective-permute-start | bytes 497672 | tf_op jit(solution)/shard_map/ppermute | solution.py:33
  65.6 13.4 %copy-start.17 = (bf16[216,384]{1,0:T(8,128)(2,1)}, bf16[216,384]{1,0:T(8,128)(2,1)S(1)}, u32[]{:S(2)}) copy-start(bf16[216,384]{1,0:T(8,128)(2,1)S(1)} %collective-permute-done.19) | copy-start | bytes 497668
  65.6 5.6 %collective-permute-start.23 = (bf16[216,384]{1,0:T(8,128)(2,1)S(1)}, bf16[216,384]{1,0:T(8,128)(2,1)S(1)}, u32[]{:S(2)}, u32[]{:S(2)}) collective-permute-start(bf16[216,384]{1,0:T(8,128)(2,1)S(1)} %collective-permute-done.19), channel_id=1, source_target_pairs={{0,2},{2,0},{4,6},{6,4},{8,10},{10,8},{12,14},{14,12},{16,18},{18,... | collective-permute-start | bytes 497672 | tf_op jit(solution)/shard_map/ppermute | solution.py:33
  66.1 8.2 %collective-permute-start.12 = (bf16[216,384]{1,0:T(8,128)(2,1)S(1)}, bf16[216,384]{1,0:T(8,128)(2,1)S(1)}, u32[]{:S(2)}, u32[]{:S(2)}) collective-permute-start(bf16[216,384]{1,0:T(8,128)(2,1)S(1)} %collective-permute-done.11), channel_id=1, source_target_pairs={{0,4},{2,6},{4,0},{6,2},{8,12},{10,14},{12,8},{14,10},{16,20},{18,... | collective-permute-start | bytes 497672 | tf_op jit(solution)/shard_map/ppermute | solution.py:33
  67.3 11.8 %copy-start.15 = (bf16[216,384]{1,0:T(8,128)(2,1)}, bf16[216,384]{1,0:T(8,128)(2,1)S(1)}, u32[]{:S(2)}) copy-start(bf16[216,384]{1,0:T(8,128)(2,1)S(1)} %collective-permute-done.22) | copy-start | bytes 497668
  67.3 9.6 %collective-permute-start.14 = (bf16[216,384]{1,0:T(8,128)(2,1)S(1)}, bf16[216,384]{1,0:T(8,128)(2,1)S(1)}, u32[]{:S(2)}, u32[]{:S(2)}) collective-permute-start(bf16[216,384]{1,0:T(8,128)(2,1)S(1)} %collective-permute-done.13), channel_id=1, source_target_pairs={{0,4},{2,6},{4,0},{6,2},{8,12},{10,14},{12,8},{14,10},{16,20},{18,... | collective-permute-start | bytes 497672 | tf_op jit(solution)/shard_map/ppermute | solution.py:33
  70.7 8.3 %copy-start.18 = (bf16[216,384]{1,0:T(8,128)(2,1)}, bf16[216,384]{1,0:T(8,128)(2,1)S(1)}, u32[]{:S(2)}) copy-start(bf16[216,384]{1,0:T(8,128)(2,1)S(1)} %collective-permute-done.21) | copy-start | bytes 497668
  70.7 8.3 %collective-permute-start.25 = (bf16[216,384]{1,0:T(8,128)(2,1)S(1)}, bf16[216,384]{1,0:T(8,128)(2,1)}, u32[]{:S(2)}, u32[]{:S(2)}) collective-permute-start(bf16[216,384]{1,0:T(8,128)(2,1)S(1)} %collective-permute-done.21), channel_id=1, source_target_pairs={{0,2},{2,0},{4,6},{6,4},{8,10},{10,8},{12,14},{14,12},{16,18},{18,... | collective-permute-start | bytes 497672 | tf_op jit(solution)/shard_map/ppermute | solution.py:33
  70.8 8.3 %copy-start.21 = (bf16[216,384]{1,0:T(8,128)(2,1)}, bf16[216,384]{1,0:T(8,128)(2,1)S(1)}, u32[]{:S(2)}) copy-start(bf16[216,384]{1,0:T(8,128)(2,1)S(1)} %collective-permute-done.24) | copy-start | bytes 497668
  70.8 11.3 %collective-permute-start.17 = (bf16[216,384]{1,0:T(8,128)(2,1)S(1)}, bf16[216,384]{1,0:T(8,128)(2,1)}, u32[]{:S(2)}, u32[]{:S(2)}) collective-permute-start(bf16[216,384]{1,0:T(8,128)(2,1)S(1)} %collective-permute-done.13), channel_id=1, source_target_pairs={{0,2},{2,0},{4,6},{6,4},{8,10},{10,8},{12,14},{14,12},{16,18},{18,... | collective-permute-start | bytes 497672 | tf_op jit(solution)/shard_map/ppermute | solution.py:33
  71.3 5.6 %copy-start.22 = (bf16[216,384]{1,0:T(8,128)(2,1)}, bf16[216,384]{1,0:T(8,128)(2,1)S(1)}, u32[]{:S(2)}) copy-start(bf16[216,384]{1,0:T(8,128)(2,1)S(1)} %collective-permute-done.23) | copy-start | bytes 497668
  71.3 10.8 %collective-permute-start.15 = (bf16[216,384]{1,0:T(8,128)(2,1)S(1)}, bf16[216,384]{1,0:T(8,128)(2,1)}, u32[]{:S(2)}, u32[]{:S(2)}) collective-permute-start(bf16[216,384]{1,0:T(8,128)(2,1)S(1)} %collective-permute-done.11), channel_id=1, source_target_pairs={{0,2},{2,0},{4,6},{6,4},{8,10},{10,8},{12,14},{14,12},{16,18},{18,... | collective-permute-start | bytes 497672 | tf_op jit(solution)/shard_map/ppermute | solution.py:33
  74.3 7.8 %copy-start.19 = (bf16[216,384]{1,0:T(8,128)(2,1)}, bf16[216,384]{1,0:T(8,128)(2,1)S(1)}, u32[]{:S(2)}) copy-start(bf16[216,384]{1,0:T(8,128)(2,1)S(1)} %collective-permute-done.12) | copy-start | bytes 497668
  74.3 7.8 %collective-permute-start.16 = (bf16[216,384]{1,0:T(8,128)(2,1)S(1)}, bf16[216,384]{1,0:T(8,128)(2,1)}, u32[]{:S(2)}, u32[]{:S(2)}) collective-permute-start(bf16[216,384]{1,0:T(8,128)(2,1)S(1)} %collective-permute-done.12), channel_id=1, source_target_pairs={{0,2},{2,0},{4,6},{6,4},{8,10},{10,8},{12,14},{14,12},{16,18},{18,... | collective-permute-start | bytes 497672 | tf_op jit(solution)/shard_map/ppermute | solution.py:33
  76.9 5.2 %copy-start.20 = (bf16[216,384]{1,0:T(8,128)(2,1)}, bf16[216,384]{1,0:T(8,128)(2,1)S(1)}, u32[]{:S(2)}) copy-start(bf16[216,384]{1,0:T(8,128)(2,1)S(1)} %collective-permute-done.14) | copy-start | bytes 497668
  76.9 5.2 %collective-permute-start.18 = (bf16[216,384]{1,0:T(8,128)(2,1)S(1)}, bf16[216,384]{1,0:T(8,128)(2,1)}, u32[]{:S(2)}, u32[]{:S(2)}) collective-permute-start(bf16[216,384]{1,0:T(8,128)(2,1)S(1)} %collective-permute-done.14), channel_id=1, source_target_pairs={{0,2},{2,0},{4,6},{6,4},{8,10},{10,8},{12,14},{14,12},{16,18},{18,... | collective-permute-start | bytes 497672 | tf_op jit(solution)/shard_map/ppermute | solution.py:33
  (4 other events, 2.8 us)

commit v5 on v4

--- a/solution.py
+++ b/solution.py
@@ -122,6 +122,14 @@
             at = pl.multiple_of((first + row_tap) * LANES, LANES)
             pieces.append(stack_ref[source, :, pl.ds(at, count * LANES)])
     return dot(weight_ref[...], jnp.concatenate(pieces, axis=0))
+
+
+def load_entry(entry_ref, gain_ref, weight_refs, wide_gain):
+    for weight_ref in weight_refs:
+        depth = weight_ref.shape[1]
+        start = entry_ref.shape[0] - depth
+        weight_ref[...] = jnp.transpose(entry_ref[start:, :].astype(F32)).astype(BF16)
+    wide_gain[...] = jnp.transpose(jnp.broadcast_to(0.5 * gain_ref[...], wide_gain.shape[::-1]))
 
 
 def activate_rows(hidden_ref, gain_ref, act_ref, base, top_row, count, height):
@@ -175,12 +183,12 @@
 
 
 def gradient_kernel(frames, rows, slabs, masks, real_rows, pad_channels, *refs):
-    me_ref, gain_ref = refs[:2]
-    refs = refs[2:]
-    weight_refs, refs = refs[:frames], refs[frames:]
+    me_ref, gain_ref, entry_ref = refs[:3]
+    refs = refs[3:]
     piece_refs, refs = refs[: len(masks)], refs[len(masks) :]
     keep_ref, send_ref, slots, stack_ref, flat_ref, cot_ref = refs[:6]
-    hid_a, hid_b, act_a, act_b, sum_ref, wide_gain, sems = refs[6:]
+    hid_a, hid_b, act_a, act_b, sum_ref, wide_gain, sems = refs[6:13]
+    weight_refs = refs[13:]
     copies = fetch(piece_refs, masks, slots, sems)
     me = me_ref[0]
     core = me & 1
@@ -195,7 +203,7 @@
     width = count * LANES
     hidden = (hid_a, hid_b)
     acts = (act_a, act_b)
-    wide_gain[...] = jnp.broadcast_to(0.5 * gain_ref[...], wide_gain.shape)
+    load_entry(entry_ref, gain_ref, weight_refs, wide_gain)
     sum_ref[...] = jnp.zeros_like(sum_ref)
     for copy in copies:
         copy.wait()
@@ -233,41 +241,42 @@
     send_ref[...] = sum_ref[pl.ds(send_at, padded), :][:real_rows].astype(BF16)
 
 
-def decode_kernel(frame, frames, rows, slabs, masks, me_ref, gain_ref, conv_hbm, *refs):
-    first_source = max(0, frame - 2)
-    sources = range(first_source, frame + 1)
-    weight_refs, refs = refs[: len(sources)], refs[len(sources) :]
+def decode_kernel(frames, rows, slabs, masks, me_ref, gain_ref, entry_ref, conv_hbm, *refs):
     piece_refs, refs = refs[: len(masks)], refs[len(masks) :]
-    out_ref, slots, stack_ref, hid_ref, flat_ref, act_ref, wide_gain, conv_ref, sems, sem = refs
-    taps = conv_ref.shape[0]
-    load = pltpu.make_async_copy(conv_hbm.at[pl.ds(27 - taps, taps)], conv_ref, sem)
+    out_ref, slots, stack_ref, hid_ref, flat_ref, act_ref, wide_gain, conv_ref, sems, sem = refs[:10]
+    weight_refs = refs[10:]
+    live = conv_ref.shape[0] // 9
+    load = pltpu.make_async_copy(conv_hbm.at[pl.ds((3 - live) * 9, live * 9)], conv_ref, sem)
     load.start()
     copies = fetch(piece_refs, masks, slots, sems)
     me = me_ref[0]
     height = slabs * rows
-    wide_gain[...] = jnp.broadcast_to(0.5 * gain_ref[...], wide_gain.shape)
+    load_entry(entry_ref, gain_ref, weight_refs, wide_gain)
     for copy in copies:
         copy.wait()
     place_latent(slots, stack_ref, me, me, 1, frames, rows, slabs)
     ext = rows + 2
-    kernels = []
-    inputs = []
-    for position, source in enumerate(sources):
-        hid_ref[...] = hidden_rows(stack_ref, weight_refs[position], source, 0, ext)
+    for frame in range(frames):
+        hid_ref[...] = hidden_rows(stack_ref, weight_refs[frame], frame, 0, ext)
         activate_rows(hid_ref, wide_gain, flat_ref, 0, me * rows - 1, ext, height)
         for row in range(ext):
             tile = flat_ref[:, row * LANES : (row + 1) * LANES].astype(F32)
             for tap in range(3):
-                act_ref[position, tap, :, row * LANES : (row + 1) * LANES] = shifted(tile, tap).astype(BF16)
+                act_ref[frame, tap, :, row * LANES : (row + 1) * LANES] = shifted(tile, tap).astype(BF16)
     load.wait()
-    for position, source in enumerate(sources):
-        plane = position * 9
-        for row_tap in range(3):
-            for col_tap in range(3):
-                kernels.append(conv_ref[plane + row_tap * 3 + col_tap])
-                inputs.append(act_ref[position, col_tap, :, row_tap * LANES : (row_tap + rows) * LANES])
-    total = dot(jnp.concatenate(kernels, axis=1), jnp.concatenate(inputs, axis=0))
-    out_ref[...] = total.astype(BF16)
+    for frame in range(frames):
+        kernels = []
+        inputs = []
+        for depth in range(max(0, 2 - frame), 3):
+            for row_tap in range(3):
+                for col_tap in range(3):
+                    kernels.append(conv_ref[(depth - (3 - live)) * 9 + row_tap * 3 + col_tap])
+                    inputs.append(
+                        act_ref[frame + depth - 2, col_tap, :, row_tap * LANES : (row_tap + rows) * LANES]
+                    )
+        total = dot(jnp.concatenate(kernels, axis=1), jnp.concatenate(inputs, axis=0))
+        for row in range(rows):
+            out_ref[:, frame, row, :] = total[:, row * LANES : (row + 1) * LANES].astype(BF16)
 
 
 def blank_kernel(blank, out_hbm, zero_ref, sems):
@@ -352,10 +361,11 @@
         if step > 1:
             partial_sum = partial_sum + other
         step //= 2
-    entry = entry_weight.reshape(channels, 3, 9 * latent_width)
-    entries = [entry[:, max(0, 2 - f) :].reshape(channels, -1) for f in range(frames)]
-    gain = norm_gain.reshape(channels, 1)
-    other, gain, *entries = lax.optimization_barrier((other, gain, *entries))
+    entry = entry_weight.transpose(1, 2, 3, 4, 0).reshape(27 * latent_width, channels)
+    gain = norm_gain.reshape(1, channels)
+    weights = [
+        pltpu.VMEM((channels, min(3, f + 1) * 9 * latent_width), BF16) for f in range(frames)
+    ]
     latent = pl.pallas_call(
         functools.partial(unpatchify_kernel, frames, tok_rows, tok_cols),
         out_shape=jax.ShapeDtypeStruct((latent_width, frames * rows * width), BF16),
@@ -400,7 +410,7 @@
             jax.ShapeDtypeStruct((real_rows, channels), F32),
             jax.ShapeDtypeStruct((real_rows, channels), BF16),
         ),
-        in_specs=[smem(), vmem()] + [vmem()] * frames + [hbm] * len(pieces),
+        in_specs=[smem(), vmem(), vmem()] + [hbm] * len(pieces),
         out_specs=(vmem(), vmem()),
         scratch_shapes=[
             pltpu.VMEM(slot_shape, BF16),
@@ -414,10 +424,11 @@
             pltpu.VMEM((live * padded, channels), F32),
             pltpu.VMEM((channels, LANES), F32),
             pltpu.SemaphoreType.DMA((slabs,)),
-        ],
+        ]
+        + weights,
         compiler_params=params(),
         name="gradient",
-    )(me, gain, *entries, *pieces)
+    )(me, gain, entry, *pieces)
     block = (keep + xor_permute(send, "seq", 1).astype(F32)).astype(BF16)
 
     columns = [m for m in range(4, slabs, 4)]
@@ -425,47 +436,34 @@
     beside = xor_permute(block, "seq", 2)
     conv = conv_weight.transpose(1, 2, 3, 0, 4).reshape(27, out_channels, channels)
 
-    def decode(frame, pieces):
-        first = max(0, frame - 2)
-        count = frame + 1 - first
-        return pl.pallas_call(
-            functools.partial(decode_kernel, frame, frames, rows, slabs, masks),
-            out_shape=jax.ShapeDtypeStruct((out_channels, rows * width), BF16),
-            in_specs=[smem(), vmem(), hbm] + [vmem()] * count + [hbm] * len(pieces),
-            out_specs=vmem(),
-            scratch_shapes=[
-                pltpu.VMEM(slot_shape, BF16),
-                pltpu.VMEM((frames, 3 * latent_width, (rows + 4) * width), BF16),
-                pltpu.VMEM((channels, (rows + 2) * width), F32),
-                pltpu.VMEM((channels, (rows + 2) * width), BF16),
-                pltpu.VMEM((count, 3, channels, (rows + 2) * width), BF16),
-                pltpu.VMEM((channels, LANES), F32),
-                pltpu.VMEM((count * 9, out_channels, channels), BF16),
-                pltpu.SemaphoreType.DMA((slabs,)),
-                pltpu.SemaphoreType.DMA(()),
-            ],
-            compiler_params=params(),
-            cost_estimate=cost(
-                count * 18 * out_channels * channels * rows * width,
-                count * 18 * out_channels * channels,
-            ),
-            name="decode",
-        )(me, gain, conv, *entries[first : frame + 1], *pieces)
-
-    gate = block
-    decoded = []
-    across = []
-    for frame in range(frames):
-        held = lax.optimization_barrier((gate, *pieces))
-        result = decode(frame, held[1:])
-        decoded.append(result)
-        gate = result
-        ready = columns[frame:] if frame == frames - 1 else columns[frame : frame + 1]
-        for mask in ready:
-            position = columns.index(mask)
-            gated = lax.optimization_barrier((direct[position], result))[0]
-            across.append(xor_permute(gated, "seq", 2))
-    decoded = jnp.stack([d.reshape(out_channels, rows, width) for d in decoded], axis=1)
+    held = lax.optimization_barrier((block, *pieces))[1:]
+    decoded = pl.pallas_call(
+        functools.partial(decode_kernel, frames, rows, slabs, masks),
+        out_shape=jax.ShapeDtypeStruct((out_channels, frames, rows, width), BF16),
+        in_specs=[smem(), vmem(), vmem(), hbm] + [hbm] * len(pieces),
+        out_specs=vmem(),
+        scratch_shapes=[
+            pltpu.VMEM(slot_shape, BF16),
+            pltpu.VMEM((frames, 3 * latent_width, (rows + 4) * width), BF16),
+            pltpu.VMEM((channels, (rows + 2) * width), F32),
+            pltpu.VMEM((channels, (rows + 2) * width), BF16),
+            pltpu.VMEM((frames, 3, channels, (rows + 2) * width), BF16),
+            pltpu.VMEM((channels, LANES), F32),
+            pltpu.VMEM((live * 9, out_channels, channels), BF16),
+            pltpu.SemaphoreType.DMA((slabs,)),
+            pltpu.SemaphoreType.DMA(()),
+        ]
+        + weights,
+        compiler_params=params(),
+        cost_estimate=cost(
+            live * 18 * frames * out_channels * channels * rows * width,
+            live * 18 * out_channels * channels,
+        ),
+        name="decode",
+    )(me, gain, entry, conv, *held)
+    gated = lax.optimization_barrier((decoded, *direct))
+    decoded, direct = gated[0], list(gated[1:])
+    across = [xor_permute(piece, "seq", 2) for piece in direct]
 
     shape = (9, pad_channels, channels)
 
@@ -485,14 +483,19 @@
             name="finish",
         )(me, *[p.reshape(shape) for p in parts], grad)
 
-    groups = [[(block, 0), (beside, 2)], []]
-    for position, mask in enumerate(columns):
-        groups[0 if position == 0 else 1] += [(direct[position], mask), (across[position], mask ^ 2)]
-    for group in groups:
+    def both_cores(group):
         parts = [p for p, _ in group] + [xor_permute(p, "seq", 1) for p, _ in group]
-        sources = [m for _, m in group] + [m ^ 1 for _, m in group]
-        if parts:
-            grad = finish(parts, sources, grad)
+        return parts, [m for _, m in group] + [m ^ 1 for _, m in group]
+
+    early = [(block, 0), (beside, 2), (direct[0], columns[0]), (across[0], columns[0] ^ 2)]
+    grad = finish(*both_cores(early), grad)
+    if columns[1:]:
+        gated = lax.optimization_barrier((grad, decoded, *across[1:]))
+        grad, decoded, across[1:] = gated[0], gated[1], list(gated[2:])
+        late = []
+        for position, mask in enumerate(columns[1:]):
+            late += [(direct[position + 1], mask), (across[position + 1], mask ^ 2)]
+        grad = finish(*both_cores(late), grad)
     if pad_channels != chip_channels:
         grad = grad.reshape(27, chips, pad_channels, channels)[:, :, :chip_channels]
     grad = grad.reshape(3, 3, 3, out_channels, channels).transpose(3, 0, 1, 2, 4)

time: 85.8 us -> 83.6 us (0.974)
  waiting for transfers between devices: 19.3 us -> 23.9 us
  Pallas kernels: 34.7 us -> 30.2 us
  local copies, waits for them, and re-layouts: 7.45 us -> 4.63 us
  starting transfers between devices: 18.9 us -> 20.3 us
  other arithmetic: 2.13 us -> 1.1 us
    ppermute x26, waiting for transfers between devices: 19.3 us -> 23.9 us  [xor_permute(): lax.ppermute(x, axis, [(i, i ^ mask) for i in range(lax.axis_size(axis))])]
    pallas_call x2 -> x1, Pallas kernels: 13.2 us -> 8.98 us  [per_device(): pl.pallas_call(functools.partial(decode_kernel, frames, rows, slabs, mask...]
    optimization_barrier x2 -> x0, local copies, waits for them, and re-layouts: 1.71 us -> none  [per_device(): other, gain, *entries = lax.optimization_barrier((other, gain, *entries))]
    ppermute x26, starting transfers between devices: 18.9 us -> 20.3 us  [xor_permute(): lax.ppermute(x, axis, [(i, i ^ mask) for i in range(lax.axis_size(axis))])]
    another operation x2 -> x0, local copies, waits for them, and re-layouts: 1.09 us -> none  [per_device(): jnp.stack([d.reshape(out_channels, rows, width) for d in decoded], axis=1)]
    another operation x1 -> x0, other arithmetic: 1.03 us -> none  [per_device(): jnp.stack([d.reshape(out_channels, rows, width) for d in decoded], axis=1)]
    slice x2 -> x0, local copies, waits for them, and re-layouts: 0.93 us -> none  [per_device(): entry[:, max(0, 2 - f):].reshape(channels, -1)]
    unnamed x53 -> x58, local copies, waits for them, and re-layouts: 2.29 us -> 2.61 us
  transfers between devices with their start and end apart: 26 -> 26, of which waited for: 8 -> 12; matrix products, arithmetic and copies ran while one was open for 8% -> 3% of each run, Pallas kernels for 23% -> 18%
where the time goes in v5:
time: 83.6 us; the launch traced here: 82.8 us
  Pallas kernels  30.2 us (36%)
  waiting for transfers between devices  23.9 us (29%)
  starting transfers between devices  20.3 us (24%)
  local copies, waits for them, and re-layouts  4.63 us (6%)
  matrix products  1.48 us (2%)
  between operations  1.2 us (1%)
  other arithmetic  1.1 us (1%)
    ppermute x26, waiting for transfers between devices, xor_permute(): lax.ppermute(x, axis, [(i, i ^ mask) for i in range(lax.axis_size(axis))])  23.9 us
    ppermute x26, starting transfers between devices, xor_permute(): lax.ppermute(x, axis, [(i, i ^ mask) for i in range(lax.axis_size(axis))])  20.3 us
    pallas_call x1, Pallas kernels, per_device(): pl.pallas_call(functools.partial(gradient_kernel, frames, rows, slabs, ma...  12 us
    pallas_call x1, Pallas kernels, per_device(): pl.pallas_call(functools.partial(decode_kernel, frames, rows, slabs, mask...  8.98 us
    pallas_call x2, Pallas kernels, finish(): pl.pallas_call(functools.partial(finish_kernel, sources), out_shape=jax.S...  5.95 us
    unnamed x58, local copies, waits for them, and re-layouts  2.61 us
  transfers between devices with their start and end apart: 26, of which 12 were waited for; matrix products, arithmetic and copies ran while one was open for 3% of the time, Pallas kernels for 18%

profile of v5, /device:TPU:0, one launch (start us, length us, event | category | flops | bytes accessed | tf_op | source)
XLA Modules:
  0.0 82.8 jit_solution(10499076200715441794)
XLA Ops:
  0.7 1.4 %reshape.76 = bf16[8,24,1024]{2,1,0:T(8,128)(2,1)S(1)} reshape(bf16[192,2,4,128]{3,2,1,0:T(4,128)(2,1)} %param.11) | data formatting | bytes 786432 | tf_op jit(solution)/shard_map/reshape | solution.py:338
  2.2 4.1 %collective-permute-start.2 = (bf16[4,24,1024]{2,1,0:T(8,128)(2,1)S(1)}, bf16[4,24,1024]{2,1,0:T(8,128)(2,1)S(1)}, u32[]{:S(2)}, u32[]{:S(2)}) collective-permute-start(bf16[4,24,1024]{2,1,0:T(8,128)(2,1)S(1)} %pad_maximum_fusion), channel_id=1, source_target_pairs={{0,16},{2,18},{4,20},{6,22},{8,24},{10,26},{12,28},{14,30},{16,0},... | collective-permute-start | bytes 589832 | tf_op jit(solution)/shard_map/ppermute | solution.py:33
  6.3 1.5 %convolution_bitcast_fusion.own_ref = f32[64,256]{1,0:T(8,128)S(1)} fusion(bf16[256,2560]{1,0:T(8,128)(2,1)S(1)} %bitcast.33, bf16[2560,64]{0,1:T(8,128)(2,1)} %param.7), kind=kOutput, calls=%fused_computation | convolution fusion | flops 83886080 | bytes 1703936 | tf_op jit(solution)/shard_map/dot_general | solution.py:354
  7.8 1.6 %collective-permute-start = (f32[64,256]{1,0:T(8,128)S(1)}, f32[64,256]{1,0:T(8,128)S(1)}, u32[]{:S(2)}, u32[]{:S(2)}) collective-permute-start(f32[64,256]{1,0:T(8,128)S(1)} %convolution_bitcast_fusion.own_ref), channel_id=1, source_target_pairs={{0,1},{1,0},{2,3},{3,2},{4,5},{5,4},{6,7},{7,6},{8,9},{9,8},{10,11... | collective-permute-start | bytes 196616 | tf_op jit(solution)/shard_map/ppermute | solution.py:33
  9.3 2.8 %collective-permute-done.other_ref = f32[64,256]{1,0:T(8,128)S(1)} collective-permute-done((f32[64,256]{1,0:T(8,128)S(1)}, f32[64,256]{1,0:T(8,128)S(1)}, u32[]{:S(2)}, u32[]{:S(2)}) %collective-permute-start) | collective-permute-done | bytes 65568 | tf_op jit(solution)/shard_map/ppermute | solution.py:33
  12.1 0.6 copy-done.27
  12.7 1.7 %unpatchify.1 = bf16[16,1024]{1,0:T(8,128)(2,1)} custom-call(f32[64,256]{1,0:T(8,128)} %copy-done.3, f32[64,256]{1,0:T(8,128)} %copy-done.27), custom_call_target="tpu_custom_call" | custom-call | tf_op jit(solution)/shard_map/unpatchify/pallas_call | solution.py:369
  14.4 1.6 %blank.1.refs_8_ = f32[3,9,192,384]{3,2,1,0:T(8,128)} custom-call(), custom_call_target="tpu_custom_call" | custom-call | bytes 2654208 | tf_op jit(solution)/shard_map/blank/pallas_call | solution.py:381
  16.0 3.4 %collective-permute-done.1 = bf16[16,1024]{1,0:T(8,128)(2,1)S(1)} collective-permute-done((bf16[16,1024]{1,0:T(8,128)(2,1)}, bf16[16,1024]{1,0:T(8,128)(2,1)S(1)}, u32[]{:S(2)}, u32[]{:S(2)}) %collective-permute-start.1) | collective-permute-done | bytes 32800 | tf_op jit(solution)/shard_map/ppermute | solution.py:33
  19.5 0.1 maximum_maximum_fusion.3
  19.5 1.6 %collective-permute-start.3 = (bf16[2,40,1024]{2,1,0:T(8,128)(2,1)S(1)}, bf16[2,40,1024]{2,1,0:T(8,128)(2,1)S(1)}, u32[]{:S(2)}, u32[]{:S(2)}) collective-permute-start(bf16[2,40,1024]{2,1,0:T(8,128)(2,1)S(1)} %get-tuple-element.57), channel_id=1, source_target_pairs={{0,4},{2,6},{4,0},{6,2},{8,12},{10,14},{12,8},{14,10},{16,20},{18,... | collective-permute-start | bytes 491528 | tf_op jit(solution)/shard_map/ppermute | solution.py:33
  21.1 1.6 %collective-permute-start.4 = (bf16[2,40,1024]{2,1,0:T(8,128)(2,1)S(1)}, bf16[2,40,1024]{2,1,0:T(8,128)(2,1)S(1)}, u32[]{:S(2)}, u32[]{:S(2)}) collective-permute-start(bf16[2,40,1024]{2,1,0:T(8,128)(2,1)S(1)} %get-tuple-element.58), channel_id=1, source_target_pairs={{0,8},{2,10},{4,12},{6,14},{8,0},{10,2},{12,4},{14,6},{16,24},{18,... | collective-permute-start | bytes 491528 | tf_op jit(solution)/shard_map/ppermute | solution.py:33
  22.7 0.4 collective-permute-start.5
  23.1 3.6 %collective-permute-done.3.refs_4_.refs_1_ = bf16[2,40,1024]{2,1,0:T(8,128)(2,1)S(1)} collective-permute-done((bf16[2,40,1024]{2,1,0:T(8,128)(2,1)S(1)}, bf16[2,40,1024]{2,1,0:T(8,128)(2,1)S(1)}, u32[]{:S(2)}, u32[]{:S(2)}) %collective-permute-start.3) | collective-permute-done | bytes 163872 | tf_op jit(solution)/shard_map/ppermute | solution.py:33
  26.7 0.5 collective-permute-start.8
  27.2 1.7 %collective-permute-done.5.refs_6_.refs_3_ = bf16[2,40,1024]{2,1,0:T(8,128)(2,1)S(1)} collective-permute-done((bf16[2,40,1024]{2,1,0:T(8,128)(2,1)S(1)}, bf16[2,40,1024]{2,1,0:T(8,128)(2,1)S(1)}, u32[]{:S(2)}, u32[]{:S(2)}) %collective-permute-start.5) | collective-permute-done | bytes 163872 | tf_op jit(solution)/shard_map/ppermute | solution.py:33
  28.9 0.6 reshape.74.refs_1_.gain_ref
  29.6 0.7 collective-permute-done.9.refs_10_.refs_7_
  30.4 0.6 copy-done.25
  31.0 12.0 %gradient.1 = (f32[216,384]{1,0:T(8,128)}, bf16[216,384]{1,0:T(8,128)(2,1)}) custom-call(s32[1]{0:T(128)} %bitcast.refs_0_.me_ref, f32[1,384]{1,0:T(1,128)} %reshape.74.refs_1_.gain_ref, bf16[432,384]{1,0:T(8,128)(2,1)} %bitcast.36, bf16[2,40,1024]{2,1,0:T(8,128)(2,1)} %copy-done.2, bf16[2,40,1024]{2,1,0:T(8,128)(2,1)} %copy-done.19, ...), custom_call_target="tpu_custom_call" | custom-call | tf_op jit(solution)/shard_map/gradient/pallas_call | solution.py:407
  43.0 0.2 collective-permute-start.10
  43.2 1.5 %collective-permute-done.10 = bf16[216,384]{1,0:T(8,128)(2,1)S(1)} collective-permute-done((bf16[216,384]{1,0:T(8,128)(2,1)}, bf16[216,384]{1,0:T(8,128)(2,1)S(1)}, u32[]{:S(2)}, u32[]{:S(2)}) %collective-permute-start.10) | collective-permute-done | bytes 165920 | tf_op jit(solution)/shard_map/ppermute | solution.py:33
  44.7 1.0 %add_convert_fusion = bf16[216,384]{1,0:T(8,128)(2,1)S(1)} fusion(f32[216,384]{1,0:T(8,128)} %get-tuple-element.25, bf16[216,384]{1,0:T(8,128)(2,1)S(1)} %collective-permute-done.10), kind=kLoop, calls=%fused_computation.1 | loop fusion | flops 248832 | bytes 663552 | tf_op jit(solution)/shard_map/convert_element_type | solution.py:432
  45.7 0.9 %collective-permute-start.12 = (bf16[216,384]{1,0:T(8,128)(2,1)S(1)}, bf16[216,384]{1,0:T(8,128)(2,1)S(1)}, u32[]{:S(2)}, u32[]{:S(2)}) collective-permute-start(bf16[216,384]{1,0:T(8,128)(2,1)S(1)} %add_convert_fusion), channel_id=1, source_target_pairs={{0,8},{2,10},{4,12},{6,14},{8,0},{10,2},{12,4},{14,6},{16,24},{18,... | collective-permute-start | bytes 497672 | tf_op jit(solution)/shard_map/ppermute | solution.py:33
  46.6 1.3 %collective-permute-start.13 = (bf16[216,384]{1,0:T(8,128)(2,1)S(1)}, bf16[216,384]{1,0:T(8,128)(2,1)S(1)}, u32[]{:S(2)}, u32[]{:S(2)}) collective-permute-start(bf16[216,384]{1,0:T(8,128)(2,1)S(1)} %add_convert_fusion), channel_id=1, source_target_pairs={{0,16},{2,18},{4,20},{6,22},{8,24},{10,26},{12,28},{14,30},{16,0},... | collective-permute-start | bytes 497672 | tf_op jit(solution)/shard_map/ppermute | solution.py:33
  47.9 2.3 %collective-permute-start.14 = (bf16[216,384]{1,0:T(8,128)(2,1)S(1)}, bf16[216,384]{1,0:T(8,128)(2,1)S(1)}, u32[]{:S(2)}, u32[]{:S(2)}) collective-permute-start(bf16[216,384]{1,0:T(8,128)(2,1)S(1)} %add_convert_fusion), channel_id=1, source_target_pairs={{0,24},{2,26},{4,28},{6,30},{8,16},{10,18},{12,20},{14,22},{16,8},... | collective-permute-start | bytes 497672 | tf_op jit(solution)/shard_map/ppermute | solution.py:33
  50.2 0.7 collective-permute-start.11
  50.9 9.0 %decode.1 = bf16[192,2,4,128]{3,2,1,0:T(4,128)(2,1)} custom-call(s32[1]{0:T(128)} %bitcast.refs_0_.me_ref, f32[1,384]{1,0:T(1,128)} %reshape.74.refs_1_.gain_ref, bf16[432,384]{1,0:T(8,128)(2,1)} %bitcast.37, bf16[27,192,384]{2,1,0:T(8,128)(2,1)} %bitcast.55, bf16[2,40,1024]{2,1,0:T(8,128)(2,1)} %copy-done.2, bf16[2,40,1024]{2,1,0:T(8,128)(2,1)} %copy-done.19, ...), custom_call_target="tpu_custom_call" | custom-call | flops 2717908992 | bytes 2654208 | tf_op jit(solution)/shard_map/decode/pallas_call | solution.py:440
  59.9 1.8 %collective-permute-done.13 = bf16[216,384]{1,0:T(8,128)(2,1)S(1)} collective-permute-done((bf16[216,384]{1,0:T(8,128)(2,1)S(1)}, bf16[216,384]{1,0:T(8,128)(2,1)S(1)}, u32[]{:S(2)}, u32[]{:S(2)}) %collective-permute-start.13) | collective-permute-done | bytes 165920 | tf_op jit(solution)/shard_map/ppermute | solution.py:33
  61.8 1.6 %collective-permute-start.15 = (bf16[216,384]{1,0:T(8,128)(2,1)S(1)}, bf16[216,384]{1,0:T(8,128)(2,1)S(1)}, u32[]{:S(2)}, u32[]{:S(2)}) collective-permute-start(bf16[216,384]{1,0:T(8,128)(2,1)S(1)} %collective-permute-done.12), channel_id=1, source_target_pairs={{0,4},{2,6},{4,0},{6,2},{8,12},{10,14},{12,8},{14,10},{16,20},{18,... | collective-permute-start | bytes 497672 | tf_op jit(solution)/shard_map/ppermute | solution.py:33
  63.3 0.5 collective-permute-start.18
  63.9 0.1 collective-permute-start.17
  63.9 3.2 %collective-permute-done.15 = bf16[216,384]{1,0:T(8,128)(2,1)S(1)} collective-permute-done((bf16[216,384]{1,0:T(8,128)(2,1)S(1)}, bf16[216,384]{1,0:T(8,128)(2,1)S(1)}, u32[]{:S(2)}, u32[]{:S(2)}) %collective-permute-start.15) | collective-permute-done | bytes 165920 | tf_op jit(solution)/shard_map/ppermute | solution.py:33
  67.2 1.5 %collective-permute-start.20 = (bf16[216,384]{1,0:T(8,128)(2,1)S(1)}, bf16[216,384]{1,0:T(8,128)(2,1)S(1)}, u32[]{:S(2)}, u32[]{:S(2)}) collective-permute-start(bf16[216,384]{1,0:T(8,128)(2,1)S(1)} %collective-permute-done.13), channel_id=1, source_target_pairs={{0,4},{2,6},{4,0},{6,2},{8,12},{10,14},{12,8},{14,10},{16,20},{18,... | collective-permute-start | bytes 497672 | tf_op jit(solution)/shard_map/ppermute | solution.py:33
  68.7 0.5 collective-permute-start.21
  69.2 0.5 collective-permute-start.24
  69.8 0.1 copy-done.13
  69.9 0.1 copy-done.15
  69.9 0.4 copy-done.16
  70.4 3.0 %finish.2.refs_8_ = f32[3,9,192,384]{3,2,1,0:T(8,128)} custom-call(s32[1]{0:T(128)} %bitcast.refs_0_.me_ref, bf16[9,24,384]{2,1,0:T(8,128)(2,1)} %bitcast.35, bf16[9,24,384]{2,1,0:T(8,128)(2,1)} %bitcast.41, bf16[9,24,384]{2,1,0:T(8,128)(2,1)} %bitcast.40, bf16[9,24,384]{2,1,0:T(8,128)(2,1)} %bitcast.44, ...), custom_call_target="tpu_custom_call", output_to_operand_aliasing={{}: (9, {})} | custom-call | bytes 3981312 | tf_op jit(solution)/shard_map/finish/pallas_call | solution.py:471
  73.4 0.8 %collective-permute-done.20 = bf16[216,384]{1,0:T(8,128)(2,1)S(1)} collective-permute-done((bf16[216,384]{1,0:T(8,128)(2,1)S(1)}, bf16[216,384]{1,0:T(8,128)(2,1)S(1)}, u32[]{:S(2)}, u32[]{:S(2)}) %collective-permute-start.20) | collective-permute-done | bytes 165920 | tf_op jit(solution)/shard_map/ppermute | solution.py:33
  74.2 3.2 %collective-permute-done.21 = bf16[216,384]{1,0:T(8,128)(2,1)S(1)} collective-permute-done((bf16[216,384]{1,0:T(8,128)(2,1)S(1)}, bf16[216,384]{1,0:T(8,128)(2,1)S(1)}, u32[]{:S(2)}, u32[]{:S(2)}) %collective-permute-start.21) | collective-permute-done | bytes 165920 | tf_op jit(solution)/shard_map/ppermute | solution.py:33
  77.4 0.5 collective-permute-start.25
  77.9 0.9 %collective-permute-done.23 = bf16[216,384]{1,0:T(8,128)(2,1)S(1)} collective-permute-done((bf16[216,384]{1,0:T(8,128)(2,1)S(1)}, bf16[216,384]{1,0:T(8,128)(2,1)S(1)}, u32[]{:S(2)}, u32[]{:S(2)}) %collective-permute-start.23) | collective-permute-done | bytes 165920 | tf_op jit(solution)/shard_map/ppermute | solution.py:33
  78.8 0.2 collective-permute-done.25
  79.0 0.4 copy-done.17
  79.4 0.2 copy-done.18
  79.7 3.0 %finish.3 = f32[3,9,192,384]{3,2,1,0:T(8,128)} custom-call(s32[1]{0:T(128)} %bitcast.refs_0_.me_ref, bf16[9,24,384]{2,1,0:T(8,128)(2,1)} %bitcast.38, bf16[9,24,384]{2,1,0:T(8,128)(2,1)} %bitcast.42, bf16[9,24,384]{2,1,0:T(8,128)(2,1)} %bitcast.39, bf16[9,24,384]{2,1,0:T(8,128)(2,1)} %bitcast.43, ...), custom_call_target="tpu_custom_call", output_to_operand_aliasing={{}: (9, {})} | custom-call | bytes 3981312 | tf_op jit(solution)/shard_map/finish/pallas_call | solution.py:471
  (76 shorter events, 0.3 us)
Async XLA Ops:
  0.6 5.7 %copy-start = (bf16[2,2,64,2560]{3,2,1,0:T(8,128)(2,1)S(1)}, bf16[2,2,64,2560]{3,2,1,0:T(8,128)(2,1)}, u32[]{:S(2)}) copy-start(bf16[2,2,64,2560]{3,2,1,0:T(8,128)(2,1)} %param.6) | copy-start | bytes 3932164
  2.2 17.3 %collective-permute-start.2 = (bf16[4,24,1024]{2,1,0:T(8,128)(2,1)S(1)}, bf16[4,24,1024]{2,1,0:T(8,128)(2,1)S(1)}, u32[]{:S(2)}, u32[]{:S(2)}) collective-permute-start(bf16[4,24,1024]{2,1,0:T(8,128)(2,1)S(1)} %pad_maximum_fusion), channel_id=1, source_target_pairs={{0,16},{2,18},{4,20},{6,22},{8,24},{10,26},{12,28},{14,30},{16,0},... | collective-permute-start | bytes 589832 | tf_op jit(solution)/shard_map/ppermute | solution.py:33
  7.8 4.3 %copy-start.3 = (f32[64,256]{1,0:T(8,128)}, f32[64,256]{1,0:T(8,128)S(1)}, u32[]{:S(2)}) copy-start(f32[64,256]{1,0:T(8,128)S(1)} %convolution_bitcast_fusion.own_ref) | copy-start | bytes 196612
  7.8 4.3 %collective-permute-start = (f32[64,256]{1,0:T(8,128)S(1)}, f32[64,256]{1,0:T(8,128)S(1)}, u32[]{:S(2)}, u32[]{:S(2)}) collective-permute-start(f32[64,256]{1,0:T(8,128)S(1)} %convolution_bitcast_fusion.own_ref), channel_id=1, source_target_pairs={{0,1},{1,0},{2,3},{3,2},{4,5},{5,4},{6,7},{7,6},{8,9},{9,8},{10,11... | collective-permute-start | bytes 196616 | tf_op jit(solution)/shard_map/ppermute | solution.py:33
  14.4 5.1 %copy-start.26 = (bf16[16,1024]{1,0:T(8,128)(2,1)S(1)}, bf16[16,1024]{1,0:T(8,128)(2,1)}, u32[]{:S(2)}) copy-start(bf16[16,1024]{1,0:T(8,128)(2,1)} %unpatchify.1) | copy-start | bytes 98308
  14.4 14.5 %copy-start.28 = (f32[384]{0:T(512)S(1)}, f32[384]{0:T(512)}, u32[]{:S(2)}) copy-start(f32[384]{0:T(512)} %param.8) | copy-start | bytes 4612
  14.4 5.0 %collective-permute-start.1 = (bf16[16,1024]{1,0:T(8,128)(2,1)}, bf16[16,1024]{1,0:T(8,128)(2,1)S(1)}, u32[]{:S(2)}, u32[]{:S(2)}) collective-permute-start(bf16[16,1024]{1,0:T(8,128)(2,1)} %unpatchify.1), channel_id=1, source_target_pairs={{0,16},{2,18},{4,20},{6,22},{8,24},{10,26},{12,28},{14,30},{16,0},... | collective-permute-start | bytes 98312 | tf_op jit(solution)/shard_map/ppermute | solution.py:33
  19.5 10.8 %copy-start.2 = (bf16[2,40,1024]{2,1,0:T(8,128)(2,1)}, bf16[2,40,1024]{2,1,0:T(8,128)(2,1)S(1)}, u32[]{:S(2)}) copy-start(bf16[2,40,1024]{2,1,0:T(8,128)(2,1)S(1)} %get-tuple-element.27.refs_3_.refs_0_) | copy-start | bytes 491524
  19.5 7.1 %collective-permute-start.3 = (bf16[2,40,1024]{2,1,0:T(8,128)(2,1)S(1)}, bf16[2,40,1024]{2,1,0:T(8,128)(2,1)S(1)}, u32[]{:S(2)}, u32[]{:S(2)}) collective-permute-start(bf16[2,40,1024]{2,1,0:T(8,128)(2,1)S(1)} %get-tuple-element.57), channel_id=1, source_target_pairs={{0,4},{2,6},{4,0},{6,2},{8,12},{10,14},{12,8},{14,10},{16,20},{18,... | collective-permute-start | bytes 491528 | tf_op jit(solution)/shard_map/ppermute | solution.py:33
  21.1 5.6 %collective-permute-start.4 = (bf16[2,40,1024]{2,1,0:T(8,128)(2,1)S(1)}, bf16[2,40,1024]{2,1,0:T(8,128)(2,1)S(1)}, u32[]{:S(2)}, u32[]{:S(2)}) collective-permute-start(bf16[2,40,1024]{2,1,0:T(8,128)(2,1)S(1)} %get-tuple-element.58), channel_id=1, source_target_pairs={{0,8},{2,10},{4,12},{6,14},{8,0},{10,2},{12,4},{14,6},{16,24},{18,... | collective-permute-start | bytes 491528 | tf_op jit(solution)/shard_map/ppermute | solution.py:33
  22.7 6.2 %collective-permute-start.5 = (bf16[2,40,1024]{2,1,0:T(8,128)(2,1)S(1)}, bf16[2,40,1024]{2,1,0:T(8,128)(2,1)S(1)}, u32[]{:S(2)}, u32[]{:S(2)}) collective-permute-start(bf16[2,40,1024]{2,1,0:T(8,128)(2,1)S(1)} %get-tuple-element.56), channel_id=1, source_target_pairs={{0,12},{2,14},{4,8},{6,10},{8,4},{10,6},{12,0},{14,2},{16,28},{18,... | collective-permute-start | bytes 491528 | tf_op jit(solution)/shard_map/ppermute | solution.py:33
  23.1 6.4 %collective-permute-start.6 = (bf16[2,40,1024]{2,1,0:T(8,128)(2,1)S(1)}, bf16[2,40,1024]{2,1,0:T(8,128)(2,1)S(1)}, u32[]{:S(2)}, u32[]{:S(2)}) collective-permute-start(bf16[2,40,1024]{2,1,0:T(8,128)(2,1)S(1)} %get-tuple-element.27.refs_3_.refs_0_), channel_id=1, source_target_pairs={{0,2},{2,0},{4,6},{6,4},{8,10},{10,8},{12,14},{14,12},{16,18},{18,... | collective-permute-start | bytes 491528 | tf_op jit(solution)/shard_map/ppermute | solution.py:33
  26.7 3.6 %copy-start.19 = (bf16[2,40,1024]{2,1,0:T(8,128)(2,1)}, bf16[2,40,1024]{2,1,0:T(8,128)(2,1)S(1)}, u32[]{:S(2)}) copy-start(bf16[2,40,1024]{2,1,0:T(8,128)(2,1)S(1)} %collective-permute-done.3.refs_4_.refs_1_) | copy-start | bytes 491524
  26.7 2.9 %collective-permute-start.7 = (bf16[2,40,1024]{2,1,0:T(8,128)(2,1)S(1)}, bf16[2,40,1024]{2,1,0:T(8,128)(2,1)S(1)}, u32[]{:S(2)}, u32[]{:S(2)}) collective-permute-start(bf16[2,40,1024]{2,1,0:T(8,128)(2,1)S(1)} %collective-permute-done.3.refs_4_.refs_1_), channel_id=1, source_target_pairs={{0,2},{2,0},{4,6},{6,4},{8,10},{10,8},{12,14},{14,12},{16,18},{18,... | collective-permute-start | bytes 491528 | tf_op jit(solution)/shard_map/ppermute | solution.py:33
  26.7 3.6 %copy-start.20 = (bf16[2,40,1024]{2,1,0:T(8,128)(2,1)}, bf16[2,40,1024]{2,1,0:T(8,128)(2,1)S(1)}, u32[]{:S(2)}) copy-start(bf16[2,40,1024]{2,1,0:T(8,128)(2,1)S(1)} %collective-permute-done.4.refs_5_.refs_2_) | copy-start | bytes 491524
  26.7 2.9 %collective-permute-start.8 = (bf16[2,40,1024]{2,1,0:T(8,128)(2,1)S(1)}, bf16[2,40,1024]{2,1,0:T(8,128)(2,1)S(1)}, u32[]{:S(2)}, u32[]{:S(2)}) collective-permute-start(bf16[2,40,1024]{2,1,0:T(8,128)(2,1)S(1)} %collective-permute-done.4.refs_5_.refs_2_), channel_id=1, source_target_pairs={{0,2},{2,0},{4,6},{6,4},{8,10},{10,8},{12,14},{14,12},{16,18},{18,... | collective-permute-start | bytes 491528 | tf_op jit(solution)/shard_map/ppermute | solution.py:33
  28.9 1.4 %copy-start.21 = (bf16[2,40,1024]{2,1,0:T(8,128)(2,1)}, bf16[2,40,1024]{2,1,0:T(8,128)(2,1)S(1)}, u32[]{:S(2)}) copy-start(bf16[2,40,1024]{2,1,0:T(8,128)(2,1)S(1)} %collective-permute-done.5.refs_6_.refs_3_) | copy-start | bytes 491524
  28.9 1.4 %collective-permute-start.9 = (bf16[2,40,1024]{2,1,0:T(8,128)(2,1)S(1)}, bf16[2,40,1024]{2,1,0:T(8,128)(2,1)S(1)}, u32[]{:S(2)}, u32[]{:S(2)}) collective-permute-start(bf16[2,40,1024]{2,1,0:T(8,128)(2,1)S(1)} %collective-permute-done.5.refs_6_.refs_3_), channel_id=1, source_target_pairs={{0,2},{2,0},{4,6},{6,4},{8,10},{10,8},{12,14},{14,12},{16,18},{18,... | collective-permute-start | bytes 491528 | tf_op jit(solution)/shard_map/ppermute | solution.py:33
  29.5 0.8 copy-start.22
  29.6 0.8 copy-start.23
  29.6 0.8 copy-start.24
  43.0 1.7 %collective-permute-start.10 = (bf16[216,384]{1,0:T(8,128)(2,1)}, bf16[216,384]{1,0:T(8,128)(2,1)S(1)}, u32[]{:S(2)}, u32[]{:S(2)}) collective-permute-start(bf16[216,384]{1,0:T(8,128)(2,1)} %get-tuple-element.26), channel_id=1, source_target_pairs={{0,2},{2,0},{4,6},{6,4},{8,10},{10,8},{12,14},{14,12},{16,18},{18,... | collective-permute-start | bytes 497672 | tf_op jit(solution)/shard_map/ppermute | solution.py:33
  45.7 17.6 %copy-start.1 = (bf16[216,384]{1,0:T(8,128)(2,1)}, bf16[216,384]{1,0:T(8,128)(2,1)S(1)}, u32[]{:S(2)}) copy-start(bf16[216,384]{1,0:T(8,128)(2,1)S(1)} %add_convert_fusion) | copy-start | bytes 497668
  45.7 14.2 %collective-permute-start.12 = (bf16[216,384]{1,0:T(8,128)(2,1)S(1)}, bf16[216,384]{1,0:T(8,128)(2,1)S(1)}, u32[]{:S(2)}, u32[]{:S(2)}) collective-permute-start(bf16[216,384]{1,0:T(8,128)(2,1)S(1)} %add_convert_fusion), channel_id=1, source_target_pairs={{0,8},{2,10},{4,12},{6,14},{8,0},{10,2},{12,4},{14,6},{16,24},{18,... | collective-permute-start | bytes 497672 | tf_op jit(solution)/shard_map/ppermute | solution.py:33
  46.6 15.1 %collective-permute-start.13 = (bf16[216,384]{1,0:T(8,128)(2,1)S(1)}, bf16[216,384]{1,0:T(8,128)(2,1)S(1)}, u32[]{:S(2)}, u32[]{:S(2)}) collective-permute-start(bf16[216,384]{1,0:T(8,128)(2,1)S(1)} %add_convert_fusion), channel_id=1, source_target_pairs={{0,16},{2,18},{4,20},{6,22},{8,24},{10,26},{12,28},{14,30},{16,0},... | collective-permute-start | bytes 497672 | tf_op jit(solution)/shard_map/ppermute | solution.py:33
  47.9 13.8 %collective-permute-start.14 = (bf16[216,384]{1,0:T(8,128)(2,1)S(1)}, bf16[216,384]{1,0:T(8,128)(2,1)S(1)}, u32[]{:S(2)}, u32[]{:S(2)}) collective-permute-start(bf16[216,384]{1,0:T(8,128)(2,1)S(1)} %add_convert_fusion), channel_id=1, source_target_pairs={{0,24},{2,26},{4,28},{6,30},{8,16},{10,18},{12,20},{14,22},{16,8},... | collective-permute-start | bytes 497672 | tf_op jit(solution)/shard_map/ppermute | solution.py:33
  50.2 13.7 %collective-permute-start.11 = (bf16[216,384]{1,0:T(8,128)(2,1)S(1)}, bf16[216,384]{1,0:T(8,128)(2,1)S(1)}, u32[]{:S(2)}, u32[]{:S(2)}) collective-permute-start(bf16[216,384]{1,0:T(8,128)(2,1)S(1)} %add_convert_fusion), channel_id=1, source_target_pairs={{0,4},{2,6},{4,0},{6,2},{8,12},{10,14},{12,8},{14,10},{16,20},{18,... | collective-permute-start | bytes 497672 | tf_op jit(solution)/shard_map/ppermute | solution.py:33
  59.9 9.8 %copy-start.6 = (bf16[216,384]{1,0:T(8,128)(2,1)}, bf16[216,384]{1,0:T(8,128)(2,1)S(1)}, u32[]{:S(2)}) copy-start(bf16[216,384]{1,0:T(8,128)(2,1)S(1)} %collective-permute-done.12) | copy-start | bytes 497668
  61.8 11.6 %copy-start.4 = (bf16[216,384]{1,0:T(8,128)(2,1)}, bf16[216,384]{1,0:T(8,128)(2,1)S(1)}, u32[]{:S(2)}) copy-start(bf16[216,384]{1,0:T(8,128)(2,1)S(1)} %collective-permute-done.13) | copy-start | bytes 497668
  61.8 11.6 %copy-start.5 = (bf16[216,384]{1,0:T(8,128)(2,1)}, bf16[216,384]{1,0:T(8,128)(2,1)S(1)}, u32[]{:S(2)}) copy-start(bf16[216,384]{1,0:T(8,128)(2,1)S(1)} %collective-permute-done.14) | copy-start | bytes 497668
  61.8 5.4 %collective-permute-start.15 = (bf16[216,384]{1,0:T(8,128)(2,1)S(1)}, bf16[216,384]{1,0:T(8,128)(2,1)S(1)}, u32[]{:S(2)}, u32[]{:S(2)}) collective-permute-start(bf16[216,384]{1,0:T(8,128)(2,1)S(1)} %collective-permute-done.12), channel_id=1, source_target_pairs={{0,4},{2,6},{4,0},{6,2},{8,12},{10,14},{12,8},{14,10},{16,20},{18,... | collective-permute-start | bytes 497672 | tf_op jit(solution)/shard_map/ppermute | solution.py:33
  63.3 5.3 %collective-permute-start.16 = (bf16[216,384]{1,0:T(8,128)(2,1)S(1)}, bf16[216,384]{1,0:T(8,128)(2,1)S(1)}, u32[]{:S(2)}, u32[]{:S(2)}) collective-permute-start(bf16[216,384]{1,0:T(8,128)(2,1)S(1)} %add_convert_fusion), channel_id=1, source_target_pairs={{0,2},{2,0},{4,6},{6,4},{8,10},{10,8},{12,14},{14,12},{16,18},{18,... | collective-permute-start | bytes 497672 | tf_op jit(solution)/shard_map/ppermute | solution.py:33
  63.3 5.9 %collective-permute-start.18 = (bf16[216,384]{1,0:T(8,128)(2,1)S(1)}, bf16[216,384]{1,0:T(8,128)(2,1)S(1)}, u32[]{:S(2)}, u32[]{:S(2)}) collective-permute-start(bf16[216,384]{1,0:T(8,128)(2,1)S(1)} %collective-permute-done.12), channel_id=1, source_target_pairs={{0,2},{2,0},{4,6},{6,4},{8,10},{10,8},{12,14},{14,12},{16,18},{18,... | collective-permute-start | bytes 497672 | tf_op jit(solution)/shard_map/ppermute | solution.py:33
  63.9 5.9 %copy-start.7 = (bf16[216,384]{1,0:T(8,128)(2,1)}, bf16[216,384]{1,0:T(8,128)(2,1)S(1)}, u32[]{:S(2)}) copy-start(bf16[216,384]{1,0:T(8,128)(2,1)S(1)} %collective-permute-done.11) | copy-start | bytes 497668
  63.9 5.4 %collective-permute-start.17 = (bf16[216,384]{1,0:T(8,128)(2,1)S(1)}, bf16[216,384]{1,0:T(8,128)(2,1)S(1)}, u32[]{:S(2)}, u32[]{:S(2)}) collective-permute-start(bf16[216,384]{1,0:T(8,128)(2,1)S(1)} %collective-permute-done.11), channel_id=1, source_target_pairs={{0,2},{2,0},{4,6},{6,4},{8,10},{10,8},{12,14},{14,12},{16,18},{18,... | collective-permute-start | bytes 497672 | tf_op jit(solution)/shard_map/ppermute | solution.py:33
  67.2 2.6 %copy-start.10 = (bf16[216,384]{1,0:T(8,128)(2,1)}, bf16[216,384]{1,0:T(8,128)(2,1)S(1)}, u32[]{:S(2)}) copy-start(bf16[216,384]{1,0:T(8,128)(2,1)S(1)} %collective-permute-done.15) | copy-start | bytes 497668
  67.2 2.6 %collective-permute-start.19 = (bf16[216,384]{1,0:T(8,128)(2,1)S(1)}, bf16[216,384]{1,0:T(8,128)(2,1)S(1)}, u32[]{:S(2)}, u32[]{:S(2)}) collective-permute-start(bf16[216,384]{1,0:T(8,128)(2,1)S(1)} %collective-permute-done.15), channel_id=1, source_target_pairs={{0,2},{2,0},{4,6},{6,4},{8,10},{10,8},{12,14},{14,12},{16,18},{18,... | collective-permute-start | bytes 497672 | tf_op jit(solution)/shard_map/ppermute | solution.py:33
  67.2 7.0 %collective-permute-start.20 = (bf16[216,384]{1,0:T(8,128)(2,1)S(1)}, bf16[216,384]{1,0:T(8,128)(2,1)S(1)}, u32[]{:S(2)}, u32[]{:S(2)}) collective-permute-start(bf16[216,384]{1,0:T(8,128)(2,1)S(1)} %collective-permute-done.13), channel_id=1, source_target_pairs={{0,4},{2,6},{4,0},{6,2},{8,12},{10,14},{12,8},{14,10},{16,20},{18,... | collective-permute-start | bytes 497672 | tf_op jit(solution)/shard_map/ppermute | solution.py:33
  68.7 1.1 %copy-start.11 = (bf16[216,384]{1,0:T(8,128)(2,1)}, bf16[216,384]{1,0:T(8,128)(2,1)S(1)}, u32[]{:S(2)}) copy-start(bf16[216,384]{1,0:T(8,128)(2,1)S(1)} %collective-permute-done.16) | copy-start | bytes 497668
  68.7 8.7 %collective-permute-start.21 = (bf16[216,384]{1,0:T(8,128)(2,1)S(1)}, bf16[216,384]{1,0:T(8,128)(2,1)S(1)}, u32[]{:S(2)}, u32[]{:S(2)}) collective-permute-start(bf16[216,384]{1,0:T(8,128)(2,1)S(1)} %collective-permute-done.14), channel_id=1, source_target_pairs={{0,4},{2,6},{4,0},{6,2},{8,12},{10,14},{12,8},{14,10},{16,20},{18,... | collective-permute-start | bytes 497672 | tf_op jit(solution)/shard_map/ppermute | solution.py:33
  69.2 8.7 %collective-permute-start.22 = (bf16[216,384]{1,0:T(8,128)(2,1)S(1)}, bf16[216,384]{1,0:T(8,128)(2,1)S(1)}, u32[]{:S(2)}, u32[]{:S(2)}) collective-permute-start(bf16[216,384]{1,0:T(8,128)(2,1)S(1)} %collective-permute-done.13), channel_id=1, source_target_pairs={{0,2},{2,0},{4,6},{6,4},{8,10},{10,8},{12,14},{14,12},{16,18},{18,... | collective-permute-start | bytes 497672 | tf_op jit(solution)/shard_map/ppermute | solution.py:33
  69.2 8.7 %collective-permute-start.24 = (bf16[216,384]{1,0:T(8,128)(2,1)S(1)}, bf16[216,384]{1,0:T(8,128)(2,1)S(1)}, u32[]{:S(2)}, u32[]{:S(2)}) collective-permute-start(bf16[216,384]{1,0:T(8,128)(2,1)S(1)} %collective-permute-done.14), channel_id=1, source_target_pairs={{0,2},{2,0},{4,6},{6,4},{8,10},{10,8},{12,14},{14,12},{16,18},{18,... | collective-permute-start | bytes 497672 | tf_op jit(solution)/shard_map/ppermute | solution.py:33
  74.2 4.8 %copy-start.8 = (bf16[216,384]{1,0:T(8,128)(2,1)}, bf16[216,384]{1,0:T(8,128)(2,1)S(1)}, u32[]{:S(2)}) copy-start(bf16[216,384]{1,0:T(8,128)(2,1)S(1)} %collective-permute-done.20) | copy-start | bytes 497668
  77.4 1.6 %copy-start.9 = (bf16[216,384]{1,0:T(8,128)(2,1)}, bf16[216,384]{1,0:T(8,128)(2,1)S(1)}, u32[]{:S(2)}) copy-start(bf16[216,384]{1,0:T(8,128)(2,1)S(1)} %collective-permute-done.21) | copy-start | bytes 497668
  77.4 1.4 %collective-permute-start.23 = (bf16[216,384]{1,0:T(8,128)(2,1)S(1)}, bf16[216,384]{1,0:T(8,128)(2,1)S(1)}, u32[]{:S(2)}, u32[]{:S(2)}) collective-permute-start(bf16[216,384]{1,0:T(8,128)(2,1)S(1)} %collective-permute-done.20), channel_id=1, source_target_pairs={{0,2},{2,0},{4,6},{6,4},{8,10},{10,8},{12,14},{14,12},{16,18},{18,... | collective-permute-start | bytes 497672 | tf_op jit(solution)/shard_map/ppermute | solution.py:33
  77.4 1.6 %collective-permute-start.25 = (bf16[216,384]{1,0:T(8,128)(2,1)S(1)}, bf16[216,384]{1,0:T(8,128)(2,1)S(1)}, u32[]{:S(2)}, u32[]{:S(2)}) collective-permute-start(bf16[216,384]{1,0:T(8,128)(2,1)S(1)} %collective-permute-done.21), channel_id=1, source_target_pairs={{0,2},{2,0},{4,6},{6,4},{8,10},{10,8},{12,14},{14,12},{16,18},{18,... | collective-permute-start | bytes 497672 | tf_op jit(solution)/shard_map/ppermute | solution.py:33
  77.9 1.1 %copy-start.12 = (bf16[216,384]{1,0:T(8,128)(2,1)}, bf16[216,384]{1,0:T(8,128)(2,1)S(1)}, u32[]{:S(2)}) copy-start(bf16[216,384]{1,0:T(8,128)(2,1)S(1)} %collective-permute-done.22) | copy-start | bytes 497668
  77.9 1.1 %copy-start.14 = (bf16[216,384]{1,0:T(8,128)(2,1)}, bf16[216,384]{1,0:T(8,128)(2,1)S(1)}, u32[]{:S(2)}) copy-start(bf16[216,384]{1,0:T(8,128)(2,1)S(1)} %collective-permute-done.24) | copy-start | bytes 497668
  (7 other events, 4.7 us)

commit v6 on v5

--- a/solution.py
+++ b/solution.py
@@ -436,7 +436,7 @@
     beside = xor_permute(block, "seq", 2)
     conv = conv_weight.transpose(1, 2, 3, 0, 4).reshape(27, out_channels, channels)
 
-    held = lax.optimization_barrier((block, *pieces))[1:]
+    held = lax.optimization_barrier((block, direct[0], *pieces))[2:]
     decoded = pl.pallas_call(
         functools.partial(decode_kernel, frames, rows, slabs, masks),
         out_shape=jax.ShapeDtypeStruct((out_channels, frames, rows, width), BF16),
@@ -455,15 +455,13 @@
         ]
         + weights,
         compiler_params=params(),
-        cost_estimate=cost(
-            live * 18 * frames * out_channels * channels * rows * width,
-            live * 18 * out_channels * channels,
-        ),
         name="decode",
     )(me, gain, entry, conv, *held)
-    gated = lax.optimization_barrier((decoded, *direct))
-    decoded, direct = gated[0], list(gated[1:])
-    across = [xor_permute(piece, "seq", 2) for piece in direct]
+    nearest = xor_permute(direct[0], "seq", 2)
+    gated = lax.optimization_barrier((decoded, block, beside, nearest, *direct))
+    decoded, block, beside, nearest = gated[:4]
+    direct = list(gated[4:])
+    across = [nearest] + [xor_permute(piece, "seq", 2) for piece in direct[1:]]
 
     shape = (9, pad_channels, channels)
 

time: 83.6 us -> 80.5 us (0.963)
  waiting for transfers between devices: 23.9 us -> 22.1 us
    ppermute x26, waiting for transfers between devices: 23.9 us -> 22.1 us  [xor_permute(): lax.ppermute(x, axis, [(i, i ^ mask) for i in range(lax.axis_size(axis))])]
    ppermute x26, starting transfers between devices: 20.3 us -> 19.5 us  [xor_permute(): lax.ppermute(x, axis, [(i, i ^ mask) for i in range(lax.axis_size(axis))])]
  transfers between devices with their start and end apart: 26 -> 26, of which waited for: 12 -> 13; matrix products, arithmetic and copies ran while one was open for 3% -> 3% of each run, Pallas kernels for 18% -> 19%
where the time goes in v6:
time: 80.5 us; the launch traced here: 80.1 us
  Pallas kernels  30.2 us (38%)
  waiting for transfers between devices  22.1 us (27%)
  starting transfers between devices  19.5 us (24%)
  local copies, waits for them, and re-layouts  4.57 us (6%)
  matrix products  1.48 us (2%)
  between operations  1.19 us (1%)
  other arithmetic  1.1 us (1%)
    ppermute x26, waiting for transfers between devices, xor_permute(): lax.ppermute(x, axis, [(i, i ^ mask) for i in range(lax.axis_size(axis))])  22.1 us
    ppermute x26, starting transfers between devices, xor_permute(): lax.ppermute(x, axis, [(i, i ^ mask) for i in range(lax.axis_size(axis))])  19.5 us
    pallas_call x1, Pallas kernels, per_device(): pl.pallas_call(functools.partial(gradient_kernel, frames, rows, slabs, ma...  12 us
    pallas_call x1, Pallas kernels, per_device(): pl.pallas_call(functools.partial(decode_kernel, frames, rows, slabs, mask...  8.98 us
    pallas_call x2, Pallas kernels, finish(): pl.pallas_call(functools.partial(finish_kernel, sources), out_shape=jax.S...  5.95 us
    unnamed x58, local copies, waits for them, and re-layouts  2.62 us
    pallas_call x1, Pallas kernels, per_device(): pl.pallas_call(functools.partial(unpatchify_kernel, frames, tok_rows, tok...  1.67 us
  transfers between devices with their start and end apart: 26, of which 13 were waited for; matrix products, arithmetic and copies ran while one was open for 3% of the time, Pallas kernels for 19%

profile of v6, /device:TPU:0, one launch (start us, length us, event | category | flops | bytes accessed | tf_op | source)
XLA Modules:
  0.0 80.1 jit_solution(7694730492236934804)
XLA Ops:
  0.7 1.4 %reshape.77 = bf16[8,24,1024]{2,1,0:T(8,128)(2,1)S(1)} reshape(bf16[192,2,4,128]{3,2,1,0:T(4,128)(2,1)} %param.11) | data formatting | bytes 786432 | tf_op jit(solution)/shard_map/reshape | solution.py:338
  2.2 4.1 %collective-permute-start.2 = (bf16[4,24,1024]{2,1,0:T(8,128)(2,1)S(1)}, bf16[4,24,1024]{2,1,0:T(8,128)(2,1)S(1)}, u32[]{:S(2)}, u32[]{:S(2)}) collective-permute-start(bf16[4,24,1024]{2,1,0:T(8,128)(2,1)S(1)} %pad_maximum_fusion), channel_id=1, source_target_pairs={{0,16},{2,18},{4,20},{6,22},{8,24},{10,26},{12,28},{14,30},{16,0},... | collective-permute-start | bytes 589832 | tf_op jit(solution)/shard_map/ppermute | solution.py:33
  6.3 1.5 %convolution_bitcast_fusion.own_ref = f32[64,256]{1,0:T(8,128)S(1)} fusion(bf16[256,2560]{1,0:T(8,128)(2,1)S(1)} %bitcast.33, bf16[2560,64]{0,1:T(8,128)(2,1)} %param.7), kind=kOutput, calls=%fused_computation | convolution fusion | flops 83886080 | bytes 1703936 | tf_op jit(solution)/shard_map/dot_general | solution.py:354
  7.8 1.6 %collective-permute-start = (f32[64,256]{1,0:T(8,128)S(1)}, f32[64,256]{1,0:T(8,128)S(1)}, u32[]{:S(2)}, u32[]{:S(2)}) collective-permute-start(f32[64,256]{1,0:T(8,128)S(1)} %convolution_bitcast_fusion.own_ref), channel_id=1, source_target_pairs={{0,1},{1,0},{2,3},{3,2},{4,5},{5,4},{6,7},{7,6},{8,9},{9,8},{10,11... | collective-permute-start | bytes 196616 | tf_op jit(solution)/shard_map/ppermute | solution.py:33
  9.3 2.8 %collective-permute-done.other_ref = f32[64,256]{1,0:T(8,128)S(1)} collective-permute-done((f32[64,256]{1,0:T(8,128)S(1)}, f32[64,256]{1,0:T(8,128)S(1)}, u32[]{:S(2)}, u32[]{:S(2)}) %collective-permute-start) | collective-permute-done | bytes 65568 | tf_op jit(solution)/shard_map/ppermute | solution.py:33
  12.1 0.6 copy-done.27
  12.7 1.7 %unpatchify.1 = bf16[16,1024]{1,0:T(8,128)(2,1)} custom-call(f32[64,256]{1,0:T(8,128)} %copy-done.10, f32[64,256]{1,0:T(8,128)} %copy-done.27), custom_call_target="tpu_custom_call" | custom-call | tf_op jit(solution)/shard_map/unpatchify/pallas_call | solution.py:369
  14.4 1.6 %blank.1.refs_8_ = f32[3,9,192,384]{3,2,1,0:T(8,128)} custom-call(), custom_call_target="tpu_custom_call" | custom-call | bytes 2654208 | tf_op jit(solution)/shard_map/blank/pallas_call | solution.py:381
  16.0 3.4 %collective-permute-done.1 = bf16[16,1024]{1,0:T(8,128)(2,1)S(1)} collective-permute-done((bf16[16,1024]{1,0:T(8,128)(2,1)}, bf16[16,1024]{1,0:T(8,128)(2,1)S(1)}, u32[]{:S(2)}, u32[]{:S(2)}) %collective-permute-start.1) | collective-permute-done | bytes 32800 | tf_op jit(solution)/shard_map/ppermute | solution.py:33
  19.6 2.6 %collective-permute-start.5 = (bf16[2,40,1024]{2,1,0:T(8,128)(2,1)S(1)}, bf16[2,40,1024]{2,1,0:T(8,128)(2,1)S(1)}, u32[]{:S(2)}, u32[]{:S(2)}) collective-permute-start(bf16[2,40,1024]{2,1,0:T(8,128)(2,1)S(1)} %get-tuple-element.62), channel_id=1, source_target_pairs={{0,12},{2,14},{4,8},{6,10},{8,4},{10,6},{12,0},{14,2},{16,28},{18,... | collective-permute-start | bytes 491528 | tf_op jit(solution)/shard_map/ppermute | solution.py:33
  22.2 0.5 collective-permute-start.3
  22.7 0.5 collective-permute-start.4
  23.1 3.7 %collective-permute-done.5.refs_6_.refs_3_ = bf16[2,40,1024]{2,1,0:T(8,128)(2,1)S(1)} collective-permute-done((bf16[2,40,1024]{2,1,0:T(8,128)(2,1)S(1)}, bf16[2,40,1024]{2,1,0:T(8,128)(2,1)S(1)}, u32[]{:S(2)}, u32[]{:S(2)}) %collective-permute-start.5) | collective-permute-done | bytes 163872 | tf_op jit(solution)/shard_map/ppermute | solution.py:33
  26.8 1.6 %collective-permute-done.3.refs_4_.refs_1_ = bf16[2,40,1024]{2,1,0:T(8,128)(2,1)S(1)} collective-permute-done((bf16[2,40,1024]{2,1,0:T(8,128)(2,1)S(1)}, bf16[2,40,1024]{2,1,0:T(8,128)(2,1)S(1)}, u32[]{:S(2)}, u32[]{:S(2)}) %collective-permute-start.3) | collective-permute-done | bytes 163872 | tf_op jit(solution)/shard_map/ppermute | solution.py:33
  28.4 0.5 collective-permute-start.8
  28.9 0.5 reshape.74.refs_1_.gain_ref
  29.5 0.3 collective-permute-done.7.refs_8_.refs_5_
  29.8 0.2 collective-permute-done.8.refs_9_.refs_6_
  30.2 0.3 copy-done.8
  30.5 0.2 copy-done.9
  30.7 12.0 %gradient.1 = (f32[216,384]{1,0:T(8,128)}, bf16[216,384]{1,0:T(8,128)(2,1)}) custom-call(s32[1]{0:T(128)} %bitcast.refs_0_.me_ref, f32[1,384]{1,0:T(1,128)} %reshape.74.refs_1_.gain_ref, bf16[432,384]{1,0:T(8,128)(2,1)} %bitcast.36, bf16[2,40,1024]{2,1,0:T(8,128)(2,1)} %copy-done.1, bf16[2,40,1024]{2,1,0:T(8,128)(2,1)} %copy-done.4, ...), custom_call_target="tpu_custom_call" | custom-call | tf_op jit(solution)/shard_map/gradient/pallas_call | solution.py:407
  42.7 0.3 collective-permute-start.10
  43.1 1.3 %collective-permute-done.10 = bf16[216,384]{1,0:T(8,128)(2,1)S(1)} collective-permute-done((bf16[216,384]{1,0:T(8,128)(2,1)}, bf16[216,384]{1,0:T(8,128)(2,1)S(1)}, u32[]{:S(2)}, u32[]{:S(2)}) %collective-permute-start.10) | collective-permute-done | bytes 165920 | tf_op jit(solution)/shard_map/ppermute | solution.py:33
  44.4 1.0 %add_convert_fusion = bf16[216,384]{1,0:T(8,128)(2,1)S(1)} fusion(f32[216,384]{1,0:T(8,128)} %get-tuple-element.28, bf16[216,384]{1,0:T(8,128)(2,1)S(1)} %collective-permute-done.10), kind=kLoop, calls=%fused_computation.1 | loop fusion | flops 248832 | bytes 663552 | tf_op jit(solution)/shard_map/convert_element_type | solution.py:432
  45.4 1.0 %collective-permute-start.11 = (bf16[216,384]{1,0:T(8,128)(2,1)S(1)}, bf16[216,384]{1,0:T(8,128)(2,1)S(1)}, u32[]{:S(2)}, u32[]{:S(2)}) collective-permute-start(bf16[216,384]{1,0:T(8,128)(2,1)S(1)} %add_convert_fusion), channel_id=1, source_target_pairs={{0,8},{2,10},{4,12},{6,14},{8,0},{10,2},{12,4},{14,6},{16,24},{18,... | collective-permute-start | bytes 497672 | tf_op jit(solution)/shard_map/ppermute | solution.py:33
  46.4 1.2 %collective-permute-start.15 = (bf16[216,384]{1,0:T(8,128)(2,1)S(1)}, bf16[216,384]{1,0:T(8,128)(2,1)S(1)}, u32[]{:S(2)}, u32[]{:S(2)}) collective-permute-start(bf16[216,384]{1,0:T(8,128)(2,1)S(1)} %add_convert_fusion), channel_id=1, source_target_pairs={{0,24},{2,26},{4,28},{6,30},{8,16},{10,18},{12,20},{14,22},{16,8},... | collective-permute-start | bytes 497672 | tf_op jit(solution)/shard_map/ppermute | solution.py:33
  47.6 1.4 %collective-permute-start.14 = (bf16[216,384]{1,0:T(8,128)(2,1)S(1)}, bf16[216,384]{1,0:T(8,128)(2,1)S(1)}, u32[]{:S(2)}, u32[]{:S(2)}) collective-permute-start(bf16[216,384]{1,0:T(8,128)(2,1)S(1)} %add_convert_fusion), channel_id=1, source_target_pairs={{0,16},{2,18},{4,20},{6,22},{8,24},{10,26},{12,28},{14,30},{16,0},... | collective-permute-start | bytes 497672 | tf_op jit(solution)/shard_map/ppermute | solution.py:33
  49.0 0.9 %collective-permute-start.12 = (bf16[216,384]{1,0:T(8,128)(2,1)S(1)}, bf16[216,384]{1,0:T(8,128)(2,1)S(1)}, u32[]{:S(2)}, u32[]{:S(2)}) collective-permute-start(bf16[216,384]{1,0:T(8,128)(2,1)S(1)} %add_convert_fusion), channel_id=1, source_target_pairs={{0,4},{2,6},{4,0},{6,2},{8,12},{10,14},{12,8},{14,10},{16,20},{18,... | collective-permute-start | bytes 497672 | tf_op jit(solution)/shard_map/ppermute | solution.py:33
  49.9 2.6 %collective-permute-done.11 = bf16[216,384]{1,0:T(8,128)(2,1)S(1)} collective-permute-done((bf16[216,384]{1,0:T(8,128)(2,1)S(1)}, bf16[216,384]{1,0:T(8,128)(2,1)S(1)}, u32[]{:S(2)}, u32[]{:S(2)}) %collective-permute-start.11) | collective-permute-done | bytes 165920 | tf_op jit(solution)/shard_map/ppermute | solution.py:33
  52.5 0.9 %collective-permute-start.13 = (bf16[216,384]{1,0:T(8,128)(2,1)S(1)}, bf16[216,384]{1,0:T(8,128)(2,1)S(1)}, u32[]{:S(2)}, u32[]{:S(2)}) collective-permute-start(bf16[216,384]{1,0:T(8,128)(2,1)S(1)} %collective-permute-done.11), channel_id=1, source_target_pairs={{0,4},{2,6},{4,0},{6,2},{8,12},{10,14},{12,8},{14,10},{16,20},{18,... | collective-permute-start | bytes 497672 | tf_op jit(solution)/shard_map/ppermute | solution.py:33
  53.3 9.0 %decode.1 = bf16[192,2,4,128]{3,2,1,0:T(4,128)(2,1)} custom-call(s32[1]{0:T(128)} %bitcast.refs_0_.me_ref, f32[1,384]{1,0:T(1,128)} %reshape.74.refs_1_.gain_ref, bf16[432,384]{1,0:T(8,128)(2,1)} %bitcast.37, bf16[27,192,384]{2,1,0:T(8,128)(2,1)} %bitcast.35, bf16[2,40,1024]{2,1,0:T(8,128)(2,1)} %copy-done.1, bf16[2,40,1024]{2,1,0:T(8,128)(2,1)} %copy-done.4, ...), custom_call_target="tpu_custom_call" | custom-call | tf_op jit(solution)/shard_map/decode/pallas_call | solution.py:440
  62.3 1.4 %collective-permute-done.14 = bf16[216,384]{1,0:T(8,128)(2,1)S(1)} collective-permute-done((bf16[216,384]{1,0:T(8,128)(2,1)S(1)}, bf16[216,384]{1,0:T(8,128)(2,1)S(1)}, u32[]{:S(2)}, u32[]{:S(2)}) %collective-permute-start.14) | collective-permute-done | bytes 165920 | tf_op jit(solution)/shard_map/ppermute | solution.py:33
  63.9 0.5 collective-permute-start.17
  64.5 0.4 collective-permute-start.19
  64.9 0.7 collective-permute-start.20
  65.6 1.3 %collective-permute-start.21 = (bf16[216,384]{1,0:T(8,128)(2,1)S(1)}, bf16[216,384]{1,0:T(8,128)(2,1)S(1)}, u32[]{:S(2)}, u32[]{:S(2)}) collective-permute-start(bf16[216,384]{1,0:T(8,128)(2,1)S(1)} %collective-permute-done.15), channel_id=1, source_target_pairs={{0,4},{2,6},{4,0},{6,2},{8,12},{10,14},{12,8},{14,10},{16,20},{18,... | collective-permute-start | bytes 497672 | tf_op jit(solution)/shard_map/ppermute | solution.py:33
  66.9 0.5 collective-permute-start.24
  67.5 0.1 copy-done.21
  67.6 0.5 copy-done.23
  68.1 3.0 %finish.2.refs_8_ = f32[3,9,192,384]{3,2,1,0:T(8,128)} custom-call(s32[1]{0:T(128)} %bitcast.refs_0_.me_ref, bf16[9,24,384]{2,1,0:T(8,128)(2,1)} %bitcast.38, bf16[9,24,384]{2,1,0:T(8,128)(2,1)} %bitcast.42, bf16[9,24,384]{2,1,0:T(8,128)(2,1)} %bitcast.41, bf16[9,24,384]{2,1,0:T(8,128)(2,1)} %bitcast.43, ...), custom_call_target="tpu_custom_call", output_to_operand_aliasing={{}: (9, {})} | custom-call | bytes 3981312 | tf_op jit(solution)/shard_map/finish/pallas_call | solution.py:469
  71.1 0.9 %collective-permute-done.20 = bf16[216,384]{1,0:T(8,128)(2,1)S(1)} collective-permute-done((bf16[216,384]{1,0:T(8,128)(2,1)S(1)}, bf16[216,384]{1,0:T(8,128)(2,1)S(1)}, u32[]{:S(2)}, u32[]{:S(2)}) %collective-permute-start.20) | collective-permute-done | bytes 165920 | tf_op jit(solution)/shard_map/ppermute | solution.py:33
  72.0 2.7 %collective-permute-done.21 = bf16[216,384]{1,0:T(8,128)(2,1)S(1)} collective-permute-done((bf16[216,384]{1,0:T(8,128)(2,1)S(1)}, bf16[216,384]{1,0:T(8,128)(2,1)S(1)}, u32[]{:S(2)}, u32[]{:S(2)}) %collective-permute-start.21) | collective-permute-done | bytes 165920 | tf_op jit(solution)/shard_map/ppermute | solution.py:33
  74.7 0.5 collective-permute-start.25
  75.2 0.9 %collective-permute-done.23 = bf16[216,384]{1,0:T(8,128)(2,1)S(1)} collective-permute-done((bf16[216,384]{1,0:T(8,128)(2,1)S(1)}, bf16[216,384]{1,0:T(8,128)(2,1)S(1)}, u32[]{:S(2)}, u32[]{:S(2)}) %collective-permute-start.23) | collective-permute-done | bytes 165920 | tf_op jit(solution)/shard_map/ppermute | solution.py:33
  76.1 0.2 collective-permute-done.25
  76.3 0.4 copy-done.24
  76.7 0.2 copy-done.25
  77.0 3.0 %finish.3 = f32[3,9,192,384]{3,2,1,0:T(8,128)} custom-call(s32[1]{0:T(128)} %bitcast.refs_0_.me_ref, bf16[9,24,384]{2,1,0:T(8,128)(2,1)} %bitcast.40, bf16[9,24,384]{2,1,0:T(8,128)(2,1)} %bitcast.44, bf16[9,24,384]{2,1,0:T(8,128)(2,1)} %bitcast.39, bf16[9,24,384]{2,1,0:T(8,128)(2,1)} %bitcast.45, ...), custom_call_target="tpu_custom_call", output_to_operand_aliasing={{}: (9, {})} | custom-call | bytes 3981312 | tf_op jit(solution)/shard_map/finish/pallas_call | solution.py:469
  (76 shorter events, 0.7 us)
Async XLA Ops:
  0.6 5.7 %copy-start = (bf16[2,2,64,2560]{3,2,1,0:T(8,128)(2,1)S(1)}, bf16[2,2,64,2560]{3,2,1,0:T(8,128)(2,1)}, u32[]{:S(2)}) copy-start(bf16[2,2,64,2560]{3,2,1,0:T(8,128)(2,1)} %param.6) | copy-start | bytes 3932164
  2.2 17.3 %collective-permute-start.2 = (bf16[4,24,1024]{2,1,0:T(8,128)(2,1)S(1)}, bf16[4,24,1024]{2,1,0:T(8,128)(2,1)S(1)}, u32[]{:S(2)}, u32[]{:S(2)}) collective-permute-start(bf16[4,24,1024]{2,1,0:T(8,128)(2,1)S(1)} %pad_maximum_fusion), channel_id=1, source_target_pairs={{0,16},{2,18},{4,20},{6,22},{8,24},{10,26},{12,28},{14,30},{16,0},... | collective-permute-start | bytes 589832 | tf_op jit(solution)/shard_map/ppermute | solution.py:33
  7.8 4.3 %copy-start.10 = (f32[64,256]{1,0:T(8,128)}, f32[64,256]{1,0:T(8,128)S(1)}, u32[]{:S(2)}) copy-start(f32[64,256]{1,0:T(8,128)S(1)} %convolution_bitcast_fusion.own_ref) | copy-start | bytes 196612
  7.8 4.3 %collective-permute-start = (f32[64,256]{1,0:T(8,128)S(1)}, f32[64,256]{1,0:T(8,128)S(1)}, u32[]{:S(2)}, u32[]{:S(2)}) collective-permute-start(f32[64,256]{1,0:T(8,128)S(1)} %convolution_bitcast_fusion.own_ref), channel_id=1, source_target_pairs={{0,1},{1,0},{2,3},{3,2},{4,5},{5,4},{6,7},{7,6},{8,9},{9,8},{10,11... | collective-permute-start | bytes 196616 | tf_op jit(solution)/shard_map/ppermute | solution.py:33
  14.4 5.1 %copy-start.26 = (bf16[16,1024]{1,0:T(8,128)(2,1)S(1)}, bf16[16,1024]{1,0:T(8,128)(2,1)}, u32[]{:S(2)}) copy-start(bf16[16,1024]{1,0:T(8,128)(2,1)} %unpatchify.1) | copy-start | bytes 98308
  14.4 14.5 %copy-start.28 = (f32[384]{0:T(512)S(1)}, f32[384]{0:T(512)}, u32[]{:S(2)}) copy-start(f32[384]{0:T(512)} %param.8) | copy-start | bytes 4612
  14.4 5.0 %collective-permute-start.1 = (bf16[16,1024]{1,0:T(8,128)(2,1)}, bf16[16,1024]{1,0:T(8,128)(2,1)S(1)}, u32[]{:S(2)}, u32[]{:S(2)}) collective-permute-start(bf16[16,1024]{1,0:T(8,128)(2,1)} %unpatchify.1), channel_id=1, source_target_pairs={{0,16},{2,18},{4,20},{6,22},{8,24},{10,26},{12,28},{14,30},{16,0},... | collective-permute-start | bytes 98312 | tf_op jit(solution)/shard_map/ppermute | solution.py:33
  19.5 10.5 %copy-start.1 = (bf16[2,40,1024]{2,1,0:T(8,128)(2,1)}, bf16[2,40,1024]{2,1,0:T(8,128)(2,1)S(1)}, u32[]{:S(2)}) copy-start(bf16[2,40,1024]{2,1,0:T(8,128)(2,1)S(1)} %get-tuple-element.30.refs_3_.refs_0_) | copy-start | bytes 491524
  19.6 7.2 %collective-permute-start.5 = (bf16[2,40,1024]{2,1,0:T(8,128)(2,1)S(1)}, bf16[2,40,1024]{2,1,0:T(8,128)(2,1)S(1)}, u32[]{:S(2)}, u32[]{:S(2)}) collective-permute-start(bf16[2,40,1024]{2,1,0:T(8,128)(2,1)S(1)} %get-tuple-element.62), channel_id=1, source_target_pairs={{0,12},{2,14},{4,8},{6,10},{8,4},{10,6},{12,0},{14,2},{16,28},{18,... | collective-permute-start | bytes 491528 | tf_op jit(solution)/shard_map/ppermute | solution.py:33
  22.2 6.2 %collective-permute-start.3 = (bf16[2,40,1024]{2,1,0:T(8,128)(2,1)S(1)}, bf16[2,40,1024]{2,1,0:T(8,128)(2,1)S(1)}, u32[]{:S(2)}, u32[]{:S(2)}) collective-permute-start(bf16[2,40,1024]{2,1,0:T(8,128)(2,1)S(1)} %get-tuple-element.63), channel_id=1, source_target_pairs={{0,4},{2,6},{4,0},{6,2},{8,12},{10,14},{12,8},{14,10},{16,20},{18,... | collective-permute-start | bytes 491528 | tf_op jit(solution)/shard_map/ppermute | solution.py:33
  22.7 5.8 %collective-permute-start.4 = (bf16[2,40,1024]{2,1,0:T(8,128)(2,1)S(1)}, bf16[2,40,1024]{2,1,0:T(8,128)(2,1)S(1)}, u32[]{:S(2)}, u32[]{:S(2)}) collective-permute-start(bf16[2,40,1024]{2,1,0:T(8,128)(2,1)S(1)} %get-tuple-element.64), channel_id=1, source_target_pairs={{0,8},{2,10},{4,12},{6,14},{8,0},{10,2},{12,4},{14,6},{16,24},{18,... | collective-permute-start | bytes 491528 | tf_op jit(solution)/shard_map/ppermute | solution.py:33
  23.1 6.4 %collective-permute-start.6 = (bf16[2,40,1024]{2,1,0:T(8,128)(2,1)S(1)}, bf16[2,40,1024]{2,1,0:T(8,128)(2,1)S(1)}, u32[]{:S(2)}, u32[]{:S(2)}) collective-permute-start(bf16[2,40,1024]{2,1,0:T(8,128)(2,1)S(1)} %get-tuple-element.30.refs_3_.refs_0_), channel_id=1, source_target_pairs={{0,2},{2,0},{4,6},{6,4},{8,10},{10,8},{12,14},{14,12},{16,18},{18,... | collective-permute-start | bytes 491528 | tf_op jit(solution)/shard_map/ppermute | solution.py:33
  26.8 3.3 %copy-start.3 = (bf16[2,40,1024]{2,1,0:T(8,128)(2,1)}, bf16[2,40,1024]{2,1,0:T(8,128)(2,1)S(1)}, u32[]{:S(2)}) copy-start(bf16[2,40,1024]{2,1,0:T(8,128)(2,1)S(1)} %collective-permute-done.5.refs_6_.refs_3_) | copy-start | bytes 491524
  26.8 2.7 %collective-permute-start.9 = (bf16[2,40,1024]{2,1,0:T(8,128)(2,1)S(1)}, bf16[2,40,1024]{2,1,0:T(8,128)(2,1)S(1)}, u32[]{:S(2)}, u32[]{:S(2)}) collective-permute-start(bf16[2,40,1024]{2,1,0:T(8,128)(2,1)S(1)} %collective-permute-done.5.refs_6_.refs_3_), channel_id=1, source_target_pairs={{0,2},{2,0},{4,6},{6,4},{8,10},{10,8},{12,14},{14,12},{16,18},{18,... | collective-permute-start | bytes 491528 | tf_op jit(solution)/shard_map/ppermute | solution.py:33
  28.4 1.6 %copy-start.4 = (bf16[2,40,1024]{2,1,0:T(8,128)(2,1)}, bf16[2,40,1024]{2,1,0:T(8,128)(2,1)S(1)}, u32[]{:S(2)}) copy-start(bf16[2,40,1024]{2,1,0:T(8,128)(2,1)S(1)} %collective-permute-done.3.refs_4_.refs_1_) | copy-start | bytes 491524
  28.4 1.4 %collective-permute-start.7 = (bf16[2,40,1024]{2,1,0:T(8,128)(2,1)S(1)}, bf16[2,40,1024]{2,1,0:T(8,128)(2,1)S(1)}, u32[]{:S(2)}, u32[]{:S(2)}) collective-permute-start(bf16[2,40,1024]{2,1,0:T(8,128)(2,1)S(1)} %collective-permute-done.3.refs_4_.refs_1_), channel_id=1, source_target_pairs={{0,2},{2,0},{4,6},{6,4},{8,10},{10,8},{12,14},{14,12},{16,18},{18,... | collective-permute-start | bytes 491528 | tf_op jit(solution)/shard_map/ppermute | solution.py:33
  28.4 1.6 %copy-start.5 = (bf16[2,40,1024]{2,1,0:T(8,128)(2,1)}, bf16[2,40,1024]{2,1,0:T(8,128)(2,1)S(1)}, u32[]{:S(2)}) copy-start(bf16[2,40,1024]{2,1,0:T(8,128)(2,1)S(1)} %collective-permute-done.4.refs_5_.refs_2_) | copy-start | bytes 491524
  28.4 1.6 %collective-permute-start.8 = (bf16[2,40,1024]{2,1,0:T(8,128)(2,1)S(1)}, bf16[2,40,1024]{2,1,0:T(8,128)(2,1)S(1)}, u32[]{:S(2)}, u32[]{:S(2)}) collective-permute-start(bf16[2,40,1024]{2,1,0:T(8,128)(2,1)S(1)} %collective-permute-done.4.refs_5_.refs_2_), channel_id=1, source_target_pairs={{0,2},{2,0},{4,6},{6,4},{8,10},{10,8},{12,14},{14,12},{16,18},{18,... | collective-permute-start | bytes 491528 | tf_op jit(solution)/shard_map/ppermute | solution.py:33
  29.5 0.7 copy-start.7
  42.7 1.7 %collective-permute-start.10 = (bf16[216,384]{1,0:T(8,128)(2,1)}, bf16[216,384]{1,0:T(8,128)(2,1)S(1)}, u32[]{:S(2)}, u32[]{:S(2)}) collective-permute-start(bf16[216,384]{1,0:T(8,128)(2,1)} %get-tuple-element.29), channel_id=1, source_target_pairs={{0,2},{2,0},{4,6},{6,4},{8,10},{10,8},{12,14},{14,12},{16,18},{18,... | collective-permute-start | bytes 497672 | tf_op jit(solution)/shard_map/ppermute | solution.py:33
  45.4 22.0 %copy-start.2 = (bf16[216,384]{1,0:T(8,128)(2,1)}, bf16[216,384]{1,0:T(8,128)(2,1)S(1)}, u32[]{:S(2)}) copy-start(bf16[216,384]{1,0:T(8,128)(2,1)S(1)} %add_convert_fusion) | copy-start | bytes 497668
  45.4 7.0 %collective-permute-start.11 = (bf16[216,384]{1,0:T(8,128)(2,1)S(1)}, bf16[216,384]{1,0:T(8,128)(2,1)S(1)}, u32[]{:S(2)}, u32[]{:S(2)}) collective-permute-start(bf16[216,384]{1,0:T(8,128)(2,1)S(1)} %add_convert_fusion), channel_id=1, source_target_pairs={{0,8},{2,10},{4,12},{6,14},{8,0},{10,2},{12,4},{14,6},{16,24},{18,... | collective-permute-start | bytes 497672 | tf_op jit(solution)/shard_map/ppermute | solution.py:33
  46.4 15.9 %collective-permute-start.15 = (bf16[216,384]{1,0:T(8,128)(2,1)S(1)}, bf16[216,384]{1,0:T(8,128)(2,1)S(1)}, u32[]{:S(2)}, u32[]{:S(2)}) collective-permute-start(bf16[216,384]{1,0:T(8,128)(2,1)S(1)} %add_convert_fusion), channel_id=1, source_target_pairs={{0,24},{2,26},{4,28},{6,30},{8,16},{10,18},{12,20},{14,22},{16,8},... | collective-permute-start | bytes 497672 | tf_op jit(solution)/shard_map/ppermute | solution.py:33
  47.6 16.1 %collective-permute-start.14 = (bf16[216,384]{1,0:T(8,128)(2,1)S(1)}, bf16[216,384]{1,0:T(8,128)(2,1)S(1)}, u32[]{:S(2)}, u32[]{:S(2)}) collective-permute-start(bf16[216,384]{1,0:T(8,128)(2,1)S(1)} %add_convert_fusion), channel_id=1, source_target_pairs={{0,16},{2,18},{4,20},{6,22},{8,24},{10,26},{12,28},{14,30},{16,0},... | collective-permute-start | bytes 497672 | tf_op jit(solution)/shard_map/ppermute | solution.py:33
  49.0 14.8 %collective-permute-start.12 = (bf16[216,384]{1,0:T(8,128)(2,1)S(1)}, bf16[216,384]{1,0:T(8,128)(2,1)S(1)}, u32[]{:S(2)}, u32[]{:S(2)}) collective-permute-start(bf16[216,384]{1,0:T(8,128)(2,1)S(1)} %add_convert_fusion), channel_id=1, source_target_pairs={{0,4},{2,6},{4,0},{6,2},{8,12},{10,14},{12,8},{14,10},{16,20},{18,... | collective-permute-start | bytes 497672 | tf_op jit(solution)/shard_map/ppermute | solution.py:33
  52.5 15.0 %copy-start.13 = (bf16[216,384]{1,0:T(8,128)(2,1)}, bf16[216,384]{1,0:T(8,128)(2,1)S(1)}, u32[]{:S(2)}) copy-start(bf16[216,384]{1,0:T(8,128)(2,1)S(1)} %collective-permute-done.11) | copy-start | bytes 497668
  52.5 11.3 %collective-permute-start.13 = (bf16[216,384]{1,0:T(8,128)(2,1)S(1)}, bf16[216,384]{1,0:T(8,128)(2,1)S(1)}, u32[]{:S(2)}, u32[]{:S(2)}) collective-permute-start(bf16[216,384]{1,0:T(8,128)(2,1)S(1)} %collective-permute-done.11), channel_id=1, source_target_pairs={{0,4},{2,6},{4,0},{6,2},{8,12},{10,14},{12,8},{14,10},{16,20},{18,... | collective-permute-start | bytes 497672 | tf_op jit(solution)/shard_map/ppermute | solution.py:33
  62.3 8.8 %copy-start.11 = (bf16[216,384]{1,0:T(8,128)(2,1)}, bf16[216,384]{1,0:T(8,128)(2,1)S(1)}, u32[]{:S(2)}) copy-start(bf16[216,384]{1,0:T(8,128)(2,1)S(1)} %collective-permute-done.15) | copy-start | bytes 497668
  63.8 7.3 %copy-start.12 = (bf16[216,384]{1,0:T(8,128)(2,1)}, bf16[216,384]{1,0:T(8,128)(2,1)S(1)}, u32[]{:S(2)}) copy-start(bf16[216,384]{1,0:T(8,128)(2,1)S(1)} %collective-permute-done.14) | copy-start | bytes 497668
  63.8 3.7 %copy-start.14 = (bf16[216,384]{1,0:T(8,128)(2,1)}, bf16[216,384]{1,0:T(8,128)(2,1)S(1)}, u32[]{:S(2)}) copy-start(bf16[216,384]{1,0:T(8,128)(2,1)S(1)} %collective-permute-done.12) | copy-start | bytes 497668
  63.8 3.7 %copy-start.15 = (bf16[216,384]{1,0:T(8,128)(2,1)}, bf16[216,384]{1,0:T(8,128)(2,1)S(1)}, u32[]{:S(2)}) copy-start(bf16[216,384]{1,0:T(8,128)(2,1)S(1)} %collective-permute-done.13) | copy-start | bytes 497668
  63.8 1.8 %collective-permute-start.16 = (bf16[216,384]{1,0:T(8,128)(2,1)S(1)}, bf16[216,384]{1,0:T(8,128)(2,1)S(1)}, u32[]{:S(2)}, u32[]{:S(2)}) collective-permute-start(bf16[216,384]{1,0:T(8,128)(2,1)S(1)} %add_convert_fusion), channel_id=1, source_target_pairs={{0,2},{2,0},{4,6},{6,4},{8,10},{10,8},{12,14},{14,12},{16,18},{18,... | collective-permute-start | bytes 497672 | tf_op jit(solution)/shard_map/ppermute | solution.py:33
  63.9 3.0 %collective-permute-start.17 = (bf16[216,384]{1,0:T(8,128)(2,1)S(1)}, bf16[216,384]{1,0:T(8,128)(2,1)S(1)}, u32[]{:S(2)}, u32[]{:S(2)}) collective-permute-start(bf16[216,384]{1,0:T(8,128)(2,1)S(1)} %collective-permute-done.12), channel_id=1, source_target_pairs={{0,2},{2,0},{4,6},{6,4},{8,10},{10,8},{12,14},{14,12},{16,18},{18,... | collective-permute-start | bytes 497672 | tf_op jit(solution)/shard_map/ppermute | solution.py:33
  64.4 2.6 %collective-permute-start.18 = (bf16[216,384]{1,0:T(8,128)(2,1)S(1)}, bf16[216,384]{1,0:T(8,128)(2,1)S(1)}, u32[]{:S(2)}, u32[]{:S(2)}) collective-permute-start(bf16[216,384]{1,0:T(8,128)(2,1)S(1)} %collective-permute-done.11), channel_id=1, source_target_pairs={{0,2},{2,0},{4,6},{6,4},{8,10},{10,8},{12,14},{14,12},{16,18},{18,... | collective-permute-start | bytes 497672 | tf_op jit(solution)/shard_map/ppermute | solution.py:33
  64.5 3.0 %collective-permute-start.19 = (bf16[216,384]{1,0:T(8,128)(2,1)S(1)}, bf16[216,384]{1,0:T(8,128)(2,1)S(1)}, u32[]{:S(2)}, u32[]{:S(2)}) collective-permute-start(bf16[216,384]{1,0:T(8,128)(2,1)S(1)} %collective-permute-done.13), channel_id=1, source_target_pairs={{0,2},{2,0},{4,6},{6,4},{8,10},{10,8},{12,14},{14,12},{16,18},{18,... | collective-permute-start | bytes 497672 | tf_op jit(solution)/shard_map/ppermute | solution.py:33
  64.9 7.1 %collective-permute-start.20 = (bf16[216,384]{1,0:T(8,128)(2,1)S(1)}, bf16[216,384]{1,0:T(8,128)(2,1)S(1)}, u32[]{:S(2)}, u32[]{:S(2)}) collective-permute-start(bf16[216,384]{1,0:T(8,128)(2,1)S(1)} %collective-permute-done.14), channel_id=1, source_target_pairs={{0,4},{2,6},{4,0},{6,2},{8,12},{10,14},{12,8},{14,10},{16,20},{18,... | collective-permute-start | bytes 497672 | tf_op jit(solution)/shard_map/ppermute | solution.py:33
  65.6 1.9 %copy-start.19 = (bf16[216,384]{1,0:T(8,128)(2,1)}, bf16[216,384]{1,0:T(8,128)(2,1)S(1)}, u32[]{:S(2)}) copy-start(bf16[216,384]{1,0:T(8,128)(2,1)S(1)} %collective-permute-done.16) | copy-start | bytes 497668
  65.6 9.0 %collective-permute-start.21 = (bf16[216,384]{1,0:T(8,128)(2,1)S(1)}, bf16[216,384]{1,0:T(8,128)(2,1)S(1)}, u32[]{:S(2)}, u32[]{:S(2)}) collective-permute-start(bf16[216,384]{1,0:T(8,128)(2,1)S(1)} %collective-permute-done.15), channel_id=1, source_target_pairs={{0,4},{2,6},{4,0},{6,2},{8,12},{10,14},{12,8},{14,10},{16,20},{18,... | collective-permute-start | bytes 497672 | tf_op jit(solution)/shard_map/ppermute | solution.py:33
  66.9 8.3 %collective-permute-start.22 = (bf16[216,384]{1,0:T(8,128)(2,1)S(1)}, bf16[216,384]{1,0:T(8,128)(2,1)S(1)}, u32[]{:S(2)}, u32[]{:S(2)}) collective-permute-start(bf16[216,384]{1,0:T(8,128)(2,1)S(1)} %collective-permute-done.14), channel_id=1, source_target_pairs={{0,2},{2,0},{4,6},{6,4},{8,10},{10,8},{12,14},{14,12},{16,18},{18,... | collective-permute-start | bytes 497672 | tf_op jit(solution)/shard_map/ppermute | solution.py:33
  66.9 0.7 copy-start.22
  66.9 8.2 %collective-permute-start.24 = (bf16[216,384]{1,0:T(8,128)(2,1)S(1)}, bf16[216,384]{1,0:T(8,128)(2,1)S(1)}, u32[]{:S(2)}, u32[]{:S(2)}) collective-permute-start(bf16[216,384]{1,0:T(8,128)(2,1)S(1)} %collective-permute-done.15), channel_id=1, source_target_pairs={{0,2},{2,0},{4,6},{6,4},{8,10},{10,8},{12,14},{14,12},{16,18},{18,... | collective-permute-start | bytes 497672 | tf_op jit(solution)/shard_map/ppermute | solution.py:33
  72.0 4.3 %copy-start.16 = (bf16[216,384]{1,0:T(8,128)(2,1)}, bf16[216,384]{1,0:T(8,128)(2,1)S(1)}, u32[]{:S(2)}) copy-start(bf16[216,384]{1,0:T(8,128)(2,1)S(1)} %collective-permute-done.20) | copy-start | bytes 497668
  74.7 1.6 %copy-start.17 = (bf16[216,384]{1,0:T(8,128)(2,1)}, bf16[216,384]{1,0:T(8,128)(2,1)S(1)}, u32[]{:S(2)}) copy-start(bf16[216,384]{1,0:T(8,128)(2,1)S(1)} %collective-permute-done.21) | copy-start | bytes 497668
  74.7 1.4 %collective-permute-start.23 = (bf16[216,384]{1,0:T(8,128)(2,1)S(1)}, bf16[216,384]{1,0:T(8,128)(2,1)S(1)}, u32[]{:S(2)}, u32[]{:S(2)}) collective-permute-start(bf16[216,384]{1,0:T(8,128)(2,1)S(1)} %collective-permute-done.20), channel_id=1, source_target_pairs={{0,2},{2,0},{4,6},{6,4},{8,10},{10,8},{12,14},{14,12},{16,18},{18,... | collective-permute-start | bytes 497672 | tf_op jit(solution)/shard_map/ppermute | solution.py:33
  74.7 1.6 %collective-permute-start.25 = (bf16[216,384]{1,0:T(8,128)(2,1)S(1)}, bf16[216,384]{1,0:T(8,128)(2,1)S(1)}, u32[]{:S(2)}, u32[]{:S(2)}) collective-permute-start(bf16[216,384]{1,0:T(8,128)(2,1)S(1)} %collective-permute-done.21), channel_id=1, source_target_pairs={{0,2},{2,0},{4,6},{6,4},{8,10},{10,8},{12,14},{14,12},{16,18},{18,... | collective-permute-start | bytes 497672 | tf_op jit(solution)/shard_map/ppermute | solution.py:33
  75.2 1.1 %copy-start.18 = (bf16[216,384]{1,0:T(8,128)(2,1)}, bf16[216,384]{1,0:T(8,128)(2,1)S(1)}, u32[]{:S(2)}) copy-start(bf16[216,384]{1,0:T(8,128)(2,1)S(1)} %collective-permute-done.22) | copy-start | bytes 497668
  75.2 1.1 %copy-start.20 = (bf16[216,384]{1,0:T(8,128)(2,1)}, bf16[216,384]{1,0:T(8,128)(2,1)S(1)}, u32[]{:S(2)}) copy-start(bf16[216,384]{1,0:T(8,128)(2,1)S(1)} %collective-permute-done.24) | copy-start | bytes 497668
  76.1 0.7 copy-start.24
  (7 other events, 4.6 us)

commit v7 on v6

--- a/solution.py
+++ b/solution.py
@@ -78,12 +78,15 @@
 
 
 def fetch(piece_refs, mask_lists, slot_ref, sems):
+    count = slot_ref.shape[1]
     copies = []
     for index, (piece_ref, masks) in enumerate(zip(piece_refs, mask_lists)):
         for position, mask in enumerate(masks):
             copies.append(
                 pltpu.make_async_copy(
-                    piece_ref.at[position], slot_ref.at[mask], sems.at[index * len(masks) + position]
+                    piece_ref.at[position, pl.ds(0, count)],
+                    slot_ref.at[mask],
+                    sems.at[index * len(masks) + position],
                 )
             )
     for copy in copies:
@@ -241,14 +244,16 @@
     send_ref[...] = sum_ref[pl.ds(send_at, padded), :][:real_rows].astype(BF16)
 
 
-def decode_kernel(frames, rows, slabs, masks, me_ref, gain_ref, entry_ref, conv_hbm, *refs):
+def decode_kernel(frame, frames, rows, slabs, masks, me_ref, gain_ref, entry_ref, conv_hbm, *refs):
+    other_refs, refs = (refs[: frames - 1], refs[frames - 1 :]) if frame == 0 else ((), refs)
+    sources = range(max(0, frame - 2), frame + 1)
     piece_refs, refs = refs[: len(masks)], refs[len(masks) :]
     out_ref, slots, stack_ref, hid_ref, flat_ref, act_ref, wide_gain, conv_ref, sems, sem = refs[:10]
     weight_refs = refs[10:]
-    live = conv_ref.shape[0] // 9
-    load = pltpu.make_async_copy(conv_hbm.at[pl.ds((3 - live) * 9, live * 9)], conv_ref, sem)
+    taps = conv_ref.shape[0]
+    copies = fetch(piece_refs, masks, slots, sems)
+    load = pltpu.make_async_copy(conv_hbm.at[pl.ds(27 - taps, taps)], conv_ref, sem)
     load.start()
-    copies = fetch(piece_refs, masks, slots, sems)
     me = me_ref[0]
     height = slabs * rows
     load_entry(entry_ref, gain_ref, weight_refs, wide_gain)
@@ -256,27 +261,30 @@
         copy.wait()
     place_latent(slots, stack_ref, me, me, 1, frames, rows, slabs)
     ext = rows + 2
-    for frame in range(frames):
-        hid_ref[...] = hidden_rows(stack_ref, weight_refs[frame], frame, 0, ext)
+    for position, source in enumerate(sources):
+        hid_ref[...] = hidden_rows(stack_ref, weight_refs[position], source, 0, ext)
         activate_rows(hid_ref, wide_gain, flat_ref, 0, me * rows - 1, ext, height)
         for row in range(ext):
             tile = flat_ref[:, row * LANES : (row + 1) * LANES].astype(F32)
             for tap in range(3):
-                act_ref[frame, tap, :, row * LANES : (row + 1) * LANES] = shifted(tile, tap).astype(BF16)
+                act_ref[position, tap, :, row * LANES : (row + 1) * LANES] = shifted(tile, tap).astype(BF16)
     load.wait()
-    for frame in range(frames):
-        kernels = []
-        inputs = []
-        for depth in range(max(0, 2 - frame), 3):
-            for row_tap in range(3):
-                for col_tap in range(3):
-                    kernels.append(conv_ref[(depth - (3 - live)) * 9 + row_tap * 3 + col_tap])
-                    inputs.append(
-                        act_ref[frame + depth - 2, col_tap, :, row_tap * LANES : (row_tap + rows) * LANES]
-                    )
-        total = dot(jnp.concatenate(kernels, axis=1), jnp.concatenate(inputs, axis=0))
-        for row in range(rows):
-            out_ref[:, frame, row, :] = total[:, row * LANES : (row + 1) * LANES].astype(BF16)
+    kernels = []
+    inputs = []
+    for position in range(len(sources)):
+        for row_tap in range(3):
+            for col_tap in range(3):
+                kernels.append(conv_ref[position * 9 + row_tap * 3 + col_tap])
+                inputs.append(act_ref[position, col_tap, :, row_tap * LANES : (row_tap + rows) * LANES])
+    total = dot(jnp.concatenate(kernels, axis=1), jnp.concatenate(inputs, axis=0))
+    for row in range(rows):
+        tile = total[:, row * LANES : (row + 1) * LANES].astype(BF16)
+        if frame == 0:
+            out_ref[:, 0, row, :] = tile
+        else:
+            out_ref[:, row, :] = tile
+    for index, other_ref in enumerate(other_refs):
+        out_ref[:, index + 1] = other_ref[...]
 
 
 def blank_kernel(blank, out_hbm, zero_ref, sems):
@@ -295,21 +303,28 @@
 def finish_kernel(pieces, me_ref, *refs):
     count = len(pieces)
     piece_refs = refs[:count]
-    out_hbm, wide_ref, sems = refs[count + 1 :]
+    out_hbm, narrow_ref, wide_ref, in_sems, out_sems = refs[count + 1 :]
     me = me_ref[0]
     channels = wide_ref.shape[2]
-    copies = []
+    loads = [
+        pltpu.make_async_copy(piece_refs[index], narrow_ref.at[index], in_sems.at[index])
+        for index in range(count)
+    ]
+    for load in loads:
+        load.start()
+    stores = []
     for index, mask in enumerate(pieces):
         source = me ^ mask
-        wide_ref[index] = piece_refs[index][...].astype(F32)
+        loads[index].wait()
+        wide_ref[index] = narrow_ref[index].astype(F32)
         at = pl.multiple_of((source >> 1) * channels, 8)
-        copy = pltpu.make_async_copy(
-            wide_ref.at[index], out_hbm.at[2 - (source & 1), :, pl.ds(at, channels), :], sems.at[index]
+        store = pltpu.make_async_copy(
+            wide_ref.at[index], out_hbm.at[2 - (source & 1), :, pl.ds(at, channels), :], out_sems.at[index]
         )
-        copy.start()
-        copies.append(copy)
-    for copy in copies:
-        copy.wait()
+        store.start()
+        stores.append(store)
+    for store in stores:
+        store.wait()
 
 
 def per_device(attn_out, w_proj, norm_gain, entry_weight, conv_weight, cotangent):
@@ -436,32 +451,29 @@
     beside = xor_permute(block, "seq", 2)
     conv = conv_weight.transpose(1, 2, 3, 0, 4).reshape(27, out_channels, channels)
 
-    held = lax.optimization_barrier((block, direct[0], *pieces))[2:]
-    decoded = pl.pallas_call(
-        functools.partial(decode_kernel, frames, rows, slabs, masks),
-        out_shape=jax.ShapeDtypeStruct((out_channels, frames, rows, width), BF16),
-        in_specs=[smem(), vmem(), vmem(), hbm] + [hbm] * len(pieces),
-        out_specs=vmem(),
-        scratch_shapes=[
-            pltpu.VMEM(slot_shape, BF16),
-            pltpu.VMEM((frames, 3 * latent_width, (rows + 4) * width), BF16),
-            pltpu.VMEM((channels, (rows + 2) * width), F32),
-            pltpu.VMEM((channels, (rows + 2) * width), BF16),
-            pltpu.VMEM((frames, 3, channels, (rows + 2) * width), BF16),
-            pltpu.VMEM((channels, LANES), F32),
-            pltpu.VMEM((live * 9, out_channels, channels), BF16),
-            pltpu.SemaphoreType.DMA((slabs,)),
-            pltpu.SemaphoreType.DMA(()),
-        ]
-        + weights,
-        compiler_params=params(),
-        name="decode",
-    )(me, gain, entry, conv, *held)
-    nearest = xor_permute(direct[0], "seq", 2)
-    gated = lax.optimization_barrier((decoded, block, beside, nearest, *direct))
-    decoded, block, beside, nearest = gated[:4]
-    direct = list(gated[4:])
-    across = [nearest] + [xor_permute(piece, "seq", 2) for piece in direct[1:]]
+    def decode(frame, held, others=()):
+        count = min(3, frame + 1)
+        last = (frames,) if frame == 0 else ()
+        return pl.pallas_call(
+            functools.partial(decode_kernel, frame, frames, rows, slabs, masks),
+            out_shape=jax.ShapeDtypeStruct((out_channels,) + last + (rows, width), BF16),
+            in_specs=[smem(), vmem(), vmem(), hbm] + [vmem()] * len(others) + [hbm] * len(pieces),
+            out_specs=vmem(),
+            scratch_shapes=[
+                pltpu.VMEM((slabs, latent_width, frames * rows * width), BF16),
+                pltpu.VMEM((frames, 3 * latent_width, (rows + 4) * width), BF16),
+                pltpu.VMEM((channels, (rows + 2) * width), F32),
+                pltpu.VMEM((channels, (rows + 2) * width), BF16),
+                pltpu.VMEM((count, 3, channels, (rows + 2) * width), BF16),
+                pltpu.VMEM((channels, LANES), F32),
+                pltpu.VMEM((count * 9, out_channels, channels), BF16),
+                pltpu.SemaphoreType.DMA((slabs,)),
+                pltpu.SemaphoreType.DMA(()),
+            ]
+            + weights[max(0, frame - 2) : frame + 1],
+            compiler_params=params(),
+            name="decode",
+        )(me, gain, entry, conv, *others, *held)
 
     shape = (9, pad_channels, channels)
 
@@ -469,15 +481,16 @@
         return pl.pallas_call(
             functools.partial(finish_kernel, sources),
             out_shape=jax.ShapeDtypeStruct(grad_shape, F32),
-            in_specs=[smem()] + [vmem()] * len(parts) + [hbm],
+            in_specs=[smem()] + [hbm] * (len(parts) + 1),
             out_specs=hbm,
             scratch_shapes=[
+                pltpu.VMEM((len(parts),) + shape, BF16),
                 pltpu.VMEM((len(parts),) + shape, F32),
+                pltpu.SemaphoreType.DMA((len(parts),)),
                 pltpu.SemaphoreType.DMA((len(parts),)),
             ],
             input_output_aliases={len(parts) + 1: 0},
             compiler_params=params(),
-            cost_estimate=cost(0, len(parts) * real_rows * channels * 6),
             name="finish",
         )(me, *[p.reshape(shape) for p in parts], grad)
 
@@ -485,14 +498,34 @@
         parts = [p for p, _ in group] + [xor_permute(p, "seq", 1) for p, _ in group]
         return parts, [m for _, m in group] + [m ^ 1 for _, m in group]
 
-    early = [(block, 0), (beside, 2), (direct[0], columns[0]), (across[0], columns[0] ^ 2)]
-    grad = finish(*both_cores(early), grad)
-    if columns[1:]:
-        gated = lax.optimization_barrier((grad, decoded, *across[1:]))
-        grad, decoded, across[1:] = gated[0], gated[1], list(gated[2:])
-        late = []
-        for position, mask in enumerate(columns[1:]):
-            late += [(direct[position + 1], mask), (across[position + 1], mask ^ 2)]
+    nearest = xor_permute(direct[0], "seq", 2)
+    held = lax.optimization_barrier((direct[0], *pieces))[1:]
+    decoded = [decode(frame, held) for frame in range(1, frames)]
+    gate = decoded[-1] if frames > 1 else block
+    half = max(1, len(direct[1:]) // 2)
+    gated = lax.optimization_barrier((gate, block, beside, nearest, *direct[: 1 + half]))
+    if frames > 1:
+        decoded[-1] = gated[0]
+    block, beside, nearest = gated[1:4]
+    direct[: 1 + half] = gated[4:]
+    second = direct[1 : 1 + half]
+    across = [xor_permute(piece, "seq", 2) for piece in second]
+    grad = finish(
+        *both_cores(
+            [(block, 0), (beside, 2), (direct[0], columns[0]), (nearest, columns[0] ^ 2)]
+        ),
+        grad,
+    )
+    third = list(lax.optimization_barrier((gate, *direct[1 + half :])))[1:]
+    across = across + [xor_permute(piece, "seq", 2) for piece in third]
+    held = lax.optimization_barrier((grad, *pieces))[1:]
+    decoded = decode(0, held, decoded)
+    gated = lax.optimization_barrier((decoded, *across))
+    decoded, across = gated[0], gated[1:]
+    late = []
+    for mask, piece, swapped in zip(columns[1:], second + third, across):
+        late += [(piece, mask), (swapped, mask ^ 2)]
+    if late:
         grad = finish(*both_cores(late), grad)
     if pad_channels != chip_channels:
         grad = grad.reshape(27, chips, pad_channels, channels)[:, :, :chip_channels]

time: 80.5 us -> 82.7 us (1.027)
  waiting for transfers between devices: 22.1 us -> 19.2 us
  starting transfers between devices: 19.5 us -> 22 us
  Pallas kernels: 30.2 us -> 32.4 us
    pallas_call x1 -> x2, Pallas kernels: 8.98 us -> 12 us  [decode(): pl.pallas_call(functools.partial(decode_kernel, frame, frames, rows, slab...]
    ppermute x26, waiting for transfers between devices: 22.1 us -> 19.2 us  [xor_permute(): lax.ppermute(x, axis, [(i, i ^ mask) for i in range(lax.axis_size(axis))])]
    ppermute x26, starting transfers between devices: 19.5 us -> 22 us  [xor_permute(): lax.ppermute(x, axis, [(i, i ^ mask) for i in range(lax.axis_size(axis))])]
  transfers between devices with their start and end apart: 26 -> 26, of which waited for: 13 -> 10; matrix products, arithmetic and copies ran while one was open for 3% -> 3% of each run, Pallas kernels for 19% -> 22%
where the time goes in v7:
time: 82.7 us; the launch traced here: 82.2 us
  Pallas kernels  32.4 us (39%)
  starting transfers between devices  22 us (27%)
  waiting for transfers between devices  19.2 us (23%)
  local copies, waits for them, and re-layouts  4.63 us (6%)
  matrix products  1.48 us (2%)
  between operations  1.28 us (2%)
  other arithmetic  1.1 us (1%)
    ppermute x26, starting transfers between devices, xor_permute(): lax.ppermute(x, axis, [(i, i ^ mask) for i in range(lax.axis_size(axis))])  22 us
    ppermute x26, waiting for transfers between devices, xor_permute(): lax.ppermute(x, axis, [(i, i ^ mask) for i in range(lax.axis_size(axis))])  19.2 us
    pallas_call x2, Pallas kernels, decode(): pl.pallas_call(functools.partial(decode_kernel, frame, frames, rows, slab...  12 us
    pallas_call x1, Pallas kernels, per_device(): pl.pallas_call(functools.partial(gradient_kernel, frames, rows, slabs, ma...  12 us
    pallas_call x2, Pallas kernels, finish(): pl.pallas_call(functools.partial(finish_kernel, sources), out_shape=jax.S...  5.13 us
    unnamed x58, local copies, waits for them, and re-layouts  2.59 us
    pallas_call x1, Pallas kernels, per_device(): pl.pallas_call(functools.partial(unpatchify_kernel, frames, tok_rows, tok...  1.66 us
  transfers between devices with their start and end apart: 26, of which 10 were waited for; matrix products, arithmetic and copies ran while one was open for 3% of the time, Pallas kernels for 22%

profile of v7, /device:TPU:0, one launch (start us, length us, event | category | flops | bytes accessed | tf_op | source)
XLA Modules:
  0.0 82.2 jit_solution(3646744653410436247)
XLA Ops:
  0.7 1.4 %reshape.77 = bf16[8,24,1024]{2,1,0:T(8,128)(2,1)S(1)} reshape(bf16[192,2,4,128]{3,2,1,0:T(4,128)(2,1)} %param.11) | data formatting | bytes 786432 | tf_op jit(solution)/shard_map/reshape | solution.py:353
  2.2 4.1 %collective-permute-start.2 = (bf16[4,24,1024]{2,1,0:T(8,128)(2,1)S(1)}, bf16[4,24,1024]{2,1,0:T(8,128)(2,1)S(1)}, u32[]{:S(2)}, u32[]{:S(2)}) collective-permute-start(bf16[4,24,1024]{2,1,0:T(8,128)(2,1)S(1)} %pad_maximum_fusion), channel_id=1, source_target_pairs={{0,16},{2,18},{4,20},{6,22},{8,24},{10,26},{12,28},{14,30},{16,0},... | collective-permute-start | bytes 589832 | tf_op jit(solution)/shard_map/ppermute | solution.py:33
  6.3 1.5 %convolution_bitcast_fusion.own_ref = f32[64,256]{1,0:T(8,128)S(1)} fusion(bf16[256,2560]{1,0:T(8,128)(2,1)S(1)} %bitcast.33, bf16[2560,64]{0,1:T(8,128)(2,1)} %param.7), kind=kOutput, calls=%fused_computation | convolution fusion | flops 83886080 | bytes 1703936 | tf_op jit(solution)/shard_map/dot_general | solution.py:369
  7.8 1.6 %collective-permute-start = (f32[64,256]{1,0:T(8,128)S(1)}, f32[64,256]{1,0:T(8,128)S(1)}, u32[]{:S(2)}, u32[]{:S(2)}) collective-permute-start(f32[64,256]{1,0:T(8,128)S(1)} %convolution_bitcast_fusion.own_ref), channel_id=1, source_target_pairs={{0,1},{1,0},{2,3},{3,2},{4,5},{5,4},{6,7},{7,6},{8,9},{9,8},{10,11... | collective-permute-start | bytes 196616 | tf_op jit(solution)/shard_map/ppermute | solution.py:33
  9.3 2.8 %collective-permute-done.other_ref = f32[64,256]{1,0:T(8,128)S(1)} collective-permute-done((f32[64,256]{1,0:T(8,128)S(1)}, f32[64,256]{1,0:T(8,128)S(1)}, u32[]{:S(2)}, u32[]{:S(2)}) %collective-permute-start) | collective-permute-done | bytes 65568 | tf_op jit(solution)/shard_map/ppermute | solution.py:33
  12.1 0.6 copy-done.27
  12.7 1.7 %unpatchify.1 = bf16[16,1024]{1,0:T(8,128)(2,1)} custom-call(f32[64,256]{1,0:T(8,128)} %copy-done.10, f32[64,256]{1,0:T(8,128)} %copy-done.27), custom_call_target="tpu_custom_call" | custom-call | tf_op jit(solution)/shard_map/unpatchify/pallas_call | solution.py:384
  14.4 1.6 %blank.1.refs_8_ = f32[3,9,192,384]{3,2,1,0:T(8,128)} custom-call(), custom_call_target="tpu_custom_call" | custom-call | bytes 2654208 | tf_op jit(solution)/shard_map/blank/pallas_call | solution.py:396
  16.0 3.4 %collective-permute-done.1 = bf16[16,1024]{1,0:T(8,128)(2,1)S(1)} collective-permute-done((bf16[16,1024]{1,0:T(8,128)(2,1)}, bf16[16,1024]{1,0:T(8,128)(2,1)S(1)}, u32[]{:S(2)}, u32[]{:S(2)}) %collective-permute-start.1) | collective-permute-done | bytes 32800 | tf_op jit(solution)/shard_map/ppermute | solution.py:33
  19.5 0.1 maximum_maximum_fusion.3
  19.5 1.6 %collective-permute-start.3 = (bf16[2,40,1024]{2,1,0:T(8,128)(2,1)S(1)}, bf16[2,40,1024]{2,1,0:T(8,128)(2,1)S(1)}, u32[]{:S(2)}, u32[]{:S(2)}) collective-permute-start(bf16[2,40,1024]{2,1,0:T(8,128)(2,1)S(1)} %get-tuple-element.77), channel_id=1, source_target_pairs={{0,4},{2,6},{4,0},{6,2},{8,12},{10,14},{12,8},{14,10},{16,20},{18,... | collective-permute-start | bytes 491528 | tf_op jit(solution)/shard_map/ppermute | solution.py:33
  21.1 1.6 %collective-permute-start.4 = (bf16[2,40,1024]{2,1,0:T(8,128)(2,1)S(1)}, bf16[2,40,1024]{2,1,0:T(8,128)(2,1)S(1)}, u32[]{:S(2)}, u32[]{:S(2)}) collective-permute-start(bf16[2,40,1024]{2,1,0:T(8,128)(2,1)S(1)} %get-tuple-element.78), channel_id=1, source_target_pairs={{0,8},{2,10},{4,12},{6,14},{8,0},{10,2},{12,4},{14,6},{16,24},{18,... | collective-permute-start | bytes 491528 | tf_op jit(solution)/shard_map/ppermute | solution.py:33
  22.7 0.4 collective-permute-start.5
  23.1 3.6 %collective-permute-done.3.refs_4_.refs_1_.refs_2_ = bf16[2,40,1024]{2,1,0:T(8,128)(2,1)S(1)} collective-permute-done((bf16[2,40,1024]{2,1,0:T(8,128)(2,1)S(1)}, bf16[2,40,1024]{2,1,0:T(8,128)(2,1)S(1)}, u32[]{:S(2)}, u32[]{:S(2)}) %collective-permute-start.3) | collective-permute-done | bytes 163872 | tf_op jit(solution)/shard_map/ppermute | solution.py:33
  26.7 0.5 collective-permute-start.8
  27.2 1.7 %collective-permute-done.5.refs_6_.refs_3_.refs_4_ = bf16[2,40,1024]{2,1,0:T(8,128)(2,1)S(1)} collective-permute-done((bf16[2,40,1024]{2,1,0:T(8,128)(2,1)S(1)}, bf16[2,40,1024]{2,1,0:T(8,128)(2,1)S(1)}, u32[]{:S(2)}, u32[]{:S(2)}) %collective-permute-start.5) | collective-permute-done | bytes 163872 | tf_op jit(solution)/shard_map/ppermute | solution.py:33
  28.9 0.6 reshape.74.refs_1_.gain_ref
  29.6 0.7 collective-permute-done.9.refs_10_.refs_7_.refs_8_
  30.4 0.6 copy-done.8
  31.0 12.0 %gradient.1 = (f32[216,384]{1,0:T(8,128)}, bf16[216,384]{1,0:T(8,128)(2,1)}) custom-call(s32[1]{0:T(128)} %bitcast.refs_0_.me_ref, f32[1,384]{1,0:T(1,128)} %reshape.74.refs_1_.gain_ref, bf16[432,384]{1,0:T(8,128)(2,1)} %bitcast.37, bf16[2,40,1024]{2,1,0:T(8,128)(2,1)} %copy-done.1, bf16[2,40,1024]{2,1,0:T(8,128)(2,1)} %copy-done.2, ...), custom_call_target="tpu_custom_call" | custom-call | tf_op jit(solution)/shard_map/gradient/pallas_call | solution.py:422
  43.0 0.2 collective-permute-start.10
  43.2 1.5 %collective-permute-done.10 = bf16[216,384]{1,0:T(8,128)(2,1)S(1)} collective-permute-done((bf16[216,384]{1,0:T(8,128)(2,1)}, bf16[216,384]{1,0:T(8,128)(2,1)S(1)}, u32[]{:S(2)}, u32[]{:S(2)}) %collective-permute-start.10) | collective-permute-done | bytes 165920 | tf_op jit(solution)/shard_map/ppermute | solution.py:33
  44.7 1.0 %add_convert_fusion = bf16[216,384]{1,0:T(8,128)(2,1)S(1)} fusion(f32[216,384]{1,0:T(8,128)} %get-tuple-element.35, bf16[216,384]{1,0:T(8,128)(2,1)S(1)} %collective-permute-done.10), kind=kLoop, calls=%fused_computation.1 | loop fusion | flops 248832 | bytes 663552 | tf_op jit(solution)/shard_map/convert_element_type | solution.py:447
  45.7 0.9 %collective-permute-start.11 = (bf16[216,384]{1,0:T(8,128)(2,1)S(1)}, bf16[216,384]{1,0:T(8,128)(2,1)S(1)}, u32[]{:S(2)}, u32[]{:S(2)}) collective-permute-start(bf16[216,384]{1,0:T(8,128)(2,1)S(1)} %add_convert_fusion), channel_id=1, source_target_pairs={{0,8},{2,10},{4,12},{6,14},{8,0},{10,2},{12,4},{14,6},{16,24},{18,... | collective-permute-start | bytes 497672 | tf_op jit(solution)/shard_map/ppermute | solution.py:33
  46.6 1.5 %collective-permute-start.12 = (bf16[216,384]{1,0:T(8,128)(2,1)S(1)}, bf16[216,384]{1,0:T(8,128)(2,1)S(1)}, u32[]{:S(2)}, u32[]{:S(2)}) collective-permute-start(bf16[216,384]{1,0:T(8,128)(2,1)S(1)} %add_convert_fusion), channel_id=1, source_target_pairs={{0,4},{2,6},{4,0},{6,2},{8,12},{10,14},{12,8},{14,10},{16,20},{18,... | collective-permute-start | bytes 497672 | tf_op jit(solution)/shard_map/ppermute | solution.py:33
  48.1 1.4 %collective-permute-start.14 = (bf16[216,384]{1,0:T(8,128)(2,1)S(1)}, bf16[216,384]{1,0:T(8,128)(2,1)S(1)}, u32[]{:S(2)}, u32[]{:S(2)}) collective-permute-start(bf16[216,384]{1,0:T(8,128)(2,1)S(1)} %add_convert_fusion), channel_id=1, source_target_pairs={{0,16},{2,18},{4,20},{6,22},{8,24},{10,26},{12,28},{14,30},{16,0},... | collective-permute-start | bytes 497672 | tf_op jit(solution)/shard_map/ppermute | solution.py:33
  49.5 4.1 %collective-permute-done.11 = bf16[216,384]{1,0:T(8,128)(2,1)S(1)} collective-permute-done((bf16[216,384]{1,0:T(8,128)(2,1)S(1)}, bf16[216,384]{1,0:T(8,128)(2,1)S(1)}, u32[]{:S(2)}, u32[]{:S(2)}) %collective-permute-start.11) | collective-permute-done | bytes 165920 | tf_op jit(solution)/shard_map/ppermute | solution.py:33
  53.5 1.0 %collective-permute-start.13 = (bf16[216,384]{1,0:T(8,128)(2,1)S(1)}, bf16[216,384]{1,0:T(8,128)(2,1)S(1)}, u32[]{:S(2)}, u32[]{:S(2)}) collective-permute-start(bf16[216,384]{1,0:T(8,128)(2,1)S(1)} %collective-permute-done.11), channel_id=1, source_target_pairs={{0,4},{2,6},{4,0},{6,2},{8,12},{10,14},{12,8},{14,10},{16,20},{18,... | collective-permute-start | bytes 497672 | tf_op jit(solution)/shard_map/ppermute | solution.py:33
  54.6 3.5 %collective-permute-start.20 = (bf16[216,384]{1,0:T(8,128)(2,1)S(1)}, bf16[216,384]{1,0:T(8,128)(2,1)S(1)}, u32[]{:S(2)}, u32[]{:S(2)}) collective-permute-start(bf16[216,384]{1,0:T(8,128)(2,1)S(1)} %add_convert_fusion), channel_id=1, source_target_pairs={{0,24},{2,26},{4,28},{6,30},{8,16},{10,18},{12,20},{14,22},{16,8},... | collective-permute-start | bytes 497672 | tf_op jit(solution)/shard_map/ppermute | solution.py:33
  58.1 6.6 %decode.2.refs_0_ = bf16[192,4,128]{2,1,0:T(4,128)(2,1)} custom-call(s32[1]{0:T(128)} %bitcast.refs_0_.me_ref, f32[1,384]{1,0:T(1,128)} %reshape.74.refs_1_.gain_ref, bf16[432,384]{1,0:T(8,128)(2,1)} %bitcast.38, bf16[27,192,384]{2,1,0:T(8,128)(2,1)} %bitcast.35, bf16[2,40,1024]{2,1,0:T(8,128)(2,1)} %copy-done.1, bf16[2,40,1024]{2,1,0:T(8,128)(2,1)} %copy-done.2, ...), custom_call_target="tpu_custom_call" | custom-call | tf_op jit(solution)/shard_map/decode/pallas_call | solution.py:457
  64.8 0.1 collective-permute-start.15
  64.9 0.5 collective-permute-start.16
  65.4 0.1 collective-permute-start.17
  65.4 0.4 collective-permute-start.18
  65.9 0.4 collective-permute-done.15
  66.2 1.7 %collective-permute-start.19 = (bf16[216,384]{1,0:T(8,128)(2,1)S(1)}, bf16[216,384]{1,0:T(8,128)(2,1)S(1)}, u32[]{:S(2)}, u32[]{:S(2)}) collective-permute-start(bf16[216,384]{1,0:T(8,128)(2,1)S(1)} %collective-permute-done.14), channel_id=1, source_target_pairs={{0,4},{2,6},{4,0},{6,2},{8,12},{10,14},{12,8},{14,10},{16,20},{18,... | collective-permute-start | bytes 497672 | tf_op jit(solution)/shard_map/ppermute | solution.py:33
  67.9 0.5 collective-permute-start.22
  68.5 0.1 copy-done.21
  68.6 0.5 copy-done.23
  69.1 2.6 %finish.2.refs_8_ = f32[3,9,192,384]{3,2,1,0:T(8,128)} custom-call(s32[1]{0:T(128)} %bitcast.refs_0_.me_ref, bf16[9,24,384]{2,1,0:T(8,128)(2,1)} %bitcast.40, bf16[9,24,384]{2,1,0:T(8,128)(2,1)} %bitcast.44, bf16[9,24,384]{2,1,0:T(8,128)(2,1)} %bitcast.43, bf16[9,24,384]{2,1,0:T(8,128)(2,1)} %bitcast.47, ...), custom_call_target="tpu_custom_call", output_to_operand_aliasing={{}: (9, {})} | custom-call | tf_op jit(solution)/shard_map/finish/pallas_call | solution.py:481
  71.7 5.4 %decode.3 = bf16[192,2,4,128]{3,2,1,0:T(4,128)(2,1)} custom-call(s32[1]{0:T(128)} %bitcast.refs_0_.me_ref, f32[1,384]{1,0:T(1,128)} %reshape.74.refs_1_.gain_ref, bf16[432,384]{1,0:T(8,128)(2,1)} %bitcast.39, bf16[27,192,384]{2,1,0:T(8,128)(2,1)} %bitcast.36, bf16[192,4,128]{2,1,0:T(4,128)(2,1)} %decode.2.refs_0_, bf16[2,40,1024]{2,1,0:T(8,128)(2,1)} %copy-done.1, ...), custom_call_target="tpu_custom_call" | custom-call | tf_op jit(solution)/shard_map/decode/pallas_call | solution.py:457
  77.1 0.1 collective-permute-start.23
  77.3 0.4 collective-permute-start.25
  77.7 0.9 %collective-permute-done.23 = bf16[216,384]{1,0:T(8,128)(2,1)S(1)} collective-permute-done((bf16[216,384]{1,0:T(8,128)(2,1)S(1)}, bf16[216,384]{1,0:T(8,128)(2,1)S(1)}, u32[]{:S(2)}, u32[]{:S(2)}) %collective-permute-start.23) | collective-permute-done | bytes 165920 | tf_op jit(solution)/shard_map/ppermute | solution.py:33
  78.6 0.2 collective-permute-done.25
  78.9 0.4 copy-done.24
  79.3 0.2 copy-done.25
  79.5 2.6 %finish.3 = f32[3,9,192,384]{3,2,1,0:T(8,128)} custom-call(s32[1]{0:T(128)} %bitcast.refs_0_.me_ref, bf16[9,24,384]{2,1,0:T(8,128)(2,1)} %bitcast.41, bf16[9,24,384]{2,1,0:T(8,128)(2,1)} %bitcast.46, bf16[9,24,384]{2,1,0:T(8,128)(2,1)} %bitcast.42, bf16[9,24,384]{2,1,0:T(8,128)(2,1)} %bitcast.45, ...), custom_call_target="tpu_custom_call", output_to_operand_aliasing={{}: (9, {})} | custom-call | tf_op jit(solution)/shard_map/finish/pallas_call | solution.py:481
  (77 shorter events, 0.3 us)
Async XLA Ops:
  0.6 5.7 %copy-start = (bf16[2,2,64,2560]{3,2,1,0:T(8,128)(2,1)S(1)}, bf16[2,2,64,2560]{3,2,1,0:T(8,128)(2,1)}, u32[]{:S(2)}) copy-start(bf16[2,2,64,2560]{3,2,1,0:T(8,128)(2,1)} %param.6) | copy-start | bytes 3932164
  2.2 17.3 %collective-permute-start.2 = (bf16[4,24,1024]{2,1,0:T(8,128)(2,1)S(1)}, bf16[4,24,1024]{2,1,0:T(8,128)(2,1)S(1)}, u32[]{:S(2)}, u32[]{:S(2)}) collective-permute-start(bf16[4,24,1024]{2,1,0:T(8,128)(2,1)S(1)} %pad_maximum_fusion), channel_id=1, source_target_pairs={{0,16},{2,18},{4,20},{6,22},{8,24},{10,26},{12,28},{14,30},{16,0},... | collective-permute-start | bytes 589832 | tf_op jit(solution)/shard_map/ppermute | solution.py:33
  7.8 4.3 %copy-start.10 = (f32[64,256]{1,0:T(8,128)}, f32[64,256]{1,0:T(8,128)S(1)}, u32[]{:S(2)}) copy-start(f32[64,256]{1,0:T(8,128)S(1)} %convolution_bitcast_fusion.own_ref) | copy-start | bytes 196612
  7.8 4.3 %collective-permute-start = (f32[64,256]{1,0:T(8,128)S(1)}, f32[64,256]{1,0:T(8,128)S(1)}, u32[]{:S(2)}, u32[]{:S(2)}) collective-permute-start(f32[64,256]{1,0:T(8,128)S(1)} %convolution_bitcast_fusion.own_ref), channel_id=1, source_target_pairs={{0,1},{1,0},{2,3},{3,2},{4,5},{5,4},{6,7},{7,6},{8,9},{9,8},{10,11... | collective-permute-start | bytes 196616 | tf_op jit(solution)/shard_map/ppermute | solution.py:33
  14.4 5.1 %copy-start.26 = (bf16[16,1024]{1,0:T(8,128)(2,1)S(1)}, bf16[16,1024]{1,0:T(8,128)(2,1)}, u32[]{:S(2)}) copy-start(bf16[16,1024]{1,0:T(8,128)(2,1)} %unpatchify.1) | copy-start | bytes 98308
  14.4 14.5 %copy-start.28 = (f32[384]{0:T(512)S(1)}, f32[384]{0:T(512)}, u32[]{:S(2)}) copy-start(f32[384]{0:T(512)} %param.8) | copy-start | bytes 4612
  14.4 5.0 %collective-permute-start.1 = (bf16[16,1024]{1,0:T(8,128)(2,1)}, bf16[16,1024]{1,0:T(8,128)(2,1)S(1)}, u32[]{:S(2)}, u32[]{:S(2)}) collective-permute-start(bf16[16,1024]{1,0:T(8,128)(2,1)} %unpatchify.1), channel_id=1, source_target_pairs={{0,16},{2,18},{4,20},{6,22},{8,24},{10,26},{12,28},{14,30},{16,0},... | collective-permute-start | bytes 98312 | tf_op jit(solution)/shard_map/ppermute | solution.py:33
  19.5 10.8 %copy-start.1 = (bf16[2,40,1024]{2,1,0:T(8,128)(2,1)}, bf16[2,40,1024]{2,1,0:T(8,128)(2,1)S(1)}, u32[]{:S(2)}) copy-start(bf16[2,40,1024]{2,1,0:T(8,128)(2,1)S(1)} %get-tuple-element.51.refs_3_.refs_0_.refs_1_) | copy-start | bytes 491524
  19.5 7.1 %collective-permute-start.3 = (bf16[2,40,1024]{2,1,0:T(8,128)(2,1)S(1)}, bf16[2,40,1024]{2,1,0:T(8,128)(2,1)S(1)}, u32[]{:S(2)}, u32[]{:S(2)}) collective-permute-start(bf16[2,40,1024]{2,1,0:T(8,128)(2,1)S(1)} %get-tuple-element.77), channel_id=1, source_target_pairs={{0,4},{2,6},{4,0},{6,2},{8,12},{10,14},{12,8},{14,10},{16,20},{18,... | collective-permute-start | bytes 491528 | tf_op jit(solution)/shard_map/ppermute | solution.py:33
  21.1 5.6 %collective-permute-start.4 = (bf16[2,40,1024]{2,1,0:T(8,128)(2,1)S(1)}, bf16[2,40,1024]{2,1,0:T(8,128)(2,1)S(1)}, u32[]{:S(2)}, u32[]{:S(2)}) collective-permute-start(bf16[2,40,1024]{2,1,0:T(8,128)(2,1)S(1)} %get-tuple-element.78), channel_id=1, source_target_pairs={{0,8},{2,10},{4,12},{6,14},{8,0},{10,2},{12,4},{14,6},{16,24},{18,... | collective-permute-start | bytes 491528 | tf_op jit(solution)/shard_map/ppermute | solution.py:33
  22.7 6.2 %collective-permute-start.5 = (bf16[2,40,1024]{2,1,0:T(8,128)(2,1)S(1)}, bf16[2,40,1024]{2,1,0:T(8,128)(2,1)S(1)}, u32[]{:S(2)}, u32[]{:S(2)}) collective-permute-start(bf16[2,40,1024]{2,1,0:T(8,128)(2,1)S(1)} %get-tuple-element.76), channel_id=1, source_target_pairs={{0,12},{2,14},{4,8},{6,10},{8,4},{10,6},{12,0},{14,2},{16,28},{18,... | collective-permute-start | bytes 491528 | tf_op jit(solution)/shard_map/ppermute | solution.py:33
  23.1 6.5 %collective-permute-start.6 = (bf16[2,40,1024]{2,1,0:T(8,128)(2,1)S(1)}, bf16[2,40,1024]{2,1,0:T(8,128)(2,1)S(1)}, u32[]{:S(2)}, u32[]{:S(2)}) collective-permute-start(bf16[2,40,1024]{2,1,0:T(8,128)(2,1)S(1)} %get-tuple-element.51.refs_3_.refs_0_.refs_1_), channel_id=1, source_target_pairs={{0,2},{2,0},{4,6},{6,4},{8,10},{10,8},{12,14},{14,12},{16,18},{18,... | collective-permute-start | bytes 491528 | tf_op jit(solution)/shard_map/ppermute | solution.py:33
  26.7 3.6 %copy-start.2 = (bf16[2,40,1024]{2,1,0:T(8,128)(2,1)}, bf16[2,40,1024]{2,1,0:T(8,128)(2,1)S(1)}, u32[]{:S(2)}) copy-start(bf16[2,40,1024]{2,1,0:T(8,128)(2,1)S(1)} %collective-permute-done.3.refs_4_.refs_1_.refs_2_) | copy-start | bytes 491524
  26.7 2.9 %collective-permute-start.7 = (bf16[2,40,1024]{2,1,0:T(8,128)(2,1)S(1)}, bf16[2,40,1024]{2,1,0:T(8,128)(2,1)S(1)}, u32[]{:S(2)}, u32[]{:S(2)}) collective-permute-start(bf16[2,40,1024]{2,1,0:T(8,128)(2,1)S(1)} %collective-permute-done.3.refs_4_.refs_1_.refs_2_), channel_id=1, source_target_pairs={{0,2},{2,0},{4,6},{6,4},{8,10},{10,8},{12,14},{14,12},{16,18},{18,... | collective-permute-start | bytes 491528 | tf_op jit(solution)/shard_map/ppermute | solution.py:33
  26.7 3.6 %copy-start.3 = (bf16[2,40,1024]{2,1,0:T(8,128)(2,1)}, bf16[2,40,1024]{2,1,0:T(8,128)(2,1)S(1)}, u32[]{:S(2)}) copy-start(bf16[2,40,1024]{2,1,0:T(8,128)(2,1)S(1)} %collective-permute-done.4.refs_5_.refs_2_.refs_3_) | copy-start | bytes 491524
  26.7 2.9 %collective-permute-start.8 = (bf16[2,40,1024]{2,1,0:T(8,128)(2,1)S(1)}, bf16[2,40,1024]{2,1,0:T(8,128)(2,1)S(1)}, u32[]{:S(2)}, u32[]{:S(2)}) collective-permute-start(bf16[2,40,1024]{2,1,0:T(8,128)(2,1)S(1)} %collective-permute-done.4.refs_5_.refs_2_.refs_3_), channel_id=1, source_target_pairs={{0,2},{2,0},{4,6},{6,4},{8,10},{10,8},{12,14},{14,12},{16,18},{18,... | collective-permute-start | bytes 491528 | tf_op jit(solution)/shard_map/ppermute | solution.py:33
  28.9 1.4 %copy-start.4 = (bf16[2,40,1024]{2,1,0:T(8,128)(2,1)}, bf16[2,40,1024]{2,1,0:T(8,128)(2,1)S(1)}, u32[]{:S(2)}) copy-start(bf16[2,40,1024]{2,1,0:T(8,128)(2,1)S(1)} %collective-permute-done.5.refs_6_.refs_3_.refs_4_) | copy-start | bytes 491524
  28.9 1.4 %collective-permute-start.9 = (bf16[2,40,1024]{2,1,0:T(8,128)(2,1)S(1)}, bf16[2,40,1024]{2,1,0:T(8,128)(2,1)S(1)}, u32[]{:S(2)}, u32[]{:S(2)}) collective-permute-start(bf16[2,40,1024]{2,1,0:T(8,128)(2,1)S(1)} %collective-permute-done.5.refs_6_.refs_3_.refs_4_), channel_id=1, source_target_pairs={{0,2},{2,0},{4,6},{6,4},{8,10},{10,8},{12,14},{14,12},{16,18},{18,... | collective-permute-start | bytes 491528 | tf_op jit(solution)/shard_map/ppermute | solution.py:33
  29.6 0.8 copy-start.5
  29.6 0.8 copy-start.6
  29.6 0.8 copy-start.7
  43.0 1.7 %collective-permute-start.10 = (bf16[216,384]{1,0:T(8,128)(2,1)}, bf16[216,384]{1,0:T(8,128)(2,1)S(1)}, u32[]{:S(2)}, u32[]{:S(2)}) collective-permute-start(bf16[216,384]{1,0:T(8,128)(2,1)} %get-tuple-element.36), channel_id=1, source_target_pairs={{0,2},{2,0},{4,6},{6,4},{8,10},{10,8},{12,14},{14,12},{16,18},{18,... | collective-permute-start | bytes 497672 | tf_op jit(solution)/shard_map/ppermute | solution.py:33
  45.7 22.7 %copy-start.9 = (bf16[216,384]{1,0:T(8,128)(2,1)}, bf16[216,384]{1,0:T(8,128)(2,1)S(1)}, u32[]{:S(2)}) copy-start(bf16[216,384]{1,0:T(8,128)(2,1)S(1)} %add_convert_fusion) | copy-start | bytes 497668
  45.7 7.8 %collective-permute-start.11 = (bf16[216,384]{1,0:T(8,128)(2,1)S(1)}, bf16[216,384]{1,0:T(8,128)(2,1)S(1)}, u32[]{:S(2)}, u32[]{:S(2)}) collective-permute-start(bf16[216,384]{1,0:T(8,128)(2,1)S(1)} %add_convert_fusion), channel_id=1, source_target_pairs={{0,8},{2,10},{4,12},{6,14},{8,0},{10,2},{12,4},{14,6},{16,24},{18,... | collective-permute-start | bytes 497672 | tf_op jit(solution)/shard_map/ppermute | solution.py:33
  46.6 18.1 %collective-permute-start.12 = (bf16[216,384]{1,0:T(8,128)(2,1)S(1)}, bf16[216,384]{1,0:T(8,128)(2,1)S(1)}, u32[]{:S(2)}, u32[]{:S(2)}) collective-permute-start(bf16[216,384]{1,0:T(8,128)(2,1)S(1)} %add_convert_fusion), channel_id=1, source_target_pairs={{0,4},{2,6},{4,0},{6,2},{8,12},{10,14},{12,8},{14,10},{16,20},{18,... | collective-permute-start | bytes 497672 | tf_op jit(solution)/shard_map/ppermute | solution.py:33
  48.1 16.6 %collective-permute-start.14 = (bf16[216,384]{1,0:T(8,128)(2,1)S(1)}, bf16[216,384]{1,0:T(8,128)(2,1)S(1)}, u32[]{:S(2)}, u32[]{:S(2)}) collective-permute-start(bf16[216,384]{1,0:T(8,128)(2,1)S(1)} %add_convert_fusion), channel_id=1, source_target_pairs={{0,16},{2,18},{4,20},{6,22},{8,24},{10,26},{12,28},{14,30},{16,0},... | collective-permute-start | bytes 497672 | tf_op jit(solution)/shard_map/ppermute | solution.py:33
  53.5 14.9 %copy-start.13 = (bf16[216,384]{1,0:T(8,128)(2,1)}, bf16[216,384]{1,0:T(8,128)(2,1)S(1)}, u32[]{:S(2)}) copy-start(bf16[216,384]{1,0:T(8,128)(2,1)S(1)} %collective-permute-done.11) | copy-start | bytes 497668
  53.5 11.2 %collective-permute-start.13 = (bf16[216,384]{1,0:T(8,128)(2,1)S(1)}, bf16[216,384]{1,0:T(8,128)(2,1)S(1)}, u32[]{:S(2)}, u32[]{:S(2)}) collective-permute-start(bf16[216,384]{1,0:T(8,128)(2,1)S(1)} %collective-permute-done.11), channel_id=1, source_target_pairs={{0,4},{2,6},{4,0},{6,2},{8,12},{10,14},{12,8},{14,10},{16,20},{18,... | collective-permute-start | bytes 497672 | tf_op jit(solution)/shard_map/ppermute | solution.py:33
  54.6 11.3 %collective-permute-start.20 = (bf16[216,384]{1,0:T(8,128)(2,1)S(1)}, bf16[216,384]{1,0:T(8,128)(2,1)S(1)}, u32[]{:S(2)}, u32[]{:S(2)}) collective-permute-start(bf16[216,384]{1,0:T(8,128)(2,1)S(1)} %add_convert_fusion), channel_id=1, source_target_pairs={{0,24},{2,26},{4,28},{6,30},{8,16},{10,18},{12,20},{14,22},{16,8},... | collective-permute-start | bytes 497672 | tf_op jit(solution)/shard_map/ppermute | solution.py:33
  64.7 3.7 %copy-start.14 = (bf16[216,384]{1,0:T(8,128)(2,1)}, bf16[216,384]{1,0:T(8,128)(2,1)S(1)}, u32[]{:S(2)}) copy-start(bf16[216,384]{1,0:T(8,128)(2,1)S(1)} %collective-permute-done.12) | copy-start | bytes 497668
  64.7 6.9 %copy-start.11 = (bf16[216,384]{1,0:T(8,128)(2,1)}, bf16[216,384]{1,0:T(8,128)(2,1)S(1)}, u32[]{:S(2)}) copy-start(bf16[216,384]{1,0:T(8,128)(2,1)S(1)} %collective-permute-done.14) | copy-start | bytes 497668
  64.8 3.7 %copy-start.17 = (bf16[216,384]{1,0:T(8,128)(2,1)}, bf16[216,384]{1,0:T(8,128)(2,1)S(1)}, u32[]{:S(2)}) copy-start(bf16[216,384]{1,0:T(8,128)(2,1)S(1)} %collective-permute-done.13) | copy-start | bytes 497668
  64.8 1.5 %collective-permute-start.15 = (bf16[216,384]{1,0:T(8,128)(2,1)S(1)}, bf16[216,384]{1,0:T(8,128)(2,1)S(1)}, u32[]{:S(2)}, u32[]{:S(2)}) collective-permute-start(bf16[216,384]{1,0:T(8,128)(2,1)S(1)} %add_convert_fusion), channel_id=1, source_target_pairs={{0,2},{2,0},{4,6},{6,4},{8,10},{10,8},{12,14},{14,12},{16,18},{18,... | collective-permute-start | bytes 497672 | tf_op jit(solution)/shard_map/ppermute | solution.py:33
  64.9 3.0 %collective-permute-start.16 = (bf16[216,384]{1,0:T(8,128)(2,1)S(1)}, bf16[216,384]{1,0:T(8,128)(2,1)S(1)}, u32[]{:S(2)}, u32[]{:S(2)}) collective-permute-start(bf16[216,384]{1,0:T(8,128)(2,1)S(1)} %collective-permute-done.12), channel_id=1, source_target_pairs={{0,2},{2,0},{4,6},{6,4},{8,10},{10,8},{12,14},{14,12},{16,18},{18,... | collective-permute-start | bytes 497672 | tf_op jit(solution)/shard_map/ppermute | solution.py:33
  65.4 2.6 %collective-permute-start.17 = (bf16[216,384]{1,0:T(8,128)(2,1)S(1)}, bf16[216,384]{1,0:T(8,128)(2,1)S(1)}, u32[]{:S(2)}, u32[]{:S(2)}) collective-permute-start(bf16[216,384]{1,0:T(8,128)(2,1)S(1)} %collective-permute-done.11), channel_id=1, source_target_pairs={{0,2},{2,0},{4,6},{6,4},{8,10},{10,8},{12,14},{14,12},{16,18},{18,... | collective-permute-start | bytes 497672 | tf_op jit(solution)/shard_map/ppermute | solution.py:33
  65.4 3.0 %collective-permute-start.18 = (bf16[216,384]{1,0:T(8,128)(2,1)S(1)}, bf16[216,384]{1,0:T(8,128)(2,1)S(1)}, u32[]{:S(2)}, u32[]{:S(2)}) collective-permute-start(bf16[216,384]{1,0:T(8,128)(2,1)S(1)} %collective-permute-done.13), channel_id=1, source_target_pairs={{0,2},{2,0},{4,6},{6,4},{8,10},{10,8},{12,14},{14,12},{16,18},{18,... | collective-permute-start | bytes 497672 | tf_op jit(solution)/shard_map/ppermute | solution.py:33
  65.9 5.8 %copy-start.12 = (bf16[216,384]{1,0:T(8,128)(2,1)}, bf16[216,384]{1,0:T(8,128)(2,1)S(1)}, u32[]{:S(2)}) copy-start(bf16[216,384]{1,0:T(8,128)(2,1)S(1)} %collective-permute-done.20) | copy-start | bytes 497668
  65.9 11.2 %collective-permute-start.21 = (bf16[216,384]{1,0:T(8,128)(2,1)S(1)}, bf16[216,384]{1,0:T(8,128)(2,1)S(1)}, u32[]{:S(2)}, u32[]{:S(2)}) collective-permute-start(bf16[216,384]{1,0:T(8,128)(2,1)S(1)} %collective-permute-done.20), channel_id=1, source_target_pairs={{0,4},{2,6},{4,0},{6,2},{8,12},{10,14},{12,8},{14,10},{16,20},{18,... | collective-permute-start | bytes 497672 | tf_op jit(solution)/shard_map/ppermute | solution.py:33
  66.2 2.2 %copy-start.20 = (bf16[216,384]{1,0:T(8,128)(2,1)}, bf16[216,384]{1,0:T(8,128)(2,1)S(1)}, u32[]{:S(2)}) copy-start(bf16[216,384]{1,0:T(8,128)(2,1)S(1)} %collective-permute-done.15) | copy-start | bytes 497668
  66.2 10.9 %collective-permute-start.19 = (bf16[216,384]{1,0:T(8,128)(2,1)S(1)}, bf16[216,384]{1,0:T(8,128)(2,1)S(1)}, u32[]{:S(2)}, u32[]{:S(2)}) collective-permute-start(bf16[216,384]{1,0:T(8,128)(2,1)S(1)} %collective-permute-done.14), channel_id=1, source_target_pairs={{0,4},{2,6},{4,0},{6,2},{8,12},{10,14},{12,8},{14,10},{16,20},{18,... | collective-permute-start | bytes 497672 | tf_op jit(solution)/shard_map/ppermute | solution.py:33
  67.9 9.8 %collective-permute-start.24 = (bf16[216,384]{1,0:T(8,128)(2,1)S(1)}, bf16[216,384]{1,0:T(8,128)(2,1)S(1)}, u32[]{:S(2)}, u32[]{:S(2)}) collective-permute-start(bf16[216,384]{1,0:T(8,128)(2,1)S(1)} %collective-permute-done.20), channel_id=1, source_target_pairs={{0,2},{2,0},{4,6},{6,4},{8,10},{10,8},{12,14},{14,12},{16,18},{18,... | collective-permute-start | bytes 497672 | tf_op jit(solution)/shard_map/ppermute | solution.py:33
  67.9 9.8 %collective-permute-start.22 = (bf16[216,384]{1,0:T(8,128)(2,1)S(1)}, bf16[216,384]{1,0:T(8,128)(2,1)S(1)}, u32[]{:S(2)}, u32[]{:S(2)}) collective-permute-start(bf16[216,384]{1,0:T(8,128)(2,1)S(1)} %collective-permute-done.14), channel_id=1, source_target_pairs={{0,2},{2,0},{4,6},{6,4},{8,10},{10,8},{12,14},{14,12},{16,18},{18,... | collective-permute-start | bytes 497672 | tf_op jit(solution)/shard_map/ppermute | solution.py:33
  77.1 1.7 %copy-start.15 = (bf16[216,384]{1,0:T(8,128)(2,1)}, bf16[216,384]{1,0:T(8,128)(2,1)S(1)}, u32[]{:S(2)}) copy-start(bf16[216,384]{1,0:T(8,128)(2,1)S(1)} %collective-permute-done.21) | copy-start | bytes 497668
  77.1 1.7 %copy-start.16 = (bf16[216,384]{1,0:T(8,128)(2,1)}, bf16[216,384]{1,0:T(8,128)(2,1)S(1)}, u32[]{:S(2)}) copy-start(bf16[216,384]{1,0:T(8,128)(2,1)S(1)} %collective-permute-done.19) | copy-start | bytes 497668
  77.1 1.5 %collective-permute-start.23 = (bf16[216,384]{1,0:T(8,128)(2,1)S(1)}, bf16[216,384]{1,0:T(8,128)(2,1)S(1)}, u32[]{:S(2)}, u32[]{:S(2)}) collective-permute-start(bf16[216,384]{1,0:T(8,128)(2,1)S(1)} %collective-permute-done.19), channel_id=1, source_target_pairs={{0,2},{2,0},{4,6},{6,4},{8,10},{10,8},{12,14},{14,12},{16,18},{18,... | collective-permute-start | bytes 497672 | tf_op jit(solution)/shard_map/ppermute | solution.py:33
  77.3 1.6 %collective-permute-start.25 = (bf16[216,384]{1,0:T(8,128)(2,1)S(1)}, bf16[216,384]{1,0:T(8,128)(2,1)S(1)}, u32[]{:S(2)}, u32[]{:S(2)}) collective-permute-start(bf16[216,384]{1,0:T(8,128)(2,1)S(1)} %collective-permute-done.21), channel_id=1, source_target_pairs={{0,2},{2,0},{4,6},{6,4},{8,10},{10,8},{12,14},{14,12},{16,18},{18,... | collective-permute-start | bytes 497672 | tf_op jit(solution)/shard_map/ppermute | solution.py:33
  77.7 1.1 %copy-start.18 = (bf16[216,384]{1,0:T(8,128)(2,1)}, bf16[216,384]{1,0:T(8,128)(2,1)S(1)}, u32[]{:S(2)}) copy-start(bf16[216,384]{1,0:T(8,128)(2,1)S(1)} %collective-permute-done.24) | copy-start | bytes 497668
  77.7 1.1 %copy-start.19 = (bf16[216,384]{1,0:T(8,128)(2,1)}, bf16[216,384]{1,0:T(8,128)(2,1)S(1)}, u32[]{:S(2)}) copy-start(bf16[216,384]{1,0:T(8,128)(2,1)S(1)} %collective-permute-done.22) | copy-start | bytes 497668
  (7 other events, 4.6 us)

commit v8 on v6

--- a/solution.py
+++ b/solution.py
@@ -77,17 +77,21 @@
     return jnp.where(lane == LANES - 1, 0.0, pltpu.roll(tile, LANES - 1, 1))
 
 
-def fetch(piece_refs, mask_lists, slot_ref, sems):
+def fetch(mixed_refs, near_refs, masks, lat_slots, cot_slots, sems):
     copies = []
-    for index, (piece_ref, masks) in enumerate(zip(piece_refs, mask_lists)):
-        for position, mask in enumerate(masks):
-            copies.append(
-                pltpu.make_async_copy(
-                    piece_ref.at[position], slot_ref.at[mask], sems.at[index * len(masks) + position]
-                )
-            )
-    for copy in copies:
-        copy.start()
+
+    def load(source, target):
+        copies.append(pltpu.make_async_copy(source, target, sems.at[len(copies)]))
+        copies[-1].start()
+
+    latent_width = lat_slots.shape[1]
+    for mixed_ref, (first, second) in zip(mixed_refs, masks):
+        load(mixed_ref.at[pl.ds(0, latent_width)], lat_slots.at[first])
+        load(mixed_ref.at[pl.ds(latent_width, latent_width)], lat_slots.at[second])
+    for mixed_ref, near_ref, (first, second) in zip(mixed_refs, near_refs, masks):
+        channels = cot_slots.shape[1]
+        load(near_ref, cot_slots.at[first])
+        load(mixed_ref.at[pl.ds(2 * latent_width, channels)], cot_slots.at[second])
     return copies
 
 
@@ -105,7 +109,7 @@
         for frame in range(frames):
             for row in needed:
                 at = (frame * rows + row) * LANES
-                tile = slot_ref[source, :latent_width, at : at + LANES].astype(F32)
+                tile = slot_ref[source, :, at : at + LANES].astype(F32)
                 if offset in (-1, slab_count):
                     tile = tile * inside
                 to = (offset * rows + row + 2) * LANES
@@ -148,10 +152,8 @@
             act_ref[chunk, pl.ds(at, LANES)] = (half + half * jnp.tanh(half)).astype(BF16)
 
 
-def place_cotangent(
-    slot_ref, flat_ref, out_ref, me, first_slab, slab_count, frames, rows, pad_channels, skip
-):
-    channels = slot_ref.shape[1] - skip
+def place_cotangent(slot_ref, flat_ref, out_ref, me, first_slab, slab_count, frames, rows, pad_channels):
+    channels = slot_ref.shape[1]
     half_rows = slab_count * rows
     group = 3 * pad_channels
     padded = out_ref.shape[0] // frames
@@ -163,7 +165,7 @@
         for frame in range(frames):
             for row in range(rows):
                 at = (frame * rows + row) * LANES
-                tile = slot_ref[source, skip:, at : at + LANES].astype(F32)
+                tile = slot_ref[source, :, at : at + LANES].astype(F32)
                 if pad_channels != channels:
                     tile = jnp.concatenate(
                         [tile, jnp.zeros((pad_channels - channels, LANES), F32)], axis=0
@@ -185,11 +187,12 @@
 def gradient_kernel(frames, rows, slabs, masks, real_rows, pad_channels, *refs):
     me_ref, gain_ref, entry_ref = refs[:3]
     refs = refs[3:]
-    piece_refs, refs = refs[: len(masks)], refs[len(masks) :]
-    keep_ref, send_ref, slots, stack_ref, flat_ref, cot_ref = refs[:6]
-    hid_a, hid_b, act_a, act_b, sum_ref, wide_gain, sems = refs[6:13]
-    weight_refs = refs[13:]
-    copies = fetch(piece_refs, masks, slots, sems)
+    count = len(masks)
+    mixed_refs, near_refs, refs = refs[:count], refs[count : 2 * count], refs[2 * count :]
+    keep_ref, send_ref, lat_slots, cot_slots, stack_ref, flat_ref, cot_ref = refs[:7]
+    hid_a, hid_b, act_a, act_b, sum_ref, wide_gain, sems = refs[7:14]
+    weight_refs = refs[14:]
+    copies = fetch(mixed_refs, near_refs, masks, lat_slots, cot_slots, sems)
     me = me_ref[0]
     core = me & 1
     slab_count = slabs // 2
@@ -205,13 +208,14 @@
     acts = (act_a, act_b)
     load_entry(entry_ref, gain_ref, weight_refs, wide_gain)
     sum_ref[...] = jnp.zeros_like(sum_ref)
-    for copy in copies:
+    for copy in copies[: 2 * count]:
         copy.wait()
-    place_latent(slots, stack_ref, me, first_slab, slab_count, frames, rows, slabs)
+    place_latent(lat_slots, stack_ref, me, first_slab, slab_count, frames, rows, slabs)
+    for copy in copies[2 * count :]:
+        copy.wait()
     hid_a[...] = hidden_rows(stack_ref, weight_refs[0], 0, 0, ext)
     place_cotangent(
-        slots, flat_ref, cot_ref, me, first_slab, slab_count, frames, rows, pad_channels,
-        stack_ref.shape[1] // 3,
+        cot_slots, flat_ref, cot_ref, me, first_slab, slab_count, frames, rows, pad_channels
     )
     for frame in range(frames):
 
@@ -248,7 +252,7 @@
     live = conv_ref.shape[0] // 9
     load = pltpu.make_async_copy(conv_hbm.at[pl.ds((3 - live) * 9, live * 9)], conv_ref, sem)
     load.start()
-    copies = fetch(piece_refs, masks, slots, sems)
+    copies = fetch(piece_refs, (), masks, slots, slots, sems)
     me = me_ref[0]
     height = slabs * rows
     load_entry(entry_ref, gain_ref, weight_refs, wide_gain)
@@ -295,21 +299,28 @@
 def finish_kernel(pieces, me_ref, *refs):
     count = len(pieces)
     piece_refs = refs[:count]
-    out_hbm, wide_ref, sems = refs[count + 1 :]
+    out_hbm, narrow_ref, wide_ref, in_sems, out_sems = refs[count + 1 :]
     me = me_ref[0]
     channels = wide_ref.shape[2]
-    copies = []
+    loads = [
+        pltpu.make_async_copy(piece_refs[index], narrow_ref.at[index], in_sems.at[index])
+        for index in range(count)
+    ]
+    for load in loads:
+        load.start()
+    stores = []
     for index, mask in enumerate(pieces):
         source = me ^ mask
-        wide_ref[index] = piece_refs[index][...].astype(F32)
+        loads[index].wait()
+        wide_ref[index] = narrow_ref[index].astype(F32)
         at = pl.multiple_of((source >> 1) * channels, 8)
-        copy = pltpu.make_async_copy(
-            wide_ref.at[index], out_hbm.at[2 - (source & 1), :, pl.ds(at, channels), :], sems.at[index]
+        store = pltpu.make_async_copy(
+            wide_ref.at[index], out_hbm.at[2 - (source & 1), :, pl.ds(at, channels), :], out_sems.at[index]
         )
-        copy.start()
-        copies.append(copy)
-    for copy in copies:
-        copy.wait()
+        store.start()
+        stores.append(store)
+    for store in stores:
+        store.wait()
 
 
 def per_device(attn_out, w_proj, norm_gain, entry_weight, conv_weight, cotangent):
@@ -335,18 +346,16 @@
     top = slabs // 2
     rest = [m for m in range(2, top, 2)]
 
+    chip = me_index // 2
     flat = cotangent.reshape(chips, chip_channels, frames * rows * width)
-    chip = me_index // 2
 
     def wanted(side):
-        return jnp.stack(
-            [
-                lax.dynamic_index_in_dim(flat, chip ^ ((m ^ side) // 2), 0, keepdims=False)
-                for m in [0] + rest
-            ]
-        )
-
-    near, far = wanted(0), wanted(top)
+        return [
+            lax.dynamic_index_in_dim(flat, chip ^ ((m ^ side) // 2), 0, keepdims=False)
+            for m in [0] + rest
+        ]
+
+    near, far = wanted(0), jnp.stack(wanted(top))
     got = xor_permute(far, "seq", top)
 
     attn_out = lax.optimization_barrier((attn_out, far))[0]
@@ -392,17 +401,22 @@
     )()
 
     across = xor_permute(latent, "seq", top)
+    nears = [near[0]] + [xor_permute(near[i + 1], "seq", m) for i, m in enumerate(rest)]
     across, grad = lax.optimization_barrier((across, grad))
-    latents = jnp.stack([latent, across])
-    pieces = []
+    got, *nears = lax.optimization_barrier((got, *nears))
+    latents = jnp.concatenate([latent, across], axis=0)
+    mixed = []
     masks = []
     for position, mask in enumerate([0] + rest):
-        both = jnp.concatenate([latents, jnp.stack([near[position], got[position]])], axis=1)
-        pieces.append(both if mask == 0 else xor_permute(both, "seq", mask))
+        both = jnp.concatenate([latents, got[position]], axis=0)
+        mixed.append(both if mask == 0 else xor_permute(both, "seq", mask))
         masks.append([mask, mask ^ top])
-    pieces = pieces + [xor_permute(p, "seq", 1) for p in pieces]
+    swapped = xor_permute(jnp.stack(nears), "seq", 1)
+    nears = nears + [swapped[i] for i in range(len(nears))]
+    mixed = mixed + [xor_permute(p, "seq", 1) for p in mixed]
     masks = masks + [[m ^ 1 for m in pair] for pair in masks]
-    slot_shape = (slabs, latent_width + chip_channels, frames * rows * width)
+    lat_slots = (slabs, latent_width, frames * rows * width)
+    cot_slots = (slabs, chip_channels, frames * rows * width)
 
     keep, send = pl.pallas_call(
         functools.partial(gradient_kernel, frames, rows, slabs, masks, real_rows, pad_channels),
@@ -410,10 +424,11 @@
             jax.ShapeDtypeStruct((real_rows, channels), F32),
             jax.ShapeDtypeStruct((real_rows, channels), BF16),
         ),
-        in_specs=[smem(), vmem(), vmem()] + [hbm] * len(pieces),
+        in_specs=[smem(), vmem(), vmem()] + [hbm] * (len(mixed) + len(nears)),
         out_specs=(vmem(), vmem()),
         scratch_shapes=[
-            pltpu.VMEM(slot_shape, BF16),
+            pltpu.VMEM(lat_slots, BF16),
+            pltpu.VMEM(cot_slots, BF16),
             pltpu.VMEM((frames, 3 * latent_width, (half_rows + 4) * width), BF16),
             pltpu.VMEM((frames, 3 * pad_channels, (half_rows + 4) * width), F32),
             pltpu.VMEM((frames * padded, lanes), BF16),
@@ -423,12 +438,12 @@
             pltpu.VMEM((channels, lanes), BF16),
             pltpu.VMEM((live * padded, channels), F32),
             pltpu.VMEM((channels, LANES), F32),
-            pltpu.SemaphoreType.DMA((slabs,)),
+            pltpu.SemaphoreType.DMA((2 * slabs,)),
         ]
         + weights,
         compiler_params=params(),
         name="gradient",
-    )(me, gain, entry, *pieces)
+    )(me, gain, entry, *mixed, *nears)
     block = (keep + xor_permute(send, "seq", 1).astype(F32)).astype(BF16)
 
     columns = [m for m in range(4, slabs, 4)]
@@ -436,14 +451,14 @@
     beside = xor_permute(block, "seq", 2)
     conv = conv_weight.transpose(1, 2, 3, 0, 4).reshape(27, out_channels, channels)
 
-    held = lax.optimization_barrier((block, direct[0], *pieces))[2:]
+    held = lax.optimization_barrier((block, direct[0], *mixed))[2:]
     decoded = pl.pallas_call(
         functools.partial(decode_kernel, frames, rows, slabs, masks),
         out_shape=jax.ShapeDtypeStruct((out_channels, frames, rows, width), BF16),
-        in_specs=[smem(), vmem(), vmem(), hbm] + [hbm] * len(pieces),
+        in_specs=[smem(), vmem(), vmem(), hbm] + [hbm] * len(mixed),
         out_specs=vmem(),
         scratch_shapes=[
-            pltpu.VMEM(slot_shape, BF16),
+            pltpu.VMEM(lat_slots, BF16),
             pltpu.VMEM((frames, 3 * latent_width, (rows + 4) * width), BF16),
             pltpu.VMEM((channels, (rows + 2) * width), F32),
             pltpu.VMEM((channels, (rows + 2) * width), BF16),
@@ -469,15 +484,16 @@
         return pl.pallas_call(
             functools.partial(finish_kernel, sources),
             out_shape=jax.ShapeDtypeStruct(grad_shape, F32),
-            in_specs=[smem()] + [vmem()] * len(parts) + [hbm],
+            in_specs=[smem()] + [hbm] * (len(parts) + 1),
             out_specs=hbm,
             scratch_shapes=[
+                pltpu.VMEM((len(parts),) + shape, BF16),
                 pltpu.VMEM((len(parts),) + shape, F32),
+                pltpu.SemaphoreType.DMA((len(parts),)),
                 pltpu.SemaphoreType.DMA((len(parts),)),
             ],
             input_output_aliases={len(parts) + 1: 0},
             compiler_params=params(),
-            cost_estimate=cost(0, len(parts) * real_rows * channels * 6),
             name="finish",
         )(me, *[p.reshape(shape) for p in parts], grad)
 

time: 80.5 us -> 82.6 us (1.026)
  starting transfers between devices: 19.5 us -> 27.2 us
  waiting for transfers between devices: 22.1 us -> 16.7 us
  Pallas kernels: 30.2 us -> 29.1 us
    ppermute x26 -> x30, starting transfers between devices: 19.5 us -> 27.2 us  [xor_permute(): lax.ppermute(x, axis, [(i, i ^ mask) for i in range(lax.axis_size(axis))])]
    ppermute x26 -> x30, waiting for transfers between devices: 22.1 us -> 16.7 us  [xor_permute(): lax.ppermute(x, axis, [(i, i ^ mask) for i in range(lax.axis_size(axis))])]
    unnamed x58 -> x66, local copies, waits for them, and re-layouts: 2.62 us -> 2.6 us
  transfers between devices with their start and end apart: 26 -> 30, of which waited for: 13 -> 12; matrix products, arithmetic and copies ran while one was open for 3% -> 3% of each run, Pallas kernels for 19% -> 18%
where the time goes in v8:
time: 82.6 us; the launch traced here: 82.1 us
  Pallas kernels  29.1 us (35%)
  starting transfers between devices  27.2 us (33%)
  waiting for transfers between devices  16.7 us (20%)
  local copies, waits for them, and re-layouts  5.28 us (6%)
  matrix products  1.48 us (2%)
  between operations  1.31 us (2%)
  other arithmetic  1.11 us (1%)
    ppermute x30, starting transfers between devices, xor_permute(): lax.ppermute(x, axis, [(i, i ^ mask) for i in range(lax.axis_size(axis))])  27.2 us
    ppermute x30, waiting for transfers between devices, xor_permute(): lax.ppermute(x, axis, [(i, i ^ mask) for i in range(lax.axis_size(axis))])  16.7 us
    pallas_call x1, Pallas kernels, per_device(): pl.pallas_call(functools.partial(gradient_kernel, frames, rows, slabs, ma...  12.1 us
    pallas_call x1, Pallas kernels, per_device(): pl.pallas_call(functools.partial(decode_kernel, frames, rows, slabs, mask...  8.62 us
    pallas_call x2, Pallas kernels, finish(): pl.pallas_call(functools.partial(finish_kernel, sources), out_shape=jax.S...  5.13 us
    unnamed x66, local copies, waits for them, and re-layouts  2.6 us
    pallas_call x1, Pallas kernels, per_device(): pl.pallas_call(functools.partial(unpatchify_kernel, frames, tok_rows, tok...  1.66 us
  transfers between devices with their start and end apart: 30, of which 12 were waited for; matrix products, arithmetic and copies ran while one was open for 3% of the time, Pallas kernels for 18%

profile of v8, /device:TPU:0, one launch (start us, length us, event | category | flops | bytes accessed | tf_op | source)
XLA Modules:
  0.0 82.1 jit_solution(15987846699856114103)
XLA Ops:
  0.7 1.4 %reshape.77 = bf16[8,24,1024]{2,1,0:T(8,128)(2,1)S(1)} reshape(bf16[192,2,4,128]{3,2,1,0:T(4,128)(2,1)} %param.11) | data formatting | bytes 786432 | tf_op jit(solution)/shard_map/reshape | solution.py:350
  2.2 4.1 %collective-permute-start.2 = (bf16[4,24,1024]{2,1,0:T(8,128)(2,1)S(1)}, bf16[4,24,1024]{2,1,0:T(8,128)(2,1)S(1)}, u32[]{:S(2)}, u32[]{:S(2)}) collective-permute-start(bf16[4,24,1024]{2,1,0:T(8,128)(2,1)S(1)} %pad_maximum_fusion), channel_id=1, source_target_pairs={{0,16},{2,18},{4,20},{6,22},{8,24},{10,26},{12,28},{14,30},{16,0},... | collective-permute-start | bytes 589832 | tf_op jit(solution)/shard_map/ppermute | solution.py:33
  6.3 1.5 %convolution_bitcast_fusion.own_ref = f32[64,256]{1,0:T(8,128)S(1)} fusion(bf16[256,2560]{1,0:T(8,128)(2,1)S(1)} %bitcast.59, bf16[2560,64]{0,1:T(8,128)(2,1)} %param.7), kind=kOutput, calls=%fused_computation | convolution fusion | flops 83886080 | bytes 1703936 | tf_op jit(solution)/shard_map/dot_general | solution.py:363
  7.8 1.6 %collective-permute-start = (f32[64,256]{1,0:T(8,128)S(1)}, f32[64,256]{1,0:T(8,128)S(1)}, u32[]{:S(2)}, u32[]{:S(2)}) collective-permute-start(f32[64,256]{1,0:T(8,128)S(1)} %convolution_bitcast_fusion.own_ref), channel_id=1, source_target_pairs={{0,1},{1,0},{2,3},{3,2},{4,5},{5,4},{6,7},{7,6},{8,9},{9,8},{10,11... | collective-permute-start | bytes 196616 | tf_op jit(solution)/shard_map/ppermute | solution.py:33
  9.3 2.5 %collective-permute-start.5 = (bf16[24,1024]{1,0:T(8,128)(2,1)S(1)}, bf16[24,1024]{1,0:T(8,128)(2,1)S(1)}, u32[]{:S(2)}, u32[]{:S(2)}) collective-permute-start(bf16[24,1024]{1,0:T(8,128)(2,1)S(1)} %get-tuple-element.60), channel_id=1, source_target_pairs={{0,12},{2,14},{4,8},{6,10},{8,4},{10,6},{12,0},{14,2},{16,28},{18,... | collective-permute-start | bytes 147464 | tf_op jit(solution)/shard_map/ppermute | solution.py:33
  11.9 0.5 collective-permute-start.4
  12.3 0.5 collective-permute-start.3
  12.8 0.6 copy-done.31
  13.5 1.7 %unpatchify.1 = bf16[16,1024]{1,0:T(8,128)(2,1)} custom-call(f32[64,256]{1,0:T(8,128)} %copy-done.11, f32[64,256]{1,0:T(8,128)} %copy-done.31), custom_call_target="tpu_custom_call" | custom-call | tf_op jit(solution)/shard_map/unpatchify/pallas_call | solution.py:378
  15.1 0.3 collective-permute-start.1
  15.5 1.6 %blank.1.refs_8_ = f32[3,9,192,384]{3,2,1,0:T(8,128)} custom-call(), custom_call_target="tpu_custom_call" | custom-call | bytes 2654208 | tf_op jit(solution)/shard_map/blank/pallas_call | solution.py:390
  17.1 3.1 %collective-permute-done.1 = bf16[16,1024]{1,0:T(8,128)(2,1)S(1)} collective-permute-done((bf16[16,1024]{1,0:T(8,128)(2,1)}, bf16[16,1024]{1,0:T(8,128)(2,1)S(1)}, u32[]{:S(2)}, u32[]{:S(2)}) %collective-permute-start.1) | collective-permute-done | bytes 32800 | tf_op jit(solution)/shard_map/ppermute | solution.py:33
  20.4 2.6 %collective-permute-start.8 = (bf16[56,1024]{1,0:T(8,128)(2,1)S(1)}, bf16[56,1024]{1,0:T(8,128)(2,1)S(1)}, u32[]{:S(2)}, u32[]{:S(2)}) collective-permute-start(bf16[56,1024]{1,0:T(8,128)(2,1)S(1)} %get-tuple-element.76), channel_id=1, source_target_pairs={{0,12},{2,14},{4,8},{6,10},{8,4},{10,6},{12,0},{14,2},{16,28},{18,... | collective-permute-start | bytes 344072 | tf_op jit(solution)/shard_map/ppermute | solution.py:33
  23.0 0.5 collective-permute-start.6
  23.5 0.4 collective-permute-start.7
  24.0 0.6 reshape.74.refs_1_.gain_ref
  24.6 2.5 %collective-permute-done.8.refs_6_.refs_3_ = bf16[56,1024]{1,0:T(8,128)(2,1)S(1)} collective-permute-done((bf16[56,1024]{1,0:T(8,128)(2,1)S(1)}, bf16[56,1024]{1,0:T(8,128)(2,1)S(1)}, u32[]{:S(2)}, u32[]{:S(2)}) %collective-permute-start.8) | collective-permute-done | bytes 114720 | tf_op jit(solution)/shard_map/ppermute | solution.py:33
  27.0 2.3 %collective-permute-done.6.refs_4_.refs_1_ = bf16[56,1024]{1,0:T(8,128)(2,1)S(1)} collective-permute-done((bf16[56,1024]{1,0:T(8,128)(2,1)S(1)}, bf16[56,1024]{1,0:T(8,128)(2,1)S(1)}, u32[]{:S(2)}, u32[]{:S(2)}) %collective-permute-start.6) | collective-permute-done | bytes 114720 | tf_op jit(solution)/shard_map/ppermute | solution.py:33
  29.5 0.4 collective-permute-start.11
  29.9 0.7 slice_bitcast_fusion
  30.9 0.3 copy-done.6
  31.4 0.2 copy-done.9
  31.5 12.1 %gradient.1 = (f32[216,384]{1,0:T(8,128)}, bf16[216,384]{1,0:T(8,128)(2,1)}) custom-call(s32[1]{0:T(128)} %bitcast.refs_0_.me_ref, f32[1,384]{1,0:T(1,128)} %reshape.74.refs_1_.gain_ref, bf16[432,384]{1,0:T(8,128)(2,1)} %bitcast.62, bf16[56,1024]{1,0:T(8,128)(2,1)} %copy-done.1, bf16[56,1024]{1,0:T(8,128)(2,1)} %copy-done.4, bf16[56,1024]{1,0:T(8,128)(2,1)} %copy-done.5, ...), custom_call_target="tpu_custom_call" | custom-call | tf_op jit(solution)/shard_map/gradient/pallas_call | solution.py:421
  43.6 0.4 collective-permute-start.14
  44.1 1.3 %collective-permute-done.14 = bf16[216,384]{1,0:T(8,128)(2,1)S(1)} collective-permute-done((bf16[216,384]{1,0:T(8,128)(2,1)}, bf16[216,384]{1,0:T(8,128)(2,1)S(1)}, u32[]{:S(2)}, u32[]{:S(2)}) %collective-permute-start.14) | collective-permute-done | bytes 165920 | tf_op jit(solution)/shard_map/ppermute | solution.py:33
  45.3 1.0 %add_convert_fusion = bf16[216,384]{1,0:T(8,128)(2,1)S(1)} fusion(f32[216,384]{1,0:T(8,128)} %get-tuple-element.38, bf16[216,384]{1,0:T(8,128)(2,1)S(1)} %collective-permute-done.14), kind=kLoop, calls=%fused_computation.1 | loop fusion | flops 248832 | bytes 663552 | tf_op jit(solution)/shard_map/convert_element_type | solution.py:447
  46.4 1.6 %collective-permute-start.15 = (bf16[216,384]{1,0:T(8,128)(2,1)S(1)}, bf16[216,384]{1,0:T(8,128)(2,1)S(1)}, u32[]{:S(2)}, u32[]{:S(2)}) collective-permute-start(bf16[216,384]{1,0:T(8,128)(2,1)S(1)} %add_convert_fusion), channel_id=1, source_target_pairs={{0,8},{2,10},{4,12},{6,14},{8,0},{10,2},{12,4},{14,6},{16,24},{18,... | collective-permute-start | bytes 497672 | tf_op jit(solution)/shard_map/ppermute | solution.py:33
  48.0 0.4 collective-permute-start.19
  48.4 1.6 %collective-permute-start.18 = (bf16[216,384]{1,0:T(8,128)(2,1)S(1)}, bf16[216,384]{1,0:T(8,128)(2,1)S(1)}, u32[]{:S(2)}, u32[]{:S(2)}) collective-permute-start(bf16[216,384]{1,0:T(8,128)(2,1)S(1)} %add_convert_fusion), channel_id=1, source_target_pairs={{0,16},{2,18},{4,20},{6,22},{8,24},{10,26},{12,28},{14,30},{16,0},... | collective-permute-start | bytes 497672 | tf_op jit(solution)/shard_map/ppermute | solution.py:33
  49.9 1.5 %collective-permute-start.16 = (bf16[216,384]{1,0:T(8,128)(2,1)S(1)}, bf16[216,384]{1,0:T(8,128)(2,1)S(1)}, u32[]{:S(2)}, u32[]{:S(2)}) collective-permute-start(bf16[216,384]{1,0:T(8,128)(2,1)S(1)} %add_convert_fusion), channel_id=1, source_target_pairs={{0,4},{2,6},{4,0},{6,2},{8,12},{10,14},{12,8},{14,10},{16,20},{18,... | collective-permute-start | bytes 497672 | tf_op jit(solution)/shard_map/ppermute | solution.py:33
  51.4 1.8 %collective-permute-done.15 = bf16[216,384]{1,0:T(8,128)(2,1)S(1)} collective-permute-done((bf16[216,384]{1,0:T(8,128)(2,1)S(1)}, bf16[216,384]{1,0:T(8,128)(2,1)S(1)}, u32[]{:S(2)}, u32[]{:S(2)}) %collective-permute-start.15) | collective-permute-done | bytes 165920 | tf_op jit(solution)/shard_map/ppermute | solution.py:33
  53.2 4.3 %collective-permute-start.17 = (bf16[216,384]{1,0:T(8,128)(2,1)S(1)}, bf16[216,384]{1,0:T(8,128)(2,1)S(1)}, u32[]{:S(2)}, u32[]{:S(2)}) collective-permute-start(bf16[216,384]{1,0:T(8,128)(2,1)S(1)} %collective-permute-done.15), channel_id=1, source_target_pairs={{0,4},{2,6},{4,0},{6,2},{8,12},{10,14},{12,8},{14,10},{16,20},{18,... | collective-permute-start | bytes 497672 | tf_op jit(solution)/shard_map/ppermute | solution.py:33
  57.5 8.6 %decode.1 = bf16[192,2,4,128]{3,2,1,0:T(4,128)(2,1)} custom-call(s32[1]{0:T(128)} %bitcast.refs_0_.me_ref, f32[1,384]{1,0:T(1,128)} %reshape.74.refs_1_.gain_ref, bf16[432,384]{1,0:T(8,128)(2,1)} %bitcast.63, bf16[27,192,384]{2,1,0:T(8,128)(2,1)} %bitcast.61, bf16[56,1024]{1,0:T(8,128)(2,1)} %copy-done.1, bf16[56,1024]{1,0:T(8,128)(2,1)} %copy-done.4, ...), custom_call_target="tpu_custom_call" | custom-call | tf_op jit(solution)/shard_map/decode/pallas_call | solution.py:455
  66.3 0.5 collective-permute-start.21
  66.9 0.4 collective-permute-start.23
  67.4 0.3 collective-permute-done.20
  67.7 1.7 %collective-permute-start.25 = (bf16[216,384]{1,0:T(8,128)(2,1)S(1)}, bf16[216,384]{1,0:T(8,128)(2,1)S(1)}, u32[]{:S(2)}, u32[]{:S(2)}) collective-permute-start(bf16[216,384]{1,0:T(8,128)(2,1)S(1)} %collective-permute-done.19), channel_id=1, source_target_pairs={{0,4},{2,6},{4,0},{6,2},{8,12},{10,14},{12,8},{14,10},{16,20},{18,... | collective-permute-start | bytes 497672 | tf_op jit(solution)/shard_map/ppermute | solution.py:33
  69.4 0.5 collective-permute-start.28
  70.1 0.5 copy-done.27
  70.5 2.6 %finish.2.refs_8_ = f32[3,9,192,384]{3,2,1,0:T(8,128)} custom-call(s32[1]{0:T(128)} %bitcast.refs_0_.me_ref, bf16[9,24,384]{2,1,0:T(8,128)(2,1)} %bitcast.64, bf16[9,24,384]{2,1,0:T(8,128)(2,1)} %bitcast.72, bf16[9,24,384]{2,1,0:T(8,128)(2,1)} %bitcast.71, bf16[9,24,384]{2,1,0:T(8,128)(2,1)} %bitcast.73, ...), custom_call_target="tpu_custom_call", output_to_operand_aliasing={{}: (9, {})} | custom-call | tf_op jit(solution)/shard_map/finish/pallas_call | solution.py:484
  73.1 1.3 %collective-permute-done.24 = bf16[216,384]{1,0:T(8,128)(2,1)S(1)} collective-permute-done((bf16[216,384]{1,0:T(8,128)(2,1)S(1)}, bf16[216,384]{1,0:T(8,128)(2,1)S(1)}, u32[]{:S(2)}, u32[]{:S(2)}) %collective-permute-start.24) | collective-permute-done | bytes 165920 | tf_op jit(solution)/shard_map/ppermute | solution.py:33
  74.4 2.7 %collective-permute-done.25 = bf16[216,384]{1,0:T(8,128)(2,1)S(1)} collective-permute-done((bf16[216,384]{1,0:T(8,128)(2,1)S(1)}, bf16[216,384]{1,0:T(8,128)(2,1)S(1)}, u32[]{:S(2)}, u32[]{:S(2)}) %collective-permute-start.25) | collective-permute-done | bytes 165920 | tf_op jit(solution)/shard_map/ppermute | solution.py:33
  77.1 0.5 collective-permute-start.29
  77.6 0.9 %collective-permute-done.27 = bf16[216,384]{1,0:T(8,128)(2,1)S(1)} collective-permute-done((bf16[216,384]{1,0:T(8,128)(2,1)S(1)}, bf16[216,384]{1,0:T(8,128)(2,1)S(1)}, u32[]{:S(2)}, u32[]{:S(2)}) %collective-permute-start.27) | collective-permute-done | bytes 165920 | tf_op jit(solution)/shard_map/ppermute | solution.py:33
  78.5 0.2 collective-permute-done.29
  78.7 0.4 copy-done.28
  79.1 0.2 copy-done.29
  79.4 2.6 %finish.3 = f32[3,9,192,384]{3,2,1,0:T(8,128)} custom-call(s32[1]{0:T(128)} %bitcast.refs_0_.me_ref, bf16[9,24,384]{2,1,0:T(8,128)(2,1)} %bitcast.70, bf16[9,24,384]{2,1,0:T(8,128)(2,1)} %bitcast.74, bf16[9,24,384]{2,1,0:T(8,128)(2,1)} %bitcast.69, bf16[9,24,384]{2,1,0:T(8,128)(2,1)} %bitcast.75, ...), custom_call_target="tpu_custom_call", output_to_operand_aliasing={{}: (9, {})} | custom-call | tf_op jit(solution)/shard_map/finish/pallas_call | solution.py:484
  (94 shorter events, 1.3 us)
Async XLA Ops:
  0.6 5.7 %copy-start = (bf16[2,2,64,2560]{3,2,1,0:T(8,128)(2,1)S(1)}, bf16[2,2,64,2560]{3,2,1,0:T(8,128)(2,1)}, u32[]{:S(2)}) copy-start(bf16[2,2,64,2560]{3,2,1,0:T(8,128)(2,1)} %param.6) | copy-start | bytes 3932164
  2.1 18.1 %copy-start.10 = (bf16[24,1024]{1,0:T(8,128)(2,1)}, bf16[24,1024]{1,0:T(8,128)(2,1)S(1)}, u32[]{:S(2)}) copy-start(bf16[24,1024]{1,0:T(8,128)(2,1)S(1)} %get-tuple-element.34.refs_11_) | copy-start | bytes 147460
  2.2 18.0 %collective-permute-start.2 = (bf16[4,24,1024]{2,1,0:T(8,128)(2,1)S(1)}, bf16[4,24,1024]{2,1,0:T(8,128)(2,1)S(1)}, u32[]{:S(2)}, u32[]{:S(2)}) collective-permute-start(bf16[4,24,1024]{2,1,0:T(8,128)(2,1)S(1)} %pad_maximum_fusion), channel_id=1, source_target_pairs={{0,16},{2,18},{4,20},{6,22},{8,24},{10,26},{12,28},{14,30},{16,0},... | collective-permute-start | bytes 589832 | tf_op jit(solution)/shard_map/ppermute | solution.py:33
  7.8 5.1 %copy-start.11 = (f32[64,256]{1,0:T(8,128)}, f32[64,256]{1,0:T(8,128)S(1)}, u32[]{:S(2)}) copy-start(f32[64,256]{1,0:T(8,128)S(1)} %convolution_bitcast_fusion.own_ref) | copy-start | bytes 196612
  7.8 5.0 %collective-permute-start = (f32[64,256]{1,0:T(8,128)S(1)}, f32[64,256]{1,0:T(8,128)S(1)}, u32[]{:S(2)}, u32[]{:S(2)}) collective-permute-start(f32[64,256]{1,0:T(8,128)S(1)} %convolution_bitcast_fusion.own_ref), channel_id=1, source_target_pairs={{0,1},{1,0},{2,3},{3,2},{4,5},{5,4},{6,7},{7,6},{8,9},{9,8},{10,11... | collective-permute-start | bytes 196616 | tf_op jit(solution)/shard_map/ppermute | solution.py:33
  9.3 10.8 %collective-permute-start.5 = (bf16[24,1024]{1,0:T(8,128)(2,1)S(1)}, bf16[24,1024]{1,0:T(8,128)(2,1)S(1)}, u32[]{:S(2)}, u32[]{:S(2)}) collective-permute-start(bf16[24,1024]{1,0:T(8,128)(2,1)S(1)} %get-tuple-element.60), channel_id=1, source_target_pairs={{0,12},{2,14},{4,8},{6,10},{8,4},{10,6},{12,0},{14,2},{16,28},{18,... | collective-permute-start | bytes 147464 | tf_op jit(solution)/shard_map/ppermute | solution.py:33
  11.9 8.3 %collective-permute-start.4 = (bf16[24,1024]{1,0:T(8,128)(2,1)S(1)}, bf16[24,1024]{1,0:T(8,128)(2,1)S(1)}, u32[]{:S(2)}, u32[]{:S(2)}) collective-permute-start(bf16[24,1024]{1,0:T(8,128)(2,1)S(1)} %get-tuple-element.61), channel_id=1, source_target_pairs={{0,8},{2,10},{4,12},{6,14},{8,0},{10,2},{12,4},{14,6},{16,24},{18,... | collective-permute-start | bytes 147464 | tf_op jit(solution)/shard_map/ppermute | solution.py:33
  12.3 7.9 %collective-permute-start.3 = (bf16[24,1024]{1,0:T(8,128)(2,1)S(1)}, bf16[24,1024]{1,0:T(8,128)(2,1)S(1)}, u32[]{:S(2)}, u32[]{:S(2)}) collective-permute-start(bf16[24,1024]{1,0:T(8,128)(2,1)S(1)} %get-tuple-element.62), channel_id=1, source_target_pairs={{0,4},{2,6},{4,0},{6,2},{8,12},{10,14},{12,8},{14,10},{16,20},{18,... | collective-permute-start | bytes 147464 | tf_op jit(solution)/shard_map/ppermute | solution.py:33
  15.1 5.2 %copy-start.30 = (bf16[16,1024]{1,0:T(8,128)(2,1)S(1)}, bf16[16,1024]{1,0:T(8,128)(2,1)}, u32[]{:S(2)}) copy-start(bf16[16,1024]{1,0:T(8,128)(2,1)} %unpatchify.1) | copy-start | bytes 98308
  15.1 8.9 %copy-start.32 = (f32[384]{0:T(512)S(1)}, f32[384]{0:T(512)}, u32[]{:S(2)}) copy-start(f32[384]{0:T(512)} %param.8) | copy-start | bytes 4612
  15.1 5.0 %collective-permute-start.1 = (bf16[16,1024]{1,0:T(8,128)(2,1)}, bf16[16,1024]{1,0:T(8,128)(2,1)S(1)}, u32[]{:S(2)}, u32[]{:S(2)}) collective-permute-start(bf16[16,1024]{1,0:T(8,128)(2,1)} %unpatchify.1), channel_id=1, source_target_pairs={{0,16},{2,18},{4,20},{6,22},{8,24},{10,26},{12,28},{14,30},{16,0},... | collective-permute-start | bytes 98312 | tf_op jit(solution)/shard_map/ppermute | solution.py:33
  20.2 10.7 %copy-start.12 = (bf16[24,1024]{1,0:T(8,128)(2,1)}, bf16[24,1024]{1,0:T(8,128)(2,1)S(1)}, u32[]{:S(2)}) copy-start(bf16[24,1024]{1,0:T(8,128)(2,1)S(1)} %collective-permute-done.5.refs_14_) | copy-start | bytes 147460
  20.2 10.7 %copy-start.13 = (bf16[24,1024]{1,0:T(8,128)(2,1)}, bf16[24,1024]{1,0:T(8,128)(2,1)S(1)}, u32[]{:S(2)}) copy-start(bf16[24,1024]{1,0:T(8,128)(2,1)S(1)} %collective-permute-done.4.refs_13_) | copy-start | bytes 147460
  20.2 10.7 %copy-start.14 = (bf16[24,1024]{1,0:T(8,128)(2,1)}, bf16[24,1024]{1,0:T(8,128)(2,1)S(1)}, u32[]{:S(2)}) copy-start(bf16[24,1024]{1,0:T(8,128)(2,1)S(1)} %collective-permute-done.3.refs_12_) | copy-start | bytes 147460
  20.3 9.6 %collective-permute-start.13 = (bf16[4,24,1024]{2,1,0:T(8,128)(2,1)S(1)}, bf16[4,24,1024]{2,1,0:T(8,128)(2,1)S(1)}, u32[]{:S(2)}, u32[]{:S(2)}) collective-permute-start(bf16[4,24,1024]{2,1,0:T(8,128)(2,1)S(1)} %pad_maximum_fusion.1), channel_id=1, source_target_pairs={{0,2},{2,0},{4,6},{6,4},{8,10},{10,8},{12,14},{14,12},{16,18},{18,... | collective-permute-start | bytes 589832 | tf_op jit(solution)/shard_map/ppermute | solution.py:33
  20.4 10.5 %copy-start.1 = (bf16[56,1024]{1,0:T(8,128)(2,1)}, bf16[56,1024]{1,0:T(8,128)(2,1)S(1)}, u32[]{:S(2)}) copy-start(bf16[56,1024]{1,0:T(8,128)(2,1)S(1)} %get-tuple-element.40.refs_3_.refs_0_) | copy-start | bytes 344068
  20.4 6.6 %collective-permute-start.8 = (bf16[56,1024]{1,0:T(8,128)(2,1)S(1)}, bf16[56,1024]{1,0:T(8,128)(2,1)S(1)}, u32[]{:S(2)}, u32[]{:S(2)}) collective-permute-start(bf16[56,1024]{1,0:T(8,128)(2,1)S(1)} %get-tuple-element.76), channel_id=1, source_target_pairs={{0,12},{2,14},{4,8},{6,10},{8,4},{10,6},{12,0},{14,2},{16,28},{18,... | collective-permute-start | bytes 344072 | tf_op jit(solution)/shard_map/ppermute | solution.py:33
  23.0 6.4 %collective-permute-start.6 = (bf16[56,1024]{1,0:T(8,128)(2,1)S(1)}, bf16[56,1024]{1,0:T(8,128)(2,1)S(1)}, u32[]{:S(2)}, u32[]{:S(2)}) collective-permute-start(bf16[56,1024]{1,0:T(8,128)(2,1)S(1)} %get-tuple-element.77), channel_id=1, source_target_pairs={{0,4},{2,6},{4,0},{6,2},{8,12},{10,14},{12,8},{14,10},{16,20},{18,... | collective-permute-start | bytes 344072 | tf_op jit(solution)/shard_map/ppermute | solution.py:33
  23.5 5.9 %collective-permute-start.7 = (bf16[56,1024]{1,0:T(8,128)(2,1)S(1)}, bf16[56,1024]{1,0:T(8,128)(2,1)S(1)}, u32[]{:S(2)}, u32[]{:S(2)}) collective-permute-start(bf16[56,1024]{1,0:T(8,128)(2,1)S(1)} %get-tuple-element.78), channel_id=1, source_target_pairs={{0,8},{2,10},{4,12},{6,14},{8,0},{10,2},{12,4},{14,6},{16,24},{18,... | collective-permute-start | bytes 344072 | tf_op jit(solution)/shard_map/ppermute | solution.py:33
  24.6 6.0 %collective-permute-start.9 = (bf16[56,1024]{1,0:T(8,128)(2,1)S(1)}, bf16[56,1024]{1,0:T(8,128)(2,1)S(1)}, u32[]{:S(2)}, u32[]{:S(2)}) collective-permute-start(bf16[56,1024]{1,0:T(8,128)(2,1)S(1)} %get-tuple-element.40.refs_3_.refs_0_), channel_id=1, source_target_pairs={{0,2},{2,0},{4,6},{6,4},{8,10},{10,8},{12,14},{14,12},{16,18},{18,... | collective-permute-start | bytes 344072 | tf_op jit(solution)/shard_map/ppermute | solution.py:33
  27.0 3.9 %copy-start.3 = (bf16[56,1024]{1,0:T(8,128)(2,1)}, bf16[56,1024]{1,0:T(8,128)(2,1)S(1)}, u32[]{:S(2)}) copy-start(bf16[56,1024]{1,0:T(8,128)(2,1)S(1)} %collective-permute-done.8.refs_6_.refs_3_) | copy-start | bytes 344068
  27.0 3.6 %collective-permute-start.12 = (bf16[56,1024]{1,0:T(8,128)(2,1)S(1)}, bf16[56,1024]{1,0:T(8,128)(2,1)S(1)}, u32[]{:S(2)}, u32[]{:S(2)}) collective-permute-start(bf16[56,1024]{1,0:T(8,128)(2,1)S(1)} %collective-permute-done.8.refs_6_.refs_3_), channel_id=1, source_target_pairs={{0,2},{2,0},{4,6},{6,4},{8,10},{10,8},{12,14},{14,12},{16,18},{18,... | collective-permute-start | bytes 344072 | tf_op jit(solution)/shard_map/ppermute | solution.py:33
  29.4 1.3 %collective-permute-start.10 = (bf16[56,1024]{1,0:T(8,128)(2,1)S(1)}, bf16[56,1024]{1,0:T(8,128)(2,1)S(1)}, u32[]{:S(2)}, u32[]{:S(2)}) collective-permute-start(bf16[56,1024]{1,0:T(8,128)(2,1)S(1)} %collective-permute-done.6.refs_4_.refs_1_), channel_id=1, source_target_pairs={{0,2},{2,0},{4,6},{6,4},{8,10},{10,8},{12,14},{14,12},{16,18},{18,... | collective-permute-start | bytes 344072 | tf_op jit(solution)/shard_map/ppermute | solution.py:33
  29.5 1.4 %collective-permute-start.11 = (bf16[56,1024]{1,0:T(8,128)(2,1)S(1)}, bf16[56,1024]{1,0:T(8,128)(2,1)S(1)}, u32[]{:S(2)}, u32[]{:S(2)}) collective-permute-start(bf16[56,1024]{1,0:T(8,128)(2,1)S(1)} %collective-permute-done.7.refs_5_.refs_2_), channel_id=1, source_target_pairs={{0,2},{2,0},{4,6},{6,4},{8,10},{10,8},{12,14},{14,12},{16,18},{18,... | collective-permute-start | bytes 344072 | tf_op jit(solution)/shard_map/ppermute | solution.py:33
  43.6 1.7 %collective-permute-start.14 = (bf16[216,384]{1,0:T(8,128)(2,1)}, bf16[216,384]{1,0:T(8,128)(2,1)S(1)}, u32[]{:S(2)}, u32[]{:S(2)}) collective-permute-start(bf16[216,384]{1,0:T(8,128)(2,1)} %get-tuple-element.39), channel_id=1, source_target_pairs={{0,2},{2,0},{4,6},{6,4},{8,10},{10,8},{12,14},{14,12},{16,18},{18,... | collective-permute-start | bytes 497672 | tf_op jit(solution)/shard_map/ppermute | solution.py:33
  46.3 23.5 %copy-start.2 = (bf16[216,384]{1,0:T(8,128)(2,1)}, bf16[216,384]{1,0:T(8,128)(2,1)S(1)}, u32[]{:S(2)}) copy-start(bf16[216,384]{1,0:T(8,128)(2,1)S(1)} %add_convert_fusion) | copy-start | bytes 497668
  46.4 6.9 %collective-permute-start.15 = (bf16[216,384]{1,0:T(8,128)(2,1)S(1)}, bf16[216,384]{1,0:T(8,128)(2,1)S(1)}, u32[]{:S(2)}, u32[]{:S(2)}) collective-permute-start(bf16[216,384]{1,0:T(8,128)(2,1)S(1)} %add_convert_fusion), channel_id=1, source_target_pairs={{0,8},{2,10},{4,12},{6,14},{8,0},{10,2},{12,4},{14,6},{16,24},{18,... | collective-permute-start | bytes 497672 | tf_op jit(solution)/shard_map/ppermute | solution.py:33
  48.0 18.1 %collective-permute-start.19 = (bf16[216,384]{1,0:T(8,128)(2,1)S(1)}, bf16[216,384]{1,0:T(8,128)(2,1)S(1)}, u32[]{:S(2)}, u32[]{:S(2)}) collective-permute-start(bf16[216,384]{1,0:T(8,128)(2,1)S(1)} %add_convert_fusion), channel_id=1, source_target_pairs={{0,24},{2,26},{4,28},{6,30},{8,16},{10,18},{12,20},{14,22},{16,8},... | collective-permute-start | bytes 497672 | tf_op jit(solution)/shard_map/ppermute | solution.py:33
  48.4 17.8 %collective-permute-start.18 = (bf16[216,384]{1,0:T(8,128)(2,1)S(1)}, bf16[216,384]{1,0:T(8,128)(2,1)S(1)}, u32[]{:S(2)}, u32[]{:S(2)}) collective-permute-start(bf16[216,384]{1,0:T(8,128)(2,1)S(1)} %add_convert_fusion), channel_id=1, source_target_pairs={{0,16},{2,18},{4,20},{6,22},{8,24},{10,26},{12,28},{14,30},{16,0},... | collective-permute-start | bytes 497672 | tf_op jit(solution)/shard_map/ppermute | solution.py:33
  49.9 16.3 %collective-permute-start.16 = (bf16[216,384]{1,0:T(8,128)(2,1)S(1)}, bf16[216,384]{1,0:T(8,128)(2,1)S(1)}, u32[]{:S(2)}, u32[]{:S(2)}) collective-permute-start(bf16[216,384]{1,0:T(8,128)(2,1)S(1)} %add_convert_fusion), channel_id=1, source_target_pairs={{0,4},{2,6},{4,0},{6,2},{8,12},{10,14},{12,8},{14,10},{16,20},{18,... | collective-permute-start | bytes 497672 | tf_op jit(solution)/shard_map/ppermute | solution.py:33
  53.2 16.6 %copy-start.17 = (bf16[216,384]{1,0:T(8,128)(2,1)}, bf16[216,384]{1,0:T(8,128)(2,1)S(1)}, u32[]{:S(2)}) copy-start(bf16[216,384]{1,0:T(8,128)(2,1)S(1)} %collective-permute-done.15) | copy-start | bytes 497668
  53.2 13.0 %collective-permute-start.17 = (bf16[216,384]{1,0:T(8,128)(2,1)S(1)}, bf16[216,384]{1,0:T(8,128)(2,1)S(1)}, u32[]{:S(2)}, u32[]{:S(2)}) collective-permute-start(bf16[216,384]{1,0:T(8,128)(2,1)S(1)} %collective-permute-done.15), channel_id=1, source_target_pairs={{0,4},{2,6},{4,0},{6,2},{8,12},{10,14},{12,8},{14,10},{16,20},{18,... | collective-permute-start | bytes 497672 | tf_op jit(solution)/shard_map/ppermute | solution.py:33
  66.1 7.0 %copy-start.15 = (bf16[216,384]{1,0:T(8,128)(2,1)}, bf16[216,384]{1,0:T(8,128)(2,1)S(1)}, u32[]{:S(2)}) copy-start(bf16[216,384]{1,0:T(8,128)(2,1)S(1)} %collective-permute-done.19) | copy-start | bytes 497668
  66.2 7.0 %copy-start.16 = (bf16[216,384]{1,0:T(8,128)(2,1)}, bf16[216,384]{1,0:T(8,128)(2,1)S(1)}, u32[]{:S(2)}) copy-start(bf16[216,384]{1,0:T(8,128)(2,1)S(1)} %collective-permute-done.18) | copy-start | bytes 497668
  66.2 3.7 %copy-start.18 = (bf16[216,384]{1,0:T(8,128)(2,1)}, bf16[216,384]{1,0:T(8,128)(2,1)S(1)}, u32[]{:S(2)}) copy-start(bf16[216,384]{1,0:T(8,128)(2,1)S(1)} %collective-permute-done.16) | copy-start | bytes 497668
  66.2 3.7 %copy-start.19 = (bf16[216,384]{1,0:T(8,128)(2,1)}, bf16[216,384]{1,0:T(8,128)(2,1)S(1)}, u32[]{:S(2)}) copy-start(bf16[216,384]{1,0:T(8,128)(2,1)S(1)} %collective-permute-done.17) | copy-start | bytes 497668
  66.2 1.5 %collective-permute-start.20 = (bf16[216,384]{1,0:T(8,128)(2,1)S(1)}, bf16[216,384]{1,0:T(8,128)(2,1)S(1)}, u32[]{:S(2)}, u32[]{:S(2)}) collective-permute-start(bf16[216,384]{1,0:T(8,128)(2,1)S(1)} %add_convert_fusion), channel_id=1, source_target_pairs={{0,2},{2,0},{4,6},{6,4},{8,10},{10,8},{12,14},{14,12},{16,18},{18,... | collective-permute-start | bytes 497672 | tf_op jit(solution)/shard_map/ppermute | solution.py:33
  66.3 3.0 %collective-permute-start.21 = (bf16[216,384]{1,0:T(8,128)(2,1)S(1)}, bf16[216,384]{1,0:T(8,128)(2,1)S(1)}, u32[]{:S(2)}, u32[]{:S(2)}) collective-permute-start(bf16[216,384]{1,0:T(8,128)(2,1)S(1)} %collective-permute-done.16), channel_id=1, source_target_pairs={{0,2},{2,0},{4,6},{6,4},{8,10},{10,8},{12,14},{14,12},{16,18},{18,... | collective-permute-start | bytes 497672 | tf_op jit(solution)/shard_map/ppermute | solution.py:33
  66.8 2.6 %collective-permute-start.22 = (bf16[216,384]{1,0:T(8,128)(2,1)S(1)}, bf16[216,384]{1,0:T(8,128)(2,1)S(1)}, u32[]{:S(2)}, u32[]{:S(2)}) collective-permute-start(bf16[216,384]{1,0:T(8,128)(2,1)S(1)} %collective-permute-done.15), channel_id=1, source_target_pairs={{0,2},{2,0},{4,6},{6,4},{8,10},{10,8},{12,14},{14,12},{16,18},{18,... | collective-permute-start | bytes 497672 | tf_op jit(solution)/shard_map/ppermute | solution.py:33
  66.9 3.0 %collective-permute-start.23 = (bf16[216,384]{1,0:T(8,128)(2,1)S(1)}, bf16[216,384]{1,0:T(8,128)(2,1)S(1)}, u32[]{:S(2)}, u32[]{:S(2)}) collective-permute-start(bf16[216,384]{1,0:T(8,128)(2,1)S(1)} %collective-permute-done.17), channel_id=1, source_target_pairs={{0,2},{2,0},{4,6},{6,4},{8,10},{10,8},{12,14},{14,12},{16,18},{18,... | collective-permute-start | bytes 497672 | tf_op jit(solution)/shard_map/ppermute | solution.py:33
  67.3 7.1 %collective-permute-start.24 = (bf16[216,384]{1,0:T(8,128)(2,1)S(1)}, bf16[216,384]{1,0:T(8,128)(2,1)S(1)}, u32[]{:S(2)}, u32[]{:S(2)}) collective-permute-start(bf16[216,384]{1,0:T(8,128)(2,1)S(1)} %collective-permute-done.18), channel_id=1, source_target_pairs={{0,4},{2,6},{4,0},{6,2},{8,12},{10,14},{12,8},{14,10},{16,20},{18,... | collective-permute-start | bytes 497672 | tf_op jit(solution)/shard_map/ppermute | solution.py:33
  67.7 2.2 %copy-start.23 = (bf16[216,384]{1,0:T(8,128)(2,1)}, bf16[216,384]{1,0:T(8,128)(2,1)S(1)}, u32[]{:S(2)}) copy-start(bf16[216,384]{1,0:T(8,128)(2,1)S(1)} %collective-permute-done.20) | copy-start | bytes 497668
  67.7 9.4 %collective-permute-start.25 = (bf16[216,384]{1,0:T(8,128)(2,1)S(1)}, bf16[216,384]{1,0:T(8,128)(2,1)S(1)}, u32[]{:S(2)}, u32[]{:S(2)}) collective-permute-start(bf16[216,384]{1,0:T(8,128)(2,1)S(1)} %collective-permute-done.19), channel_id=1, source_target_pairs={{0,4},{2,6},{4,0},{6,2},{8,12},{10,14},{12,8},{14,10},{16,20},{18,... | collective-permute-start | bytes 497672 | tf_op jit(solution)/shard_map/ppermute | solution.py:33
  69.3 8.3 %collective-permute-start.26 = (bf16[216,384]{1,0:T(8,128)(2,1)S(1)}, bf16[216,384]{1,0:T(8,128)(2,1)S(1)}, u32[]{:S(2)}, u32[]{:S(2)}) collective-permute-start(bf16[216,384]{1,0:T(8,128)(2,1)S(1)} %collective-permute-done.18), channel_id=1, source_target_pairs={{0,2},{2,0},{4,6},{6,4},{8,10},{10,8},{12,14},{14,12},{16,18},{18,... | collective-permute-start | bytes 497672 | tf_op jit(solution)/shard_map/ppermute | solution.py:33
  69.4 8.2 %collective-permute-start.28 = (bf16[216,384]{1,0:T(8,128)(2,1)S(1)}, bf16[216,384]{1,0:T(8,128)(2,1)S(1)}, u32[]{:S(2)}, u32[]{:S(2)}) collective-permute-start(bf16[216,384]{1,0:T(8,128)(2,1)S(1)} %collective-permute-done.19), channel_id=1, source_target_pairs={{0,2},{2,0},{4,6},{6,4},{8,10},{10,8},{12,14},{14,12},{16,18},{18,... | collective-permute-start | bytes 497672 | tf_op jit(solution)/shard_map/ppermute | solution.py:33
  74.4 4.3 %copy-start.20 = (bf16[216,384]{1,0:T(8,128)(2,1)}, bf16[216,384]{1,0:T(8,128)(2,1)S(1)}, u32[]{:S(2)}) copy-start(bf16[216,384]{1,0:T(8,128)(2,1)S(1)} %collective-permute-done.24) | copy-start | bytes 497668
  77.1 1.4 %collective-permute-start.27 = (bf16[216,384]{1,0:T(8,128)(2,1)S(1)}, bf16[216,384]{1,0:T(8,128)(2,1)S(1)}, u32[]{:S(2)}, u32[]{:S(2)}) collective-permute-start(bf16[216,384]{1,0:T(8,128)(2,1)S(1)} %collective-permute-done.24), channel_id=1, source_target_pairs={{0,2},{2,0},{4,6},{6,4},{8,10},{10,8},{12,14},{14,12},{16,18},{18,... | collective-permute-start | bytes 497672 | tf_op jit(solution)/shard_map/ppermute | solution.py:33
  77.1 1.6 %collective-permute-start.29 = (bf16[216,384]{1,0:T(8,128)(2,1)S(1)}, bf16[216,384]{1,0:T(8,128)(2,1)S(1)}, u32[]{:S(2)}, u32[]{:S(2)}) collective-permute-start(bf16[216,384]{1,0:T(8,128)(2,1)S(1)} %collective-permute-done.25), channel_id=1, source_target_pairs={{0,2},{2,0},{4,6},{6,4},{8,10},{10,8},{12,14},{14,12},{16,18},{18,... | collective-permute-start | bytes 497672 | tf_op jit(solution)/shard_map/ppermute | solution.py:33
  (15 other events, 13.5 us)

commit v9 on v6

--- a/solution.py
+++ b/solution.py
@@ -39,33 +39,6 @@
 
 def dot_t(a, b):
     return lax.dot_general(a, b, (((1,), (1,)), ((), ())), preferred_element_type=F32)
-
-
-def unpatchify_kernel(frames, tok_rows, tok_cols, own_ref, other_ref, out_ref):
-    latent_width = out_ref.shape[0]
-    features = (own_ref[...] + other_ref[...]).astype(BF16)
-    width = 2 * tok_cols
-    span = tok_rows * tok_cols
-    source = lax.broadcasted_iota(jnp.int32, (span, tok_rows * width), 0)
-    target = lax.broadcasted_iota(jnp.int32, (span, tok_rows * width), 1)
-    same_row = source // tok_cols == target // width
-    column = source % tok_cols
-    even = (same_row & (target % width == 2 * column)).astype(BF16)
-    odd = (same_row & (target % width == 2 * column + 1)).astype(BF16)
-    for frame in range(frames):
-        tokens = features[:, frame * span : (frame + 1) * span]
-        left = dot(tokens, even)
-        right = dot(tokens, odd)
-        for row in range(tok_rows):
-            cols = slice(row * width, (row + 1) * width)
-            for half in range(2):
-                base = half * 2 * latent_width
-                cells = (
-                    left[base : base + latent_width, cols]
-                    + right[base + latent_width : base + 2 * latent_width, cols]
-                )
-                at = (frame * 2 * tok_rows + 2 * row + half) * width
-                out_ref[:, at : at + width] = cells.astype(BF16)
 
 
 def shifted(tile, shift):
@@ -78,12 +51,15 @@
 
 
 def fetch(piece_refs, mask_lists, slot_ref, sems):
+    count = slot_ref.shape[1]
     copies = []
     for index, (piece_ref, masks) in enumerate(zip(piece_refs, mask_lists)):
         for position, mask in enumerate(masks):
             copies.append(
                 pltpu.make_async_copy(
-                    piece_ref.at[position], slot_ref.at[mask], sems.at[index * len(masks) + position]
+                    piece_ref.at[position, pl.ds(0, count)],
+                    slot_ref.at[mask],
+                    sems.at[index * len(masks) + position],
                 )
             )
     for copy in copies:
@@ -91,12 +67,46 @@
     return copies
 
 
-def place_latent(slot_ref, stack_ref, me, first_slab, slab_count, frames, rows, slabs):
+def selection(tok_rows, tok_cols):
+    span = tok_rows * tok_cols
+    width = 2 * tok_cols
+    shape = (2 * span, 3 * tok_rows * width)
+    source = lax.broadcasted_iota(jnp.int32, shape, 0)
+    target = lax.broadcasted_iota(jnp.int32, shape, 1)
+    token = source % span
+    cell = 2 * (token % tok_cols) + source // span
+    shift = target // (tok_rows * width)
+    same_row = token // tok_cols == (target // width) % tok_rows
+    return (same_row & (target % width + shift - 1 == cell)).astype(F32).astype(BF16)
+
+
+def place_latent(slot_ref, select, stack_ref, me, first_slab, slab_count, frames, rows, slabs):
     latent_width = stack_ref.shape[1] // 3
+    tok_rows = rows // 2
+    span = select.shape[0] // 2
     for offset in range(-1, slab_count + 1):
         slab = first_slab + offset
         inside = ((slab >= 0) & (slab < slabs)).astype(F32)
         source = jnp.clip(slab, 0, slabs - 1) ^ me
+        blocks = []
+        for frame in range(frames):
+            for half in range(2):
+                sides = [
+                    slot_ref[
+                        source,
+                        :latent_width,
+                        ((half * 2 + side) * frames + frame) * span : (
+                            (half * 2 + side) * frames + frame + 1
+                        )
+                        * span,
+                    ]
+                    for side in range(2)
+                ]
+                blocks.append(jnp.concatenate(sides, axis=1))
+        cells = dot(jnp.concatenate(blocks, axis=0), select)
+        if offset in (-1, slab_count):
+            cells = cells * inside
+        cells = cells.astype(BF16)
         needed = range(rows)
         if offset == -1:
             needed = range(rows - 2, rows)
@@ -104,15 +114,13 @@
             needed = range(2)
         for frame in range(frames):
             for row in needed:
-                at = (frame * rows + row) * LANES
-                tile = slot_ref[source, :latent_width, at : at + LANES].astype(F32)
-                if offset in (-1, slab_count):
-                    tile = tile * inside
+                at_row = (frame * 2 + row % 2) * latent_width
                 to = (offset * rows + row + 2) * LANES
                 for shift in range(3):
+                    at = (shift * tok_rows + row // 2) * LANES
                     stack_ref[
                         frame, shift * latent_width : (shift + 1) * latent_width, to : to + LANES
-                    ] = shifted(tile, shift).astype(BF16)
+                    ] = cells[at_row : at_row + latent_width, at : at + LANES]
 
 
 def hidden_rows(stack_ref, weight_ref, frame, first, count):
@@ -182,7 +190,7 @@
             )
 
 
-def gradient_kernel(frames, rows, slabs, masks, real_rows, pad_channels, *refs):
+def gradient_kernel(frames, rows, slabs, tok_cols, masks, real_rows, pad_channels, *refs):
     me_ref, gain_ref, entry_ref = refs[:3]
     refs = refs[3:]
     piece_refs, refs = refs[: len(masks)], refs[len(masks) :]
@@ -204,10 +212,11 @@
     hidden = (hid_a, hid_b)
     acts = (act_a, act_b)
     load_entry(entry_ref, gain_ref, weight_refs, wide_gain)
+    select = selection(rows // 2, tok_cols)
     sum_ref[...] = jnp.zeros_like(sum_ref)
     for copy in copies:
         copy.wait()
-    place_latent(slots, stack_ref, me, first_slab, slab_count, frames, rows, slabs)
+    place_latent(slots, select, stack_ref, me, first_slab, slab_count, frames, rows, slabs)
     hid_a[...] = hidden_rows(stack_ref, weight_refs[0], 0, 0, ext)
     place_cotangent(
         slots, flat_ref, cot_ref, me, first_slab, slab_count, frames, rows, pad_channels,
@@ -241,7 +250,7 @@
     send_ref[...] = sum_ref[pl.ds(send_at, padded), :][:real_rows].astype(BF16)
 
 
-def decode_kernel(frames, rows, slabs, masks, me_ref, gain_ref, entry_ref, conv_hbm, *refs):
+def decode_kernel(frames, rows, slabs, tok_cols, masks, me_ref, gain_ref, entry_ref, conv_hbm, *refs):
     piece_refs, refs = refs[: len(masks)], refs[len(masks) :]
     out_ref, slots, stack_ref, hid_ref, flat_ref, act_ref, wide_gain, conv_ref, sems, sem = refs[:10]
     weight_refs = refs[10:]
@@ -252,9 +261,10 @@
     me = me_ref[0]
     height = slabs * rows
     load_entry(entry_ref, gain_ref, weight_refs, wide_gain)
+    select = selection(rows // 2, tok_cols)
     for copy in copies:
         copy.wait()
-    place_latent(slots, stack_ref, me, me, 1, frames, rows, slabs)
+    place_latent(slots, select, stack_ref, me, me, 1, frames, rows, slabs)
     ext = rows + 2
     for frame in range(frames):
         hid_ref[...] = hidden_rows(stack_ref, weight_refs[frame], frame, 0, ext)
@@ -295,21 +305,28 @@
 def finish_kernel(pieces, me_ref, *refs):
     count = len(pieces)
     piece_refs = refs[:count]
-    out_hbm, wide_ref, sems = refs[count + 1 :]
+    out_hbm, narrow_ref, wide_ref, in_sems, out_sems = refs[count + 1 :]
     me = me_ref[0]
     channels = wide_ref.shape[2]
-    copies = []
+    loads = [
+        pltpu.make_async_copy(piece_refs[index], narrow_ref.at[index], in_sems.at[index])
+        for index in range(count)
+    ]
+    for load in loads:
+        load.start()
+    stores = []
     for index, mask in enumerate(pieces):
         source = me ^ mask
-        wide_ref[index] = piece_refs[index][...].astype(F32)
+        loads[index].wait()
+        wide_ref[index] = narrow_ref[index].astype(F32)
         at = pl.multiple_of((source >> 1) * channels, 8)
-        copy = pltpu.make_async_copy(
-            wide_ref.at[index], out_hbm.at[2 - (source & 1), :, pl.ds(at, channels), :], sems.at[index]
+        store = pltpu.make_async_copy(
+            wide_ref.at[index], out_hbm.at[2 - (source & 1), :, pl.ds(at, channels), :], out_sems.at[index]
         )
-        copy.start()
-        copies.append(copy)
-    for copy in copies:
-        copy.wait()
+        store.start()
+        stores.append(store)
+    for store in stores:
+        store.wait()
 
 
 def per_device(attn_out, w_proj, norm_gain, entry_weight, conv_weight, cotangent):
@@ -366,14 +383,10 @@
     weights = [
         pltpu.VMEM((channels, min(3, f + 1) * 9 * latent_width), BF16) for f in range(frames)
     ]
-    latent = pl.pallas_call(
-        functools.partial(unpatchify_kernel, frames, tok_rows, tok_cols),
-        out_shape=jax.ShapeDtypeStruct((latent_width, frames * rows * width), BF16),
-        in_specs=[vmem(), vmem()],
-        out_specs=vmem(),
-        compiler_params=params(),
-        name="unpatchify",
-    )(partial_sum, other)
+    features = (partial_sum + other).astype(BF16)
+    latent = jnp.concatenate(
+        [features[i * latent_width : (i + 1) * latent_width] for i in range(4)], axis=1
+    )
 
     blank = 3 - live
     hbm = pl.BlockSpec(memory_space=pl.ANY)
@@ -405,7 +418,9 @@
     slot_shape = (slabs, latent_width + chip_channels, frames * rows * width)
 
     keep, send = pl.pallas_call(
-        functools.partial(gradient_kernel, frames, rows, slabs, masks, real_rows, pad_channels),
+        functools.partial(
+            gradient_kernel, frames, rows, slabs, tok_cols, masks, real_rows, pad_channels
+        ),
         out_shape=(
             jax.ShapeDtypeStruct((real_rows, channels), F32),
             jax.ShapeDtypeStruct((real_rows, channels), BF16),
@@ -438,12 +453,12 @@
 
     held = lax.optimization_barrier((block, direct[0], *pieces))[2:]
     decoded = pl.pallas_call(
-        functools.partial(decode_kernel, frames, rows, slabs, masks),
+        functools.partial(decode_kernel, frames, rows, slabs, tok_cols, masks),
         out_shape=jax.ShapeDtypeStruct((out_channels, frames, rows, width), BF16),
         in_specs=[smem(), vmem(), vmem(), hbm] + [hbm] * len(pieces),
         out_specs=vmem(),
         scratch_shapes=[
-            pltpu.VMEM(slot_shape, BF16),
+            pltpu.VMEM((slabs, latent_width, frames * rows * width), BF16),
             pltpu.VMEM((frames, 3 * latent_width, (rows + 4) * width), BF16),
             pltpu.VMEM((channels, (rows + 2) * width), F32),
             pltpu.VMEM((channels, (rows + 2) * width), BF16),
@@ -469,10 +484,12 @@
         return pl.pallas_call(
             functools.partial(finish_kernel, sources),
             out_shape=jax.ShapeDtypeStruct(grad_shape, F32),
-            in_specs=[smem()] + [vmem()] * len(parts) + [hbm],
+            in_specs=[smem()] + [hbm] * (len(parts) + 1),
             out_specs=hbm,
             scratch_shapes=[
+                pltpu.VMEM((len(parts),) + shape, BF16),
                 pltpu.VMEM((len(parts),) + shape, F32),
+                pltpu.SemaphoreType.DMA((len(parts),)),
                 pltpu.SemaphoreType.DMA((len(parts),)),
             ],
             input_output_aliases={len(parts) + 1: 0},

time: 80.5 us -> 83.2 us (1.034)
  starting transfers between devices: 19.5 us -> 24.2 us
  Pallas kernels: 30.2 us -> 28.1 us
    ppermute x26, starting transfers between devices: 19.5 us -> 24.2 us  [xor_permute(): lax.ppermute(x, axis, [(i, i ^ mask) for i in range(lax.axis_size(axis))])]
    pallas_call x3 -> x2, Pallas kernels: 22.7 us -> 21.4 us  [the longest x1 12.7 us: per_device(): pl.pallas_call(functools.partial(gradient_kernel, frames, rows, slabs, to...]
    unnamed x58 -> x52, local copies, waits for them, and re-layouts: 2.62 us -> 1.98 us
  transfers between devices with their start and end apart: 26 -> 26, of which waited for: 13 -> 12; matrix products, arithmetic and copies ran while one was open for 3% -> 1% of each run, Pallas kernels for 19% -> 15%
where the time goes in v9:
time: 83.2 us; the launch traced here: 82.8 us
  Pallas kernels  28.1 us (34%)
  starting transfers between devices  24.2 us (29%)
  waiting for transfers between devices  22.7 us (27%)
  local copies, waits for them, and re-layouts  3.99 us (5%)
  matrix products  1.48 us (2%)
  between operations  1.2 us (1%)
  other arithmetic  1.12 us (1%)
    ppermute x26, starting transfers between devices, xor_permute(): lax.ppermute(x, axis, [(i, i ^ mask) for i in range(lax.axis_size(axis))])  24.2 us
    ppermute x26, waiting for transfers between devices, xor_permute(): lax.ppermute(x, axis, [(i, i ^ mask) for i in range(lax.axis_size(axis))])  22.7 us
    pallas_call x1, Pallas kernels, per_device(): pl.pallas_call(functools.partial(gradient_kernel, frames, rows, slabs, to...  12.7 us
    pallas_call x1, Pallas kernels, per_device(): pl.pallas_call(functools.partial(decode_kernel, frames, rows, slabs, tok_...  8.65 us
    pallas_call x2, Pallas kernels, finish(): pl.pallas_call(functools.partial(finish_kernel, sources), out_shape=jax.S...  5.13 us
    unnamed x52, local copies, waits for them, and re-layouts  1.98 us
  transfers between devices with their start and end apart: 26, of which 12 were waited for; matrix products, arithmetic and copies ran while one was open for 1% of the time, Pallas kernels for 15%

profile of v9, /device:TPU:0, one launch (start us, length us, event | category | flops | bytes accessed | tf_op | source)
XLA Modules:
  0.0 82.8 jit_solution(6867907121783355013)
XLA Ops:
  0.7 1.4 %reshape.77 = bf16[8,24,1024]{2,1,0:T(8,128)(2,1)S(1)} reshape(bf16[192,2,4,128]{3,2,1,0:T(4,128)(2,1)} %param.11) | data formatting | bytes 786432 | tf_op jit(solution)/shard_map/reshape | solution.py:355
  2.2 1.5 %convolution_bitcast_fusion = f32[64,256]{1,0:T(8,128)S(1)} fusion(bf16[256,2560]{1,0:T(8,128)(2,1)S(1)} %bitcast.34, bf16[2560,64]{0,1:T(8,128)(2,1)} %param.7), kind=kOutput, calls=%fused_computation | convolution fusion | flops 83886080 | bytes 1703936 | tf_op jit(solution)/shard_map/dot_general | solution.py:371
  3.7 3.0 %collective-permute-start = (f32[64,256]{1,0:T(8,128)S(1)}, f32[64,256]{1,0:T(8,128)S(1)}, u32[]{:S(2)}, u32[]{:S(2)}) collective-permute-start(f32[64,256]{1,0:T(8,128)S(1)} %convolution_bitcast_fusion), channel_id=1, source_target_pairs={{0,1},{1,0},{2,3},{3,2},{4,5},{5,4},{6,7},{7,6},{8,9},{9,8},{10,11... | collective-permute-start | bytes 196616 | tf_op jit(solution)/shard_map/ppermute | solution.py:33
  6.7 2.6 %collective-permute-start.2 = (bf16[4,24,1024]{2,1,0:T(8,128)(2,1)S(1)}, bf16[4,24,1024]{2,1,0:T(8,128)(2,1)S(1)}, u32[]{:S(2)}, u32[]{:S(2)}) collective-permute-start(bf16[4,24,1024]{2,1,0:T(8,128)(2,1)S(1)} %pad_maximum_fusion), channel_id=1, source_target_pairs={{0,16},{2,18},{4,20},{6,22},{8,24},{10,26},{12,28},{14,30},{16,0},... | collective-permute-start | bytes 589832 | tf_op jit(solution)/shard_map/ppermute | solution.py:33
  9.3 2.8 %collective-permute-start.1 = (bf16[16,1024]{1,0:T(8,128)(2,1)S(1)}, bf16[16,1024]{1,0:T(8,128)(2,1)S(1)}, u32[]{:S(2)}, u32[]{:S(2)}) collective-permute-start(bf16[16,1024]{1,0:T(8,128)(2,1)S(1)} %get-tuple-element.67), channel_id=1, source_target_pairs={{0,16},{2,18},{4,20},{6,22},{8,24},{10,26},{12,28},{14,30},{16,0},... | collective-permute-start | bytes 98312 | tf_op jit(solution)/shard_map/ppermute | solution.py:33
  12.2 1.6 %blank.1.refs_8_ = f32[3,9,192,384]{3,2,1,0:T(8,128)} custom-call(), custom_call_target="tpu_custom_call" | custom-call | bytes 2654208 | tf_op jit(solution)/shard_map/blank/pallas_call | solution.py:394
  13.8 5.8 %collective-permute-done.1 = bf16[16,1024]{1,0:T(8,128)(2,1)S(1)} collective-permute-done((bf16[16,1024]{1,0:T(8,128)(2,1)S(1)}, bf16[16,1024]{1,0:T(8,128)(2,1)S(1)}, u32[]{:S(2)}, u32[]{:S(2)}) %collective-permute-start.1) | collective-permute-done | bytes 32800 | tf_op jit(solution)/shard_map/ppermute | solution.py:33
  19.7 1.7 %collective-permute-start.5 = (bf16[2,40,1024]{2,1,0:T(8,128)(2,1)S(1)}, bf16[2,40,1024]{2,1,0:T(8,128)(2,1)S(1)}, u32[]{:S(2)}, u32[]{:S(2)}) collective-permute-start(bf16[2,40,1024]{2,1,0:T(8,128)(2,1)S(1)} %get-tuple-element.62), channel_id=1, source_target_pairs={{0,12},{2,14},{4,8},{6,10},{8,4},{10,6},{12,0},{14,2},{16,28},{18,... | collective-permute-start | bytes 491528 | tf_op jit(solution)/shard_map/ppermute | solution.py:33
  21.4 0.5 collective-permute-start.3
  21.9 1.4 %collective-permute-start.4 = (bf16[2,40,1024]{2,1,0:T(8,128)(2,1)S(1)}, bf16[2,40,1024]{2,1,0:T(8,128)(2,1)S(1)}, u32[]{:S(2)}, u32[]{:S(2)}) collective-permute-start(bf16[2,40,1024]{2,1,0:T(8,128)(2,1)S(1)} %get-tuple-element.64), channel_id=1, source_target_pairs={{0,8},{2,10},{4,12},{6,14},{8,0},{10,2},{12,4},{14,6},{16,24},{18,... | collective-permute-start | bytes 491528 | tf_op jit(solution)/shard_map/ppermute | solution.py:33
  23.2 3.8 %collective-permute-done.5.refs_6_.refs_3_ = bf16[2,40,1024]{2,1,0:T(8,128)(2,1)S(1)} collective-permute-done((bf16[2,40,1024]{2,1,0:T(8,128)(2,1)S(1)}, bf16[2,40,1024]{2,1,0:T(8,128)(2,1)S(1)}, u32[]{:S(2)}, u32[]{:S(2)}) %collective-permute-start.5) | collective-permute-done | bytes 163872 | tf_op jit(solution)/shard_map/ppermute | solution.py:33
  27.1 2.2 %collective-permute-done.3.refs_4_.refs_1_ = bf16[2,40,1024]{2,1,0:T(8,128)(2,1)S(1)} collective-permute-done((bf16[2,40,1024]{2,1,0:T(8,128)(2,1)S(1)}, bf16[2,40,1024]{2,1,0:T(8,128)(2,1)S(1)}, u32[]{:S(2)}, u32[]{:S(2)}) %collective-permute-start.3) | collective-permute-done | bytes 163872 | tf_op jit(solution)/shard_map/ppermute | solution.py:33
  29.3 0.5 collective-permute-start.8
  29.8 0.6 reshape.74.refs_1_.gain_ref
  30.4 0.3 collective-permute-done.7.refs_8_.refs_5_
  30.6 0.2 collective-permute-done.8.refs_9_.refs_6_
  30.9 0.1 copy-done.6
  31.1 0.2 copy-done.8
  31.3 0.2 copy-done.9
  31.5 12.7 %gradient.1 = (f32[216,384]{1,0:T(8,128)}, bf16[216,384]{1,0:T(8,128)(2,1)}) custom-call(s32[1]{0:T(128)} %bitcast.refs_0_.me_ref, f32[1,384]{1,0:T(1,128)} %reshape.74.refs_1_.gain_ref, bf16[432,384]{1,0:T(8,128)(2,1)} %bitcast.37, bf16[2,40,1024]{2,1,0:T(8,128)(2,1)} %copy-done.1, bf16[2,40,1024]{2,1,0:T(8,128)(2,1)} %copy-done.4, ...), custom_call_target="tpu_custom_call" | custom-call | tf_op jit(solution)/shard_map/gradient/pallas_call | solution.py:420
  44.3 0.3 collective-permute-start.10
  44.6 1.3 %collective-permute-done.10 = bf16[216,384]{1,0:T(8,128)(2,1)S(1)} collective-permute-done((bf16[216,384]{1,0:T(8,128)(2,1)}, bf16[216,384]{1,0:T(8,128)(2,1)S(1)}, u32[]{:S(2)}, u32[]{:S(2)}) %collective-permute-start.10) | collective-permute-done | bytes 165920 | tf_op jit(solution)/shard_map/ppermute | solution.py:33
  45.9 1.0 %add_convert_fusion = bf16[216,384]{1,0:T(8,128)(2,1)S(1)} fusion(f32[216,384]{1,0:T(8,128)} %get-tuple-element.28, bf16[216,384]{1,0:T(8,128)(2,1)S(1)} %collective-permute-done.10), kind=kLoop, calls=%fused_computation.1 | loop fusion | flops 248832 | bytes 663552 | tf_op jit(solution)/shard_map/convert_element_type | solution.py:447
  47.0 1.7 %collective-permute-start.11 = (bf16[216,384]{1,0:T(8,128)(2,1)S(1)}, bf16[216,384]{1,0:T(8,128)(2,1)S(1)}, u32[]{:S(2)}, u32[]{:S(2)}) collective-permute-start(bf16[216,384]{1,0:T(8,128)(2,1)S(1)} %add_convert_fusion), channel_id=1, source_target_pairs={{0,8},{2,10},{4,12},{6,14},{8,0},{10,2},{12,4},{14,6},{16,24},{18,... | collective-permute-start | bytes 497672 | tf_op jit(solution)/shard_map/ppermute | solution.py:33
  48.7 3.1 %collective-permute-start.15 = (bf16[216,384]{1,0:T(8,128)(2,1)S(1)}, bf16[216,384]{1,0:T(8,128)(2,1)S(1)}, u32[]{:S(2)}, u32[]{:S(2)}) collective-permute-start(bf16[216,384]{1,0:T(8,128)(2,1)S(1)} %add_convert_fusion), channel_id=1, source_target_pairs={{0,24},{2,26},{4,28},{6,30},{8,16},{10,18},{12,20},{14,22},{16,8},... | collective-permute-start | bytes 497672 | tf_op jit(solution)/shard_map/ppermute | solution.py:33
  51.9 0.1 collective-permute-start.14
  52.0 0.8 %collective-permute-start.12 = (bf16[216,384]{1,0:T(8,128)(2,1)S(1)}, bf16[216,384]{1,0:T(8,128)(2,1)S(1)}, u32[]{:S(2)}, u32[]{:S(2)}) collective-permute-start(bf16[216,384]{1,0:T(8,128)(2,1)S(1)} %add_convert_fusion), channel_id=1, source_target_pairs={{0,4},{2,6},{4,0},{6,2},{8,12},{10,14},{12,8},{14,10},{16,20},{18,... | collective-permute-start | bytes 497672 | tf_op jit(solution)/shard_map/ppermute | solution.py:33
  52.8 0.7 collective-permute-done.11
  53.4 1.5 %collective-permute-start.13 = (bf16[216,384]{1,0:T(8,128)(2,1)S(1)}, bf16[216,384]{1,0:T(8,128)(2,1)S(1)}, u32[]{:S(2)}, u32[]{:S(2)}) collective-permute-start(bf16[216,384]{1,0:T(8,128)(2,1)S(1)} %collective-permute-done.11), channel_id=1, source_target_pairs={{0,4},{2,6},{4,0},{6,2},{8,12},{10,14},{12,8},{14,10},{16,20},{18,... | collective-permute-start | bytes 497672 | tf_op jit(solution)/shard_map/ppermute | solution.py:33
  54.9 8.7 %decode.1 = bf16[192,2,4,128]{3,2,1,0:T(4,128)(2,1)} custom-call(s32[1]{0:T(128)} %bitcast.refs_0_.me_ref, f32[1,384]{1,0:T(1,128)} %reshape.74.refs_1_.gain_ref, bf16[432,384]{1,0:T(8,128)(2,1)} %bitcast.38, bf16[27,192,384]{2,1,0:T(8,128)(2,1)} %bitcast.36, bf16[2,40,1024]{2,1,0:T(8,128)(2,1)} %copy-done.1, bf16[2,40,1024]{2,1,0:T(8,128)(2,1)} %copy-done.4, ...), custom_call_target="tpu_custom_call" | custom-call | tf_op jit(solution)/shard_map/decode/pallas_call | solution.py:455
  63.6 3.3 %collective-permute-done.14 = bf16[216,384]{1,0:T(8,128)(2,1)S(1)} collective-permute-done((bf16[216,384]{1,0:T(8,128)(2,1)S(1)}, bf16[216,384]{1,0:T(8,128)(2,1)S(1)}, u32[]{:S(2)}, u32[]{:S(2)}) %collective-permute-start.14) | collective-permute-done | bytes 165920 | tf_op jit(solution)/shard_map/ppermute | solution.py:33
  67.0 0.5 collective-permute-start.17
  67.5 0.1 collective-permute-start.18
  67.6 0.4 collective-permute-start.19
  68.0 1.0 %collective-permute-start.20 = (bf16[216,384]{1,0:T(8,128)(2,1)S(1)}, bf16[216,384]{1,0:T(8,128)(2,1)S(1)}, u32[]{:S(2)}, u32[]{:S(2)}) collective-permute-start(bf16[216,384]{1,0:T(8,128)(2,1)S(1)} %collective-permute-done.14), channel_id=1, source_target_pairs={{0,4},{2,6},{4,0},{6,2},{8,12},{10,14},{12,8},{14,10},{16,20},{18,... | collective-permute-start | bytes 497672 | tf_op jit(solution)/shard_map/ppermute | solution.py:33
  69.0 1.1 %collective-permute-start.21 = (bf16[216,384]{1,0:T(8,128)(2,1)S(1)}, bf16[216,384]{1,0:T(8,128)(2,1)S(1)}, u32[]{:S(2)}, u32[]{:S(2)}) collective-permute-start(bf16[216,384]{1,0:T(8,128)(2,1)S(1)} %collective-permute-done.15), channel_id=1, source_target_pairs={{0,4},{2,6},{4,0},{6,2},{8,12},{10,14},{12,8},{14,10},{16,20},{18,... | collective-permute-start | bytes 497672 | tf_op jit(solution)/shard_map/ppermute | solution.py:33
  70.1 0.5 collective-permute-start.24
  70.6 0.1 copy-done.20
  70.7 0.5 copy-done.22
  71.2 2.6 %finish.2.refs_8_ = f32[3,9,192,384]{3,2,1,0:T(8,128)} custom-call(s32[1]{0:T(128)} %bitcast.refs_0_.me_ref, bf16[9,24,384]{2,1,0:T(8,128)(2,1)} %bitcast.39, bf16[9,24,384]{2,1,0:T(8,128)(2,1)} %bitcast.43, bf16[9,24,384]{2,1,0:T(8,128)(2,1)} %bitcast.42, bf16[9,24,384]{2,1,0:T(8,128)(2,1)} %bitcast.44, ...), custom_call_target="tpu_custom_call", output_to_operand_aliasing={{}: (9, {})} | custom-call | bytes 3981312 | tf_op jit(solution)/shard_map/finish/pallas_call | solution.py:484
  73.8 1.3 %collective-permute-done.20 = bf16[216,384]{1,0:T(8,128)(2,1)S(1)} collective-permute-done((bf16[216,384]{1,0:T(8,128)(2,1)S(1)}, bf16[216,384]{1,0:T(8,128)(2,1)S(1)}, u32[]{:S(2)}, u32[]{:S(2)}) %collective-permute-start.20) | collective-permute-done | bytes 165920 | tf_op jit(solution)/shard_map/ppermute | solution.py:33
  75.1 2.7 %collective-permute-done.21 = bf16[216,384]{1,0:T(8,128)(2,1)S(1)} collective-permute-done((bf16[216,384]{1,0:T(8,128)(2,1)S(1)}, bf16[216,384]{1,0:T(8,128)(2,1)S(1)}, u32[]{:S(2)}, u32[]{:S(2)}) %collective-permute-start.21) | collective-permute-done | bytes 165920 | tf_op jit(solution)/shard_map/ppermute | solution.py:33
  77.8 0.5 collective-permute-start.25
  78.3 0.9 %collective-permute-done.23 = bf16[216,384]{1,0:T(8,128)(2,1)S(1)} collective-permute-done((bf16[216,384]{1,0:T(8,128)(2,1)S(1)}, bf16[216,384]{1,0:T(8,128)(2,1)S(1)}, u32[]{:S(2)}, u32[]{:S(2)}) %collective-permute-start.23) | collective-permute-done | bytes 165920 | tf_op jit(solution)/shard_map/ppermute | solution.py:33
  79.2 0.2 collective-permute-done.25
  79.4 0.4 copy-done.23
  79.8 0.2 copy-done.24
  80.1 2.6 %finish.3 = f32[3,9,192,384]{3,2,1,0:T(8,128)} custom-call(s32[1]{0:T(128)} %bitcast.refs_0_.me_ref, bf16[9,24,384]{2,1,0:T(8,128)(2,1)} %bitcast.41, bf16[9,24,384]{2,1,0:T(8,128)(2,1)} %bitcast.45, bf16[9,24,384]{2,1,0:T(8,128)(2,1)} %bitcast.40, bf16[9,24,384]{2,1,0:T(8,128)(2,1)} %bitcast.46, ...), custom_call_target="tpu_custom_call", output_to_operand_aliasing={{}: (9, {})} | custom-call | bytes 3981312 | tf_op jit(solution)/shard_map/finish/pallas_call | solution.py:484
  (72 shorter events, 0.5 us)
Async XLA Ops:
  0.6 1.6 %copy-start = (bf16[2,2,64,2560]{3,2,1,0:T(8,128)(2,1)S(1)}, bf16[2,2,64,2560]{3,2,1,0:T(8,128)(2,1)}, u32[]{:S(2)}) copy-start(bf16[2,2,64,2560]{3,2,1,0:T(8,128)(2,1)} %param.6) | copy-start | bytes 3932164
  3.7 5.6 %collective-permute-start = (f32[64,256]{1,0:T(8,128)S(1)}, f32[64,256]{1,0:T(8,128)S(1)}, u32[]{:S(2)}, u32[]{:S(2)}) collective-permute-start(f32[64,256]{1,0:T(8,128)S(1)} %convolution_bitcast_fusion), channel_id=1, source_target_pairs={{0,1},{1,0},{2,3},{3,2},{4,5},{5,4},{6,7},{7,6},{8,9},{9,8},{10,11... | collective-permute-start | bytes 196616 | tf_op jit(solution)/shard_map/ppermute | solution.py:33
  6.7 12.9 %collective-permute-start.2 = (bf16[4,24,1024]{2,1,0:T(8,128)(2,1)S(1)}, bf16[4,24,1024]{2,1,0:T(8,128)(2,1)S(1)}, u32[]{:S(2)}, u32[]{:S(2)}) collective-permute-start(bf16[4,24,1024]{2,1,0:T(8,128)(2,1)S(1)} %pad_maximum_fusion), channel_id=1, source_target_pairs={{0,16},{2,18},{4,20},{6,22},{8,24},{10,26},{12,28},{14,30},{16,0},... | collective-permute-start | bytes 589832 | tf_op jit(solution)/shard_map/ppermute | solution.py:33
  9.3 20.5 %copy-start.25 = (f32[384]{0:T(512)S(1)}, f32[384]{0:T(512)}, u32[]{:S(2)}) copy-start(f32[384]{0:T(512)} %param.8) | copy-start | bytes 4612
  9.3 10.2 %collective-permute-start.1 = (bf16[16,1024]{1,0:T(8,128)(2,1)S(1)}, bf16[16,1024]{1,0:T(8,128)(2,1)S(1)}, u32[]{:S(2)}, u32[]{:S(2)}) collective-permute-start(bf16[16,1024]{1,0:T(8,128)(2,1)S(1)} %get-tuple-element.67), channel_id=1, source_target_pairs={{0,16},{2,18},{4,20},{6,22},{8,24},{10,26},{12,28},{14,30},{16,0},... | collective-permute-start | bytes 98312 | tf_op jit(solution)/shard_map/ppermute | solution.py:33
  19.7 11.2 %copy-start.1 = (bf16[2,40,1024]{2,1,0:T(8,128)(2,1)}, bf16[2,40,1024]{2,1,0:T(8,128)(2,1)S(1)}, u32[]{:S(2)}) copy-start(bf16[2,40,1024]{2,1,0:T(8,128)(2,1)S(1)} %get-tuple-element.30.refs_3_.refs_0_) | copy-start | bytes 491524
  19.7 7.4 %collective-permute-start.5 = (bf16[2,40,1024]{2,1,0:T(8,128)(2,1)S(1)}, bf16[2,40,1024]{2,1,0:T(8,128)(2,1)S(1)}, u32[]{:S(2)}, u32[]{:S(2)}) collective-permute-start(bf16[2,40,1024]{2,1,0:T(8,128)(2,1)S(1)} %get-tuple-element.62), channel_id=1, source_target_pairs={{0,12},{2,14},{4,8},{6,10},{8,4},{10,6},{12,0},{14,2},{16,28},{18,... | collective-permute-start | bytes 491528 | tf_op jit(solution)/shard_map/ppermute | solution.py:33
  21.4 7.9 %collective-permute-start.3 = (bf16[2,40,1024]{2,1,0:T(8,128)(2,1)S(1)}, bf16[2,40,1024]{2,1,0:T(8,128)(2,1)S(1)}, u32[]{:S(2)}, u32[]{:S(2)}) collective-permute-start(bf16[2,40,1024]{2,1,0:T(8,128)(2,1)S(1)} %get-tuple-element.63), channel_id=1, source_target_pairs={{0,4},{2,6},{4,0},{6,2},{8,12},{10,14},{12,8},{14,10},{16,20},{18,... | collective-permute-start | bytes 491528 | tf_op jit(solution)/shard_map/ppermute | solution.py:33
  21.9 7.4 %collective-permute-start.4 = (bf16[2,40,1024]{2,1,0:T(8,128)(2,1)S(1)}, bf16[2,40,1024]{2,1,0:T(8,128)(2,1)S(1)}, u32[]{:S(2)}, u32[]{:S(2)}) collective-permute-start(bf16[2,40,1024]{2,1,0:T(8,128)(2,1)S(1)} %get-tuple-element.64), channel_id=1, source_target_pairs={{0,8},{2,10},{4,12},{6,14},{8,0},{10,2},{12,4},{14,6},{16,24},{18,... | collective-permute-start | bytes 491528 | tf_op jit(solution)/shard_map/ppermute | solution.py:33
  23.2 7.2 %collective-permute-start.6 = (bf16[2,40,1024]{2,1,0:T(8,128)(2,1)S(1)}, bf16[2,40,1024]{2,1,0:T(8,128)(2,1)S(1)}, u32[]{:S(2)}, u32[]{:S(2)}) collective-permute-start(bf16[2,40,1024]{2,1,0:T(8,128)(2,1)S(1)} %get-tuple-element.30.refs_3_.refs_0_), channel_id=1, source_target_pairs={{0,2},{2,0},{4,6},{6,4},{8,10},{10,8},{12,14},{14,12},{16,18},{18,... | collective-permute-start | bytes 491528 | tf_op jit(solution)/shard_map/ppermute | solution.py:33
  27.1 3.8 %copy-start.3 = (bf16[2,40,1024]{2,1,0:T(8,128)(2,1)}, bf16[2,40,1024]{2,1,0:T(8,128)(2,1)S(1)}, u32[]{:S(2)}) copy-start(bf16[2,40,1024]{2,1,0:T(8,128)(2,1)S(1)} %collective-permute-done.5.refs_6_.refs_3_) | copy-start | bytes 491524
  27.1 3.3 %collective-permute-start.9 = (bf16[2,40,1024]{2,1,0:T(8,128)(2,1)S(1)}, bf16[2,40,1024]{2,1,0:T(8,128)(2,1)S(1)}, u32[]{:S(2)}, u32[]{:S(2)}) collective-permute-start(bf16[2,40,1024]{2,1,0:T(8,128)(2,1)S(1)} %collective-permute-done.5.refs_6_.refs_3_), channel_id=1, source_target_pairs={{0,2},{2,0},{4,6},{6,4},{8,10},{10,8},{12,14},{14,12},{16,18},{18,... | collective-permute-start | bytes 491528 | tf_op jit(solution)/shard_map/ppermute | solution.py:33
  29.2 1.6 %copy-start.4 = (bf16[2,40,1024]{2,1,0:T(8,128)(2,1)}, bf16[2,40,1024]{2,1,0:T(8,128)(2,1)S(1)}, u32[]{:S(2)}) copy-start(bf16[2,40,1024]{2,1,0:T(8,128)(2,1)S(1)} %collective-permute-done.3.refs_4_.refs_1_) | copy-start | bytes 491524
  29.3 1.4 %collective-permute-start.7 = (bf16[2,40,1024]{2,1,0:T(8,128)(2,1)S(1)}, bf16[2,40,1024]{2,1,0:T(8,128)(2,1)S(1)}, u32[]{:S(2)}, u32[]{:S(2)}) collective-permute-start(bf16[2,40,1024]{2,1,0:T(8,128)(2,1)S(1)} %collective-permute-done.3.refs_4_.refs_1_), channel_id=1, source_target_pairs={{0,2},{2,0},{4,6},{6,4},{8,10},{10,8},{12,14},{14,12},{16,18},{18,... | collective-permute-start | bytes 491528 | tf_op jit(solution)/shard_map/ppermute | solution.py:33
  29.3 1.6 %copy-start.5 = (bf16[2,40,1024]{2,1,0:T(8,128)(2,1)}, bf16[2,40,1024]{2,1,0:T(8,128)(2,1)S(1)}, u32[]{:S(2)}) copy-start(bf16[2,40,1024]{2,1,0:T(8,128)(2,1)S(1)} %collective-permute-done.4.refs_5_.refs_2_) | copy-start | bytes 491524
  29.3 1.6 %collective-permute-start.8 = (bf16[2,40,1024]{2,1,0:T(8,128)(2,1)S(1)}, bf16[2,40,1024]{2,1,0:T(8,128)(2,1)S(1)}, u32[]{:S(2)}, u32[]{:S(2)}) collective-permute-start(bf16[2,40,1024]{2,1,0:T(8,128)(2,1)S(1)} %collective-permute-done.4.refs_5_.refs_2_), channel_id=1, source_target_pairs={{0,2},{2,0},{4,6},{6,4},{8,10},{10,8},{12,14},{14,12},{16,18},{18,... | collective-permute-start | bytes 491528 | tf_op jit(solution)/shard_map/ppermute | solution.py:33
  30.4 0.7 copy-start.6
  30.4 0.7 copy-start.7
  30.6 0.7 copy-start.8
  30.9 0.7 copy-start.9
  44.3 1.7 %collective-permute-start.10 = (bf16[216,384]{1,0:T(8,128)(2,1)}, bf16[216,384]{1,0:T(8,128)(2,1)S(1)}, u32[]{:S(2)}, u32[]{:S(2)}) collective-permute-start(bf16[216,384]{1,0:T(8,128)(2,1)} %get-tuple-element.29), channel_id=1, source_target_pairs={{0,2},{2,0},{4,6},{6,4},{8,10},{10,8},{12,14},{14,12},{16,18},{18,... | collective-permute-start | bytes 497672 | tf_op jit(solution)/shard_map/ppermute | solution.py:33
  46.9 23.6 %copy-start.2 = (bf16[216,384]{1,0:T(8,128)(2,1)}, bf16[216,384]{1,0:T(8,128)(2,1)S(1)}, u32[]{:S(2)}) copy-start(bf16[216,384]{1,0:T(8,128)(2,1)S(1)} %add_convert_fusion) | copy-start | bytes 497668
  47.0 6.5 %collective-permute-start.11 = (bf16[216,384]{1,0:T(8,128)(2,1)S(1)}, bf16[216,384]{1,0:T(8,128)(2,1)S(1)}, u32[]{:S(2)}, u32[]{:S(2)}) collective-permute-start(bf16[216,384]{1,0:T(8,128)(2,1)S(1)} %add_convert_fusion), channel_id=1, source_target_pairs={{0,8},{2,10},{4,12},{6,14},{8,0},{10,2},{12,4},{14,6},{16,24},{18,... | collective-permute-start | bytes 497672 | tf_op jit(solution)/shard_map/ppermute | solution.py:33
  48.7 14.9 %collective-permute-start.15 = (bf16[216,384]{1,0:T(8,128)(2,1)S(1)}, bf16[216,384]{1,0:T(8,128)(2,1)S(1)}, u32[]{:S(2)}, u32[]{:S(2)}) collective-permute-start(bf16[216,384]{1,0:T(8,128)(2,1)S(1)} %add_convert_fusion), channel_id=1, source_target_pairs={{0,24},{2,26},{4,28},{6,30},{8,16},{10,18},{12,20},{14,22},{16,8},... | collective-permute-start | bytes 497672 | tf_op jit(solution)/shard_map/ppermute | solution.py:33
  51.9 15.0 %collective-permute-start.14 = (bf16[216,384]{1,0:T(8,128)(2,1)S(1)}, bf16[216,384]{1,0:T(8,128)(2,1)S(1)}, u32[]{:S(2)}, u32[]{:S(2)}) collective-permute-start(bf16[216,384]{1,0:T(8,128)(2,1)S(1)} %add_convert_fusion), channel_id=1, source_target_pairs={{0,16},{2,18},{4,20},{6,22},{8,24},{10,26},{12,28},{14,30},{16,0},... | collective-permute-start | bytes 497672 | tf_op jit(solution)/shard_map/ppermute | solution.py:33
  52.0 14.9 %collective-permute-start.12 = (bf16[216,384]{1,0:T(8,128)(2,1)S(1)}, bf16[216,384]{1,0:T(8,128)(2,1)S(1)}, u32[]{:S(2)}, u32[]{:S(2)}) collective-permute-start(bf16[216,384]{1,0:T(8,128)(2,1)S(1)} %add_convert_fusion), channel_id=1, source_target_pairs={{0,4},{2,6},{4,0},{6,2},{8,12},{10,14},{12,8},{14,10},{16,20},{18,... | collective-permute-start | bytes 497672 | tf_op jit(solution)/shard_map/ppermute | solution.py:33
  53.4 17.1 %copy-start.12 = (bf16[216,384]{1,0:T(8,128)(2,1)}, bf16[216,384]{1,0:T(8,128)(2,1)S(1)}, u32[]{:S(2)}) copy-start(bf16[216,384]{1,0:T(8,128)(2,1)S(1)} %collective-permute-done.11) | copy-start | bytes 497668
  53.4 13.4 %collective-permute-start.13 = (bf16[216,384]{1,0:T(8,128)(2,1)S(1)}, bf16[216,384]{1,0:T(8,128)(2,1)S(1)}, u32[]{:S(2)}, u32[]{:S(2)}) collective-permute-start(bf16[216,384]{1,0:T(8,128)(2,1)S(1)} %collective-permute-done.11), channel_id=1, source_target_pairs={{0,4},{2,6},{4,0},{6,2},{8,12},{10,14},{12,8},{14,10},{16,20},{18,... | collective-permute-start | bytes 497672 | tf_op jit(solution)/shard_map/ppermute | solution.py:33
  63.6 10.2 %copy-start.10 = (bf16[216,384]{1,0:T(8,128)(2,1)}, bf16[216,384]{1,0:T(8,128)(2,1)S(1)}, u32[]{:S(2)}) copy-start(bf16[216,384]{1,0:T(8,128)(2,1)S(1)} %collective-permute-done.15) | copy-start | bytes 497668
  66.9 6.9 %copy-start.11 = (bf16[216,384]{1,0:T(8,128)(2,1)}, bf16[216,384]{1,0:T(8,128)(2,1)S(1)}, u32[]{:S(2)}) copy-start(bf16[216,384]{1,0:T(8,128)(2,1)S(1)} %collective-permute-done.14) | copy-start | bytes 497668
  66.9 3.7 %copy-start.13 = (bf16[216,384]{1,0:T(8,128)(2,1)}, bf16[216,384]{1,0:T(8,128)(2,1)S(1)}, u32[]{:S(2)}) copy-start(bf16[216,384]{1,0:T(8,128)(2,1)S(1)} %collective-permute-done.12) | copy-start | bytes 497668
  66.9 3.7 %copy-start.14 = (bf16[216,384]{1,0:T(8,128)(2,1)}, bf16[216,384]{1,0:T(8,128)(2,1)S(1)}, u32[]{:S(2)}) copy-start(bf16[216,384]{1,0:T(8,128)(2,1)S(1)} %collective-permute-done.13) | copy-start | bytes 497668
  66.9 2.1 %collective-permute-start.16 = (bf16[216,384]{1,0:T(8,128)(2,1)S(1)}, bf16[216,384]{1,0:T(8,128)(2,1)S(1)}, u32[]{:S(2)}, u32[]{:S(2)}) collective-permute-start(bf16[216,384]{1,0:T(8,128)(2,1)S(1)} %add_convert_fusion), channel_id=1, source_target_pairs={{0,2},{2,0},{4,6},{6,4},{8,10},{10,8},{12,14},{14,12},{16,18},{18,... | collective-permute-start | bytes 497672 | tf_op jit(solution)/shard_map/ppermute | solution.py:33
  67.0 3.0 %collective-permute-start.17 = (bf16[216,384]{1,0:T(8,128)(2,1)S(1)}, bf16[216,384]{1,0:T(8,128)(2,1)S(1)}, u32[]{:S(2)}, u32[]{:S(2)}) collective-permute-start(bf16[216,384]{1,0:T(8,128)(2,1)S(1)} %collective-permute-done.12), channel_id=1, source_target_pairs={{0,2},{2,0},{4,6},{6,4},{8,10},{10,8},{12,14},{14,12},{16,18},{18,... | collective-permute-start | bytes 497672 | tf_op jit(solution)/shard_map/ppermute | solution.py:33
  67.5 2.6 %collective-permute-start.18 = (bf16[216,384]{1,0:T(8,128)(2,1)S(1)}, bf16[216,384]{1,0:T(8,128)(2,1)S(1)}, u32[]{:S(2)}, u32[]{:S(2)}) collective-permute-start(bf16[216,384]{1,0:T(8,128)(2,1)S(1)} %collective-permute-done.11), channel_id=1, source_target_pairs={{0,2},{2,0},{4,6},{6,4},{8,10},{10,8},{12,14},{14,12},{16,18},{18,... | collective-permute-start | bytes 497672 | tf_op jit(solution)/shard_map/ppermute | solution.py:33
  67.6 3.0 %collective-permute-start.19 = (bf16[216,384]{1,0:T(8,128)(2,1)S(1)}, bf16[216,384]{1,0:T(8,128)(2,1)S(1)}, u32[]{:S(2)}, u32[]{:S(2)}) collective-permute-start(bf16[216,384]{1,0:T(8,128)(2,1)S(1)} %collective-permute-done.13), channel_id=1, source_target_pairs={{0,2},{2,0},{4,6},{6,4},{8,10},{10,8},{12,14},{14,12},{16,18},{18,... | collective-permute-start | bytes 497672 | tf_op jit(solution)/shard_map/ppermute | solution.py:33
  68.0 7.1 %collective-permute-start.20 = (bf16[216,384]{1,0:T(8,128)(2,1)S(1)}, bf16[216,384]{1,0:T(8,128)(2,1)S(1)}, u32[]{:S(2)}, u32[]{:S(2)}) collective-permute-start(bf16[216,384]{1,0:T(8,128)(2,1)S(1)} %collective-permute-done.14), channel_id=1, source_target_pairs={{0,4},{2,6},{4,0},{6,2},{8,12},{10,14},{12,8},{14,10},{16,20},{18,... | collective-permute-start | bytes 497672 | tf_op jit(solution)/shard_map/ppermute | solution.py:33
  69.0 1.6 %copy-start.18 = (bf16[216,384]{1,0:T(8,128)(2,1)}, bf16[216,384]{1,0:T(8,128)(2,1)S(1)}, u32[]{:S(2)}) copy-start(bf16[216,384]{1,0:T(8,128)(2,1)S(1)} %collective-permute-done.16) | copy-start | bytes 497668
  69.0 8.8 %collective-permute-start.21 = (bf16[216,384]{1,0:T(8,128)(2,1)S(1)}, bf16[216,384]{1,0:T(8,128)(2,1)S(1)}, u32[]{:S(2)}, u32[]{:S(2)}) collective-permute-start(bf16[216,384]{1,0:T(8,128)(2,1)S(1)} %collective-permute-done.15), channel_id=1, source_target_pairs={{0,4},{2,6},{4,0},{6,2},{8,12},{10,14},{12,8},{14,10},{16,20},{18,... | collective-permute-start | bytes 497672 | tf_op jit(solution)/shard_map/ppermute | solution.py:33
  70.0 8.3 %collective-permute-start.22 = (bf16[216,384]{1,0:T(8,128)(2,1)S(1)}, bf16[216,384]{1,0:T(8,128)(2,1)S(1)}, u32[]{:S(2)}, u32[]{:S(2)}) collective-permute-start(bf16[216,384]{1,0:T(8,128)(2,1)S(1)} %collective-permute-done.14), channel_id=1, source_target_pairs={{0,2},{2,0},{4,6},{6,4},{8,10},{10,8},{12,14},{14,12},{16,18},{18,... | collective-permute-start | bytes 497672 | tf_op jit(solution)/shard_map/ppermute | solution.py:33
  70.0 0.7 copy-start.21
  70.1 8.2 %collective-permute-start.24 = (bf16[216,384]{1,0:T(8,128)(2,1)S(1)}, bf16[216,384]{1,0:T(8,128)(2,1)S(1)}, u32[]{:S(2)}, u32[]{:S(2)}) collective-permute-start(bf16[216,384]{1,0:T(8,128)(2,1)S(1)} %collective-permute-done.15), channel_id=1, source_target_pairs={{0,2},{2,0},{4,6},{6,4},{8,10},{10,8},{12,14},{14,12},{16,18},{18,... | collective-permute-start | bytes 497672 | tf_op jit(solution)/shard_map/ppermute | solution.py:33
  75.1 4.3 %copy-start.15 = (bf16[216,384]{1,0:T(8,128)(2,1)}, bf16[216,384]{1,0:T(8,128)(2,1)S(1)}, u32[]{:S(2)}) copy-start(bf16[216,384]{1,0:T(8,128)(2,1)S(1)} %collective-permute-done.20) | copy-start | bytes 497668
  77.8 1.6 %copy-start.16 = (bf16[216,384]{1,0:T(8,128)(2,1)}, bf16[216,384]{1,0:T(8,128)(2,1)S(1)}, u32[]{:S(2)}) copy-start(bf16[216,384]{1,0:T(8,128)(2,1)S(1)} %collective-permute-done.21) | copy-start | bytes 497668
  77.8 1.4 %collective-permute-start.23 = (bf16[216,384]{1,0:T(8,128)(2,1)S(1)}, bf16[216,384]{1,0:T(8,128)(2,1)S(1)}, u32[]{:S(2)}, u32[]{:S(2)}) collective-permute-start(bf16[216,384]{1,0:T(8,128)(2,1)S(1)} %collective-permute-done.20), channel_id=1, source_target_pairs={{0,2},{2,0},{4,6},{6,4},{8,10},{10,8},{12,14},{14,12},{16,18},{18,... | collective-permute-start | bytes 497672 | tf_op jit(solution)/shard_map/ppermute | solution.py:33
  77.8 1.6 %collective-permute-start.25 = (bf16[216,384]{1,0:T(8,128)(2,1)S(1)}, bf16[216,384]{1,0:T(8,128)(2,1)S(1)}, u32[]{:S(2)}, u32[]{:S(2)}) collective-permute-start(bf16[216,384]{1,0:T(8,128)(2,1)S(1)} %collective-permute-done.21), channel_id=1, source_target_pairs={{0,2},{2,0},{4,6},{6,4},{8,10},{10,8},{12,14},{14,12},{16,18},{18,... | collective-permute-start | bytes 497672 | tf_op jit(solution)/shard_map/ppermute | solution.py:33
  78.3 1.1 %copy-start.17 = (bf16[216,384]{1,0:T(8,128)(2,1)}, bf16[216,384]{1,0:T(8,128)(2,1)S(1)}, u32[]{:S(2)}) copy-start(bf16[216,384]{1,0:T(8,128)(2,1)S(1)} %collective-permute-done.22) | copy-start | bytes 497668
  78.3 1.1 %copy-start.19 = (bf16[216,384]{1,0:T(8,128)(2,1)}, bf16[216,384]{1,0:T(8,128)(2,1)S(1)}, u32[]{:S(2)}) copy-start(bf16[216,384]{1,0:T(8,128)(2,1)S(1)} %collective-permute-done.24) | copy-start | bytes 497668
  (4 other events, 2.6 us)

commit v10 on v6

--- a/solution.py
+++ b/solution.py
@@ -78,12 +78,15 @@
 
 
 def fetch(piece_refs, mask_lists, slot_ref, sems):
+    count = slot_ref.shape[1]
     copies = []
     for index, (piece_ref, masks) in enumerate(zip(piece_refs, mask_lists)):
         for position, mask in enumerate(masks):
             copies.append(
                 pltpu.make_async_copy(
-                    piece_ref.at[position], slot_ref.at[mask], sems.at[index * len(masks) + position]
+                    piece_ref.at[position, pl.ds(0, count)],
+                    slot_ref.at[mask],
+                    sems.at[index * len(masks) + position],
                 )
             )
     for copy in copies:
@@ -295,21 +298,28 @@
 def finish_kernel(pieces, me_ref, *refs):
     count = len(pieces)
     piece_refs = refs[:count]
-    out_hbm, wide_ref, sems = refs[count + 1 :]
+    out_hbm, narrow_ref, wide_ref, in_sems, out_sems = refs[count + 1 :]
     me = me_ref[0]
     channels = wide_ref.shape[2]
-    copies = []
+    loads = [
+        pltpu.make_async_copy(piece_refs[index], narrow_ref.at[index], in_sems.at[index])
+        for index in range(count)
+    ]
+    for load in loads:
+        load.start()
+    stores = []
     for index, mask in enumerate(pieces):
         source = me ^ mask
-        wide_ref[index] = piece_refs[index][...].astype(F32)
+        loads[index].wait()
+        wide_ref[index] = narrow_ref[index].astype(F32)
         at = pl.multiple_of((source >> 1) * channels, 8)
-        copy = pltpu.make_async_copy(
-            wide_ref.at[index], out_hbm.at[2 - (source & 1), :, pl.ds(at, channels), :], sems.at[index]
+        store = pltpu.make_async_copy(
+            wide_ref.at[index], out_hbm.at[2 - (source & 1), :, pl.ds(at, channels), :], out_sems.at[index]
         )
-        copy.start()
-        copies.append(copy)
-    for copy in copies:
-        copy.wait()
+        store.start()
+        stores.append(store)
+    for store in stores:
+        store.wait()
 
 
 def per_device(attn_out, w_proj, norm_gain, entry_weight, conv_weight, cotangent):
@@ -443,7 +453,7 @@
         in_specs=[smem(), vmem(), vmem(), hbm] + [hbm] * len(pieces),
         out_specs=vmem(),
         scratch_shapes=[
-            pltpu.VMEM(slot_shape, BF16),
+            pltpu.VMEM((slabs, latent_width, frames * rows * width), BF16),
             pltpu.VMEM((frames, 3 * latent_width, (rows + 4) * width), BF16),
             pltpu.VMEM((channels, (rows + 2) * width), F32),
             pltpu.VMEM((channels, (rows + 2) * width), BF16),
@@ -469,10 +479,12 @@
         return pl.pallas_call(
             functools.partial(finish_kernel, sources),
             out_shape=jax.ShapeDtypeStruct(grad_shape, F32),
-            in_specs=[smem()] + [vmem()] * len(parts) + [hbm],
+            in_specs=[smem()] + [hbm] * (len(parts) + 1),
             out_specs=hbm,
             scratch_shapes=[
+                pltpu.VMEM((len(parts),) + shape, BF16),
                 pltpu.VMEM((len(parts),) + shape, F32),
+                pltpu.SemaphoreType.DMA((len(parts),)),
                 pltpu.SemaphoreType.DMA((len(parts),)),
             ],
             input_output_aliases={len(parts) + 1: 0},

time: 80.5 us -> 80.1 us (level)
  Pallas kernels: 30.2 us -> 29.1 us
    pallas_call x2, Pallas kernels: 5.95 us -> 5.13 us  [finish(): pl.pallas_call(functools.partial(finish_kernel, sources), out_shape=jax.S...]
  transfers between devices with their start and end apart: 26 -> 26, of which waited for: 13 -> 13; matrix products, arithmetic and copies ran while one was open for 3% -> 3% of each run, Pallas kernels for 19% -> 18%
where the time goes in v10:
time: 80.1 us; the launch traced here: 79.7 us
  Pallas kernels  29.1 us (36%)
  waiting for transfers between devices  22.8 us (28%)
  starting transfers between devices  19.5 us (24%)
  local copies, waits for them, and re-layouts  4.57 us (6%)
  matrix products  1.48 us (2%)
  between operations  1.19 us (1%)
  other arithmetic  1.1 us (1%)
    ppermute x26, waiting for transfers between devices, xor_permute(): lax.ppermute(x, axis, [(i, i ^ mask) for i in range(lax.axis_size(axis))])  22.8 us
    ppermute x26, starting transfers between devices, xor_permute(): lax.ppermute(x, axis, [(i, i ^ mask) for i in range(lax.axis_size(axis))])  19.5 us
    pallas_call x1, Pallas kernels, per_device(): pl.pallas_call(functools.partial(gradient_kernel, frames, rows, slabs, ma...  12 us
    pallas_call x1, Pallas kernels, per_device(): pl.pallas_call(functools.partial(decode_kernel, frames, rows, slabs, mask...  8.64 us
    pallas_call x2, Pallas kernels, finish(): pl.pallas_call(functools.partial(finish_kernel, sources), out_shape=jax.S...  5.13 us
    unnamed x58, local copies, waits for them, and re-layouts  2.62 us
    pallas_call x1, Pallas kernels, per_device(): pl.pallas_call(functools.partial(unpatchify_kernel, frames, tok_rows, tok...  1.67 us
  transfers between devices with their start and end apart: 26, of which 13 were waited for; matrix products, arithmetic and copies ran while one was open for 3% of the time, Pallas kernels for 18%

profile of v10, /device:TPU:0, one launch (start us, length us, event | category | flops | bytes accessed | tf_op | source)
XLA Modules:
  0.0 79.7 jit_solution(781947326105923388)
XLA Ops:
  0.7 1.4 %reshape.77 = bf16[8,24,1024]{2,1,0:T(8,128)(2,1)S(1)} reshape(bf16[192,2,4,128]{3,2,1,0:T(4,128)(2,1)} %param.11) | data formatting | bytes 786432 | tf_op jit(solution)/shard_map/reshape | solution.py:348
  2.2 4.1 %collective-permute-start.2 = (bf16[4,24,1024]{2,1,0:T(8,128)(2,1)S(1)}, bf16[4,24,1024]{2,1,0:T(8,128)(2,1)S(1)}, u32[]{:S(2)}, u32[]{:S(2)}) collective-permute-start(bf16[4,24,1024]{2,1,0:T(8,128)(2,1)S(1)} %pad_maximum_fusion), channel_id=1, source_target_pairs={{0,16},{2,18},{4,20},{6,22},{8,24},{10,26},{12,28},{14,30},{16,0},... | collective-permute-start | bytes 589832 | tf_op jit(solution)/shard_map/ppermute | solution.py:33
  6.3 1.5 %convolution_bitcast_fusion.own_ref = f32[64,256]{1,0:T(8,128)S(1)} fusion(bf16[256,2560]{1,0:T(8,128)(2,1)S(1)} %bitcast.33, bf16[2560,64]{0,1:T(8,128)(2,1)} %param.7), kind=kOutput, calls=%fused_computation | convolution fusion | flops 83886080 | bytes 1703936 | tf_op jit(solution)/shard_map/dot_general | solution.py:364
  7.8 1.6 %collective-permute-start = (f32[64,256]{1,0:T(8,128)S(1)}, f32[64,256]{1,0:T(8,128)S(1)}, u32[]{:S(2)}, u32[]{:S(2)}) collective-permute-start(f32[64,256]{1,0:T(8,128)S(1)} %convolution_bitcast_fusion.own_ref), channel_id=1, source_target_pairs={{0,1},{1,0},{2,3},{3,2},{4,5},{5,4},{6,7},{7,6},{8,9},{9,8},{10,11... | collective-permute-start | bytes 196616 | tf_op jit(solution)/shard_map/ppermute | solution.py:33
  9.3 2.8 %collective-permute-done.other_ref = f32[64,256]{1,0:T(8,128)S(1)} collective-permute-done((f32[64,256]{1,0:T(8,128)S(1)}, f32[64,256]{1,0:T(8,128)S(1)}, u32[]{:S(2)}, u32[]{:S(2)}) %collective-permute-start) | collective-permute-done | bytes 65568 | tf_op jit(solution)/shard_map/ppermute | solution.py:33
  12.1 0.6 copy-done.27
  12.7 1.7 %unpatchify.1 = bf16[16,1024]{1,0:T(8,128)(2,1)} custom-call(f32[64,256]{1,0:T(8,128)} %copy-done.10, f32[64,256]{1,0:T(8,128)} %copy-done.27), custom_call_target="tpu_custom_call" | custom-call | tf_op jit(solution)/shard_map/unpatchify/pallas_call | solution.py:379
  14.4 1.6 %blank.1.refs_8_ = f32[3,9,192,384]{3,2,1,0:T(8,128)} custom-call(), custom_call_target="tpu_custom_call" | custom-call | bytes 2654208 | tf_op jit(solution)/shard_map/blank/pallas_call | solution.py:391
  16.0 3.4 %collective-permute-done.1 = bf16[16,1024]{1,0:T(8,128)(2,1)S(1)} collective-permute-done((bf16[16,1024]{1,0:T(8,128)(2,1)}, bf16[16,1024]{1,0:T(8,128)(2,1)S(1)}, u32[]{:S(2)}, u32[]{:S(2)}) %collective-permute-start.1) | collective-permute-done | bytes 32800 | tf_op jit(solution)/shard_map/ppermute | solution.py:33
  19.6 2.6 %collective-permute-start.5 = (bf16[2,40,1024]{2,1,0:T(8,128)(2,1)S(1)}, bf16[2,40,1024]{2,1,0:T(8,128)(2,1)S(1)}, u32[]{:S(2)}, u32[]{:S(2)}) collective-permute-start(bf16[2,40,1024]{2,1,0:T(8,128)(2,1)S(1)} %get-tuple-element.62), channel_id=1, source_target_pairs={{0,12},{2,14},{4,8},{6,10},{8,4},{10,6},{12,0},{14,2},{16,28},{18,... | collective-permute-start | bytes 491528 | tf_op jit(solution)/shard_map/ppermute | solution.py:33
  22.2 0.5 collective-permute-start.3
  22.7 0.5 collective-permute-start.4
  23.1 3.7 %collective-permute-done.5.refs_6_.refs_3_ = bf16[2,40,1024]{2,1,0:T(8,128)(2,1)S(1)} collective-permute-done((bf16[2,40,1024]{2,1,0:T(8,128)(2,1)S(1)}, bf16[2,40,1024]{2,1,0:T(8,128)(2,1)S(1)}, u32[]{:S(2)}, u32[]{:S(2)}) %collective-permute-start.5) | collective-permute-done | bytes 163872 | tf_op jit(solution)/shard_map/ppermute | solution.py:33
  26.8 1.6 %collective-permute-done.3.refs_4_.refs_1_ = bf16[2,40,1024]{2,1,0:T(8,128)(2,1)S(1)} collective-permute-done((bf16[2,40,1024]{2,1,0:T(8,128)(2,1)S(1)}, bf16[2,40,1024]{2,1,0:T(8,128)(2,1)S(1)}, u32[]{:S(2)}, u32[]{:S(2)}) %collective-permute-start.3) | collective-permute-done | bytes 163872 | tf_op jit(solution)/shard_map/ppermute | solution.py:33
  28.4 0.5 collective-permute-start.8
  28.9 0.5 reshape.74.refs_1_.gain_ref
  29.5 0.3 collective-permute-done.7.refs_8_.refs_5_
  29.8 0.2 collective-permute-done.8.refs_9_.refs_6_
  30.2 0.3 copy-done.8
  30.5 0.2 copy-done.9
  30.7 12.0 %gradient.1 = (f32[216,384]{1,0:T(8,128)}, bf16[216,384]{1,0:T(8,128)(2,1)}) custom-call(s32[1]{0:T(128)} %bitcast.refs_0_.me_ref, f32[1,384]{1,0:T(1,128)} %reshape.74.refs_1_.gain_ref, bf16[432,384]{1,0:T(8,128)(2,1)} %bitcast.36, bf16[2,40,1024]{2,1,0:T(8,128)(2,1)} %copy-done.1, bf16[2,40,1024]{2,1,0:T(8,128)(2,1)} %copy-done.4, ...), custom_call_target="tpu_custom_call" | custom-call | tf_op jit(solution)/shard_map/gradient/pallas_call | solution.py:417
  42.7 0.3 collective-permute-start.10
  43.1 1.3 %collective-permute-done.10 = bf16[216,384]{1,0:T(8,128)(2,1)S(1)} collective-permute-done((bf16[216,384]{1,0:T(8,128)(2,1)}, bf16[216,384]{1,0:T(8,128)(2,1)S(1)}, u32[]{:S(2)}, u32[]{:S(2)}) %collective-permute-start.10) | collective-permute-done | bytes 165920 | tf_op jit(solution)/shard_map/ppermute | solution.py:33
  44.4 1.0 %add_convert_fusion = bf16[216,384]{1,0:T(8,128)(2,1)S(1)} fusion(f32[216,384]{1,0:T(8,128)} %get-tuple-element.28, bf16[216,384]{1,0:T(8,128)(2,1)S(1)} %collective-permute-done.10), kind=kLoop, calls=%fused_computation.1 | loop fusion | flops 248832 | bytes 663552 | tf_op jit(solution)/shard_map/convert_element_type | solution.py:442
  45.4 1.0 %collective-permute-start.11 = (bf16[216,384]{1,0:T(8,128)(2,1)S(1)}, bf16[216,384]{1,0:T(8,128)(2,1)S(1)}, u32[]{:S(2)}, u32[]{:S(2)}) collective-permute-start(bf16[216,384]{1,0:T(8,128)(2,1)S(1)} %add_convert_fusion), channel_id=1, source_target_pairs={{0,8},{2,10},{4,12},{6,14},{8,0},{10,2},{12,4},{14,6},{16,24},{18,... | collective-permute-start | bytes 497672 | tf_op jit(solution)/shard_map/ppermute | solution.py:33
  46.4 1.2 %collective-permute-start.15 = (bf16[216,384]{1,0:T(8,128)(2,1)S(1)}, bf16[216,384]{1,0:T(8,128)(2,1)S(1)}, u32[]{:S(2)}, u32[]{:S(2)}) collective-permute-start(bf16[216,384]{1,0:T(8,128)(2,1)S(1)} %add_convert_fusion), channel_id=1, source_target_pairs={{0,24},{2,26},{4,28},{6,30},{8,16},{10,18},{12,20},{14,22},{16,8},... | collective-permute-start | bytes 497672 | tf_op jit(solution)/shard_map/ppermute | solution.py:33
  47.6 1.4 %collective-permute-start.14 = (bf16[216,384]{1,0:T(8,128)(2,1)S(1)}, bf16[216,384]{1,0:T(8,128)(2,1)S(1)}, u32[]{:S(2)}, u32[]{:S(2)}) collective-permute-start(bf16[216,384]{1,0:T(8,128)(2,1)S(1)} %add_convert_fusion), channel_id=1, source_target_pairs={{0,16},{2,18},{4,20},{6,22},{8,24},{10,26},{12,28},{14,30},{16,0},... | collective-permute-start | bytes 497672 | tf_op jit(solution)/shard_map/ppermute | solution.py:33
  49.0 0.9 %collective-permute-start.12 = (bf16[216,384]{1,0:T(8,128)(2,1)S(1)}, bf16[216,384]{1,0:T(8,128)(2,1)S(1)}, u32[]{:S(2)}, u32[]{:S(2)}) collective-permute-start(bf16[216,384]{1,0:T(8,128)(2,1)S(1)} %add_convert_fusion), channel_id=1, source_target_pairs={{0,4},{2,6},{4,0},{6,2},{8,12},{10,14},{12,8},{14,10},{16,20},{18,... | collective-permute-start | bytes 497672 | tf_op jit(solution)/shard_map/ppermute | solution.py:33
  49.9 2.6 %collective-permute-done.11 = bf16[216,384]{1,0:T(8,128)(2,1)S(1)} collective-permute-done((bf16[216,384]{1,0:T(8,128)(2,1)S(1)}, bf16[216,384]{1,0:T(8,128)(2,1)S(1)}, u32[]{:S(2)}, u32[]{:S(2)}) %collective-permute-start.11) | collective-permute-done | bytes 165920 | tf_op jit(solution)/shard_map/ppermute | solution.py:33
  52.5 0.9 %collective-permute-start.13 = (bf16[216,384]{1,0:T(8,128)(2,1)S(1)}, bf16[216,384]{1,0:T(8,128)(2,1)S(1)}, u32[]{:S(2)}, u32[]{:S(2)}) collective-permute-start(bf16[216,384]{1,0:T(8,128)(2,1)S(1)} %collective-permute-done.11), channel_id=1, source_target_pairs={{0,4},{2,6},{4,0},{6,2},{8,12},{10,14},{12,8},{14,10},{16,20},{18,... | collective-permute-start | bytes 497672 | tf_op jit(solution)/shard_map/ppermute | solution.py:33
  53.3 8.6 %decode.1 = bf16[192,2,4,128]{3,2,1,0:T(4,128)(2,1)} custom-call(s32[1]{0:T(128)} %bitcast.refs_0_.me_ref, f32[1,384]{1,0:T(1,128)} %reshape.74.refs_1_.gain_ref, bf16[432,384]{1,0:T(8,128)(2,1)} %bitcast.37, bf16[27,192,384]{2,1,0:T(8,128)(2,1)} %bitcast.35, bf16[2,40,1024]{2,1,0:T(8,128)(2,1)} %copy-done.1, bf16[2,40,1024]{2,1,0:T(8,128)(2,1)} %copy-done.4, ...), custom_call_target="tpu_custom_call" | custom-call | tf_op jit(solution)/shard_map/decode/pallas_call | solution.py:450
  62.0 1.8 %collective-permute-done.14 = bf16[216,384]{1,0:T(8,128)(2,1)S(1)} collective-permute-done((bf16[216,384]{1,0:T(8,128)(2,1)S(1)}, bf16[216,384]{1,0:T(8,128)(2,1)S(1)}, u32[]{:S(2)}, u32[]{:S(2)}) %collective-permute-start.14) | collective-permute-done | bytes 165920 | tf_op jit(solution)/shard_map/ppermute | solution.py:33
  63.9 0.5 collective-permute-start.17
  64.5 0.4 collective-permute-start.19
  64.9 0.7 collective-permute-start.20
  65.6 1.3 %collective-permute-start.21 = (bf16[216,384]{1,0:T(8,128)(2,1)S(1)}, bf16[216,384]{1,0:T(8,128)(2,1)S(1)}, u32[]{:S(2)}, u32[]{:S(2)}) collective-permute-start(bf16[216,384]{1,0:T(8,128)(2,1)S(1)} %collective-permute-done.15), channel_id=1, source_target_pairs={{0,4},{2,6},{4,0},{6,2},{8,12},{10,14},{12,8},{14,10},{16,20},{18,... | collective-permute-start | bytes 497672 | tf_op jit(solution)/shard_map/ppermute | solution.py:33
  66.9 0.5 collective-permute-start.24
  67.5 0.1 copy-done.21
  67.6 0.5 copy-done.23
  68.1 2.6 %finish.2.refs_8_ = f32[3,9,192,384]{3,2,1,0:T(8,128)} custom-call(s32[1]{0:T(128)} %bitcast.refs_0_.me_ref, bf16[9,24,384]{2,1,0:T(8,128)(2,1)} %bitcast.38, bf16[9,24,384]{2,1,0:T(8,128)(2,1)} %bitcast.42, bf16[9,24,384]{2,1,0:T(8,128)(2,1)} %bitcast.41, bf16[9,24,384]{2,1,0:T(8,128)(2,1)} %bitcast.43, ...), custom_call_target="tpu_custom_call", output_to_operand_aliasing={{}: (9, {})} | custom-call | bytes 3981312 | tf_op jit(solution)/shard_map/finish/pallas_call | solution.py:479
  70.7 1.3 %collective-permute-done.20 = bf16[216,384]{1,0:T(8,128)(2,1)S(1)} collective-permute-done((bf16[216,384]{1,0:T(8,128)(2,1)S(1)}, bf16[216,384]{1,0:T(8,128)(2,1)S(1)}, u32[]{:S(2)}, u32[]{:S(2)}) %collective-permute-start.20) | collective-permute-done | bytes 165920 | tf_op jit(solution)/shard_map/ppermute | solution.py:33
  72.0 2.7 %collective-permute-done.21 = bf16[216,384]{1,0:T(8,128)(2,1)S(1)} collective-permute-done((bf16[216,384]{1,0:T(8,128)(2,1)S(1)}, bf16[216,384]{1,0:T(8,128)(2,1)S(1)}, u32[]{:S(2)}, u32[]{:S(2)}) %collective-permute-start.21) | collective-permute-done | bytes 165920 | tf_op jit(solution)/shard_map/ppermute | solution.py:33
  74.7 0.5 collective-permute-start.25
  75.2 0.9 %collective-permute-done.23 = bf16[216,384]{1,0:T(8,128)(2,1)S(1)} collective-permute-done((bf16[216,384]{1,0:T(8,128)(2,1)S(1)}, bf16[216,384]{1,0:T(8,128)(2,1)S(1)}, u32[]{:S(2)}, u32[]{:S(2)}) %collective-permute-start.23) | collective-permute-done | bytes 165920 | tf_op jit(solution)/shard_map/ppermute | solution.py:33
  76.1 0.2 collective-permute-done.25
  76.3 0.4 copy-done.24
  76.7 0.2 copy-done.25
  77.0 2.6 %finish.3 = f32[3,9,192,384]{3,2,1,0:T(8,128)} custom-call(s32[1]{0:T(128)} %bitcast.refs_0_.me_ref, bf16[9,24,384]{2,1,0:T(8,128)(2,1)} %bitcast.40, bf16[9,24,384]{2,1,0:T(8,128)(2,1)} %bitcast.44, bf16[9,24,384]{2,1,0:T(8,128)(2,1)} %bitcast.39, bf16[9,24,384]{2,1,0:T(8,128)(2,1)} %bitcast.45, ...), custom_call_target="tpu_custom_call", output_to_operand_aliasing={{}: (9, {})} | custom-call | bytes 3981312 | tf_op jit(solution)/shard_map/finish/pallas_call | solution.py:479
  (76 shorter events, 0.7 us)
Async XLA Ops:
  0.6 5.7 %copy-start = (bf16[2,2,64,2560]{3,2,1,0:T(8,128)(2,1)S(1)}, bf16[2,2,64,2560]{3,2,1,0:T(8,128)(2,1)}, u32[]{:S(2)}) copy-start(bf16[2,2,64,2560]{3,2,1,0:T(8,128)(2,1)} %param.6) | copy-start | bytes 3932164
  2.2 17.3 %collective-permute-start.2 = (bf16[4,24,1024]{2,1,0:T(8,128)(2,1)S(1)}, bf16[4,24,1024]{2,1,0:T(8,128)(2,1)S(1)}, u32[]{:S(2)}, u32[]{:S(2)}) collective-permute-start(bf16[4,24,1024]{2,1,0:T(8,128)(2,1)S(1)} %pad_maximum_fusion), channel_id=1, source_target_pairs={{0,16},{2,18},{4,20},{6,22},{8,24},{10,26},{12,28},{14,30},{16,0},... | collective-permute-start | bytes 589832 | tf_op jit(solution)/shard_map/ppermute | solution.py:33
  7.8 4.3 %copy-start.10 = (f32[64,256]{1,0:T(8,128)}, f32[64,256]{1,0:T(8,128)S(1)}, u32[]{:S(2)}) copy-start(f32[64,256]{1,0:T(8,128)S(1)} %convolution_bitcast_fusion.own_ref) | copy-start | bytes 196612
  7.8 4.3 %collective-permute-start = (f32[64,256]{1,0:T(8,128)S(1)}, f32[64,256]{1,0:T(8,128)S(1)}, u32[]{:S(2)}, u32[]{:S(2)}) collective-permute-start(f32[64,256]{1,0:T(8,128)S(1)} %convolution_bitcast_fusion.own_ref), channel_id=1, source_target_pairs={{0,1},{1,0},{2,3},{3,2},{4,5},{5,4},{6,7},{7,6},{8,9},{9,8},{10,11... | collective-permute-start | bytes 196616 | tf_op jit(solution)/shard_map/ppermute | solution.py:33
  14.4 5.1 %copy-start.26 = (bf16[16,1024]{1,0:T(8,128)(2,1)S(1)}, bf16[16,1024]{1,0:T(8,128)(2,1)}, u32[]{:S(2)}) copy-start(bf16[16,1024]{1,0:T(8,128)(2,1)} %unpatchify.1) | copy-start | bytes 98308
  14.4 14.5 %copy-start.28 = (f32[384]{0:T(512)S(1)}, f32[384]{0:T(512)}, u32[]{:S(2)}) copy-start(f32[384]{0:T(512)} %param.8) | copy-start | bytes 4612
  14.4 5.0 %collective-permute-start.1 = (bf16[16,1024]{1,0:T(8,128)(2,1)}, bf16[16,1024]{1,0:T(8,128)(2,1)S(1)}, u32[]{:S(2)}, u32[]{:S(2)}) collective-permute-start(bf16[16,1024]{1,0:T(8,128)(2,1)} %unpatchify.1), channel_id=1, source_target_pairs={{0,16},{2,18},{4,20},{6,22},{8,24},{10,26},{12,28},{14,30},{16,0},... | collective-permute-start | bytes 98312 | tf_op jit(solution)/shard_map/ppermute | solution.py:33
  19.5 10.5 %copy-start.1 = (bf16[2,40,1024]{2,1,0:T(8,128)(2,1)}, bf16[2,40,1024]{2,1,0:T(8,128)(2,1)S(1)}, u32[]{:S(2)}) copy-start(bf16[2,40,1024]{2,1,0:T(8,128)(2,1)S(1)} %get-tuple-element.30.refs_3_.refs_0_) | copy-start | bytes 491524
  19.6 7.2 %collective-permute-start.5 = (bf16[2,40,1024]{2,1,0:T(8,128)(2,1)S(1)}, bf16[2,40,1024]{2,1,0:T(8,128)(2,1)S(1)}, u32[]{:S(2)}, u32[]{:S(2)}) collective-permute-start(bf16[2,40,1024]{2,1,0:T(8,128)(2,1)S(1)} %get-tuple-element.62), channel_id=1, source_target_pairs={{0,12},{2,14},{4,8},{6,10},{8,4},{10,6},{12,0},{14,2},{16,28},{18,... | collective-permute-start | bytes 491528 | tf_op jit(solution)/shard_map/ppermute | solution.py:33
  22.2 6.2 %collective-permute-start.3 = (bf16[2,40,1024]{2,1,0:T(8,128)(2,1)S(1)}, bf16[2,40,1024]{2,1,0:T(8,128)(2,1)S(1)}, u32[]{:S(2)}, u32[]{:S(2)}) collective-permute-start(bf16[2,40,1024]{2,1,0:T(8,128)(2,1)S(1)} %get-tuple-element.63), channel_id=1, source_target_pairs={{0,4},{2,6},{4,0},{6,2},{8,12},{10,14},{12,8},{14,10},{16,20},{18,... | collective-permute-start | bytes 491528 | tf_op jit(solution)/shard_map/ppermute | solution.py:33
  22.7 5.8 %collective-permute-start.4 = (bf16[2,40,1024]{2,1,0:T(8,128)(2,1)S(1)}, bf16[2,40,1024]{2,1,0:T(8,128)(2,1)S(1)}, u32[]{:S(2)}, u32[]{:S(2)}) collective-permute-start(bf16[2,40,1024]{2,1,0:T(8,128)(2,1)S(1)} %get-tuple-element.64), channel_id=1, source_target_pairs={{0,8},{2,10},{4,12},{6,14},{8,0},{10,2},{12,4},{14,6},{16,24},{18,... | collective-permute-start | bytes 491528 | tf_op jit(solution)/shard_map/ppermute | solution.py:33
  23.1 6.4 %collective-permute-start.6 = (bf16[2,40,1024]{2,1,0:T(8,128)(2,1)S(1)}, bf16[2,40,1024]{2,1,0:T(8,128)(2,1)S(1)}, u32[]{:S(2)}, u32[]{:S(2)}) collective-permute-start(bf16[2,40,1024]{2,1,0:T(8,128)(2,1)S(1)} %get-tuple-element.30.refs_3_.refs_0_), channel_id=1, source_target_pairs={{0,2},{2,0},{4,6},{6,4},{8,10},{10,8},{12,14},{14,12},{16,18},{18,... | collective-permute-start | bytes 491528 | tf_op jit(solution)/shard_map/ppermute | solution.py:33
  26.8 3.3 %copy-start.3 = (bf16[2,40,1024]{2,1,0:T(8,128)(2,1)}, bf16[2,40,1024]{2,1,0:T(8,128)(2,1)S(1)}, u32[]{:S(2)}) copy-start(bf16[2,40,1024]{2,1,0:T(8,128)(2,1)S(1)} %collective-permute-done.5.refs_6_.refs_3_) | copy-start | bytes 491524
  26.8 2.7 %collective-permute-start.9 = (bf16[2,40,1024]{2,1,0:T(8,128)(2,1)S(1)}, bf16[2,40,1024]{2,1,0:T(8,128)(2,1)S(1)}, u32[]{:S(2)}, u32[]{:S(2)}) collective-permute-start(bf16[2,40,1024]{2,1,0:T(8,128)(2,1)S(1)} %collective-permute-done.5.refs_6_.refs_3_), channel_id=1, source_target_pairs={{0,2},{2,0},{4,6},{6,4},{8,10},{10,8},{12,14},{14,12},{16,18},{18,... | collective-permute-start | bytes 491528 | tf_op jit(solution)/shard_map/ppermute | solution.py:33
  28.4 1.6 %copy-start.4 = (bf16[2,40,1024]{2,1,0:T(8,128)(2,1)}, bf16[2,40,1024]{2,1,0:T(8,128)(2,1)S(1)}, u32[]{:S(2)}) copy-start(bf16[2,40,1024]{2,1,0:T(8,128)(2,1)S(1)} %collective-permute-done.3.refs_4_.refs_1_) | copy-start | bytes 491524
  28.4 1.4 %collective-permute-start.7 = (bf16[2,40,1024]{2,1,0:T(8,128)(2,1)S(1)}, bf16[2,40,1024]{2,1,0:T(8,128)(2,1)S(1)}, u32[]{:S(2)}, u32[]{:S(2)}) collective-permute-start(bf16[2,40,1024]{2,1,0:T(8,128)(2,1)S(1)} %collective-permute-done.3.refs_4_.refs_1_), channel_id=1, source_target_pairs={{0,2},{2,0},{4,6},{6,4},{8,10},{10,8},{12,14},{14,12},{16,18},{18,... | collective-permute-start | bytes 491528 | tf_op jit(solution)/shard_map/ppermute | solution.py:33
  28.4 1.6 %copy-start.5 = (bf16[2,40,1024]{2,1,0:T(8,128)(2,1)}, bf16[2,40,1024]{2,1,0:T(8,128)(2,1)S(1)}, u32[]{:S(2)}) copy-start(bf16[2,40,1024]{2,1,0:T(8,128)(2,1)S(1)} %collective-permute-done.4.refs_5_.refs_2_) | copy-start | bytes 491524
  28.4 1.6 %collective-permute-start.8 = (bf16[2,40,1024]{2,1,0:T(8,128)(2,1)S(1)}, bf16[2,40,1024]{2,1,0:T(8,128)(2,1)S(1)}, u32[]{:S(2)}, u32[]{:S(2)}) collective-permute-start(bf16[2,40,1024]{2,1,0:T(8,128)(2,1)S(1)} %collective-permute-done.4.refs_5_.refs_2_), channel_id=1, source_target_pairs={{0,2},{2,0},{4,6},{6,4},{8,10},{10,8},{12,14},{14,12},{16,18},{18,... | collective-permute-start | bytes 491528 | tf_op jit(solution)/shard_map/ppermute | solution.py:33
  29.5 0.7 copy-start.7
  42.7 1.7 %collective-permute-start.10 = (bf16[216,384]{1,0:T(8,128)(2,1)}, bf16[216,384]{1,0:T(8,128)(2,1)S(1)}, u32[]{:S(2)}, u32[]{:S(2)}) collective-permute-start(bf16[216,384]{1,0:T(8,128)(2,1)} %get-tuple-element.29), channel_id=1, source_target_pairs={{0,2},{2,0},{4,6},{6,4},{8,10},{10,8},{12,14},{14,12},{16,18},{18,... | collective-permute-start | bytes 497672 | tf_op jit(solution)/shard_map/ppermute | solution.py:33
  45.4 22.0 %copy-start.2 = (bf16[216,384]{1,0:T(8,128)(2,1)}, bf16[216,384]{1,0:T(8,128)(2,1)S(1)}, u32[]{:S(2)}) copy-start(bf16[216,384]{1,0:T(8,128)(2,1)S(1)} %add_convert_fusion) | copy-start | bytes 497668
  45.4 7.0 %collective-permute-start.11 = (bf16[216,384]{1,0:T(8,128)(2,1)S(1)}, bf16[216,384]{1,0:T(8,128)(2,1)S(1)}, u32[]{:S(2)}, u32[]{:S(2)}) collective-permute-start(bf16[216,384]{1,0:T(8,128)(2,1)S(1)} %add_convert_fusion), channel_id=1, source_target_pairs={{0,8},{2,10},{4,12},{6,14},{8,0},{10,2},{12,4},{14,6},{16,24},{18,... | collective-permute-start | bytes 497672 | tf_op jit(solution)/shard_map/ppermute | solution.py:33
  46.4 15.6 %collective-permute-start.15 = (bf16[216,384]{1,0:T(8,128)(2,1)S(1)}, bf16[216,384]{1,0:T(8,128)(2,1)S(1)}, u32[]{:S(2)}, u32[]{:S(2)}) collective-permute-start(bf16[216,384]{1,0:T(8,128)(2,1)S(1)} %add_convert_fusion), channel_id=1, source_target_pairs={{0,24},{2,26},{4,28},{6,30},{8,16},{10,18},{12,20},{14,22},{16,8},... | collective-permute-start | bytes 497672 | tf_op jit(solution)/shard_map/ppermute | solution.py:33
  47.6 16.1 %collective-permute-start.14 = (bf16[216,384]{1,0:T(8,128)(2,1)S(1)}, bf16[216,384]{1,0:T(8,128)(2,1)S(1)}, u32[]{:S(2)}, u32[]{:S(2)}) collective-permute-start(bf16[216,384]{1,0:T(8,128)(2,1)S(1)} %add_convert_fusion), channel_id=1, source_target_pairs={{0,16},{2,18},{4,20},{6,22},{8,24},{10,26},{12,28},{14,30},{16,0},... | collective-permute-start | bytes 497672 | tf_op jit(solution)/shard_map/ppermute | solution.py:33
  49.0 14.8 %collective-permute-start.12 = (bf16[216,384]{1,0:T(8,128)(2,1)S(1)}, bf16[216,384]{1,0:T(8,128)(2,1)S(1)}, u32[]{:S(2)}, u32[]{:S(2)}) collective-permute-start(bf16[216,384]{1,0:T(8,128)(2,1)S(1)} %add_convert_fusion), channel_id=1, source_target_pairs={{0,4},{2,6},{4,0},{6,2},{8,12},{10,14},{12,8},{14,10},{16,20},{18,... | collective-permute-start | bytes 497672 | tf_op jit(solution)/shard_map/ppermute | solution.py:33
  52.5 15.0 %copy-start.13 = (bf16[216,384]{1,0:T(8,128)(2,1)}, bf16[216,384]{1,0:T(8,128)(2,1)S(1)}, u32[]{:S(2)}) copy-start(bf16[216,384]{1,0:T(8,128)(2,1)S(1)} %collective-permute-done.11) | copy-start | bytes 497668
  52.5 11.3 %collective-permute-start.13 = (bf16[216,384]{1,0:T(8,128)(2,1)S(1)}, bf16[216,384]{1,0:T(8,128)(2,1)S(1)}, u32[]{:S(2)}, u32[]{:S(2)}) collective-permute-start(bf16[216,384]{1,0:T(8,128)(2,1)S(1)} %collective-permute-done.11), channel_id=1, source_target_pairs={{0,4},{2,6},{4,0},{6,2},{8,12},{10,14},{12,8},{14,10},{16,20},{18,... | collective-permute-start | bytes 497672 | tf_op jit(solution)/shard_map/ppermute | solution.py:33
  62.0 8.7 %copy-start.11 = (bf16[216,384]{1,0:T(8,128)(2,1)}, bf16[216,384]{1,0:T(8,128)(2,1)S(1)}, u32[]{:S(2)}) copy-start(bf16[216,384]{1,0:T(8,128)(2,1)S(1)} %collective-permute-done.15) | copy-start | bytes 497668
  63.8 6.9 %copy-start.12 = (bf16[216,384]{1,0:T(8,128)(2,1)}, bf16[216,384]{1,0:T(8,128)(2,1)S(1)}, u32[]{:S(2)}) copy-start(bf16[216,384]{1,0:T(8,128)(2,1)S(1)} %collective-permute-done.14) | copy-start | bytes 497668
  63.8 3.7 %copy-start.14 = (bf16[216,384]{1,0:T(8,128)(2,1)}, bf16[216,384]{1,0:T(8,128)(2,1)S(1)}, u32[]{:S(2)}) copy-start(bf16[216,384]{1,0:T(8,128)(2,1)S(1)} %collective-permute-done.12) | copy-start | bytes 497668
  63.8 3.7 %copy-start.15 = (bf16[216,384]{1,0:T(8,128)(2,1)}, bf16[216,384]{1,0:T(8,128)(2,1)S(1)}, u32[]{:S(2)}) copy-start(bf16[216,384]{1,0:T(8,128)(2,1)S(1)} %collective-permute-done.13) | copy-start | bytes 497668
  63.8 1.8 %collective-permute-start.16 = (bf16[216,384]{1,0:T(8,128)(2,1)S(1)}, bf16[216,384]{1,0:T(8,128)(2,1)S(1)}, u32[]{:S(2)}, u32[]{:S(2)}) collective-permute-start(bf16[216,384]{1,0:T(8,128)(2,1)S(1)} %add_convert_fusion), channel_id=1, source_target_pairs={{0,2},{2,0},{4,6},{6,4},{8,10},{10,8},{12,14},{14,12},{16,18},{18,... | collective-permute-start | bytes 497672 | tf_op jit(solution)/shard_map/ppermute | solution.py:33
  63.9 3.0 %collective-permute-start.17 = (bf16[216,384]{1,0:T(8,128)(2,1)S(1)}, bf16[216,384]{1,0:T(8,128)(2,1)S(1)}, u32[]{:S(2)}, u32[]{:S(2)}) collective-permute-start(bf16[216,384]{1,0:T(8,128)(2,1)S(1)} %collective-permute-done.12), channel_id=1, source_target_pairs={{0,2},{2,0},{4,6},{6,4},{8,10},{10,8},{12,14},{14,12},{16,18},{18,... | collective-permute-start | bytes 497672 | tf_op jit(solution)/shard_map/ppermute | solution.py:33
  64.4 2.6 %collective-permute-start.18 = (bf16[216,384]{1,0:T(8,128)(2,1)S(1)}, bf16[216,384]{1,0:T(8,128)(2,1)S(1)}, u32[]{:S(2)}, u32[]{:S(2)}) collective-permute-start(bf16[216,384]{1,0:T(8,128)(2,1)S(1)} %collective-permute-done.11), channel_id=1, source_target_pairs={{0,2},{2,0},{4,6},{6,4},{8,10},{10,8},{12,14},{14,12},{16,18},{18,... | collective-permute-start | bytes 497672 | tf_op jit(solution)/shard_map/ppermute | solution.py:33
  64.5 3.0 %collective-permute-start.19 = (bf16[216,384]{1,0:T(8,128)(2,1)S(1)}, bf16[216,384]{1,0:T(8,128)(2,1)S(1)}, u32[]{:S(2)}, u32[]{:S(2)}) collective-permute-start(bf16[216,384]{1,0:T(8,128)(2,1)S(1)} %collective-permute-done.13), channel_id=1, source_target_pairs={{0,2},{2,0},{4,6},{6,4},{8,10},{10,8},{12,14},{14,12},{16,18},{18,... | collective-permute-start | bytes 497672 | tf_op jit(solution)/shard_map/ppermute | solution.py:33
  64.9 7.1 %collective-permute-start.20 = (bf16[216,384]{1,0:T(8,128)(2,1)S(1)}, bf16[216,384]{1,0:T(8,128)(2,1)S(1)}, u32[]{:S(2)}, u32[]{:S(2)}) collective-permute-start(bf16[216,384]{1,0:T(8,128)(2,1)S(1)} %collective-permute-done.14), channel_id=1, source_target_pairs={{0,4},{2,6},{4,0},{6,2},{8,12},{10,14},{12,8},{14,10},{16,20},{18,... | collective-permute-start | bytes 497672 | tf_op jit(solution)/shard_map/ppermute | solution.py:33
  65.6 1.9 %copy-start.19 = (bf16[216,384]{1,0:T(8,128)(2,1)}, bf16[216,384]{1,0:T(8,128)(2,1)S(1)}, u32[]{:S(2)}) copy-start(bf16[216,384]{1,0:T(8,128)(2,1)S(1)} %collective-permute-done.16) | copy-start | bytes 497668
  65.6 9.0 %collective-permute-start.21 = (bf16[216,384]{1,0:T(8,128)(2,1)S(1)}, bf16[216,384]{1,0:T(8,128)(2,1)S(1)}, u32[]{:S(2)}, u32[]{:S(2)}) collective-permute-start(bf16[216,384]{1,0:T(8,128)(2,1)S(1)} %collective-permute-done.15), channel_id=1, source_target_pairs={{0,4},{2,6},{4,0},{6,2},{8,12},{10,14},{12,8},{14,10},{16,20},{18,... | collective-permute-start | bytes 497672 | tf_op jit(solution)/shard_map/ppermute | solution.py:33
  66.9 8.3 %collective-permute-start.22 = (bf16[216,384]{1,0:T(8,128)(2,1)S(1)}, bf16[216,384]{1,0:T(8,128)(2,1)S(1)}, u32[]{:S(2)}, u32[]{:S(2)}) collective-permute-start(bf16[216,384]{1,0:T(8,128)(2,1)S(1)} %collective-permute-done.14), channel_id=1, source_target_pairs={{0,2},{2,0},{4,6},{6,4},{8,10},{10,8},{12,14},{14,12},{16,18},{18,... | collective-permute-start | bytes 497672 | tf_op jit(solution)/shard_map/ppermute | solution.py:33
  66.9 0.7 copy-start.22
  66.9 8.2 %collective-permute-start.24 = (bf16[216,384]{1,0:T(8,128)(2,1)S(1)}, bf16[216,384]{1,0:T(8,128)(2,1)S(1)}, u32[]{:S(2)}, u32[]{:S(2)}) collective-permute-start(bf16[216,384]{1,0:T(8,128)(2,1)S(1)} %collective-permute-done.15), channel_id=1, source_target_pairs={{0,2},{2,0},{4,6},{6,4},{8,10},{10,8},{12,14},{14,12},{16,18},{18,... | collective-permute-start | bytes 497672 | tf_op jit(solution)/shard_map/ppermute | solution.py:33
  72.0 4.3 %copy-start.16 = (bf16[216,384]{1,0:T(8,128)(2,1)}, bf16[216,384]{1,0:T(8,128)(2,1)S(1)}, u32[]{:S(2)}) copy-start(bf16[216,384]{1,0:T(8,128)(2,1)S(1)} %collective-permute-done.20) | copy-start | bytes 497668
  74.7 1.6 %copy-start.17 = (bf16[216,384]{1,0:T(8,128)(2,1)}, bf16[216,384]{1,0:T(8,128)(2,1)S(1)}, u32[]{:S(2)}) copy-start(bf16[216,384]{1,0:T(8,128)(2,1)S(1)} %collective-permute-done.21) | copy-start | bytes 497668
  74.7 1.4 %collective-permute-start.23 = (bf16[216,384]{1,0:T(8,128)(2,1)S(1)}, bf16[216,384]{1,0:T(8,128)(2,1)S(1)}, u32[]{:S(2)}, u32[]{:S(2)}) collective-permute-start(bf16[216,384]{1,0:T(8,128)(2,1)S(1)} %collective-permute-done.20), channel_id=1, source_target_pairs={{0,2},{2,0},{4,6},{6,4},{8,10},{10,8},{12,14},{14,12},{16,18},{18,... | collective-permute-start | bytes 497672 | tf_op jit(solution)/shard_map/ppermute | solution.py:33
  74.7 1.6 %collective-permute-start.25 = (bf16[216,384]{1,0:T(8,128)(2,1)S(1)}, bf16[216,384]{1,0:T(8,128)(2,1)S(1)}, u32[]{:S(2)}, u32[]{:S(2)}) collective-permute-start(bf16[216,384]{1,0:T(8,128)(2,1)S(1)} %collective-permute-done.21), channel_id=1, source_target_pairs={{0,2},{2,0},{4,6},{6,4},{8,10},{10,8},{12,14},{14,12},{16,18},{18,... | collective-permute-start | bytes 497672 | tf_op jit(solution)/shard_map/ppermute | solution.py:33
  75.2 1.1 %copy-start.18 = (bf16[216,384]{1,0:T(8,128)(2,1)}, bf16[216,384]{1,0:T(8,128)(2,1)S(1)}, u32[]{:S(2)}) copy-start(bf16[216,384]{1,0:T(8,128)(2,1)S(1)} %collective-permute-done.22) | copy-start | bytes 497668
  75.2 1.1 %copy-start.20 = (bf16[216,384]{1,0:T(8,128)(2,1)}, bf16[216,384]{1,0:T(8,128)(2,1)S(1)}, u32[]{:S(2)}) copy-start(bf16[216,384]{1,0:T(8,128)(2,1)S(1)} %collective-permute-done.24) | copy-start | bytes 497668
  76.1 0.7 copy-start.24
  (7 other events, 4.6 us)

commit v11 on v10

--- a/solution.py
+++ b/solution.py
@@ -41,9 +41,9 @@
     return lax.dot_general(a, b, (((1,), (1,)), ((), ())), preferred_element_type=F32)
 
 
-def unpatchify_kernel(frames, tok_rows, tok_cols, own_ref, other_ref, out_ref):
+def unpatchify_kernel(frames, tok_rows, tok_cols, sum_ref, out_ref):
     latent_width = out_ref.shape[0]
-    features = (own_ref[...] + other_ref[...]).astype(BF16)
+    features = sum_ref[...]
     width = 2 * tok_cols
     span = tok_rows * tok_cols
     source = lax.broadcasted_iota(jnp.int32, (span, tok_rows * width), 0)
@@ -379,11 +379,11 @@
     latent = pl.pallas_call(
         functools.partial(unpatchify_kernel, frames, tok_rows, tok_cols),
         out_shape=jax.ShapeDtypeStruct((latent_width, frames * rows * width), BF16),
-        in_specs=[vmem(), vmem()],
+        in_specs=[vmem()],
         out_specs=vmem(),
         compiler_params=params(),
         name="unpatchify",
-    )(partial_sum, other)
+    )((partial_sum + other).astype(BF16))
 
     blank = 3 - live
     hbm = pl.BlockSpec(memory_space=pl.ANY)

time: 80.1 us -> 82.6 us (1.031)
  starting transfers between devices: 19.5 us -> 24 us
  waiting for transfers between devices: 22.8 us -> 20.9 us
    ppermute x26, starting transfers between devices: 19.5 us -> 24 us  [xor_permute(): lax.ppermute(x, axis, [(i, i ^ mask) for i in range(lax.axis_size(axis))])]
    ppermute x26, waiting for transfers between devices: 22.8 us -> 20.9 us  [xor_permute(): lax.ppermute(x, axis, [(i, i ^ mask) for i in range(lax.axis_size(axis))])]
    unnamed x58 -> x54, local copies, waits for them, and re-layouts: 2.62 us -> 1.97 us
  transfers between devices with their start and end apart: 26 -> 26, of which waited for: 13 -> 12; matrix products, arithmetic and copies ran while one was open for 3% -> 1% of each run, Pallas kernels for 18% -> 17%
where the time goes in v11:
time: 82.6 us; the launch traced here: 82.1 us
  Pallas kernels  28.9 us (35%)
  starting transfers between devices  24 us (29%)
  waiting for transfers between devices  20.9 us (25%)
  local copies, waits for them, and re-layouts  3.98 us (5%)
  other arithmetic  1.73 us (2%)
  matrix products  1.48 us (2%)
  between operations  1.19 us (1%)
    ppermute x26, starting transfers between devices, xor_permute(): lax.ppermute(x, axis, [(i, i ^ mask) for i in range(lax.axis_size(axis))])  24 us
    ppermute x26, waiting for transfers between devices, xor_permute(): lax.ppermute(x, axis, [(i, i ^ mask) for i in range(lax.axis_size(axis))])  20.9 us
    pallas_call x1, Pallas kernels, per_device(): pl.pallas_call(functools.partial(gradient_kernel, frames, rows, slabs, ma...  12 us
    pallas_call x1, Pallas kernels, per_device(): pl.pallas_call(functools.partial(decode_kernel, frames, rows, slabs, mask...  8.61 us
    pallas_call x2, Pallas kernels, finish(): pl.pallas_call(functools.partial(finish_kernel, sources), out_shape=jax.S...  5.13 us
    unnamed x54, local copies, waits for them, and re-layouts  1.97 us
  transfers between devices with their start and end apart: 26, of which 12 were waited for; matrix products, arithmetic and copies ran while one was open for 1% of the time, Pallas kernels for 17%

profile of v11, /device:TPU:0, one launch (start us, length us, event | category | flops | bytes accessed | tf_op | source)
XLA Modules:
  0.0 82.1 jit_solution(16688042878585223228)
XLA Ops:
  0.7 1.4 %reshape.77 = bf16[8,24,1024]{2,1,0:T(8,128)(2,1)S(1)} reshape(bf16[192,2,4,128]{3,2,1,0:T(4,128)(2,1)} %param.11) | data formatting | bytes 786432 | tf_op jit(solution)/shard_map/reshape | solution.py:348
  2.2 1.5 %convolution_bitcast_fusion = f32[64,256]{1,0:T(8,128)S(1)} fusion(bf16[256,2560]{1,0:T(8,128)(2,1)S(1)} %bitcast.33, bf16[2560,64]{0,1:T(8,128)(2,1)} %param.7), kind=kOutput, calls=%fused_computation | convolution fusion | flops 83886080 | bytes 1703936 | tf_op jit(solution)/shard_map/dot_general | solution.py:364
  3.7 3.0 %collective-permute-start = (f32[64,256]{1,0:T(8,128)S(1)}, f32[64,256]{1,0:T(8,128)S(1)}, u32[]{:S(2)}, u32[]{:S(2)}) collective-permute-start(f32[64,256]{1,0:T(8,128)S(1)} %convolution_bitcast_fusion), channel_id=1, source_target_pairs={{0,1},{1,0},{2,3},{3,2},{4,5},{5,4},{6,7},{7,6},{8,9},{9,8},{10,11... | collective-permute-start | bytes 196616 | tf_op jit(solution)/shard_map/ppermute | solution.py:33
  6.7 2.6 %collective-permute-start.2 = (bf16[4,24,1024]{2,1,0:T(8,128)(2,1)S(1)}, bf16[4,24,1024]{2,1,0:T(8,128)(2,1)S(1)}, u32[]{:S(2)}, u32[]{:S(2)}) collective-permute-start(bf16[4,24,1024]{2,1,0:T(8,128)(2,1)S(1)} %pad_maximum_fusion), channel_id=1, source_target_pairs={{0,16},{2,18},{4,20},{6,22},{8,24},{10,26},{12,28},{14,30},{16,0},... | collective-permute-start | bytes 589832 | tf_op jit(solution)/shard_map/ppermute | solution.py:33
  9.3 0.6 add_convert_fusion.1.sum_ref
  9.9 1.5 %unpatchify.1 = bf16[16,1024]{1,0:T(8,128)(2,1)} custom-call(bf16[64,256]{1,0:T(8,128)(2,1)} %add_convert_fusion.1.sum_ref), custom_call_target="tpu_custom_call" | custom-call | tf_op jit(solution)/shard_map/unpatchify/pallas_call | solution.py:379
  11.4 2.8 %collective-permute-start.1 = (bf16[16,1024]{1,0:T(8,128)(2,1)}, bf16[16,1024]{1,0:T(8,128)(2,1)S(1)}, u32[]{:S(2)}, u32[]{:S(2)}) collective-permute-start(bf16[16,1024]{1,0:T(8,128)(2,1)} %unpatchify.1), channel_id=1, source_target_pairs={{0,16},{2,18},{4,20},{6,22},{8,24},{10,26},{12,28},{14,30},{16,0},... | collective-permute-start | bytes 98312 | tf_op jit(solution)/shard_map/ppermute | solution.py:33
  14.2 1.6 %blank.1.refs_8_ = f32[3,9,192,384]{3,2,1,0:T(8,128)} custom-call(), custom_call_target="tpu_custom_call" | custom-call | bytes 2654208 | tf_op jit(solution)/shard_map/blank/pallas_call | solution.py:391
  15.8 3.8 %collective-permute-done.1 = bf16[16,1024]{1,0:T(8,128)(2,1)S(1)} collective-permute-done((bf16[16,1024]{1,0:T(8,128)(2,1)}, bf16[16,1024]{1,0:T(8,128)(2,1)S(1)}, u32[]{:S(2)}, u32[]{:S(2)}) %collective-permute-start.1) | collective-permute-done | bytes 32800 | tf_op jit(solution)/shard_map/ppermute | solution.py:33
  19.7 1.8 %collective-permute-start.5 = (bf16[2,40,1024]{2,1,0:T(8,128)(2,1)S(1)}, bf16[2,40,1024]{2,1,0:T(8,128)(2,1)S(1)}, u32[]{:S(2)}, u32[]{:S(2)}) collective-permute-start(bf16[2,40,1024]{2,1,0:T(8,128)(2,1)S(1)} %get-tuple-element.62), channel_id=1, source_target_pairs={{0,12},{2,14},{4,8},{6,10},{8,4},{10,6},{12,0},{14,2},{16,28},{18,... | collective-permute-start | bytes 491528 | tf_op jit(solution)/shard_map/ppermute | solution.py:33
  21.5 0.5 collective-permute-start.3
  22.0 1.2 %collective-permute-start.4 = (bf16[2,40,1024]{2,1,0:T(8,128)(2,1)S(1)}, bf16[2,40,1024]{2,1,0:T(8,128)(2,1)S(1)}, u32[]{:S(2)}, u32[]{:S(2)}) collective-permute-start(bf16[2,40,1024]{2,1,0:T(8,128)(2,1)S(1)} %get-tuple-element.64), channel_id=1, source_target_pairs={{0,8},{2,10},{4,12},{6,14},{8,0},{10,2},{12,4},{14,6},{16,24},{18,... | collective-permute-start | bytes 491528 | tf_op jit(solution)/shard_map/ppermute | solution.py:33
  23.2 3.7 %collective-permute-done.5.refs_6_.refs_3_ = bf16[2,40,1024]{2,1,0:T(8,128)(2,1)S(1)} collective-permute-done((bf16[2,40,1024]{2,1,0:T(8,128)(2,1)S(1)}, bf16[2,40,1024]{2,1,0:T(8,128)(2,1)S(1)}, u32[]{:S(2)}, u32[]{:S(2)}) %collective-permute-start.5) | collective-permute-done | bytes 163872 | tf_op jit(solution)/shard_map/ppermute | solution.py:33
  27.0 2.4 %collective-permute-done.3.refs_4_.refs_1_ = bf16[2,40,1024]{2,1,0:T(8,128)(2,1)S(1)} collective-permute-done((bf16[2,40,1024]{2,1,0:T(8,128)(2,1)S(1)}, bf16[2,40,1024]{2,1,0:T(8,128)(2,1)S(1)}, u32[]{:S(2)}, u32[]{:S(2)}) %collective-permute-start.3) | collective-permute-done | bytes 163872 | tf_op jit(solution)/shard_map/ppermute | solution.py:33
  29.4 0.5 collective-permute-start.8
  29.9 0.6 reshape.74.refs_1_.gain_ref
  30.5 0.3 collective-permute-done.7.refs_8_.refs_5_
  30.8 0.2 collective-permute-done.8.refs_9_.refs_6_
  31.0 0.1 copy-done.6
  31.2 0.2 copy-done.8
  31.4 0.2 copy-done.9
  31.6 12.0 %gradient.1 = (f32[216,384]{1,0:T(8,128)}, bf16[216,384]{1,0:T(8,128)(2,1)}) custom-call(s32[1]{0:T(128)} %bitcast.refs_0_.me_ref, f32[1,384]{1,0:T(1,128)} %reshape.74.refs_1_.gain_ref, bf16[432,384]{1,0:T(8,128)(2,1)} %bitcast.36, bf16[2,40,1024]{2,1,0:T(8,128)(2,1)} %copy-done.1, bf16[2,40,1024]{2,1,0:T(8,128)(2,1)} %copy-done.4, ...), custom_call_target="tpu_custom_call" | custom-call | tf_op jit(solution)/shard_map/gradient/pallas_call | solution.py:417
  43.7 0.3 collective-permute-start.10
  44.0 1.3 %collective-permute-done.10 = bf16[216,384]{1,0:T(8,128)(2,1)S(1)} collective-permute-done((bf16[216,384]{1,0:T(8,128)(2,1)}, bf16[216,384]{1,0:T(8,128)(2,1)S(1)}, u32[]{:S(2)}, u32[]{:S(2)}) %collective-permute-start.10) | collective-permute-done | bytes 165920 | tf_op jit(solution)/shard_map/ppermute | solution.py:33
  45.3 1.0 %add_convert_fusion = bf16[216,384]{1,0:T(8,128)(2,1)S(1)} fusion(f32[216,384]{1,0:T(8,128)} %get-tuple-element.28, bf16[216,384]{1,0:T(8,128)(2,1)S(1)} %collective-permute-done.10), kind=kLoop, calls=%fused_computation.1 | loop fusion | flops 248832 | bytes 663552 | tf_op jit(solution)/shard_map/convert_element_type | solution.py:442
  46.4 1.7 %collective-permute-start.11 = (bf16[216,384]{1,0:T(8,128)(2,1)S(1)}, bf16[216,384]{1,0:T(8,128)(2,1)S(1)}, u32[]{:S(2)}, u32[]{:S(2)}) collective-permute-start(bf16[216,384]{1,0:T(8,128)(2,1)S(1)} %add_convert_fusion), channel_id=1, source_target_pairs={{0,8},{2,10},{4,12},{6,14},{8,0},{10,2},{12,4},{14,6},{16,24},{18,... | collective-permute-start | bytes 497672 | tf_op jit(solution)/shard_map/ppermute | solution.py:33
  48.1 3.1 %collective-permute-start.15 = (bf16[216,384]{1,0:T(8,128)(2,1)S(1)}, bf16[216,384]{1,0:T(8,128)(2,1)S(1)}, u32[]{:S(2)}, u32[]{:S(2)}) collective-permute-start(bf16[216,384]{1,0:T(8,128)(2,1)S(1)} %add_convert_fusion), channel_id=1, source_target_pairs={{0,24},{2,26},{4,28},{6,30},{8,16},{10,18},{12,20},{14,22},{16,8},... | collective-permute-start | bytes 497672 | tf_op jit(solution)/shard_map/ppermute | solution.py:33
  51.3 0.8 %collective-permute-start.12 = (bf16[216,384]{1,0:T(8,128)(2,1)S(1)}, bf16[216,384]{1,0:T(8,128)(2,1)S(1)}, u32[]{:S(2)}, u32[]{:S(2)}) collective-permute-start(bf16[216,384]{1,0:T(8,128)(2,1)S(1)} %add_convert_fusion), channel_id=1, source_target_pairs={{0,4},{2,6},{4,0},{6,2},{8,12},{10,14},{12,8},{14,10},{16,20},{18,... | collective-permute-start | bytes 497672 | tf_op jit(solution)/shard_map/ppermute | solution.py:33
  52.1 0.8 collective-permute-done.11
  52.9 1.4 %collective-permute-start.13 = (bf16[216,384]{1,0:T(8,128)(2,1)S(1)}, bf16[216,384]{1,0:T(8,128)(2,1)S(1)}, u32[]{:S(2)}, u32[]{:S(2)}) collective-permute-start(bf16[216,384]{1,0:T(8,128)(2,1)S(1)} %collective-permute-done.11), channel_id=1, source_target_pairs={{0,4},{2,6},{4,0},{6,2},{8,12},{10,14},{12,8},{14,10},{16,20},{18,... | collective-permute-start | bytes 497672 | tf_op jit(solution)/shard_map/ppermute | solution.py:33
  54.2 8.6 %decode.1 = bf16[192,2,4,128]{3,2,1,0:T(4,128)(2,1)} custom-call(s32[1]{0:T(128)} %bitcast.refs_0_.me_ref, f32[1,384]{1,0:T(1,128)} %reshape.74.refs_1_.gain_ref, bf16[432,384]{1,0:T(8,128)(2,1)} %bitcast.37, bf16[27,192,384]{2,1,0:T(8,128)(2,1)} %bitcast.35, bf16[2,40,1024]{2,1,0:T(8,128)(2,1)} %copy-done.1, bf16[2,40,1024]{2,1,0:T(8,128)(2,1)} %copy-done.4, ...), custom_call_target="tpu_custom_call" | custom-call | tf_op jit(solution)/shard_map/decode/pallas_call | solution.py:450
  62.9 3.3 %collective-permute-done.14 = bf16[216,384]{1,0:T(8,128)(2,1)S(1)} collective-permute-done((bf16[216,384]{1,0:T(8,128)(2,1)S(1)}, bf16[216,384]{1,0:T(8,128)(2,1)S(1)}, u32[]{:S(2)}, u32[]{:S(2)}) %collective-permute-start.14) | collective-permute-done | bytes 165920 | tf_op jit(solution)/shard_map/ppermute | solution.py:33
  66.3 0.5 collective-permute-start.17
  66.9 0.4 collective-permute-start.19
  67.3 1.0 %collective-permute-start.20 = (bf16[216,384]{1,0:T(8,128)(2,1)S(1)}, bf16[216,384]{1,0:T(8,128)(2,1)S(1)}, u32[]{:S(2)}, u32[]{:S(2)}) collective-permute-start(bf16[216,384]{1,0:T(8,128)(2,1)S(1)} %collective-permute-done.14), channel_id=1, source_target_pairs={{0,4},{2,6},{4,0},{6,2},{8,12},{10,14},{12,8},{14,10},{16,20},{18,... | collective-permute-start | bytes 497672 | tf_op jit(solution)/shard_map/ppermute | solution.py:33
  68.3 1.1 %collective-permute-start.21 = (bf16[216,384]{1,0:T(8,128)(2,1)S(1)}, bf16[216,384]{1,0:T(8,128)(2,1)S(1)}, u32[]{:S(2)}, u32[]{:S(2)}) collective-permute-start(bf16[216,384]{1,0:T(8,128)(2,1)S(1)} %collective-permute-done.15), channel_id=1, source_target_pairs={{0,4},{2,6},{4,0},{6,2},{8,12},{10,14},{12,8},{14,10},{16,20},{18,... | collective-permute-start | bytes 497672 | tf_op jit(solution)/shard_map/ppermute | solution.py:33
  69.4 0.5 collective-permute-start.24
  69.9 0.1 copy-done.20
  70.1 0.5 copy-done.22
  70.5 2.6 %finish.2.refs_8_ = f32[3,9,192,384]{3,2,1,0:T(8,128)} custom-call(s32[1]{0:T(128)} %bitcast.refs_0_.me_ref, bf16[9,24,384]{2,1,0:T(8,128)(2,1)} %bitcast.38, bf16[9,24,384]{2,1,0:T(8,128)(2,1)} %bitcast.42, bf16[9,24,384]{2,1,0:T(8,128)(2,1)} %bitcast.41, bf16[9,24,384]{2,1,0:T(8,128)(2,1)} %bitcast.43, ...), custom_call_target="tpu_custom_call", output_to_operand_aliasing={{}: (9, {})} | custom-call | bytes 3981312 | tf_op jit(solution)/shard_map/finish/pallas_call | solution.py:479
  73.1 1.3 %collective-permute-done.20 = bf16[216,384]{1,0:T(8,128)(2,1)S(1)} collective-permute-done((bf16[216,384]{1,0:T(8,128)(2,1)S(1)}, bf16[216,384]{1,0:T(8,128)(2,1)S(1)}, u32[]{:S(2)}, u32[]{:S(2)}) %collective-permute-start.20) | collective-permute-done | bytes 165920 | tf_op jit(solution)/shard_map/ppermute | solution.py:33
  74.4 2.7 %collective-permute-done.21 = bf16[216,384]{1,0:T(8,128)(2,1)S(1)} collective-permute-done((bf16[216,384]{1,0:T(8,128)(2,1)S(1)}, bf16[216,384]{1,0:T(8,128)(2,1)S(1)}, u32[]{:S(2)}, u32[]{:S(2)}) %collective-permute-start.21) | collective-permute-done | bytes 165920 | tf_op jit(solution)/shard_map/ppermute | solution.py:33
  77.1 0.5 collective-permute-start.25
  77.6 0.9 %collective-permute-done.23 = bf16[216,384]{1,0:T(8,128)(2,1)S(1)} collective-permute-done((bf16[216,384]{1,0:T(8,128)(2,1)S(1)}, bf16[216,384]{1,0:T(8,128)(2,1)S(1)}, u32[]{:S(2)}, u32[]{:S(2)}) %collective-permute-start.23) | collective-permute-done | bytes 165920 | tf_op jit(solution)/shard_map/ppermute | solution.py:33
  78.5 0.2 collective-permute-done.25
  78.8 0.4 copy-done.23
  79.2 0.2 copy-done.24
  79.4 2.6 %finish.3 = f32[3,9,192,384]{3,2,1,0:T(8,128)} custom-call(s32[1]{0:T(128)} %bitcast.refs_0_.me_ref, bf16[9,24,384]{2,1,0:T(8,128)(2,1)} %bitcast.40, bf16[9,24,384]{2,1,0:T(8,128)(2,1)} %bitcast.44, bf16[9,24,384]{2,1,0:T(8,128)(2,1)} %bitcast.39, bf16[9,24,384]{2,1,0:T(8,128)(2,1)} %bitcast.45, ...), custom_call_target="tpu_custom_call", output_to_operand_aliasing={{}: (9, {})} | custom-call | bytes 3981312 | tf_op jit(solution)/shard_map/finish/pallas_call | solution.py:479
  (73 shorter events, 0.6 us)
Async XLA Ops:
  0.6 1.6 %copy-start = (bf16[2,2,64,2560]{3,2,1,0:T(8,128)(2,1)S(1)}, bf16[2,2,64,2560]{3,2,1,0:T(8,128)(2,1)}, u32[]{:S(2)}) copy-start(bf16[2,2,64,2560]{3,2,1,0:T(8,128)(2,1)} %param.6) | copy-start | bytes 3932164
  3.7 5.6 %collective-permute-start = (f32[64,256]{1,0:T(8,128)S(1)}, f32[64,256]{1,0:T(8,128)S(1)}, u32[]{:S(2)}, u32[]{:S(2)}) collective-permute-start(f32[64,256]{1,0:T(8,128)S(1)} %convolution_bitcast_fusion), channel_id=1, source_target_pairs={{0,1},{1,0},{2,3},{3,2},{4,5},{5,4},{6,7},{7,6},{8,9},{9,8},{10,11... | collective-permute-start | bytes 196616 | tf_op jit(solution)/shard_map/ppermute | solution.py:33
  6.7 12.9 %collective-permute-start.2 = (bf16[4,24,1024]{2,1,0:T(8,128)(2,1)S(1)}, bf16[4,24,1024]{2,1,0:T(8,128)(2,1)S(1)}, u32[]{:S(2)}, u32[]{:S(2)}) collective-permute-start(bf16[4,24,1024]{2,1,0:T(8,128)(2,1)S(1)} %pad_maximum_fusion), channel_id=1, source_target_pairs={{0,16},{2,18},{4,20},{6,22},{8,24},{10,26},{12,28},{14,30},{16,0},... | collective-permute-start | bytes 589832 | tf_op jit(solution)/shard_map/ppermute | solution.py:33
  11.4 8.1 %copy-start.25 = (bf16[16,1024]{1,0:T(8,128)(2,1)S(1)}, bf16[16,1024]{1,0:T(8,128)(2,1)}, u32[]{:S(2)}) copy-start(bf16[16,1024]{1,0:T(8,128)(2,1)} %unpatchify.1) | copy-start | bytes 98308
  11.4 18.4 %copy-start.26 = (f32[384]{0:T(512)S(1)}, f32[384]{0:T(512)}, u32[]{:S(2)}) copy-start(f32[384]{0:T(512)} %param.8) | copy-start | bytes 4612
  11.4 8.1 %collective-permute-start.1 = (bf16[16,1024]{1,0:T(8,128)(2,1)}, bf16[16,1024]{1,0:T(8,128)(2,1)S(1)}, u32[]{:S(2)}, u32[]{:S(2)}) collective-permute-start(bf16[16,1024]{1,0:T(8,128)(2,1)} %unpatchify.1), channel_id=1, source_target_pairs={{0,16},{2,18},{4,20},{6,22},{8,24},{10,26},{12,28},{14,30},{16,0},... | collective-permute-start | bytes 98312 | tf_op jit(solution)/shard_map/ppermute | solution.py:33
  19.7 11.3 %copy-start.1 = (bf16[2,40,1024]{2,1,0:T(8,128)(2,1)}, bf16[2,40,1024]{2,1,0:T(8,128)(2,1)S(1)}, u32[]{:S(2)}) copy-start(bf16[2,40,1024]{2,1,0:T(8,128)(2,1)S(1)} %get-tuple-element.30.refs_3_.refs_0_) | copy-start | bytes 491524
  19.7 7.3 %collective-permute-start.5 = (bf16[2,40,1024]{2,1,0:T(8,128)(2,1)S(1)}, bf16[2,40,1024]{2,1,0:T(8,128)(2,1)S(1)}, u32[]{:S(2)}, u32[]{:S(2)}) collective-permute-start(bf16[2,40,1024]{2,1,0:T(8,128)(2,1)S(1)} %get-tuple-element.62), channel_id=1, source_target_pairs={{0,12},{2,14},{4,8},{6,10},{8,4},{10,6},{12,0},{14,2},{16,28},{18,... | collective-permute-start | bytes 491528 | tf_op jit(solution)/shard_map/ppermute | solution.py:33
  21.5 7.9 %collective-permute-start.3 = (bf16[2,40,1024]{2,1,0:T(8,128)(2,1)S(1)}, bf16[2,40,1024]{2,1,0:T(8,128)(2,1)S(1)}, u32[]{:S(2)}, u32[]{:S(2)}) collective-permute-start(bf16[2,40,1024]{2,1,0:T(8,128)(2,1)S(1)} %get-tuple-element.63), channel_id=1, source_target_pairs={{0,4},{2,6},{4,0},{6,2},{8,12},{10,14},{12,8},{14,10},{16,20},{18,... | collective-permute-start | bytes 491528 | tf_op jit(solution)/shard_map/ppermute | solution.py:33
  22.0 7.4 %collective-permute-start.4 = (bf16[2,40,1024]{2,1,0:T(8,128)(2,1)S(1)}, bf16[2,40,1024]{2,1,0:T(8,128)(2,1)S(1)}, u32[]{:S(2)}, u32[]{:S(2)}) collective-permute-start(bf16[2,40,1024]{2,1,0:T(8,128)(2,1)S(1)} %get-tuple-element.64), channel_id=1, source_target_pairs={{0,8},{2,10},{4,12},{6,14},{8,0},{10,2},{12,4},{14,6},{16,24},{18,... | collective-permute-start | bytes 491528 | tf_op jit(solution)/shard_map/ppermute | solution.py:33
  23.2 7.3 %collective-permute-start.6 = (bf16[2,40,1024]{2,1,0:T(8,128)(2,1)S(1)}, bf16[2,40,1024]{2,1,0:T(8,128)(2,1)S(1)}, u32[]{:S(2)}, u32[]{:S(2)}) collective-permute-start(bf16[2,40,1024]{2,1,0:T(8,128)(2,1)S(1)} %get-tuple-element.30.refs_3_.refs_0_), channel_id=1, source_target_pairs={{0,2},{2,0},{4,6},{6,4},{8,10},{10,8},{12,14},{14,12},{16,18},{18,... | collective-permute-start | bytes 491528 | tf_op jit(solution)/shard_map/ppermute | solution.py:33
  27.0 4.0 %copy-start.3 = (bf16[2,40,1024]{2,1,0:T(8,128)(2,1)}, bf16[2,40,1024]{2,1,0:T(8,128)(2,1)S(1)}, u32[]{:S(2)}) copy-start(bf16[2,40,1024]{2,1,0:T(8,128)(2,1)S(1)} %collective-permute-done.5.refs_6_.refs_3_) | copy-start | bytes 491524
  27.0 3.5 %collective-permute-start.9 = (bf16[2,40,1024]{2,1,0:T(8,128)(2,1)S(1)}, bf16[2,40,1024]{2,1,0:T(8,128)(2,1)S(1)}, u32[]{:S(2)}, u32[]{:S(2)}) collective-permute-start(bf16[2,40,1024]{2,1,0:T(8,128)(2,1)S(1)} %collective-permute-done.5.refs_6_.refs_3_), channel_id=1, source_target_pairs={{0,2},{2,0},{4,6},{6,4},{8,10},{10,8},{12,14},{14,12},{16,18},{18,... | collective-permute-start | bytes 491528 | tf_op jit(solution)/shard_map/ppermute | solution.py:33
  29.4 1.6 %copy-start.4 = (bf16[2,40,1024]{2,1,0:T(8,128)(2,1)}, bf16[2,40,1024]{2,1,0:T(8,128)(2,1)S(1)}, u32[]{:S(2)}) copy-start(bf16[2,40,1024]{2,1,0:T(8,128)(2,1)S(1)} %collective-permute-done.3.refs_4_.refs_1_) | copy-start | bytes 491524
  29.4 1.4 %collective-permute-start.7 = (bf16[2,40,1024]{2,1,0:T(8,128)(2,1)S(1)}, bf16[2,40,1024]{2,1,0:T(8,128)(2,1)S(1)}, u32[]{:S(2)}, u32[]{:S(2)}) collective-permute-start(bf16[2,40,1024]{2,1,0:T(8,128)(2,1)S(1)} %collective-permute-done.3.refs_4_.refs_1_), channel_id=1, source_target_pairs={{0,2},{2,0},{4,6},{6,4},{8,10},{10,8},{12,14},{14,12},{16,18},{18,... | collective-permute-start | bytes 491528 | tf_op jit(solution)/shard_map/ppermute | solution.py:33
  29.4 1.6 %copy-start.5 = (bf16[2,40,1024]{2,1,0:T(8,128)(2,1)}, bf16[2,40,1024]{2,1,0:T(8,128)(2,1)S(1)}, u32[]{:S(2)}) copy-start(bf16[2,40,1024]{2,1,0:T(8,128)(2,1)S(1)} %collective-permute-done.4.refs_5_.refs_2_) | copy-start | bytes 491524
  29.4 1.6 %collective-permute-start.8 = (bf16[2,40,1024]{2,1,0:T(8,128)(2,1)S(1)}, bf16[2,40,1024]{2,1,0:T(8,128)(2,1)S(1)}, u32[]{:S(2)}, u32[]{:S(2)}) collective-permute-start(bf16[2,40,1024]{2,1,0:T(8,128)(2,1)S(1)} %collective-permute-done.4.refs_5_.refs_2_), channel_id=1, source_target_pairs={{0,2},{2,0},{4,6},{6,4},{8,10},{10,8},{12,14},{14,12},{16,18},{18,... | collective-permute-start | bytes 491528 | tf_op jit(solution)/shard_map/ppermute | solution.py:33
  30.5 0.7 copy-start.7
  43.7 1.7 %collective-permute-start.10 = (bf16[216,384]{1,0:T(8,128)(2,1)}, bf16[216,384]{1,0:T(8,128)(2,1)S(1)}, u32[]{:S(2)}, u32[]{:S(2)}) collective-permute-start(bf16[216,384]{1,0:T(8,128)(2,1)} %get-tuple-element.29), channel_id=1, source_target_pairs={{0,2},{2,0},{4,6},{6,4},{8,10},{10,8},{12,14},{14,12},{16,18},{18,... | collective-permute-start | bytes 497672 | tf_op jit(solution)/shard_map/ppermute | solution.py:33
  46.4 23.5 %copy-start.2 = (bf16[216,384]{1,0:T(8,128)(2,1)}, bf16[216,384]{1,0:T(8,128)(2,1)S(1)}, u32[]{:S(2)}) copy-start(bf16[216,384]{1,0:T(8,128)(2,1)S(1)} %add_convert_fusion) | copy-start | bytes 497668
  46.4 6.5 %collective-permute-start.11 = (bf16[216,384]{1,0:T(8,128)(2,1)S(1)}, bf16[216,384]{1,0:T(8,128)(2,1)S(1)}, u32[]{:S(2)}, u32[]{:S(2)}) collective-permute-start(bf16[216,384]{1,0:T(8,128)(2,1)S(1)} %add_convert_fusion), channel_id=1, source_target_pairs={{0,8},{2,10},{4,12},{6,14},{8,0},{10,2},{12,4},{14,6},{16,24},{18,... | collective-permute-start | bytes 497672 | tf_op jit(solution)/shard_map/ppermute | solution.py:33
  48.1 14.8 %collective-permute-start.15 = (bf16[216,384]{1,0:T(8,128)(2,1)S(1)}, bf16[216,384]{1,0:T(8,128)(2,1)S(1)}, u32[]{:S(2)}, u32[]{:S(2)}) collective-permute-start(bf16[216,384]{1,0:T(8,128)(2,1)S(1)} %add_convert_fusion), channel_id=1, source_target_pairs={{0,24},{2,26},{4,28},{6,30},{8,16},{10,18},{12,20},{14,22},{16,8},... | collective-permute-start | bytes 497672 | tf_op jit(solution)/shard_map/ppermute | solution.py:33
  51.2 15.0 %collective-permute-start.14 = (bf16[216,384]{1,0:T(8,128)(2,1)S(1)}, bf16[216,384]{1,0:T(8,128)(2,1)S(1)}, u32[]{:S(2)}, u32[]{:S(2)}) collective-permute-start(bf16[216,384]{1,0:T(8,128)(2,1)S(1)} %add_convert_fusion), channel_id=1, source_target_pairs={{0,16},{2,18},{4,20},{6,22},{8,24},{10,26},{12,28},{14,30},{16,0},... | collective-permute-start | bytes 497672 | tf_op jit(solution)/shard_map/ppermute | solution.py:33
  51.3 14.9 %collective-permute-start.12 = (bf16[216,384]{1,0:T(8,128)(2,1)S(1)}, bf16[216,384]{1,0:T(8,128)(2,1)S(1)}, u32[]{:S(2)}, u32[]{:S(2)}) collective-permute-start(bf16[216,384]{1,0:T(8,128)(2,1)S(1)} %add_convert_fusion), channel_id=1, source_target_pairs={{0,4},{2,6},{4,0},{6,2},{8,12},{10,14},{12,8},{14,10},{16,20},{18,... | collective-permute-start | bytes 497672 | tf_op jit(solution)/shard_map/ppermute | solution.py:33
  52.9 17.0 %copy-start.12 = (bf16[216,384]{1,0:T(8,128)(2,1)}, bf16[216,384]{1,0:T(8,128)(2,1)S(1)}, u32[]{:S(2)}) copy-start(bf16[216,384]{1,0:T(8,128)(2,1)S(1)} %collective-permute-done.11) | copy-start | bytes 497668
  52.9 13.3 %collective-permute-start.13 = (bf16[216,384]{1,0:T(8,128)(2,1)S(1)}, bf16[216,384]{1,0:T(8,128)(2,1)S(1)}, u32[]{:S(2)}, u32[]{:S(2)}) collective-permute-start(bf16[216,384]{1,0:T(8,128)(2,1)S(1)} %collective-permute-done.11), channel_id=1, source_target_pairs={{0,4},{2,6},{4,0},{6,2},{8,12},{10,14},{12,8},{14,10},{16,20},{18,... | collective-permute-start | bytes 497672 | tf_op jit(solution)/shard_map/ppermute | solution.py:33
  62.9 10.2 %copy-start.10 = (bf16[216,384]{1,0:T(8,128)(2,1)}, bf16[216,384]{1,0:T(8,128)(2,1)S(1)}, u32[]{:S(2)}) copy-start(bf16[216,384]{1,0:T(8,128)(2,1)S(1)} %collective-permute-done.15) | copy-start | bytes 497668
  66.2 6.9 %copy-start.11 = (bf16[216,384]{1,0:T(8,128)(2,1)}, bf16[216,384]{1,0:T(8,128)(2,1)S(1)}, u32[]{:S(2)}) copy-start(bf16[216,384]{1,0:T(8,128)(2,1)S(1)} %collective-permute-done.14) | copy-start | bytes 497668
  66.2 3.7 %copy-start.13 = (bf16[216,384]{1,0:T(8,128)(2,1)}, bf16[216,384]{1,0:T(8,128)(2,1)S(1)}, u32[]{:S(2)}) copy-start(bf16[216,384]{1,0:T(8,128)(2,1)S(1)} %collective-permute-done.12) | copy-start | bytes 497668
  66.2 3.7 %copy-start.14 = (bf16[216,384]{1,0:T(8,128)(2,1)}, bf16[216,384]{1,0:T(8,128)(2,1)S(1)}, u32[]{:S(2)}) copy-start(bf16[216,384]{1,0:T(8,128)(2,1)S(1)} %collective-permute-done.13) | copy-start | bytes 497668
  66.2 2.1 %collective-permute-start.16 = (bf16[216,384]{1,0:T(8,128)(2,1)S(1)}, bf16[216,384]{1,0:T(8,128)(2,1)S(1)}, u32[]{:S(2)}, u32[]{:S(2)}) collective-permute-start(bf16[216,384]{1,0:T(8,128)(2,1)S(1)} %add_convert_fusion), channel_id=1, source_target_pairs={{0,2},{2,0},{4,6},{6,4},{8,10},{10,8},{12,14},{14,12},{16,18},{18,... | collective-permute-start | bytes 497672 | tf_op jit(solution)/shard_map/ppermute | solution.py:33
  66.3 3.0 %collective-permute-start.17 = (bf16[216,384]{1,0:T(8,128)(2,1)S(1)}, bf16[216,384]{1,0:T(8,128)(2,1)S(1)}, u32[]{:S(2)}, u32[]{:S(2)}) collective-permute-start(bf16[216,384]{1,0:T(8,128)(2,1)S(1)} %collective-permute-done.12), channel_id=1, source_target_pairs={{0,2},{2,0},{4,6},{6,4},{8,10},{10,8},{12,14},{14,12},{16,18},{18,... | collective-permute-start | bytes 497672 | tf_op jit(solution)/shard_map/ppermute | solution.py:33
  66.8 2.6 %collective-permute-start.18 = (bf16[216,384]{1,0:T(8,128)(2,1)S(1)}, bf16[216,384]{1,0:T(8,128)(2,1)S(1)}, u32[]{:S(2)}, u32[]{:S(2)}) collective-permute-start(bf16[216,384]{1,0:T(8,128)(2,1)S(1)} %collective-permute-done.11), channel_id=1, source_target_pairs={{0,2},{2,0},{4,6},{6,4},{8,10},{10,8},{12,14},{14,12},{16,18},{18,... | collective-permute-start | bytes 497672 | tf_op jit(solution)/shard_map/ppermute | solution.py:33
  66.9 3.0 %collective-permute-start.19 = (bf16[216,384]{1,0:T(8,128)(2,1)S(1)}, bf16[216,384]{1,0:T(8,128)(2,1)S(1)}, u32[]{:S(2)}, u32[]{:S(2)}) collective-permute-start(bf16[216,384]{1,0:T(8,128)(2,1)S(1)} %collective-permute-done.13), channel_id=1, source_target_pairs={{0,2},{2,0},{4,6},{6,4},{8,10},{10,8},{12,14},{14,12},{16,18},{18,... | collective-permute-start | bytes 497672 | tf_op jit(solution)/shard_map/ppermute | solution.py:33
  67.3 7.1 %collective-permute-start.20 = (bf16[216,384]{1,0:T(8,128)(2,1)S(1)}, bf16[216,384]{1,0:T(8,128)(2,1)S(1)}, u32[]{:S(2)}, u32[]{:S(2)}) collective-permute-start(bf16[216,384]{1,0:T(8,128)(2,1)S(1)} %collective-permute-done.14), channel_id=1, source_target_pairs={{0,4},{2,6},{4,0},{6,2},{8,12},{10,14},{12,8},{14,10},{16,20},{18,... | collective-permute-start | bytes 497672 | tf_op jit(solution)/shard_map/ppermute | solution.py:33
  68.3 1.6 %copy-start.18 = (bf16[216,384]{1,0:T(8,128)(2,1)}, bf16[216,384]{1,0:T(8,128)(2,1)S(1)}, u32[]{:S(2)}) copy-start(bf16[216,384]{1,0:T(8,128)(2,1)S(1)} %collective-permute-done.16) | copy-start | bytes 497668
  68.3 8.8 %collective-permute-start.21 = (bf16[216,384]{1,0:T(8,128)(2,1)S(1)}, bf16[216,384]{1,0:T(8,128)(2,1)S(1)}, u32[]{:S(2)}, u32[]{:S(2)}) collective-permute-start(bf16[216,384]{1,0:T(8,128)(2,1)S(1)} %collective-permute-done.15), channel_id=1, source_target_pairs={{0,4},{2,6},{4,0},{6,2},{8,12},{10,14},{12,8},{14,10},{16,20},{18,... | collective-permute-start | bytes 497672 | tf_op jit(solution)/shard_map/ppermute | solution.py:33
  69.4 0.7 copy-start.20
  69.4 8.3 %collective-permute-start.22 = (bf16[216,384]{1,0:T(8,128)(2,1)S(1)}, bf16[216,384]{1,0:T(8,128)(2,1)S(1)}, u32[]{:S(2)}, u32[]{:S(2)}) collective-permute-start(bf16[216,384]{1,0:T(8,128)(2,1)S(1)} %collective-permute-done.14), channel_id=1, source_target_pairs={{0,2},{2,0},{4,6},{6,4},{8,10},{10,8},{12,14},{14,12},{16,18},{18,... | collective-permute-start | bytes 497672 | tf_op jit(solution)/shard_map/ppermute | solution.py:33
  69.4 0.7 copy-start.21
  69.4 8.2 %collective-permute-start.24 = (bf16[216,384]{1,0:T(8,128)(2,1)S(1)}, bf16[216,384]{1,0:T(8,128)(2,1)S(1)}, u32[]{:S(2)}, u32[]{:S(2)}) collective-permute-start(bf16[216,384]{1,0:T(8,128)(2,1)S(1)} %collective-permute-done.15), channel_id=1, source_target_pairs={{0,2},{2,0},{4,6},{6,4},{8,10},{10,8},{12,14},{14,12},{16,18},{18,... | collective-permute-start | bytes 497672 | tf_op jit(solution)/shard_map/ppermute | solution.py:33
  74.4 4.3 %copy-start.15 = (bf16[216,384]{1,0:T(8,128)(2,1)}, bf16[216,384]{1,0:T(8,128)(2,1)S(1)}, u32[]{:S(2)}) copy-start(bf16[216,384]{1,0:T(8,128)(2,1)S(1)} %collective-permute-done.20) | copy-start | bytes 497668
  77.1 1.6 %copy-start.16 = (bf16[216,384]{1,0:T(8,128)(2,1)}, bf16[216,384]{1,0:T(8,128)(2,1)S(1)}, u32[]{:S(2)}) copy-start(bf16[216,384]{1,0:T(8,128)(2,1)S(1)} %collective-permute-done.21) | copy-start | bytes 497668
  77.1 1.4 %collective-permute-start.23 = (bf16[216,384]{1,0:T(8,128)(2,1)S(1)}, bf16[216,384]{1,0:T(8,128)(2,1)S(1)}, u32[]{:S(2)}, u32[]{:S(2)}) collective-permute-start(bf16[216,384]{1,0:T(8,128)(2,1)S(1)} %collective-permute-done.20), channel_id=1, source_target_pairs={{0,2},{2,0},{4,6},{6,4},{8,10},{10,8},{12,14},{14,12},{16,18},{18,... | collective-permute-start | bytes 497672 | tf_op jit(solution)/shard_map/ppermute | solution.py:33
  77.1 1.6 %collective-permute-start.25 = (bf16[216,384]{1,0:T(8,128)(2,1)S(1)}, bf16[216,384]{1,0:T(8,128)(2,1)S(1)}, u32[]{:S(2)}, u32[]{:S(2)}) collective-permute-start(bf16[216,384]{1,0:T(8,128)(2,1)S(1)} %collective-permute-done.21), channel_id=1, source_target_pairs={{0,2},{2,0},{4,6},{6,4},{8,10},{10,8},{12,14},{14,12},{16,18},{18,... | collective-permute-start | bytes 497672 | tf_op jit(solution)/shard_map/ppermute | solution.py:33
  77.6 1.1 %copy-start.17 = (bf16[216,384]{1,0:T(8,128)(2,1)}, bf16[216,384]{1,0:T(8,128)(2,1)S(1)}, u32[]{:S(2)}) copy-start(bf16[216,384]{1,0:T(8,128)(2,1)S(1)} %collective-permute-done.22) | copy-start | bytes 497668
  77.6 1.1 %copy-start.19 = (bf16[216,384]{1,0:T(8,128)(2,1)}, bf16[216,384]{1,0:T(8,128)(2,1)S(1)}, u32[]{:S(2)}) copy-start(bf16[216,384]{1,0:T(8,128)(2,1)S(1)} %collective-permute-done.24) | copy-start | bytes 497668
  78.5 0.7 copy-start.23
  (5 other events, 3.3 us)
